TPU v7x, 32 devices: a whole 2x2x4 slice. The times are simulated.
32 devices in a mesh: tm: 8 (over y, x, core), space: 4 (over z).
Axes of the slice: x: 2, y: 2, z: 4, core: 2. Of those that a mesh axis runs over, the one named last changes fastest.
Arguments:
- start_block: float32 [16, 32, 8192], P('tm', None, 'space'), as said below
- stiffness_tiles: float32 [16, 320, 128, 128], P('tm', 'space'), as said below
- tile_columns: int32 [16, 320], P('tm', 'space'), may hold values from 0 to 63, as said below
Outputs:
- ritz_basis: float32 [16, 32, 8192], P('tm', None, 'space')
- first_basis: float32 [16, 32, 8192], P('tm', None, 'space')
- ritz_matrix: float32 [32, 32], replicated
Inputs may be any that keep to these rules, and one draw needn't show every extreme that they name: `tile_columns`: in every slice, block row r has its 5 tiles listed together in row order; the first names column block r, the others distinct column blocks (r + o) mod 64 with 0 < |o| <= 8; in every slice some block row has o = -8 and o = 8. `stiffness_tiles`: real entries. `start_block`: real entries.
All inputs are finite; a program needn't handle non-finite values.
Results may differ from a plain program's by a relative error of at most 0.00018.
Values sent between devices are 32-bit elements; how exact they have to be, the bound alone decides.
No kernel may reach another device: no remote copies, remote signals or barrier semaphores. Data moves between devices by JAX's collectives and lax.ppermute only.
A program may use at most 192 MiB of HBM per device.

v0:
```python
import jax
import jax.numpy as jnp
from jax import lax
from jax.sharding import PartitionSpec as P

TILE = 128
TPR = 5
HB = 8


CENTER = 6.5
RADIUS = 3.5
INFLATION_FACTOR = 0.8
accurate = lax.Precision.HIGHEST


def with_halo(cells, sides, width, closed):
    for axis, dim in sides:
        count = lax.axis_size(axis)
        ends = count if closed else count - 1
        head = lax.slice_in_dim(cells, 0, width, axis=dim)
        tail = lax.slice_in_dim(cells, cells.shape[dim] - width, cells.shape[dim], axis=dim)
        cells = jnp.concatenate(
            [
                lax.ppermute(tail, axis, [(i, (i + 1) % count) for i in range(ends)]),
                cells,
                lax.ppermute(head, axis, [((i + 1) % count, i) for i in range(ends)]),
            ],
            axis=dim,
        )
    return cells


def spatial_component(wide_vectors, tile_groups, column_groups):
    slices, width, extended_points = wide_vectors.shape
    wide_blocks = extended_points // TILE
    out_blocks = tile_groups.shape[1] // TPR

    def one_slice(slice_vec, tile_set, col_list):
        picked = jnp.take(slice_vec.reshape(width, wide_blocks, TILE), col_list, axis=1)
        products = jnp.einsum("nrc,knc->knr", tile_set, picked, precision=accurate)
        return (
            products.reshape(width, out_blocks, TPR, TILE)
            .sum(axis=2)
            .reshape(width, out_blocks * TILE)
        )

    return jax.vmap(one_slice)(wide_vectors, tile_groups, column_groups)


def temporal_component(vectors, degree):
    near_slices = with_halo(vectors, (("tm", 0),), 1, False)
    return degree[:, None, None] * vectors - near_slices[:-2] - near_slices[2:]


def apply_operator(vectors, tile_groups, column_groups, degree):
    extended_points = with_halo(vectors, (("space", 2),), HB * TILE, True)
    return spatial_component(
        extended_points, tile_groups, column_groups
    ) + INFLATION_FACTOR * temporal_component(vectors, degree)


def chebyshev_filter(vectors, operator):
    previous = vectors
    current = (operator(vectors) - CENTER * vectors) / RADIUS
    for step in range(2):
        following = 2.0 * (operator(current) - CENTER * current) / RADIUS - previous
        previous, current = (current, following)
    return current


def gram_terms(left_block, right_block):
    return jnp.einsum("sjp,skp->jk", left_block, right_block, precision=accurate)


def inverse_factor(gram_matrix):
    cholesky_factor = jnp.linalg.cholesky(gram_matrix)
    identity = jnp.eye(gram_matrix.shape[0], dtype=jnp.float32)
    return lax.linalg.triangular_solve(cholesky_factor, identity, left_side=True, lower=True)


def mix_vectors(matrix, vectors):
    return jnp.einsum("jk,skp->sjp", matrix, vectors, precision=accurate)


def body(start_block, stiffness_tiles, tile_columns):
    slices = start_block.shape[0]
    local_points = start_block.shape[2]
    local_blocks = local_points // TILE
    first_block = lax.axis_index("space") * local_blocks
    blocks_all = lax.axis_size("space") * local_blocks
    column_groups = (tile_columns - first_block + HB) % blocks_all
    count_all = slices * local_points * lax.axis_size("tm") * lax.axis_size("space")
    slice_index = lax.axis_index("tm") * slices + jnp.arange(slices, dtype=jnp.int32)
    last_slice = lax.axis_size("tm") * slices - 1
    degree = (
        2.0
        - (slice_index == 0).astype(jnp.float32)
        - (slice_index == last_slice).astype(jnp.float32)
    )

    def operator(vectors):
        return apply_operator(vectors, stiffness_tiles, column_groups, degree)

    def run_filter(vectors):
        return chebyshev_filter(vectors, operator)

    filtered = run_filter(start_block)
    first_gram = lax.psum(gram_terms(filtered, filtered), ("tm", "space")) / count_all
    first_basis = mix_vectors(inverse_factor(first_gram), filtered)
    second = run_filter(first_basis)
    second_gram = lax.psum(gram_terms(second, second), ("tm", "space")) / count_all
    ritz_basis = mix_vectors(inverse_factor(second_gram), second)
    image_block = operator(ritz_basis)
    ritz_matrix = lax.psum(gram_terms(ritz_basis, image_block), ("tm", "space")) / count_all
    return (ritz_basis, first_basis, ritz_matrix)


def solution(mesh):
    placed = (P("tm", None, "space"), P("tm", "space", None, None), P("tm", "space"))
    return jax.shard_map(
        body,
        mesh=mesh,
        in_specs=placed,
        out_specs=(P("tm", None, "space"), P("tm", None, "space"), P()),
        check_vma=False,
    )
```

profile of v0, /device:TPU:0, one launch (start us, length us, event | category | flops | bytes accessed | tf_op | source)
XLA Modules:
  0.0 426.9 jit_solution(2295299034075395820)
XLA Ops:
  1.7 3.1 collective-permute-start
  14.0 4.2 collective-permute-done.1
  19.3 3.8 gather_fusion
  23.1 19.4 %fusion.12 = f32[2,80,32,128]{3,2,1,0:T(8,128)S(1)} fusion(f32[2,80,128,128]{3,2,1,0:T(8,128)} %param.9, f32[2,80,32,128]{3,2,1,0:T(8,128)} %bitcast.210, pred[2,80]{1,0:T(4,128)(4,1)S(1)} %get-tuple-element.22), kind=kOutput, calls=%fused_computation.19 | convolution fusion | flops 1007288320 | bytes 15728800 | tf_op jit(solution)/shard_map/vmap(nrc,knc->knr)/dot_general | solution.py:41
  51.9 4.4 %collective-permute-done.4 = f32[2,32,1024]{2,1,0:T(8,128)S(1)} collective-permute-done((f32[2,32,1024]{2,1,0:T(8,128)S(1)}, f32[2,32,1024]{2,1,0:T(8,128)S(1)}, u32[]{:S(2)}, u32[]{:S(2)}) %collective-permute-start.4) | collective-permute-done | bytes 262176 | tf_op jit(solution)/shard_map/ppermute | solution.py:25
  56.3 3.6 collective-permute-done.5
  60.1 3.8 gather_fusion.1
  63.9 20.5 %fusion.10 = f32[2,80,32,128]{3,2,1,0:T(8,128)} fusion(f32[2,80,128,128]{3,2,1,0:T(8,128)} %param.9, f32[2,80,32,128]{3,2,1,0:T(8,128)} %bitcast.211, pred[2,80]{1,0:T(4,128)(4,1)S(1)} %get-tuple-element.22), kind=kOutput, calls=%fused_computation.17 | convolution fusion | flops 1007288320 | bytes 15728800 | tf_op jit(solution)/shard_map/vmap(nrc,knc->knr)/dot_general | solution.py:41
  88.1 3.5 collective-permute-start.9
  94.5 4.3 %collective-permute-done.8 = f32[2,32,1024]{2,1,0:T(8,128)S(1)} collective-permute-done((f32[2,32,1024]{2,1,0:T(8,128)S(1)}, f32[2,32,1024]{2,1,0:T(8,128)S(1)}, u32[]{:S(2)}, u32[]{:S(2)}) %collective-permute-start.8) | collective-permute-done | bytes 262176 | tf_op jit(solution)/shard_map/ppermute | solution.py:25
  101.4 3.8 gather_fusion.2
  105.2 20.5 %fusion.8 = f32[2,80,32,128]{3,2,1,0:T(8,128)} fusion(f32[2,80,128,128]{3,2,1,0:T(8,128)} %param.9, f32[2,80,32,128]{3,2,1,0:T(8,128)} %bitcast.212, pred[2,80]{1,0:T(4,128)(4,1)S(1)} %get-tuple-element.22), kind=kOutput, calls=%fused_computation.15 | convolution fusion | flops 1007288320 | bytes 15728800 | tf_op jit(solution)/shard_map/vmap(nrc,knc->knr)/dot_general | solution.py:41
  128.6 40.3 %psum.21 = f32[32,32]{0,1:T(8,128)S(1)} all-reduce(f32[32,32]{0,1:T(8,128)S(1)} %convolution_bitcast_fusion.6), channel_id=1, replica_groups=mesh['tm'=8,'space'=4] {'tm','space'}, use_global_device_ids=true, to_apply=%region_3.5 | all-reduce | flops 1024 | bytes 8192 | tf_op jit(solution)/shard_map/psum | solution.py:109
  169.0 2.9 cholesky.44
  177.1 3.3 collective-permute-start.13
  189.9 3.8 gather_fusion.3
  193.6 19.4 %fusion.6 = f32[2,80,32,128]{3,2,1,0:T(8,128)S(1)} fusion(f32[2,80,128,128]{3,2,1,0:T(8,128)} %param.9, f32[2,80,32,128]{3,2,1,0:T(8,128)} %bitcast.213, pred[2,80]{1,0:T(4,128)(4,1)S(1)} %get-tuple-element.22), kind=kOutput, calls=%fused_computation.13 | convolution fusion | flops 1007288320 | bytes 15728800 | tf_op jit(solution)/shard_map/vmap(nrc,knc->knr)/dot_general | solution.py:41
  222.4 4.4 %collective-permute-done.16 = f32[2,32,1024]{2,1,0:T(8,128)S(1)} collective-permute-done((f32[2,32,1024]{2,1,0:T(8,128)S(1)}, f32[2,32,1024]{2,1,0:T(8,128)S(1)}, u32[]{:S(2)}, u32[]{:S(2)}) %collective-permute-start.16) | collective-permute-done | bytes 262176 | tf_op jit(solution)/shard_map/ppermute | solution.py:25
  229.6 3.8 gather_fusion.4
  233.3 20.5 %fusion.4 = f32[2,80,32,128]{3,2,1,0:T(8,128)} fusion(f32[2,80,128,128]{3,2,1,0:T(8,128)} %param.9, f32[2,80,32,128]{3,2,1,0:T(8,128)} %bitcast.214, pred[2,80]{1,0:T(4,128)(4,1)S(1)} %get-tuple-element.22), kind=kOutput, calls=%fused_computation.11 | convolution fusion | flops 1007288320 | bytes 15728800 | tf_op jit(solution)/shard_map/vmap(nrc,knc->knr)/dot_general | solution.py:41
  258.0 3.0 collective-permute-start.21
  263.9 4.3 %collective-permute-done.20 = f32[2,32,1024]{2,1,0:T(8,128)S(1)} collective-permute-done((f32[2,32,1024]{2,1,0:T(8,128)S(1)}, f32[2,32,1024]{2,1,0:T(8,128)S(1)}, u32[]{:S(2)}, u32[]{:S(2)}) %collective-permute-start.20) | collective-permute-done | bytes 262176 | tf_op jit(solution)/shard_map/ppermute | solution.py:25
  268.3 3.2 collective-permute-done.21
  271.7 3.8 gather_fusion.5
  275.4 20.5 %fusion.2 = f32[2,80,32,128]{3,2,1,0:T(8,128)} fusion(f32[2,80,128,128]{3,2,1,0:T(8,128)} %param.9, f32[2,80,32,128]{3,2,1,0:T(8,128)} %bitcast.215, pred[2,80]{1,0:T(4,128)(4,1)S(1)} %get-tuple-element.22), kind=kOutput, calls=%fused_computation.9 | convolution fusion | flops 1007288320 | bytes 15728800 | tf_op jit(solution)/shard_map/vmap(nrc,knc->knr)/dot_general | solution.py:41
  298.8 39.3 %psum.22 = f32[32,32]{0,1:T(8,128)S(1)} all-reduce(f32[32,32]{0,1:T(8,128)S(1)} %convolution_bitcast_fusion.4), channel_id=1, replica_groups=mesh['tm'=8,'space'=4] {'tm','space'}, use_global_device_ids=true, to_apply=%region_9.13 | all-reduce | flops 1024 | bytes 8192 | tf_op jit(solution)/shard_map/psum | solution.py:112
  338.2 2.9 cholesky.55
  353.3 3.5 collective-permute-done.24
  356.9 2.8 collective-permute-done.25
  359.8 3.8 gather_fusion.6
  363.6 19.4 %fusion = f32[2,80,32,128]{3,2,1,0:T(8,128)S(1)} fusion(f32[2,80,128,128]{3,2,1,0:T(8,128)} %param.9, f32[2,80,32,128]{3,2,1,0:T(8,128)} %bitcast.209, pred[2,80]{1,0:T(4,128)(4,1)S(1)} %get-tuple-element.22), kind=kOutput, calls=%fused_computation.7 | convolution fusion | flops 1007288320 | bytes 15728800 | tf_op jit(solution)/shard_map/vmap(nrc,knc->knr)/dot_general | solution.py:41
  386.0 39.8 %psum.23 = f32[32,32]{0,1:T(8,128)S(1)} all-reduce(f32[32,32]{0,1:T(8,128)S(1)} %convolution_bitcast_fusion.2), channel_id=1, replica_groups=mesh['tm'=8,'space'=4] {'tm','space'}, use_global_device_ids=true, to_apply=%region_11.15 | all-reduce | flops 1024 | bytes 8192 | tf_op jit(solution)/shard_map/psum | solution.py:115
  (111 shorter events, 85.8 us)
Async XLA Ops:
  1.7 12.3 %collective-permute-start = (f32[2,32,1024]{2,1,0:T(8,128)S(1)}, f32[2,32,1024]{2,1,0:T(8,128)S(1)}, u32[]{:S(2)}, u32[]{:S(2)}) collective-permute-start(f32[2,32,1024]{2,1,0:T(8,128)S(1)} %get-tuple-element.48), channel_id=1, source_target_pairs={{0,1},{1,2},{2,3},{3,0},{4,5},{5,6},{6,7},{7,4},{8,9},{9,10},{10,1... | collective-permute-start | bytes 786440 | tf_op jit(solution)/shard_map/ppermute | solution.py:25
  4.8 13.4 %collective-permute-start.1 = (f32[2,32,1024]{2,1,0:T(8,128)S(1)}, f32[2,32,1024]{2,1,0:T(8,128)S(1)}, u32[]{:S(2)}, u32[]{:S(2)}) collective-permute-start(f32[2,32,1024]{2,1,0:T(8,128)S(1)} %get-tuple-element.49), channel_id=1, source_target_pairs={{1,0},{2,1},{3,2},{0,3},{5,4},{6,5},{7,6},{4,7},{9,8},{10,9},{11,1... | collective-permute-start | bytes 786440 | tf_op jit(solution)/shard_map/ppermute | solution.py:27
  8.6 35.1 %collective-permute-start.2 = (f32[1,32,2048]{2,1,0:T(8,128)}, f32[1,32,2048]{2,1,0:T(8,128)}, u32[]{:S(2)}, u32[]{:S(2)}) collective-permute-start(f32[1,32,2048]{2,1,0:T(8,128)} %get-tuple-element.50), channel_id=1, source_target_pairs={{0,4},{4,8},{8,12},{12,16},{16,20},{20,24},{24,28},{1,5},{5,9},{9,... | collective-permute-start | bytes 786440 | tf_op jit(solution)/shard_map/ppermute | solution.py:25
  10.8 32.9 %collective-permute-start.3 = (f32[1,32,2048]{2,1,0:T(8,128)S(1)}, f32[1,32,2048]{2,1,0:T(8,128)}, u32[]{:S(2)}, u32[]{:S(2)}) collective-permute-start(f32[1,32,2048]{2,1,0:T(8,128)S(1)} %get-tuple-element.51), channel_id=1, source_target_pairs={{4,0},{8,4},{12,8},{16,12},{20,16},{24,20},{28,24},{5,1},{9,5},{13... | collective-permute-start | bytes 786440 | tf_op jit(solution)/shard_map/ppermute | solution.py:27
  42.5 1.2 copy-start.2
  45.2 11.1 %collective-permute-start.4 = (f32[2,32,1024]{2,1,0:T(8,128)S(1)}, f32[2,32,1024]{2,1,0:T(8,128)S(1)}, u32[]{:S(2)}, u32[]{:S(2)}) collective-permute-start(f32[2,32,1024]{2,1,0:T(8,128)S(1)} %get-tuple-element.46), channel_id=1, source_target_pairs={{0,1},{1,2},{2,3},{3,0},{4,5},{5,6},{6,7},{7,4},{8,9},{9,10},{10,1... | collective-permute-start | bytes 786440 | tf_op jit(solution)/shard_map/ppermute | solution.py:25
  46.4 13.6 %collective-permute-start.5 = (f32[2,32,1024]{2,1,0:T(8,128)S(1)}, f32[2,32,1024]{2,1,0:T(8,128)S(1)}, u32[]{:S(2)}, u32[]{:S(2)}) collective-permute-start(f32[2,32,1024]{2,1,0:T(8,128)S(1)} %get-tuple-element.47), channel_id=1, source_target_pairs={{1,0},{2,1},{3,2},{0,3},{5,4},{6,5},{7,6},{4,7},{9,8},{10,9},{11,1... | collective-permute-start | bytes 786440 | tf_op jit(solution)/shard_map/ppermute | solution.py:27
  49.1 37.3 %collective-permute-start.6 = (f32[1,32,2048]{2,1,0:T(8,128)S(1)}, f32[1,32,2048]{2,1,0:T(8,128)S(1)}, u32[]{:S(2)}, u32[]{:S(2)}) collective-permute-start(f32[1,32,2048]{2,1,0:T(8,128)S(1)} %get-tuple-element.44), channel_id=1, source_target_pairs={{0,4},{4,8},{8,12},{12,16},{16,20},{20,24},{24,28},{1,5},{5,9},{9,... | collective-permute-start | bytes 786440 | tf_op jit(solution)/shard_map/ppermute | solution.py:25
  50.4 36.0 %collective-permute-start.7 = (f32[1,32,2048]{2,1,0:T(8,128)S(1)}, f32[1,32,2048]{2,1,0:T(8,128)}, u32[]{:S(2)}, u32[]{:S(2)}) collective-permute-start(f32[1,32,2048]{2,1,0:T(8,128)S(1)} %get-tuple-element.45), channel_id=1, source_target_pairs={{4,0},{8,4},{12,8},{16,12},{20,16},{24,20},{28,24},{5,1},{9,5},{13... | collective-permute-start | bytes 786440 | tf_op jit(solution)/shard_map/ppermute | solution.py:27
  87.7 11.1 %collective-permute-start.8 = (f32[2,32,1024]{2,1,0:T(8,128)S(1)}, f32[2,32,1024]{2,1,0:T(8,128)S(1)}, u32[]{:S(2)}, u32[]{:S(2)}) collective-permute-start(f32[2,32,1024]{2,1,0:T(8,128)S(1)} %get-tuple-element.42), channel_id=1, source_target_pairs={{0,1},{1,2},{2,3},{3,0},{4,5},{5,6},{6,7},{7,4},{8,9},{9,10},{10,1... | collective-permute-start | bytes 786440 | tf_op jit(solution)/shard_map/ppermute | solution.py:25
  88.1 13.1 %collective-permute-start.9 = (f32[2,32,1024]{2,1,0:T(8,128)S(1)}, f32[2,32,1024]{2,1,0:T(8,128)S(1)}, u32[]{:S(2)}, u32[]{:S(2)}) collective-permute-start(f32[2,32,1024]{2,1,0:T(8,128)S(1)} %get-tuple-element.43), channel_id=1, source_target_pairs={{1,0},{2,1},{3,2},{0,3},{5,4},{6,5},{7,6},{4,7},{9,8},{10,9},{11,1... | collective-permute-start | bytes 786440 | tf_op jit(solution)/shard_map/ppermute | solution.py:27
  91.6 36.1 %collective-permute-start.10 = (f32[1,32,2048]{2,1,0:T(8,128)S(1)}, f32[1,32,2048]{2,1,0:T(8,128)S(1)}, u32[]{:S(2)}, u32[]{:S(2)}) collective-permute-start(f32[1,32,2048]{2,1,0:T(8,128)S(1)} %get-tuple-element.40), channel_id=1, source_target_pairs={{0,4},{4,8},{8,12},{12,16},{16,20},{20,24},{24,28},{1,5},{5,9},{9,... | collective-permute-start | bytes 786440 | tf_op jit(solution)/shard_map/ppermute | solution.py:25
  93.0 34.8 %collective-permute-start.11 = (f32[1,32,2048]{2,1,0:T(8,128)S(1)}, f32[1,32,2048]{2,1,0:T(8,128)S(1)}, u32[]{:S(2)}, u32[]{:S(2)}) collective-permute-start(f32[1,32,2048]{2,1,0:T(8,128)S(1)} %get-tuple-element.41), channel_id=1, source_target_pairs={{4,0},{8,4},{12,8},{16,12},{20,16},{24,20},{28,24},{5,1},{9,5},{13... | collective-permute-start | bytes 786440 | tf_op jit(solution)/shard_map/ppermute | solution.py:27
  176.5 79.4 %copy-start.1 = (f32[2,32,2048]{2,1,0:T(8,128)}, f32[2,32,2048]{2,1,0:T(8,128)S(1)}, u32[]{:S(2)}) copy-start(f32[2,32,2048]{2,1,0:T(8,128)S(1)} %convolution_bitcast_fusion.1) | copy-start | bytes 1572868
  176.6 11.1 %collective-permute-start.12 = (f32[2,32,1024]{2,1,0:T(8,128)S(1)}, f32[2,32,1024]{2,1,0:T(8,128)S(1)}, u32[]{:S(2)}, u32[]{:S(2)}) collective-permute-start(f32[2,32,1024]{2,1,0:T(8,128)S(1)} %get-tuple-element.36), channel_id=1, source_target_pairs={{0,1},{1,2},{2,3},{3,0},{4,5},{5,6},{6,7},{7,4},{8,9},{9,10},{10,1... | collective-permute-start | bytes 786440 | tf_op jit(solution)/shard_map/ppermute | solution.py:25
  177.1 12.6 %collective-permute-start.13 = (f32[2,32,1024]{2,1,0:T(8,128)S(1)}, f32[2,32,1024]{2,1,0:T(8,128)S(1)}, u32[]{:S(2)}, u32[]{:S(2)}) collective-permute-start(f32[2,32,1024]{2,1,0:T(8,128)S(1)} %get-tuple-element.37), channel_id=1, source_target_pairs={{1,0},{2,1},{3,2},{0,3},{5,4},{6,5},{7,6},{4,7},{9,8},{10,9},{11,1... | collective-permute-start | bytes 786440 | tf_op jit(solution)/shard_map/ppermute | solution.py:27
  181.2 33.0 %collective-permute-start.14 = (f32[1,32,2048]{2,1,0:T(8,128)}, f32[1,32,2048]{2,1,0:T(8,128)}, u32[]{:S(2)}, u32[]{:S(2)}) collective-permute-start(f32[1,32,2048]{2,1,0:T(8,128)} %get-tuple-element.38), channel_id=1, source_target_pairs={{0,4},{4,8},{8,12},{12,16},{16,20},{20,24},{24,28},{1,5},{5,9},{9,... | collective-permute-start | bytes 786440 | tf_op jit(solution)/shard_map/ppermute | solution.py:25
  183.2 31.0 %collective-permute-start.15 = (f32[1,32,2048]{2,1,0:T(8,128)S(1)}, f32[1,32,2048]{2,1,0:T(8,128)}, u32[]{:S(2)}, u32[]{:S(2)}) collective-permute-start(f32[1,32,2048]{2,1,0:T(8,128)S(1)} %get-tuple-element.39), channel_id=1, source_target_pairs={{4,0},{8,4},{12,8},{16,12},{20,16},{24,20},{28,24},{5,1},{9,5},{13... | collective-permute-start | bytes 786440 | tf_op jit(solution)/shard_map/ppermute | solution.py:27
  215.7 11.1 %collective-permute-start.16 = (f32[2,32,1024]{2,1,0:T(8,128)S(1)}, f32[2,32,1024]{2,1,0:T(8,128)S(1)}, u32[]{:S(2)}, u32[]{:S(2)}) collective-permute-start(f32[2,32,1024]{2,1,0:T(8,128)S(1)} %get-tuple-element.34), channel_id=1, source_target_pairs={{0,1},{1,2},{2,3},{3,0},{4,5},{5,6},{6,7},{7,4},{8,9},{9,10},{10,1... | collective-permute-start | bytes 786440 | tf_op jit(solution)/shard_map/ppermute | solution.py:25
  216.9 12.5 %collective-permute-start.17 = (f32[2,32,1024]{2,1,0:T(8,128)S(1)}, f32[2,32,1024]{2,1,0:T(8,128)S(1)}, u32[]{:S(2)}, u32[]{:S(2)}) collective-permute-start(f32[2,32,1024]{2,1,0:T(8,128)S(1)} %get-tuple-element.35), channel_id=1, source_target_pairs={{1,0},{2,1},{3,2},{0,3},{5,4},{6,5},{7,6},{4,7},{9,8},{10,9},{11,1... | collective-permute-start | bytes 786440 | tf_op jit(solution)/shard_map/ppermute | solution.py:27
  219.6 36.3 %collective-permute-start.18 = (f32[1,32,2048]{2,1,0:T(8,128)S(1)}, f32[1,32,2048]{2,1,0:T(8,128)S(1)}, u32[]{:S(2)}, u32[]{:S(2)}) collective-permute-start(f32[1,32,2048]{2,1,0:T(8,128)S(1)} %get-tuple-element.32), channel_id=1, source_target_pairs={{0,4},{4,8},{8,12},{12,16},{16,20},{20,24},{24,28},{1,5},{5,9},{9,... | collective-permute-start | bytes 786440 | tf_op jit(solution)/shard_map/ppermute | solution.py:25
  220.9 35.0 %collective-permute-start.19 = (f32[1,32,2048]{2,1,0:T(8,128)S(1)}, f32[1,32,2048]{2,1,0:T(8,128)}, u32[]{:S(2)}, u32[]{:S(2)}) collective-permute-start(f32[1,32,2048]{2,1,0:T(8,128)S(1)} %get-tuple-element.33), channel_id=1, source_target_pairs={{4,0},{8,4},{12,8},{16,12},{20,16},{24,20},{28,24},{5,1},{9,5},{13... | collective-permute-start | bytes 786440 | tf_op jit(solution)/shard_map/ppermute | solution.py:27
  257.2 11.1 %collective-permute-start.20 = (f32[2,32,1024]{2,1,0:T(8,128)S(1)}, f32[2,32,1024]{2,1,0:T(8,128)S(1)}, u32[]{:S(2)}, u32[]{:S(2)}) collective-permute-start(f32[2,32,1024]{2,1,0:T(8,128)S(1)} %get-tuple-element.30), channel_id=1, source_target_pairs={{0,1},{1,2},{2,3},{3,0},{4,5},{5,6},{6,7},{7,4},{8,9},{9,10},{10,1... | collective-permute-start | bytes 786440 | tf_op jit(solution)/shard_map/ppermute | solution.py:25
  258.0 13.5 %collective-permute-start.21 = (f32[2,32,1024]{2,1,0:T(8,128)S(1)}, f32[2,32,1024]{2,1,0:T(8,128)S(1)}, u32[]{:S(2)}, u32[]{:S(2)}) collective-permute-start(f32[2,32,1024]{2,1,0:T(8,128)S(1)} %get-tuple-element.31), channel_id=1, source_target_pairs={{1,0},{2,1},{3,2},{0,3},{5,4},{6,5},{7,6},{4,7},{9,8},{10,9},{11,1... | collective-permute-start | bytes 786440 | tf_op jit(solution)/shard_map/ppermute | solution.py:27
  261.1 36.9 %collective-permute-start.22 = (f32[1,32,2048]{2,1,0:T(8,128)S(1)}, f32[1,32,2048]{2,1,0:T(8,128)S(1)}, u32[]{:S(2)}, u32[]{:S(2)}) collective-permute-start(f32[1,32,2048]{2,1,0:T(8,128)S(1)} %get-tuple-element.28), channel_id=1, source_target_pairs={{0,4},{4,8},{8,12},{12,16},{16,20},{20,24},{24,28},{1,5},{5,9},{9,... | collective-permute-start | bytes 786440 | tf_op jit(solution)/shard_map/ppermute | solution.py:25
  262.4 35.6 %collective-permute-start.23 = (f32[1,32,2048]{2,1,0:T(8,128)S(1)}, f32[1,32,2048]{2,1,0:T(8,128)S(1)}, u32[]{:S(2)}, u32[]{:S(2)}) collective-permute-start(f32[1,32,2048]{2,1,0:T(8,128)S(1)} %get-tuple-element.29), channel_id=1, source_target_pairs={{4,0},{8,4},{12,8},{16,12},{20,16},{24,20},{28,24},{5,1},{9,5},{13... | collective-permute-start | bytes 786440 | tf_op jit(solution)/shard_map/ppermute | solution.py:27
  345.7 38.5 %copy-start = (f32[2,32,2048]{2,1,0:T(8,128)}, f32[2,32,2048]{2,1,0:T(8,128)S(1)}, u32[]{:S(2)}) copy-start(f32[2,32,2048]{2,1,0:T(8,128)S(1)} %convolution_bitcast_fusion) | copy-start | bytes 1572868
  345.8 11.1 %collective-permute-start.24 = (f32[2,32,1024]{2,1,0:T(8,128)S(1)}, f32[2,32,1024]{2,1,0:T(8,128)S(1)}, u32[]{:S(2)}, u32[]{:S(2)}) collective-permute-start(f32[2,32,1024]{2,1,0:T(8,128)S(1)} %get-tuple-element.26), channel_id=1, source_target_pairs={{0,1},{1,2},{2,3},{3,0},{4,5},{5,6},{6,7},{7,4},{8,9},{9,10},{10,1... | collective-permute-start | bytes 786440 | tf_op jit(solution)/shard_map/ppermute | solution.py:25
  347.1 12.6 %collective-permute-start.25 = (f32[2,32,1024]{2,1,0:T(8,128)S(1)}, f32[2,32,1024]{2,1,0:T(8,128)S(1)}, u32[]{:S(2)}, u32[]{:S(2)}) collective-permute-start(f32[2,32,1024]{2,1,0:T(8,128)S(1)} %get-tuple-element.27), channel_id=1, source_target_pairs={{1,0},{2,1},{3,2},{0,3},{5,4},{6,5},{7,6},{4,7},{9,8},{10,9},{11,1... | collective-permute-start | bytes 786440 | tf_op jit(solution)/shard_map/ppermute | solution.py:27
  350.5 33.7 %collective-permute-start.26 = (f32[1,32,2048]{2,1,0:T(8,128)}, f32[1,32,2048]{2,1,0:T(8,128)S(1)}, u32[]{:S(2)}, u32[]{:S(2)}) collective-permute-start(f32[1,32,2048]{2,1,0:T(8,128)} %get-tuple-element.24), channel_id=1, source_target_pairs={{0,4},{4,8},{8,12},{12,16},{16,20},{20,24},{24,28},{1,5},{5,9},{9,... | collective-permute-start | bytes 786440 | tf_op jit(solution)/shard_map/ppermute | solution.py:25
  351.8 32.4 %collective-permute-start.27 = (f32[1,32,2048]{2,1,0:T(8,128)}, f32[1,32,2048]{2,1,0:T(8,128)}, u32[]{:S(2)}, u32[]{:S(2)}) collective-permute-start(f32[1,32,2048]{2,1,0:T(8,128)} %get-tuple-element.25), channel_id=1, source_target_pairs={{4,0},{8,4},{12,8},{16,12},{20,16},{24,20},{28,24},{5,1},{9,5},{13... | collective-permute-start | bytes 786440 | tf_op jit(solution)/shard_map/ppermute | solution.py:27
where the time goes:
time: 435 us; the launch traced here: 427 us
  matrix products  145 us (33%)
  blocking collectives  119 us (27%)
  starting transfers between devices  49.6 us (11%)
  waiting for transfers between devices  45.9 us (11%)
  other arithmetic  33.7 us (8%)
  local copies, waits for them, and re-layouts  32.1 us (7%)
    dot_general x7, matrix products, one_slice(): products = jnp.einsum('nrc,knc->knr', tile_set, picked, precision=accurate)  140 us
    psum x1, blocking collectives, body(): lax.psum(gram_terms(filtered, filtered), ('tm', 'space')) / count_all  40.3 us
    psum x1, blocking collectives, body(): lax.psum(gram_terms(ritz_basis, image_block), ('tm', 'space')) / count_all  39.8 us
    psum x1, blocking collectives, body(): lax.psum(gram_terms(second, second), ('tm', 'space')) / count_all  39.3 us
    ppermute x14, starting transfers between devices, with_halo(): lax.ppermute(head, axis, [((i + 1) % count, i) for i in range(ends)])  30.3 us
    gather x8, local copies, waits for them, and re-layouts, one_slice(): jnp.take(slice_vec.reshape(width, wide_blocks, TILE), col_list, axis=1)  26.4 us
    ppermute x14, waiting for transfers between devices, with_halo(): lax.ppermute(tail, axis, [(i, (i + 1) % count) for i in range(ends)])  24.9 us
    ppermute x14, waiting for transfers between devices, with_halo(): lax.ppermute(head, axis, [((i + 1) % count, i) for i in range(ends)])  21.1 us
  transfers between devices with their start and end apart: 28, of which 14 were waited for; matrix products, arithmetic and copies ran while one was open for 43% of the time, Pallas kernels for 0%

commit v1 on v0

v1 whole, which is shorter than its diff:
```python
import functools

import jax
import jax.numpy as jnp
from jax import lax
from jax.experimental import pallas as pl
from jax.experimental.pallas import tpu as pltpu
from jax.sharding import PartitionSpec as P

TILE = 128
TPR = 5
HB = 8
CENTER = 6.5
RADIUS = 3.5
INFLATION_FACTOR = 0.8

F32 = jnp.float32
BF16 = jnp.bfloat16
VM = pltpu.VMEM
NT = (((1,), (1,)), ((), ()))
NN = (((1,), (0,)), ((), ()))
WHOLE = pl.BlockSpec(memory_space=VM)
SCALARS = pl.BlockSpec(memory_space=pltpu.SMEM)


def near(x):
    return pltpu.with_memory_space_constraint(x, VM)


def split(x):
    high = x.astype(BF16)
    return high, (x - high.astype(F32)).astype(BF16)


def stacked(x):
    return jnp.concatenate(split(x), axis=0)


def call(kernel, ins, outs, scratch=(), specs=None, flops=0, moved=0, name=None, out_vmem=True):
    out_shape = [VM(s, d) if out_vmem else jax.ShapeDtypeStruct(s, d) for s, d in outs]
    return pl.pallas_call(
        kernel,
        out_shape=out_shape,
        in_specs=specs,
        out_specs=[WHOLE] * len(outs),
        scratch_shapes=list(scratch),
        name=name,
        cost_estimate=pl.CostEstimate(flops=flops, bytes_accessed=moved, transcendentals=0),
        compiler_params=pltpu.CompilerParams(vmem_limit_bytes=48 << 20),
    )(*ins)


def prep_kernel(tiles_ref, out_ref):
    high, low = split(tiles_ref[...])
    out_ref[:, :, :TILE, :] = high
    out_ref[:, :, TILE:, :] = low


def prep(tiles):
    slices, count = tiles.shape[:2]
    step = 16
    return pl.pallas_call(
        prep_kernel,
        grid=(slices, count // step),
        out_shape=VM((slices, count, 2 * TILE, TILE), BF16),
        in_specs=[pl.BlockSpec((1, step, TILE, TILE), lambda s, i: (s, i, 0, 0))],
        out_specs=pl.BlockSpec((1, step, 2 * TILE, TILE), lambda s, i: (s, i, 0, 0)),
        name="prep",
        cost_estimate=pl.CostEstimate(
            flops=0, bytes_accessed=2 * 4 * tiles.size, transcendentals=0
        ),
        compiler_params=pltpu.CompilerParams(vmem_limit_bytes=32 << 20),
    )(tiles)


def edges(y_ref, head_ref, tail_ref, first_ref, last_ref):
    width = HB * TILE
    points = y_ref.shape[2]
    head_ref[...] = y_ref[:, :, :width]
    tail_ref[...] = y_ref[:, :, points - width :]
    first_ref[...] = y_ref[:1]
    last_ref[...] = y_ref[y_ref.shape[0] - 1 :]


def edge_shapes(shape):
    slices, width, points = shape
    side = (slices, width, HB * TILE)
    return [(shape, F32), (side, F32), (side, F32), ((1, width, points), F32), ((1, width, points), F32)]


def start_kernel(x_ref, y_ref, *edge_refs):
    y_ref[...] = x_ref[...]
    edges(y_ref, *edge_refs)


def start(block):
    return call(
        start_kernel, [block], edge_shapes(block.shape), specs=[WHOLE], moved=16 * block.size, name="start"
    )


def matmul_tile(lhs, tile):
    return lax.dot_general(lhs, tile, NT, preferred_element_type=F32)


def fold(product, width):
    return product[:width, :TILE] + product[:width, TILE:] + product[width:, :TILE]


def local_kernel(place_ref, tiles_ref, y_ref, out_ref, halves_ref):
    slices, width, points = y_ref.shape
    blocks = points // TILE
    for s in range(slices):
        for b in range(blocks):
            halves_ref[s, b] = stacked(y_ref[s, :, b * TILE : (b + 1) * TILE])
        halves_ref[s, blocks] = jnp.zeros((2 * width, TILE), BF16)

    def row(i, carry):
        s, r = i // blocks, i % blocks
        total = None
        for n in range(TPR):
            where = place_ref[s, r * TPR + n] - HB
            inside = jnp.logical_and(where >= 0, where < blocks)
            where = jnp.where(inside, where, blocks)
            term = matmul_tile(halves_ref[s, where], tiles_ref[s, r * TPR + n])
            total = term if total is None else total + term
        out_ref[s, :, pl.ds(pl.multiple_of(r * TILE, TILE), TILE)] = fold(total, width)
        return carry

    lax.fori_loop(0, slices * blocks, row, 0, unroll=4)


def local_part(place, tiles, y):
    slices, width, points = y.shape
    blocks = points // TILE
    return call(
        local_kernel,
        [place, near(tiles), near(y)],
        [(y.shape, F32)],
        specs=[SCALARS, WHOLE, WHOLE],
        scratch=[VM((slices, blocks + 1, 2 * width, TILE), BF16)],
        flops=2 * slices * blocks * TPR * 4 * width * TILE * TILE,
        moved=8 * y.size,
        name="local",
    )[0]


def mix(matrix, y):
    high, low = split(matrix)
    y_high, y_low = split(y)
    left = jnp.concatenate([high, low, high], axis=1)
    right = jnp.concatenate([y_high, y_high, y_low], axis=0)
    return lax.dot_general(left, right, NN, preferred_element_type=F32)


def inner(left, right):
    width = left.shape[0]
    p = lax.dot_general(stacked(left), stacked(right), NT, preferred_element_type=F32)
    return (p[:width, :width] + p[width:, width:]) + (p[:width, width:] + p[width:, :width])


def finish_kernel(mode, scale, *refs):
    refs = list(refs)
    take = lambda n: [refs.pop(0) for _ in range(n)]
    place_ref, degree_ref, tiles_ref, part_ref, y_ref = take(5)
    left_ref, right_ref, before_ref, after_ref = take(4)
    previous_ref = take(1)[0] if mode in ("step", "gram", "mixed") else None
    matrix_ref = take(1)[0] if mode == "mixed" else None
    if mode == "image":
        (gram_ref,) = take(1)
    else:
        new_ref, *edge_refs = take(5)
        gram_ref = take(1)[0] if mode in ("gram", "mixed") else None
    halves_ref = take(1)[0]
    if mode == "image":
        new_ref = take(1)[0]
    slices, width, points = y_ref.shape
    blocks = points // TILE
    for s in range(slices):
        for b in range(HB):
            halves_ref[s, b] = stacked(left_ref[s, :, b * TILE : (b + 1) * TILE])
            halves_ref[s, HB + b] = stacked(right_ref[s, :, b * TILE : (b + 1) * TILE])
        halves_ref[s, 2 * HB] = jnp.zeros((2 * width, TILE), BF16)

    for s in range(slices):

        def row(r, carry, s=s):
            total = None
            for n in range(1, TPR):
                where = place_ref[s, r * TPR + n]
                right = where >= HB + blocks
                where = jnp.where(right, where - blocks, jnp.where(where < HB, where, 2 * HB))
                term = matmul_tile(halves_ref[s, where], tiles_ref[s, r * TPR + n])
                total = term if total is None else total + term
            here = pl.ds(pl.multiple_of(r * TILE, TILE), TILE)
            y = y_ref[s, :, here]
            before = before_ref[0, :, here] if s == 0 else y_ref[s - 1, :, here]
            after = after_ref[0, :, here] if s == slices - 1 else y_ref[s + 1, :, here]
            image = part_ref[s, :, here] + fold(total, width)
            image = image + INFLATION_FACTOR * (degree_ref[s] * y - before - after)
            if mode != "image":
                image = (image - CENTER * y) * scale
                if previous_ref is not None:
                    image = image - previous_ref[s, :, here]
            new_ref[s, :, here] = image
            return carry

        lax.fori_loop(0, blocks, row, 0, unroll=4)

    if mode == "mixed":
        for s in range(slices):
            new_ref[s] = mix(matrix_ref[...], new_ref[s])
    if mode != "image":
        edges(new_ref, *edge_refs)
    if gram_ref is not None:
        base_ref = y_ref if mode == "image" else new_ref
        total = inner(base_ref[0], new_ref[0])
        for s in range(1, slices):
            total = total + inner(base_ref[s], new_ref[s])
        gram_ref[...] = total


def finish(mode, scale, place, degree, tiles, part, y, halo, previous=None, matrix=None):
    slices, width, points = y.shape
    blocks = points // TILE
    ins = [place, degree] + [near(v) for v in (tiles, part, y, *halo)]
    specs = [SCALARS, SCALARS] + [WHOLE] * 7
    for extra in (previous, matrix):
        if extra is not None:
            ins.append(near(extra))
            specs.append(WHOLE)
    outs = [] if mode == "image" else edge_shapes(y.shape)
    if mode in ("gram", "mixed", "image"):
        outs = outs + [((width, width), F32)]
    scratch = [VM((slices, 2 * HB + 1, 2 * width, TILE), BF16)]
    if mode == "image":
        scratch.append(VM(y.shape, F32))
    return call(
        functools.partial(finish_kernel, mode, scale),
        ins,
        outs,
        scratch=scratch,
        specs=specs,
        flops=2 * slices * blocks * TPR * 4 * width * TILE * TILE,
        moved=24 * y.size,
        name="finish_" + mode,
    )


def inverse_factor(gram):
    width = gram.shape[0]
    rows = lax.broadcasted_iota(jnp.int32, (width, width), 0)
    columns = lax.broadcasted_iota(jnp.int32, (width, width), 1)
    inverse = (rows == columns).astype(F32)
    row_of = lax.broadcasted_iota(jnp.int32, (width, 1), 0)
    for j in range(width):
        root = lax.rsqrt(gram[j : j + 1, j : j + 1])
        gram_row = gram[j : j + 1, :] * root
        inverse_row = inverse[j : j + 1, :] * root
        column = jnp.where(row_of > j, gram[:, j : j + 1] * root, 0.0)
        gram = gram - column * gram_row
        inverse = jnp.where(row_of == j, inverse_row, inverse - column * inverse_row)
    return inverse


def orth_kernel(count, gram_ref, y_ref, out_ref, matrix_ref):
    matrix = inverse_factor(gram_ref[...] * (1.0 / count))
    matrix_ref[...] = matrix
    for s in range(y_ref.shape[0]):
        out_ref[s] = mix(matrix, y_ref[s])


def orth(gram, y, count):
    width = gram.shape[0]
    return pl.pallas_call(
        functools.partial(orth_kernel, float(count)),
        out_shape=[jax.ShapeDtypeStruct(y.shape, F32), VM((width, width), F32)],
        in_specs=[WHOLE, WHOLE],
        out_specs=[WHOLE, WHOLE],
        name="orth",
        cost_estimate=pl.CostEstimate(flops=2 * width * y.size, bytes_accessed=8 * y.size, transcendentals=0),
        compiler_params=pltpu.CompilerParams(vmem_limit_bytes=16 << 20),
    )(near(gram), near(y))


def ritz_kernel(count, matrix_ref, inner_ref, out_ref):
    high = lax.Precision.HIGHEST
    matrix = matrix_ref[...]
    half = lax.dot_general(matrix, inner_ref[...] * (1.0 / count), NN, precision=high, preferred_element_type=F32)
    out_ref[...] = lax.dot_general(half, matrix, NT, precision=high, preferred_element_type=F32)


def ritz(matrix, product, count):
    return call(
        functools.partial(ritz_kernel, float(count)),
        [near(matrix), near(product)],
        [(product.shape, F32)],
        specs=[WHOLE, WHOLE],
        name="ritz",
        moved=4 * product.size,
        out_vmem=False,
    )[0]


def total_over(value, axis):
    count = lax.axis_size(axis)
    stride = 1
    while stride < count:
        value = value + lax.ppermute(value, axis, [(i, i ^ stride) for i in range(count)])
        stride *= 2
    return value


def exchange(edge):
    head, tail, first, last = edge
    ring = lax.axis_size("space")
    line = lax.axis_size("tm")
    left = lax.ppermute(tail, "space", [(i, (i + 1) % ring) for i in range(ring)])
    right = lax.ppermute(head, "space", [((i + 1) % ring, i) for i in range(ring)])
    before = lax.ppermute(last, "tm", [(i, i + 1) for i in range(line - 1)])
    after = lax.ppermute(first, "tm", [(i + 1, i) for i in range(line - 1)])
    return left, right, before, after


def body(start_block, stiffness_tiles, tile_columns):
    slices, width, local_points = start_block.shape
    local_blocks = local_points // TILE
    first_block = lax.axis_index("space") * local_blocks
    blocks_all = lax.axis_size("space") * local_blocks
    place = (tile_columns - first_block + HB) % blocks_all
    count_all = slices * local_points * lax.axis_size("tm") * lax.axis_size("space")
    slice_index = lax.axis_index("tm") * slices + jnp.arange(slices, dtype=jnp.int32)
    last_slice = lax.axis_size("tm") * slices - 1
    degree = 2.0 - (slice_index == 0).astype(F32) - (slice_index == last_slice).astype(F32)

    y, *edge = start(start_block)
    tiles = prep(stiffness_tiles)

    def apply(mode, scale, y, edge, previous=None, matrix=None):
        halo = exchange(edge)
        part = local_part(place, tiles, y)
        return finish(mode, scale, place, degree, tiles, part, y, halo, previous, matrix)

    def run_filter(y, edge, mode, matrix=None):
        y0 = y
        y1, *edge = apply("first", 1.0 / RADIUS, y0, edge)
        y2, *edge = apply("step", 2.0 / RADIUS, y1, edge, y0)
        out = apply(mode, 2.0 / RADIUS, y2, edge, y1, matrix() if matrix else None)
        return out[0], out[1:5], out[5]

    filtered, edge, gram = run_filter(y, edge, "gram")
    kept = {}

    def first_matrix():
        total = total_over(total_over(gram, "tm"), "space")
        kept["first"], matrix = orth(total, filtered, count_all)
        return matrix

    second, edge, gram_two = run_filter(filtered, edge, "mixed", first_matrix)
    (product,) = apply("image", 1.0, second, edge)
    ritz_basis, matrix = orth(total_over(total_over(gram_two, "tm"), "space"), second, count_all)
    product = total_over(total_over(product, "tm"), "space")
    return ritz_basis, kept["first"], ritz(matrix, product, count_all)


def solution(mesh):
    placed = (P("tm", None, "space"), P("tm", "space", None, None), P("tm", "space"))
    return jax.shard_map(
        body,
        mesh=mesh,
        in_specs=placed,
        out_specs=(P("tm", None, "space"), P("tm", None, "space"), P()),
        check_vma=False,
    )
```

time: 435 us -> 205 us (0.47); the launches traced: 427 us -> 204 us
  matrix products: 145 us -> 0 us
  blocking collectives: 119 us -> 0 us
  Pallas kernels: 0 us -> 81.4 us
  starting transfers between devices: 49.6 us -> 81.8 us
  other arithmetic: 33.7 us -> 1.84 us
  waiting for transfers between devices: 45.9 us -> 25.3 us
  local copies, waits for them, and re-layouts: 32.1 us -> 13 us
    dot_general x12 -> x0, matrix products: 144 us -> none  [the longest x7 140 us: one_slice(): products = jnp.einsum('nrc,knc->knr', tile_set, picked, precision=accurate)]
    psum x3 -> x0, blocking collectives: 119 us -> none  [the longest x1 40.3 us: body(): lax.psum(gram_terms(filtered, filtered), ('tm', 'space')) / count_all]
    pallas_call x0 -> x19, Pallas kernels: none -> 81.4 us  [the longest x16 72.6 us: call(): pl.pallas_call(kernel, out_shape=out_shape, in_specs=specs, out_specs=[WH...]
    ppermute x28 -> x43, starting transfers between devices: 49.6 us -> 81.8 us  [the longest x7 28 us: exchange(): before = lax.ppermute(last, 'tm', [(i, i + 1) for i in range(line - 1)])]
    gather x8 -> x0, local copies, waits for them, and re-layouts: 26.4 us -> none  [one_slice(): jnp.take(slice_vec.reshape(width, wide_blocks, TILE), col_list, axis=1)]
    ppermute x28 -> x43, waiting for transfers between devices: 45.9 us -> 25.3 us  [the longest x15 25.2 us: total_over(): lax.ppermute(value, axis, [(i, i ^ stride) for i in range(count)])]
    another operation x10 -> x0, other arithmetic: 13.4 us -> none  [the longest x6 7.19 us: inverse_factor(): cholesky_factor = jnp.linalg.cholesky(gram_matrix)]
    unnamed x7 -> x8, local copies, waits for them, and re-layouts: 0.7 us -> 13 us
  transfers between devices with their start and end apart: 28 -> 43, of which waited for: 14 -> 11; matrix products, arithmetic and copies ran while one was open for 43% -> 1% of each run, Pallas kernels for 0% -> 25%
where the time goes in v1:
time: 205 us; the launch traced here: 204 us
  starting transfers between devices  81.8 us (40%)
  Pallas kernels  81.4 us (40%)
  waiting for transfers between devices  25.3 us (12%)
  local copies, waits for them, and re-layouts  13 us (6%)
    pallas_call x16, Pallas kernels, call(): pl.pallas_call(kernel, out_shape=out_shape, in_specs=specs, out_specs=[WH...  72.6 us
    ppermute x7, starting transfers between devices, exchange(): before = lax.ppermute(last, 'tm', [(i, i + 1) for i in range(line - 1)])  28 us
    ppermute x15, waiting for transfers between devices, total_over(): lax.ppermute(value, axis, [(i, i ^ stride) for i in range(count)])  25.2 us
    ppermute x7, starting transfers between devices, exchange(): lax.ppermute(head, 'space', [((i + 1) % ring, i) for i in range(ring)])  24.5 us
    ppermute x15, starting transfers between devices, total_over(): lax.ppermute(value, axis, [(i, i ^ stride) for i in range(count)])  16.2 us
    unnamed x8, local copies, waits for them, and re-layouts  13 us
    ppermute x7, starting transfers between devices, exchange(): after = lax.ppermute(first, 'tm', [(i + 1, i) for i in range(line - 1)])  9.23 us
    pallas_call x2, Pallas kernels, orth(): pl.pallas_call(functools.partial(orth_kernel, float(count)), out_shape=[j...  7.36 us
  transfers between devices with their start and end apart: 43, of which 11 were waited for; matrix products, arithmetic and copies ran while one was open for 1% of the time, Pallas kernels for 25%

profile of v1, /device:TPU:0, one launch (start us, length us, event | category | flops | bytes accessed | tf_op | source)
XLA Modules:
  0.0 204.4 jit_solution(1622937530054176565)
XLA Ops:
  11.0 4.0 %copy-done.2 = f32[2,80,128,128]{3,2,1,0:T(8,128)S(1)} copy-done((f32[2,80,128,128]{3,2,1,0:T(8,128)S(1)}, f32[2,80,128,128]{3,2,1,0:T(8,128)}, u32[]{:S(2)}) %copy-start.2) | copy-done | bytes 10485784
  16.4 4.0 %copy-done = bf16[2,80,256,128]{3,2,1,0:T(8,128)(2,1)} copy-done((bf16[2,80,256,128]{3,2,1,0:T(8,128)(2,1)}, bf16[2,80,256,128]{3,2,1,0:T(8,128)(2,1)S(1)}, u32[]{:S(2)}) %copy-start) | copy-done | bytes 10485784
  20.5 4.0 %copy-done.1 = bf16[2,80,256,128]{3,2,1,0:T(8,128)(2,1)S(1)} copy-done((bf16[2,80,256,128]{3,2,1,0:T(8,128)(2,1)S(1)}, bf16[2,80,256,128]{3,2,1,0:T(8,128)(2,1)}, u32[]{:S(2)}) %copy-start.1) | copy-done | bytes 10485784
  24.4 5.3 %local.7.refs_3_ = f32[2,32,2048]{2,1,0:T(8,128)S(1)} custom-call(s32[2,80]{1,0:T(2,128)} %and_select_fusion.place_ref.refs_0_, bf16[2,80,256,128]{3,2,1,0:T(8,128)(2,1)S(1)} %copy-done.1, f32[2,32,2048]{2,1,0:T(8,128)S(1)} %get-tuple-element.44.y_ref.refs_4_.refs_9_), custom_call_target="tpu_custom_call" | custom-call | flops 671088640 | bytes 1048576 | tf_op jit(solution)/shard_map/local/pallas_call | solution.py:41
  30.3 4.7 %finish_first.2 = (f32[2,32,2048]{2,1,0:T(8,128)S(1)}, f32[2,32,1024]{2,1,0:T(8,128)S(1)}, f32[2,32,1024]{2,1,0:T(8,128)S(1)}, f32[1,32,2048]{2,1,0:T(8,128)S(1)}, f32[1,32,2048]{2,1,0:T(8,128)S(1)}) custom-call(s32[2,80]{1,0:T(2,128)} %and_select_fusion.place_ref.refs_0_, f32[2]{0:T(128)} %fusion.2.refs_1_, bf16[2,80,256,128]{3,2,1,0:T(8,128)(2,1)S(1)} %copy-done.1, ...), custom_call_target="tpu_custom_call" | custom-call | flops 671088640 | bytes 3145728 | tf_op jit(solution)/shard_map/finish_first/pallas_call | solution.py:41
  35.1 3.8 %collective-permute-start.5 = (f32[2,32,1024]{2,1,0:T(8,128)S(1)}, f32[2,32,1024]{2,1,0:T(8,128)S(1)}, u32[]{:S(2)}, u32[]{:S(2)}) collective-permute-start(f32[2,32,1024]{2,1,0:T(8,128)S(1)} %get-tuple-element.51), channel_id=1, source_target_pairs={{1,0},{2,1},{3,2},{0,3},{5,4},{6,5},{7,6},{4,7},{9,8},{10,9},{11,1... | collective-permute-start | bytes 786440 | tf_op jit(solution)/shard_map/ppermute | solution.py:319
  38.9 4.2 %collective-permute-start.6 = (f32[1,32,2048]{2,1,0:T(8,128)S(1)}, f32[1,32,2048]{2,1,0:T(8,128)S(1)}, u32[]{:S(2)}, u32[]{:S(2)}) collective-permute-start(f32[1,32,2048]{2,1,0:T(8,128)S(1)} %get-tuple-element.52), channel_id=1, source_target_pairs={{0,4},{4,8},{8,12},{12,16},{16,20},{20,24},{24,28},{1,5},{5,9},{9,... | collective-permute-start | bytes 786440 | tf_op jit(solution)/shard_map/ppermute | solution.py:320
  44.3 5.3 %local.8.refs_3_ = f32[2,32,2048]{2,1,0:T(8,128)S(1)} custom-call(s32[2,80]{1,0:T(2,128)} %and_select_fusion.place_ref.refs_0_, bf16[2,80,256,128]{3,2,1,0:T(8,128)(2,1)S(1)} %copy-done.1, f32[2,32,2048]{2,1,0:T(8,128)S(1)} %get-tuple-element.49.y_ref.refs_4_.refs_9_), custom_call_target="tpu_custom_call" | custom-call | flops 671088640 | bytes 1048576 | tf_op jit(solution)/shard_map/local/pallas_call | solution.py:41
  49.7 4.7 %finish_step.2 = (f32[2,32,2048]{2,1,0:T(8,128)S(1)}, f32[2,32,1024]{2,1,0:T(8,128)S(1)}, f32[2,32,1024]{2,1,0:T(8,128)S(1)}, f32[1,32,2048]{2,1,0:T(8,128)S(1)}, f32[1,32,2048]{2,1,0:T(8,128)S(1)}) custom-call(s32[2,80]{1,0:T(2,128)} %and_select_fusion.place_ref.refs_0_, f32[2]{0:T(128)} %fusion.2.refs_1_, bf16[2,80,256,128]{3,2,1,0:T(8,128)(2,1)S(1)} %copy-done.1, ...), custom_call_target="tpu_custom_call" | custom-call | flops 671088640 | bytes 3145728 | tf_op jit(solution)/shard_map/finish_step/pallas_call | solution.py:41
  58.3 5.6 %collective-permute-start.10 = (f32[1,32,2048]{2,1,0:T(8,128)S(1)}, f32[1,32,2048]{2,1,0:T(8,128)S(1)}, u32[]{:S(2)}, u32[]{:S(2)}) collective-permute-start(f32[1,32,2048]{2,1,0:T(8,128)S(1)} %get-tuple-element.57), channel_id=1, source_target_pairs={{0,4},{4,8},{8,12},{12,16},{16,20},{20,24},{24,28},{1,5},{5,9},{9,... | collective-permute-start | bytes 786440 | tf_op jit(solution)/shard_map/ppermute | solution.py:320
  65.2 5.3 %local.9.refs_3_ = f32[2,32,2048]{2,1,0:T(8,128)S(1)} custom-call(s32[2,80]{1,0:T(2,128)} %and_select_fusion.place_ref.refs_0_, bf16[2,80,256,128]{3,2,1,0:T(8,128)(2,1)S(1)} %copy-done.1, f32[2,32,2048]{2,1,0:T(8,128)S(1)} %get-tuple-element.54.y_ref.refs_4_), custom_call_target="tpu_custom_call" | custom-call | flops 671088640 | bytes 1048576 | tf_op jit(solution)/shard_map/local/pallas_call | solution.py:41
  70.6 5.1 %finish_gram.1 = (f32[2,32,2048]{2,1,0:T(8,128)S(1)}, f32[2,32,1024]{2,1,0:T(8,128)S(1)}, f32[2,32,1024]{2,1,0:T(8,128)S(1)}, f32[1,32,2048]{2,1,0:T(8,128)S(1)}...) custom-call(s32[2,80]{1,0:T(2,128)} %and_select_fusion.place_ref.refs_0_, f32[2]{0:T(128)} %fusion.2.refs_1_, ...), custom_call_target="tpu_custom_call" | custom-call | flops 671088640 | bytes 3145728 | tf_op jit(solution)/shard_map/finish_gram/pallas_call | solution.py:41
  75.7 3.8 %collective-permute-start.13 = (f32[2,32,1024]{2,1,0:T(8,128)S(1)}, f32[2,32,1024]{2,1,0:T(8,128)S(1)}, u32[]{:S(2)}, u32[]{:S(2)}) collective-permute-start(f32[2,32,1024]{2,1,0:T(8,128)S(1)} %get-tuple-element.61), channel_id=1, source_target_pairs={{1,0},{2,1},{3,2},{0,3},{5,4},{6,5},{7,6},{4,7},{9,8},{10,9},{11,1... | collective-permute-start | bytes 786440 | tf_op jit(solution)/shard_map/ppermute | solution.py:319
  79.5 5.2 %collective-permute-start.14 = (f32[1,32,2048]{2,1,0:T(8,128)S(1)}, f32[1,32,2048]{2,1,0:T(8,128)S(1)}, u32[]{:S(2)}, u32[]{:S(2)}) collective-permute-start(f32[1,32,2048]{2,1,0:T(8,128)S(1)} %get-tuple-element.62), channel_id=1, source_target_pairs={{0,4},{4,8},{8,12},{12,16},{16,20},{20,24},{24,28},{1,5},{5,9},{9,... | collective-permute-start | bytes 786440 | tf_op jit(solution)/shard_map/ppermute | solution.py:320
  86.0 5.3 %local.10.refs_3_ = f32[2,32,2048]{2,1,0:T(8,128)S(1)} custom-call(s32[2,80]{1,0:T(2,128)} %and_select_fusion.place_ref.refs_0_, bf16[2,80,256,128]{3,2,1,0:T(8,128)(2,1)S(1)} %copy-done.1, f32[2,32,2048]{2,1,0:T(8,128)S(1)} %get-tuple-element.59.y_ref.refs_4_.refs_9_), custom_call_target="tpu_custom_call" | custom-call | flops 671088640 | bytes 1048576 | tf_op jit(solution)/shard_map/local/pallas_call | solution.py:41
  91.4 4.7 %finish_first.3 = (f32[2,32,2048]{2,1,0:T(8,128)S(1)}, f32[2,32,1024]{2,1,0:T(8,128)S(1)}, f32[2,32,1024]{2,1,0:T(8,128)S(1)}, f32[1,32,2048]{2,1,0:T(8,128)S(1)}, f32[1,32,2048]{2,1,0:T(8,128)S(1)}) custom-call(s32[2,80]{1,0:T(2,128)} %and_select_fusion.place_ref.refs_0_, f32[2]{0:T(128)} %fusion.2.refs_1_, bf16[2,80,256,128]{3,2,1,0:T(8,128)(2,1)S(1)} %copy-done.1, ...), custom_call_target="tpu_custom_call" | custom-call | flops 671088640 | bytes 3145728 | tf_op jit(solution)/shard_map/finish_first/pallas_call | solution.py:41
  96.1 3.8 %collective-permute-start.17 = (f32[2,32,1024]{2,1,0:T(8,128)S(1)}, f32[2,32,1024]{2,1,0:T(8,128)S(1)}, u32[]{:S(2)}, u32[]{:S(2)}) collective-permute-start(f32[2,32,1024]{2,1,0:T(8,128)S(1)} %get-tuple-element.66), channel_id=1, source_target_pairs={{1,0},{2,1},{3,2},{0,3},{5,4},{6,5},{7,6},{4,7},{9,8},{10,9},{11,1... | collective-permute-start | bytes 786440 | tf_op jit(solution)/shard_map/ppermute | solution.py:319
  99.9 5.2 %collective-permute-start.18 = (f32[1,32,2048]{2,1,0:T(8,128)S(1)}, f32[1,32,2048]{2,1,0:T(8,128)S(1)}, u32[]{:S(2)}, u32[]{:S(2)}) collective-permute-start(f32[1,32,2048]{2,1,0:T(8,128)S(1)} %get-tuple-element.67), channel_id=1, source_target_pairs={{0,4},{4,8},{8,12},{12,16},{16,20},{20,24},{24,28},{1,5},{5,9},{9,... | collective-permute-start | bytes 786440 | tf_op jit(solution)/shard_map/ppermute | solution.py:320
  106.4 5.3 %local.11.refs_3_ = f32[2,32,2048]{2,1,0:T(8,128)S(1)} custom-call(s32[2,80]{1,0:T(2,128)} %and_select_fusion.place_ref.refs_0_, bf16[2,80,256,128]{3,2,1,0:T(8,128)(2,1)S(1)} %copy-done.1, f32[2,32,2048]{2,1,0:T(8,128)S(1)} %get-tuple-element.64.y_ref.refs_4_.refs_9_), custom_call_target="tpu_custom_call" | custom-call | flops 671088640 | bytes 1048576 | tf_op jit(solution)/shard_map/local/pallas_call | solution.py:41
  111.8 4.7 %finish_step.3 = (f32[2,32,2048]{2,1,0:T(8,128)S(1)}, f32[2,32,1024]{2,1,0:T(8,128)S(1)}, f32[2,32,1024]{2,1,0:T(8,128)S(1)}, f32[1,32,2048]{2,1,0:T(8,128)S(1)}, f32[1,32,2048]{2,1,0:T(8,128)S(1)}) custom-call(s32[2,80]{1,0:T(2,128)} %and_select_fusion.place_ref.refs_0_, f32[2]{0:T(128)} %fusion.2.refs_1_, bf16[2,80,256,128]{3,2,1,0:T(8,128)(2,1)S(1)} %copy-done.1, ...), custom_call_target="tpu_custom_call" | custom-call | flops 671088640 | bytes 3145728 | tf_op jit(solution)/shard_map/finish_step/pallas_call | solution.py:41
  116.5 3.8 %collective-permute-start.21 = (f32[2,32,1024]{2,1,0:T(8,128)S(1)}, f32[2,32,1024]{2,1,0:T(8,128)S(1)}, u32[]{:S(2)}, u32[]{:S(2)}) collective-permute-start(f32[2,32,1024]{2,1,0:T(8,128)S(1)} %get-tuple-element.71), channel_id=1, source_target_pairs={{1,0},{2,1},{3,2},{0,3},{5,4},{6,5},{7,6},{4,7},{9,8},{10,9},{11,1... | collective-permute-start | bytes 786440 | tf_op jit(solution)/shard_map/ppermute | solution.py:319
  120.4 5.2 %collective-permute-start.22 = (f32[1,32,2048]{2,1,0:T(8,128)S(1)}, f32[1,32,2048]{2,1,0:T(8,128)S(1)}, u32[]{:S(2)}, u32[]{:S(2)}) collective-permute-start(f32[1,32,2048]{2,1,0:T(8,128)S(1)} %get-tuple-element.72), channel_id=1, source_target_pairs={{0,4},{4,8},{8,12},{12,16},{16,20},{20,24},{24,28},{1,5},{5,9},{9,... | collective-permute-start | bytes 786440 | tf_op jit(solution)/shard_map/ppermute | solution.py:320
  129.0 3.7 %collective-permute-start.25 = (f32[32,32]{1,0:T(8,128)S(1)}, f32[32,32]{1,0:T(8,128)S(1)}, u32[]{:S(2)}, u32[]{:S(2)}) collective-permute-start(f32[32,32]{1,0:T(8,128)S(1)} %add.68), channel_id=1, source_target_pairs={{0,8},{4,12},{8,0},{12,4},{16,24},{20,28},{24,16},{28,20},{1,9},{5... | collective-permute-start | bytes 12296 | tf_op jit(solution)/shard_map/ppermute | solution.py:309
  132.7 3.8 %collective-permute-done.25 = f32[32,32]{1,0:T(8,128)S(1)} collective-permute-done((f32[32,32]{1,0:T(8,128)S(1)}, f32[32,32]{1,0:T(8,128)S(1)}, u32[]{:S(2)}, u32[]{:S(2)}) %collective-permute-start.25) | collective-permute-done | bytes 4128 | tf_op jit(solution)/shard_map/ppermute | solution.py:309
  140.3 3.7 %collective-permute-done.27 = f32[32,32]{1,0:T(8,128)S(1)} collective-permute-done((f32[32,32]{1,0:T(8,128)S(1)}, f32[32,32]{1,0:T(8,128)S(1)}, u32[]{:S(2)}, u32[]{:S(2)}) %collective-permute-start.27) | collective-permute-done | bytes 4128 | tf_op jit(solution)/shard_map/ppermute | solution.py:309
  144.1 4.6 %collective-permute-done.28 = f32[32,32]{1,0:T(8,128)S(1)} collective-permute-done((f32[32,32]{1,0:T(8,128)S(1)}, f32[32,32]{1,0:T(8,128)S(1)}, u32[]{:S(2)}, u32[]{:S(2)}) %collective-permute-start.28) | collective-permute-done | bytes 4128 | tf_op jit(solution)/shard_map/ppermute | solution.py:309
  148.7 3.7 %orth.2 = (f32[2,32,2048]{2,1,0:T(8,128)}, f32[32,32]{1,0:T(8,128)S(1)}) custom-call(f32[32,32]{1,0:T(8,128)S(1)} %add.72.gram_ref, f32[2,32,2048]{2,1,0:T(8,128)S(1)} %get-tuple-element.59.y_ref.refs_4_.refs_9_), custom_call_target="tpu_custom_call" | custom-call | flops 8388608 | bytes 1048576 | tf_op jit(solution)/shard_map/orth/pallas_call | solution.py:275
  152.4 5.3 %local.12.refs_3_ = f32[2,32,2048]{2,1,0:T(8,128)S(1)} custom-call(s32[2,80]{1,0:T(2,128)} %and_select_fusion.place_ref.refs_0_, bf16[2,80,256,128]{3,2,1,0:T(8,128)(2,1)S(1)} %copy-done.1, f32[2,32,2048]{2,1,0:T(8,128)S(1)} %get-tuple-element.69.y_ref.refs_4_), custom_call_target="tpu_custom_call" | custom-call | flops 671088640 | bytes 1048576 | tf_op jit(solution)/shard_map/local/pallas_call | solution.py:41
  157.8 5.3 %finish_mixed.1 = (f32[2,32,2048]{2,1,0:T(8,128)S(1)}, f32[2,32,1024]{2,1,0:T(8,128)S(1)}, f32[2,32,1024]{2,1,0:T(8,128)S(1)}, f32[1,32,2048]{2,1,0:T(8,128)S(1)...) custom-call(s32[2,80]{1,0:T(2,128)} %and_select_fusion.place_ref.refs_0_, f32[2]{0:T(128)} %fusion.2.refs_1_, ...), custom_call_target="tpu_custom_call" | custom-call | flops 671088640 | bytes 3145728 | tf_op jit(solution)/shard_map/finish_mixed/pallas_call | solution.py:41
  163.2 3.7 %collective-permute-start.35 = (f32[2,32,1024]{2,1,0:T(8,128)S(1)}, f32[2,32,1024]{2,1,0:T(8,128)S(1)}, u32[]{:S(2)}, u32[]{:S(2)}) collective-permute-start(f32[2,32,1024]{2,1,0:T(8,128)S(1)} %get-tuple-element.82), channel_id=1, source_target_pairs={{1,0},{2,1},{3,2},{0,3},{5,4},{6,5},{7,6},{4,7},{9,8},{10,9},{11,1... | collective-permute-start | bytes 786440 | tf_op jit(solution)/shard_map/ppermute | solution.py:319
  172.2 5.3 %local.13.refs_3_ = f32[2,32,2048]{2,1,0:T(8,128)S(1)} custom-call(s32[2,80]{1,0:T(2,128)} %and_select_fusion.place_ref.refs_0_, bf16[2,80,256,128]{3,2,1,0:T(8,128)(2,1)S(1)} %copy-done.1, f32[2,32,2048]{2,1,0:T(8,128)S(1)} %get-tuple-element.77.y_ref.refs_4_), custom_call_target="tpu_custom_call" | custom-call | flops 671088640 | bytes 1048576 | tf_op jit(solution)/shard_map/local/pallas_call | solution.py:41
  177.5 5.0 %finish_image.1 = f32[32,32]{1,0:T(8,128)S(1)} custom-call(s32[2,80]{1,0:T(2,128)} %and_select_fusion.place_ref.refs_0_, f32[2]{0:T(128)} %fusion.2.refs_1_, bf16[2,80,256,128]{3,2,1,0:T(8,128)(2,1)S(1)} %copy-done.1, f32[2,32,2048]{2,1,0:T(8,128)S(1)} %local.13.refs_3_, f32[2,32,2048]{2,1,0:T(8,128)S(1)} %get-tuple-element.77.y_ref.refs_4_, ...), custom_call_target="tpu_custom_call" | custom-call | flops 671088640 | bytes 3145728 | tf_op jit(solution)/shard_map/finish_image/pallas_call | solution.py:41
  (98 shorter events, 56.0 us)
Async XLA Ops:
  1.8 28.5 %collective-permute-start = (f32[2,32,1024]{2,1,0:T(8,128)S(1)}, f32[2,32,1024]{2,1,0:T(8,128)S(1)}, u32[]{:S(2)}, u32[]{:S(2)}) collective-permute-start(f32[2,32,1024]{2,1,0:T(8,128)S(1)} %get-tuple-element.45), channel_id=1, source_target_pairs={{0,1},{1,2},{2,3},{3,0},{4,5},{5,6},{6,7},{7,4},{8,9},{9,10},{10,1... | collective-permute-start | bytes 786440 | tf_op jit(solution)/shard_map/ppermute | solution.py:318
  4.9 25.4 %collective-permute-start.1 = (f32[2,32,1024]{2,1,0:T(8,128)S(1)}, f32[2,32,1024]{2,1,0:T(8,128)S(1)}, u32[]{:S(2)}, u32[]{:S(2)}) collective-permute-start(f32[2,32,1024]{2,1,0:T(8,128)S(1)} %get-tuple-element.46), channel_id=1, source_target_pairs={{1,0},{2,1},{3,2},{0,3},{5,4},{6,5},{7,6},{4,7},{9,8},{10,9},{11,1... | collective-permute-start | bytes 786440 | tf_op jit(solution)/shard_map/ppermute | solution.py:319
  6.9 23.4 %collective-permute-start.2 = (f32[1,32,2048]{2,1,0:T(8,128)S(1)}, f32[1,32,2048]{2,1,0:T(8,128)S(1)}, u32[]{:S(2)}, u32[]{:S(2)}) collective-permute-start(f32[1,32,2048]{2,1,0:T(8,128)S(1)} %get-tuple-element.47), channel_id=1, source_target_pairs={{0,4},{4,8},{8,12},{12,16},{16,20},{20,24},{24,28},{1,5},{5,9},{9,... | collective-permute-start | bytes 786440 | tf_op jit(solution)/shard_map/ppermute | solution.py:320
  8.4 21.9 %collective-permute-start.3 = (f32[1,32,2048]{2,1,0:T(8,128)S(1)}, f32[1,32,2048]{2,1,0:T(8,128)S(1)}, u32[]{:S(2)}, u32[]{:S(2)}) collective-permute-start(f32[1,32,2048]{2,1,0:T(8,128)S(1)} %get-tuple-element.48), channel_id=1, source_target_pairs={{4,0},{8,4},{12,8},{16,12},{20,16},{24,20},{28,24},{5,1},{9,5},{13... | collective-permute-start | bytes 786440 | tf_op jit(solution)/shard_map/ppermute | solution.py:321
  35.0 14.7 %collective-permute-start.4 = (f32[2,32,1024]{2,1,0:T(8,128)S(1)}, f32[2,32,1024]{2,1,0:T(8,128)S(1)}, u32[]{:S(2)}, u32[]{:S(2)}) collective-permute-start(f32[2,32,1024]{2,1,0:T(8,128)S(1)} %get-tuple-element.50), channel_id=1, source_target_pairs={{0,1},{1,2},{2,3},{3,0},{4,5},{5,6},{6,7},{7,4},{8,9},{9,10},{10,1... | collective-permute-start | bytes 786440 | tf_op jit(solution)/shard_map/ppermute | solution.py:318
  35.1 14.7 %collective-permute-start.5 = (f32[2,32,1024]{2,1,0:T(8,128)S(1)}, f32[2,32,1024]{2,1,0:T(8,128)S(1)}, u32[]{:S(2)}, u32[]{:S(2)}) collective-permute-start(f32[2,32,1024]{2,1,0:T(8,128)S(1)} %get-tuple-element.51), channel_id=1, source_target_pairs={{1,0},{2,1},{3,2},{0,3},{5,4},{6,5},{7,6},{4,7},{9,8},{10,9},{11,1... | collective-permute-start | bytes 786440 | tf_op jit(solution)/shard_map/ppermute | solution.py:319
  38.9 10.8 %collective-permute-start.6 = (f32[1,32,2048]{2,1,0:T(8,128)S(1)}, f32[1,32,2048]{2,1,0:T(8,128)S(1)}, u32[]{:S(2)}, u32[]{:S(2)}) collective-permute-start(f32[1,32,2048]{2,1,0:T(8,128)S(1)} %get-tuple-element.52), channel_id=1, source_target_pairs={{0,4},{4,8},{8,12},{12,16},{16,20},{20,24},{24,28},{1,5},{5,9},{9,... | collective-permute-start | bytes 786440 | tf_op jit(solution)/shard_map/ppermute | solution.py:320
  43.0 6.7 %collective-permute-start.7 = (f32[1,32,2048]{2,1,0:T(8,128)S(1)}, f32[1,32,2048]{2,1,0:T(8,128)S(1)}, u32[]{:S(2)}, u32[]{:S(2)}) collective-permute-start(f32[1,32,2048]{2,1,0:T(8,128)S(1)} %get-tuple-element.53), channel_id=1, source_target_pairs={{4,0},{8,4},{12,8},{16,12},{20,16},{24,20},{28,24},{5,1},{9,5},{13... | collective-permute-start | bytes 786440 | tf_op jit(solution)/shard_map/ppermute | solution.py:321
  54.4 16.1 %collective-permute-start.8 = (f32[2,32,1024]{2,1,0:T(8,128)S(1)}, f32[2,32,1024]{2,1,0:T(8,128)S(1)}, u32[]{:S(2)}, u32[]{:S(2)}) collective-permute-start(f32[2,32,1024]{2,1,0:T(8,128)S(1)} %get-tuple-element.55), channel_id=1, source_target_pairs={{0,1},{1,2},{2,3},{3,0},{4,5},{5,6},{6,7},{7,4},{8,9},{9,10},{10,1... | collective-permute-start | bytes 786440 | tf_op jit(solution)/shard_map/ppermute | solution.py:318
  54.8 15.7 %collective-permute-start.9 = (f32[2,32,1024]{2,1,0:T(8,128)S(1)}, f32[2,32,1024]{2,1,0:T(8,128)S(1)}, u32[]{:S(2)}, u32[]{:S(2)}) collective-permute-start(f32[2,32,1024]{2,1,0:T(8,128)S(1)} %get-tuple-element.56), channel_id=1, source_target_pairs={{1,0},{2,1},{3,2},{0,3},{5,4},{6,5},{7,6},{4,7},{9,8},{10,9},{11,1... | collective-permute-start | bytes 786440 | tf_op jit(solution)/shard_map/ppermute | solution.py:319
  58.3 12.2 %collective-permute-start.10 = (f32[1,32,2048]{2,1,0:T(8,128)S(1)}, f32[1,32,2048]{2,1,0:T(8,128)S(1)}, u32[]{:S(2)}, u32[]{:S(2)}) collective-permute-start(f32[1,32,2048]{2,1,0:T(8,128)S(1)} %get-tuple-element.57), channel_id=1, source_target_pairs={{0,4},{4,8},{8,12},{12,16},{16,20},{20,24},{24,28},{1,5},{5,9},{9,... | collective-permute-start | bytes 786440 | tf_op jit(solution)/shard_map/ppermute | solution.py:320
  63.9 6.7 %collective-permute-start.11 = (f32[1,32,2048]{2,1,0:T(8,128)S(1)}, f32[1,32,2048]{2,1,0:T(8,128)S(1)}, u32[]{:S(2)}, u32[]{:S(2)}) collective-permute-start(f32[1,32,2048]{2,1,0:T(8,128)S(1)} %get-tuple-element.58), channel_id=1, source_target_pairs={{4,0},{8,4},{12,8},{16,12},{20,16},{24,20},{28,24},{5,1},{9,5},{13... | collective-permute-start | bytes 786440 | tf_op jit(solution)/shard_map/ppermute | solution.py:321
  75.6 15.7 %collective-permute-start.12 = (f32[2,32,1024]{2,1,0:T(8,128)S(1)}, f32[2,32,1024]{2,1,0:T(8,128)S(1)}, u32[]{:S(2)}, u32[]{:S(2)}) collective-permute-start(f32[2,32,1024]{2,1,0:T(8,128)S(1)} %get-tuple-element.60), channel_id=1, source_target_pairs={{0,1},{1,2},{2,3},{3,0},{4,5},{5,6},{6,7},{7,4},{8,9},{9,10},{10,1... | collective-permute-start | bytes 786440 | tf_op jit(solution)/shard_map/ppermute | solution.py:318
  75.7 15.7 %collective-permute-start.13 = (f32[2,32,1024]{2,1,0:T(8,128)S(1)}, f32[2,32,1024]{2,1,0:T(8,128)S(1)}, u32[]{:S(2)}, u32[]{:S(2)}) collective-permute-start(f32[2,32,1024]{2,1,0:T(8,128)S(1)} %get-tuple-element.61), channel_id=1, source_target_pairs={{1,0},{2,1},{3,2},{0,3},{5,4},{6,5},{7,6},{4,7},{9,8},{10,9},{11,1... | collective-permute-start | bytes 786440 | tf_op jit(solution)/shard_map/ppermute | solution.py:319
  79.5 11.9 %collective-permute-start.14 = (f32[1,32,2048]{2,1,0:T(8,128)S(1)}, f32[1,32,2048]{2,1,0:T(8,128)S(1)}, u32[]{:S(2)}, u32[]{:S(2)}) collective-permute-start(f32[1,32,2048]{2,1,0:T(8,128)S(1)} %get-tuple-element.62), channel_id=1, source_target_pairs={{0,4},{4,8},{8,12},{12,16},{16,20},{20,24},{24,28},{1,5},{5,9},{9,... | collective-permute-start | bytes 786440 | tf_op jit(solution)/shard_map/ppermute | solution.py:320
  84.7 6.7 %collective-permute-start.15 = (f32[1,32,2048]{2,1,0:T(8,128)S(1)}, f32[1,32,2048]{2,1,0:T(8,128)S(1)}, u32[]{:S(2)}, u32[]{:S(2)}) collective-permute-start(f32[1,32,2048]{2,1,0:T(8,128)S(1)} %get-tuple-element.63), channel_id=1, source_target_pairs={{4,0},{8,4},{12,8},{16,12},{20,16},{24,20},{28,24},{5,1},{9,5},{13... | collective-permute-start | bytes 786440 | tf_op jit(solution)/shard_map/ppermute | solution.py:321
  96.1 15.7 %collective-permute-start.16 = (f32[2,32,1024]{2,1,0:T(8,128)S(1)}, f32[2,32,1024]{2,1,0:T(8,128)S(1)}, u32[]{:S(2)}, u32[]{:S(2)}) collective-permute-start(f32[2,32,1024]{2,1,0:T(8,128)S(1)} %get-tuple-element.65), channel_id=1, source_target_pairs={{0,1},{1,2},{2,3},{3,0},{4,5},{5,6},{6,7},{7,4},{8,9},{9,10},{10,1... | collective-permute-start | bytes 786440 | tf_op jit(solution)/shard_map/ppermute | solution.py:318
  96.1 15.6 %collective-permute-start.17 = (f32[2,32,1024]{2,1,0:T(8,128)S(1)}, f32[2,32,1024]{2,1,0:T(8,128)S(1)}, u32[]{:S(2)}, u32[]{:S(2)}) collective-permute-start(f32[2,32,1024]{2,1,0:T(8,128)S(1)} %get-tuple-element.66), channel_id=1, source_target_pairs={{1,0},{2,1},{3,2},{0,3},{5,4},{6,5},{7,6},{4,7},{9,8},{10,9},{11,1... | collective-permute-start | bytes 786440 | tf_op jit(solution)/shard_map/ppermute | solution.py:319
  99.9 11.8 %collective-permute-start.18 = (f32[1,32,2048]{2,1,0:T(8,128)S(1)}, f32[1,32,2048]{2,1,0:T(8,128)S(1)}, u32[]{:S(2)}, u32[]{:S(2)}) collective-permute-start(f32[1,32,2048]{2,1,0:T(8,128)S(1)} %get-tuple-element.67), channel_id=1, source_target_pairs={{0,4},{4,8},{8,12},{12,16},{16,20},{20,24},{24,28},{1,5},{5,9},{9,... | collective-permute-start | bytes 786440 | tf_op jit(solution)/shard_map/ppermute | solution.py:320
  105.1 6.7 %collective-permute-start.19 = (f32[1,32,2048]{2,1,0:T(8,128)S(1)}, f32[1,32,2048]{2,1,0:T(8,128)S(1)}, u32[]{:S(2)}, u32[]{:S(2)}) collective-permute-start(f32[1,32,2048]{2,1,0:T(8,128)S(1)} %get-tuple-element.68), channel_id=1, source_target_pairs={{4,0},{8,4},{12,8},{16,12},{20,16},{24,20},{28,24},{5,1},{9,5},{13... | collective-permute-start | bytes 786440 | tf_op jit(solution)/shard_map/ppermute | solution.py:321
  116.5 41.2 %collective-permute-start.20 = (f32[2,32,1024]{2,1,0:T(8,128)S(1)}, f32[2,32,1024]{2,1,0:T(8,128)S(1)}, u32[]{:S(2)}, u32[]{:S(2)}) collective-permute-start(f32[2,32,1024]{2,1,0:T(8,128)S(1)} %get-tuple-element.70), channel_id=1, source_target_pairs={{0,1},{1,2},{2,3},{3,0},{4,5},{5,6},{6,7},{7,4},{8,9},{9,10},{10,1... | collective-permute-start | bytes 786440 | tf_op jit(solution)/shard_map/ppermute | solution.py:318
  116.5 41.2 %collective-permute-start.21 = (f32[2,32,1024]{2,1,0:T(8,128)S(1)}, f32[2,32,1024]{2,1,0:T(8,128)S(1)}, u32[]{:S(2)}, u32[]{:S(2)}) collective-permute-start(f32[2,32,1024]{2,1,0:T(8,128)S(1)} %get-tuple-element.71), channel_id=1, source_target_pairs={{1,0},{2,1},{3,2},{0,3},{5,4},{6,5},{7,6},{4,7},{9,8},{10,9},{11,1... | collective-permute-start | bytes 786440 | tf_op jit(solution)/shard_map/ppermute | solution.py:319
  120.4 37.4 %collective-permute-start.22 = (f32[1,32,2048]{2,1,0:T(8,128)S(1)}, f32[1,32,2048]{2,1,0:T(8,128)S(1)}, u32[]{:S(2)}, u32[]{:S(2)}) collective-permute-start(f32[1,32,2048]{2,1,0:T(8,128)S(1)} %get-tuple-element.72), channel_id=1, source_target_pairs={{0,4},{4,8},{8,12},{12,16},{16,20},{20,24},{24,28},{1,5},{5,9},{9,... | collective-permute-start | bytes 786440 | tf_op jit(solution)/shard_map/ppermute | solution.py:320
  125.5 32.2 %collective-permute-start.23 = (f32[1,32,2048]{2,1,0:T(8,128)S(1)}, f32[1,32,2048]{2,1,0:T(8,128)S(1)}, u32[]{:S(2)}, u32[]{:S(2)}) collective-permute-start(f32[1,32,2048]{2,1,0:T(8,128)S(1)} %get-tuple-element.73), channel_id=1, source_target_pairs={{4,0},{8,4},{12,8},{16,12},{20,16},{24,20},{28,24},{5,1},{9,5},{13... | collective-permute-start | bytes 786440 | tf_op jit(solution)/shard_map/ppermute | solution.py:321
  129.0 7.6 %collective-permute-start.25 = (f32[32,32]{1,0:T(8,128)S(1)}, f32[32,32]{1,0:T(8,128)S(1)}, u32[]{:S(2)}, u32[]{:S(2)}) collective-permute-start(f32[32,32]{1,0:T(8,128)S(1)} %add.68), channel_id=1, source_target_pairs={{0,8},{4,12},{8,0},{12,4},{16,24},{20,28},{24,16},{28,20},{1,9},{5... | collective-permute-start | bytes 12296 | tf_op jit(solution)/shard_map/ppermute | solution.py:309
  163.1 14.4 %collective-permute-start.34 = (f32[2,32,1024]{2,1,0:T(8,128)S(1)}, f32[2,32,1024]{2,1,0:T(8,128)S(1)}, u32[]{:S(2)}, u32[]{:S(2)}) collective-permute-start(f32[2,32,1024]{2,1,0:T(8,128)S(1)} %get-tuple-element.81), channel_id=1, source_target_pairs={{0,1},{1,2},{2,3},{3,0},{4,5},{5,6},{6,7},{7,4},{8,9},{9,10},{10,1... | collective-permute-start | bytes 786440 | tf_op jit(solution)/shard_map/ppermute | solution.py:318
  163.2 14.3 %collective-permute-start.35 = (f32[2,32,1024]{2,1,0:T(8,128)S(1)}, f32[2,32,1024]{2,1,0:T(8,128)S(1)}, u32[]{:S(2)}, u32[]{:S(2)}) collective-permute-start(f32[2,32,1024]{2,1,0:T(8,128)S(1)} %get-tuple-element.82), channel_id=1, source_target_pairs={{1,0},{2,1},{3,2},{0,3},{5,4},{6,5},{7,6},{4,7},{9,8},{10,9},{11,1... | collective-permute-start | bytes 786440 | tf_op jit(solution)/shard_map/ppermute | solution.py:319
  166.9 10.6 %collective-permute-start.36 = (f32[1,32,2048]{2,1,0:T(8,128)S(1)}, f32[1,32,2048]{2,1,0:T(8,128)S(1)}, u32[]{:S(2)}, u32[]{:S(2)}) collective-permute-start(f32[1,32,2048]{2,1,0:T(8,128)S(1)} %get-tuple-element.83), channel_id=1, source_target_pairs={{0,4},{4,8},{8,12},{12,16},{16,20},{20,24},{24,28},{1,5},{5,9},{9,... | collective-permute-start | bytes 786440 | tf_op jit(solution)/shard_map/ppermute | solution.py:320
  168.2 9.3 %collective-permute-start.37 = (f32[1,32,2048]{2,1,0:T(8,128)S(1)}, f32[1,32,2048]{2,1,0:T(8,128)S(1)}, u32[]{:S(2)}, u32[]{:S(2)}) collective-permute-start(f32[1,32,2048]{2,1,0:T(8,128)S(1)} %get-tuple-element.84), channel_id=1, source_target_pairs={{4,0},{8,4},{12,8},{16,12},{20,16},{24,20},{28,24},{5,1},{9,5},{13... | collective-permute-start | bytes 786440 | tf_op jit(solution)/shard_map/ppermute | solution.py:321
  169.7 13.3 %collective-permute-start.29 = (f32[32,32]{1,0:T(8,128)S(1)}, f32[32,32]{1,0:T(8,128)S(1)}, u32[]{:S(2)}, u32[]{:S(2)}) collective-permute-start(f32[32,32]{1,0:T(8,128)S(1)} %get-tuple-element.76), channel_id=1, source_target_pairs={{0,4},{4,0},{8,12},{12,8},{16,20},{20,16},{24,28},{28,24},{1,5},{5... | collective-permute-start | bytes 12296 | tf_op jit(solution)/shard_map/ppermute | solution.py:309
  195.1 4.7 %collective-permute-start.33 = (f32[32,32]{1,0:T(8,128)S(1)}, f32[32,32]{1,0:T(8,128)S(1)}, u32[]{:S(2)}, u32[]{:S(2)}) collective-permute-start(f32[32,32]{1,0:T(8,128)S(1)} %add.76), channel_id=1, source_target_pairs={{0,2},{1,3},{2,0},{3,1},{4,6},{5,7},{6,4},{7,5},{8,10},{9,11},{10,... | collective-permute-start | bytes 12296 | tf_op jit(solution)/shard_map/ppermute | solution.py:309
  197.4 6.1 %collective-permute-start.42 = (f32[32,32]{1,0:T(8,128)S(1)}, f32[32,32]{1,0:T(8,128)S(1)}, u32[]{:S(2)}, u32[]{:S(2)}) collective-permute-start(f32[32,32]{1,0:T(8,128)S(1)} %add.81), channel_id=1, source_target_pairs={{0,2},{1,3},{2,0},{3,1},{4,6},{5,7},{6,4},{7,5},{8,10},{9,11},{10,... | collective-permute-start | bytes 12296 | tf_op jit(solution)/shard_map/ppermute | solution.py:309
  (15 other events, 54.2 us)

commit v2 on v1

--- a/solution.py
+++ b/solution.py
@@ -46,40 +46,58 @@
         scratch_shapes=list(scratch),
         name=name,
         cost_estimate=pl.CostEstimate(flops=flops, bytes_accessed=moved, transcendentals=0),
-        compiler_params=pltpu.CompilerParams(vmem_limit_bytes=48 << 20),
+        compiler_params=pltpu.CompilerParams(vmem_limit_bytes=6 << 20),
     )(*ins)
 
 
 def prep_kernel(tiles_ref, out_ref):
-    high, low = split(tiles_ref[...])
-    out_ref[:, :, :TILE, :] = high
-    out_ref[:, :, TILE:, :] = low
+    for r in range(out_ref.shape[1]):
+        for n in range(TPR):
+            high, low = split(tiles_ref[0, r * TPR + n])
+            out_ref[0, r, :TILE, n * TILE : (n + 1) * TILE] = high
+            out_ref[0, r, TILE:, n * TILE : (n + 1) * TILE] = low
 
 
 def prep(tiles):
     slices, count = tiles.shape[:2]
-    step = 16
+    rows = count // TPR
+    step = 4
     return pl.pallas_call(
         prep_kernel,
-        grid=(slices, count // step),
-        out_shape=VM((slices, count, 2 * TILE, TILE), BF16),
-        in_specs=[pl.BlockSpec((1, step, TILE, TILE), lambda s, i: (s, i, 0, 0))],
-        out_specs=pl.BlockSpec((1, step, 2 * TILE, TILE), lambda s, i: (s, i, 0, 0)),
+        grid=(slices, rows // step),
+        out_shape=VM((slices, rows, 2 * TILE, TPR * TILE), BF16),
+        in_specs=[pl.BlockSpec((1, step * TPR, TILE, TILE), lambda s, i: (s, i, 0, 0))],
+        out_specs=pl.BlockSpec((1, step, 2 * TILE, TPR * TILE), lambda s, i: (s, i, 0, 0)),
         name="prep",
         cost_estimate=pl.CostEstimate(
             flops=0, bytes_accessed=2 * 4 * tiles.size, transcendentals=0
         ),
-        compiler_params=pltpu.CompilerParams(vmem_limit_bytes=32 << 20),
+        compiler_params=pltpu.CompilerParams(vmem_limit_bytes=8 << 20),
     )(tiles)
 
 
-def edges(y_ref, head_ref, tail_ref, first_ref, last_ref):
+def edges(odd_ref, y_ref, inner_ref, outer_ref, near_ref, far_ref):
     width = HB * TILE
     points = y_ref.shape[2]
-    head_ref[...] = y_ref[:, :, :width]
-    tail_ref[...] = y_ref[:, :, points - width :]
-    first_ref[...] = y_ref[:1]
-    last_ref[...] = y_ref[y_ref.shape[0] - 1 :]
+    final = y_ref.shape[0] - 1
+    head = lambda: y_ref[:, :, :width]
+    tail = lambda: y_ref[:, :, points - width :]
+    first = lambda: y_ref[:1]
+    last = lambda: y_ref[final:]
+    for axis, inner, outer, low, high in (
+        (0, inner_ref, outer_ref, head, tail),
+        (1, near_ref, far_ref, first, last),
+    ):
+
+        @pl.when(odd_ref[axis] == 0)
+        def _(inner=inner, outer=outer, low=low, high=high):
+            inner[...] = high()
+            outer[...] = low()
+
+        @pl.when(odd_ref[axis] != 0)
+        def _(inner=inner, outer=outer, low=low, high=high):
+            inner[...] = low()
+            outer[...] = high()
 
 
 def edge_shapes(shape):
@@ -88,23 +106,29 @@
     return [(shape, F32), (side, F32), (side, F32), ((1, width, points), F32), ((1, width, points), F32)]
 
 
-def start_kernel(x_ref, y_ref, *edge_refs):
+def start_kernel(odd_ref, x_ref, y_ref, *edge_refs):
     y_ref[...] = x_ref[...]
-    edges(y_ref, *edge_refs)
-
-
-def start(block):
+    edges(odd_ref, y_ref, *edge_refs)
+
+
+def start(odd, block):
     return call(
-        start_kernel, [block], edge_shapes(block.shape), specs=[WHOLE], moved=16 * block.size, name="start"
+        start_kernel,
+        [odd, block],
+        edge_shapes(block.shape),
+        specs=[SCALARS, WHOLE],
+        moved=16 * block.size,
+        name="start",
     )
-
-
-def matmul_tile(lhs, tile):
-    return lax.dot_general(lhs, tile, NT, preferred_element_type=F32)
 
 
 def fold(product, width):
     return product[:width, :TILE] + product[:width, TILE:] + product[width:, :TILE]
+
+
+def row_product(halves_ref, places, tiles, width):
+    left = jnp.concatenate([halves_ref[where] for where in places], axis=1)
+    return fold(lax.dot_general(left, tiles, NT, preferred_element_type=F32), width)
 
 
 def local_kernel(place_ref, tiles_ref, y_ref, out_ref, halves_ref):
@@ -112,19 +136,18 @@
     blocks = points // TILE
     for s in range(slices):
         for b in range(blocks):
-            halves_ref[s, b] = stacked(y_ref[s, :, b * TILE : (b + 1) * TILE])
-        halves_ref[s, blocks] = jnp.zeros((2 * width, TILE), BF16)
+            halves_ref[s * blocks + b] = stacked(y_ref[s, :, b * TILE : (b + 1) * TILE])
+    halves_ref[slices * blocks] = jnp.zeros((2 * width, TILE), BF16)
 
     def row(i, carry):
         s, r = i // blocks, i % blocks
-        total = None
+        places = []
         for n in range(TPR):
             where = place_ref[s, r * TPR + n] - HB
             inside = jnp.logical_and(where >= 0, where < blocks)
-            where = jnp.where(inside, where, blocks)
-            term = matmul_tile(halves_ref[s, where], tiles_ref[s, r * TPR + n])
-            total = term if total is None else total + term
-        out_ref[s, :, pl.ds(pl.multiple_of(r * TILE, TILE), TILE)] = fold(total, width)
+            places.append(jnp.where(inside, s * blocks + where, slices * blocks))
+        here = pl.ds(pl.multiple_of(r * TILE, TILE), TILE)
+        out_ref[s, :, here] = row_product(halves_ref, places, tiles_ref[s, r], width)
         return carry
 
     lax.fori_loop(0, slices * blocks, row, 0, unroll=4)
@@ -138,7 +161,7 @@
         [place, near(tiles), near(y)],
         [(y.shape, F32)],
         specs=[SCALARS, WHOLE, WHOLE],
-        scratch=[VM((slices, blocks + 1, 2 * width, TILE), BF16)],
+        scratch=[VM((slices * blocks + 1, 2 * width, TILE), BF16)],
         flops=2 * slices * blocks * TPR * 4 * width * TILE * TILE,
         moved=8 * y.size,
         name="local",
@@ -162,8 +185,8 @@
 def finish_kernel(mode, scale, *refs):
     refs = list(refs)
     take = lambda n: [refs.pop(0) for _ in range(n)]
-    place_ref, degree_ref, tiles_ref, part_ref, y_ref = take(5)
-    left_ref, right_ref, before_ref, after_ref = take(4)
+    place_ref, odd_ref, tiles_ref, part_ref, y_ref = take(5)
+    inner_ref, outer_ref, near_ref, far_ref = take(4)
     previous_ref = take(1)[0] if mode in ("step", "gram", "mixed") else None
     matrix_ref = take(1)[0] if mode == "mixed" else None
     if mode == "image":
@@ -178,26 +201,47 @@
     blocks = points // TILE
     for s in range(slices):
         for b in range(HB):
-            halves_ref[s, b] = stacked(left_ref[s, :, b * TILE : (b + 1) * TILE])
-            halves_ref[s, HB + b] = stacked(right_ref[s, :, b * TILE : (b + 1) * TILE])
-        halves_ref[s, 2 * HB] = jnp.zeros((2 * width, TILE), BF16)
+            at = s * 2 * HB + b
+            halves_ref[at] = stacked(inner_ref[s, :, b * TILE : (b + 1) * TILE])
+            halves_ref[at + HB] = stacked(outer_ref[s, :, b * TILE : (b + 1) * TILE])
+    zero = slices * 2 * HB
+    halves_ref[zero] = jnp.zeros((2 * width, TILE), BF16)
+    left_at = jnp.where(odd_ref[0] == 0, HB, 0)
+    right_at = HB - left_at - HB - blocks
+    time_odd = odd_ref[1] != 0
+    opening = odd_ref[2] != 0
+    closing = odd_ref[3] != 0
 
     for s in range(slices):
-
-        def row(r, carry, s=s):
-            total = None
+        degree = 2.0
+        if s == 0:
+            degree = degree - jnp.where(opening, 1.0, 0.0)
+        if s == slices - 1:
+            degree = degree - jnp.where(closing, 1.0, 0.0)
+
+        def row(r, carry, s=s, degree=degree):
+            places = []
             for n in range(1, TPR):
                 where = place_ref[s, r * TPR + n]
                 right = where >= HB + blocks
-                where = jnp.where(right, where - blocks, jnp.where(where < HB, where, 2 * HB))
-                term = matmul_tile(halves_ref[s, where], tiles_ref[s, r * TPR + n])
-                total = term if total is None else total + term
+                left = where < HB
+                at = s * 2 * HB + where + jnp.where(right, right_at, left_at)
+                places.append(jnp.where(jnp.logical_or(left, right), at, zero))
+            product = row_product(halves_ref, places, tiles_ref[s, r, :, TILE:], width)
             here = pl.ds(pl.multiple_of(r * TILE, TILE), TILE)
             y = y_ref[s, :, here]
-            before = before_ref[0, :, here] if s == 0 else y_ref[s - 1, :, here]
-            after = after_ref[0, :, here] if s == slices - 1 else y_ref[s + 1, :, here]
-            image = part_ref[s, :, here] + fold(total, width)
-            image = image + INFLATION_FACTOR * (degree_ref[s] * y - before - after)
+            if s == 0:
+                before = jnp.where(time_odd, near_ref[0, :, here], far_ref[0, :, here])
+                before = jnp.where(opening, 0.0, before)
+            else:
+                before = y_ref[s - 1, :, here]
+            if s == slices - 1:
+                after = jnp.where(time_odd, far_ref[0, :, here], near_ref[0, :, here])
+                after = jnp.where(closing, 0.0, after)
+            else:
+                after = y_ref[s + 1, :, here]
+            image = part_ref[s, :, here] + product
+            image = image + INFLATION_FACTOR * (degree * y - before - after)
             if mode != "image":
                 image = (image - CENTER * y) * scale
                 if previous_ref is not None:
@@ -211,7 +255,7 @@
         for s in range(slices):
             new_ref[s] = mix(matrix_ref[...], new_ref[s])
     if mode != "image":
-        edges(new_ref, *edge_refs)
+        edges(odd_ref, new_ref, *edge_refs)
     if gram_ref is not None:
         base_ref = y_ref if mode == "image" else new_ref
         total = inner(base_ref[0], new_ref[0])
@@ -220,10 +264,10 @@
         gram_ref[...] = total
 
 
-def finish(mode, scale, place, degree, tiles, part, y, halo, previous=None, matrix=None):
+def finish(mode, scale, place, odd, tiles, part, y, halo, previous=None, matrix=None):
     slices, width, points = y.shape
     blocks = points // TILE
-    ins = [place, degree] + [near(v) for v in (tiles, part, y, *halo)]
+    ins = [place, odd] + [near(v) for v in (tiles, part, y, *halo)]
     specs = [SCALARS, SCALARS] + [WHOLE] * 7
     for extra in (previous, matrix):
         if extra is not None:
@@ -232,7 +276,7 @@
     outs = [] if mode == "image" else edge_shapes(y.shape)
     if mode in ("gram", "mixed", "image"):
         outs = outs + [((width, width), F32)]
-    scratch = [VM((slices, 2 * HB + 1, 2 * width, TILE), BF16)]
+    scratch = [VM((slices * 2 * HB + 1, 2 * width, TILE), BF16)]
     if mode == "image":
         scratch.append(VM(y.shape, F32))
     return call(
@@ -279,7 +323,7 @@
         out_specs=[WHOLE, WHOLE],
         name="orth",
         cost_estimate=pl.CostEstimate(flops=2 * width * y.size, bytes_accessed=8 * y.size, transcendentals=0),
-        compiler_params=pltpu.CompilerParams(vmem_limit_bytes=16 << 20),
+        compiler_params=pltpu.CompilerParams(vmem_limit_bytes=6 << 20),
     )(near(gram), near(y))
 
 
@@ -311,15 +355,23 @@
     return value
 
 
+def inner_pairs(axis):
+    count = lax.axis_size(axis)
+    return [(i, i ^ 1) for i in range(count)]
+
+
+def outer_pairs(axis):
+    count = lax.axis_size(axis)
+    return [(i, (i + 1) % count if i % 2 else (i - 1) % count) for i in range(count)]
+
+
 def exchange(edge):
-    head, tail, first, last = edge
-    ring = lax.axis_size("space")
-    line = lax.axis_size("tm")
-    left = lax.ppermute(tail, "space", [(i, (i + 1) % ring) for i in range(ring)])
-    right = lax.ppermute(head, "space", [((i + 1) % ring, i) for i in range(ring)])
-    before = lax.ppermute(last, "tm", [(i, i + 1) for i in range(line - 1)])
-    after = lax.ppermute(first, "tm", [(i + 1, i) for i in range(line - 1)])
-    return left, right, before, after
+    inner, outer, near_slice, far_slice = edge
+    inner = lax.ppermute(inner, "space", inner_pairs("space"))
+    outer = lax.ppermute(outer, "space", outer_pairs("space"))
+    far_slice = lax.ppermute(far_slice, "tm", outer_pairs("tm"))
+    near_slice = lax.ppermute(near_slice, "tm", inner_pairs("tm"))
+    return inner, outer, near_slice, far_slice
 
 
 def body(start_block, stiffness_tiles, tile_columns):
@@ -329,17 +381,19 @@
     blocks_all = lax.axis_size("space") * local_blocks
     place = (tile_columns - first_block + HB) % blocks_all
     count_all = slices * local_points * lax.axis_size("tm") * lax.axis_size("space")
-    slice_index = lax.axis_index("tm") * slices + jnp.arange(slices, dtype=jnp.int32)
-    last_slice = lax.axis_size("tm") * slices - 1
-    degree = 2.0 - (slice_index == 0).astype(F32) - (slice_index == last_slice).astype(F32)
-
-    y, *edge = start(start_block)
+    time_index = lax.axis_index("tm")
+    ends = (time_index == 0, time_index == lax.axis_size("tm") - 1)
+    odd = jnp.stack(
+        [lax.axis_index("space") % 2, time_index % 2, ends[0].astype(jnp.int32), ends[1].astype(jnp.int32)]
+    )
+
+    y, *edge = start(odd, start_block)
     tiles = prep(stiffness_tiles)
 
     def apply(mode, scale, y, edge, previous=None, matrix=None):
         halo = exchange(edge)
         part = local_part(place, tiles, y)
-        return finish(mode, scale, place, degree, tiles, part, y, halo, previous, matrix)
+        return finish(mode, scale, place, odd, tiles, part, y, halo, previous, matrix)
 
     def run_filter(y, edge, mode, matrix=None):
         y0 = y

time: 205 us -> 172 us (0.84)
  starting transfers between devices: 81.8 us -> 49.8 us
  waiting for transfers between devices: 25.3 us -> 38.8 us
  local copies, waits for them, and re-layouts: 13 us -> 5.05 us
  Pallas kernels: 81.4 us -> 76.8 us
    ppermute x28, starting transfers between devices: 65.6 us -> 37.8 us  [the longest x7 15.9 us: exchange(): far_slice = lax.ppermute(far_slice, 'tm', outer_pairs('tm'))]
    ppermute x28, waiting for transfers between devices: 0.07 us -> 15.8 us  [the longest x7 8.41 us: exchange(): outer = lax.ppermute(outer, 'space', outer_pairs('space'))]
    unnamed x8 -> x6, local copies, waits for them, and re-layouts: 13 us -> 5.05 us
    pallas_call x16, Pallas kernels: 72.6 us -> 67.7 us  [call(): pl.pallas_call(kernel, out_shape=out_shape, in_specs=specs, out_specs=[WH...]
    ppermute x15, starting transfers between devices: 16.2 us -> 12 us  [total_over(): lax.ppermute(value, axis, [(i, i ^ stride) for i in range(count)])]
    ppermute x15, waiting for transfers between devices: 25.2 us -> 23 us  [total_over(): lax.ppermute(value, axis, [(i, i ^ stride) for i in range(count)])]
  transfers between devices with their start and end apart: 43 -> 43, of which waited for: 11 -> 18; matrix products, arithmetic and copies ran while one was open for 1% -> 0% of each run, Pallas kernels for 25% -> 28%
where the time goes in v2:
time: 172 us
  Pallas kernels  76.8 us (45%)
  starting transfers between devices  49.8 us (29%)
  waiting for transfers between devices  38.8 us (23%)
  local copies, waits for them, and re-layouts  5.05 us (3%)
    pallas_call x16, Pallas kernels, call(): pl.pallas_call(kernel, out_shape=out_shape, in_specs=specs, out_specs=[WH...  67.7 us
    ppermute x15, waiting for transfers between devices, total_over(): lax.ppermute(value, axis, [(i, i ^ stride) for i in range(count)])  23 us
    ppermute x7, starting transfers between devices, exchange(): far_slice = lax.ppermute(far_slice, 'tm', outer_pairs('tm'))  15.9 us
    ppermute x7, starting transfers between devices, exchange(): outer = lax.ppermute(outer, 'space', outer_pairs('space'))  12.4 us
    ppermute x15, starting transfers between devices, total_over(): lax.ppermute(value, axis, [(i, i ^ stride) for i in range(count)])  12 us
    ppermute x7, starting transfers between devices, exchange(): inner = lax.ppermute(inner, 'space', inner_pairs('space'))  9.54 us
    ppermute x7, waiting for transfers between devices, exchange(): outer = lax.ppermute(outer, 'space', outer_pairs('space'))  8.41 us
    pallas_call x2, Pallas kernels, orth(): pl.pallas_call(functools.partial(orth_kernel, float(count)), out_shape=[j...  7.36 us
  transfers between devices with their start and end apart: 43, of which 18 were waited for; matrix products, arithmetic and copies ran while one was open for 0% of the time, Pallas kernels for 28%

profile of v2, /device:TPU:0, one launch (start us, length us, event | category | flops | bytes accessed | tf_op | source)
XLA Modules:
  0.0 171.5 jit_solution(14651060314864863946)
XLA Ops:
  2.4 3.1 %collective-permute-start = (f32[2,32,1024]{2,1,0:T(8,128)S(1)}, f32[2,32,1024]{2,1,0:T(8,128)S(1)}, u32[]{:S(2)}, u32[]{:S(2)}) collective-permute-start(f32[2,32,1024]{2,1,0:T(8,128)S(1)} %get-tuple-element.45), channel_id=1, source_target_pairs={{0,1},{1,0},{2,3},{3,2},{4,5},{5,4},{6,7},{7,6},{8,9},{9,8},{10,11... | collective-permute-start | bytes 786440 | tf_op jit(solution)/shard_map/ppermute | solution.py:370
  5.5 2.5 %collective-permute-start.1 = (f32[2,32,1024]{2,1,0:T(8,128)S(1)}, f32[2,32,1024]{2,1,0:T(8,128)S(1)}, u32[]{:S(2)}, u32[]{:S(2)}) collective-permute-start(f32[2,32,1024]{2,1,0:T(8,128)S(1)} %get-tuple-element.46), channel_id=1, source_target_pairs={{0,3},{1,2},{2,1},{3,0},{4,7},{5,6},{6,5},{7,4},{8,11},{9,10},{10,... | collective-permute-start | bytes 786440 | tf_op jit(solution)/shard_map/ppermute | solution.py:371
  8.0 2.6 %collective-permute-start.3 = (f32[1,32,2048]{2,1,0:T(8,128)S(1)}, f32[1,32,2048]{2,1,0:T(8,128)S(1)}, u32[]{:S(2)}, u32[]{:S(2)}) collective-permute-start(f32[1,32,2048]{2,1,0:T(8,128)S(1)} %get-tuple-element.48), channel_id=1, source_target_pairs={{0,28},{4,8},{8,4},{12,16},{16,12},{20,24},{24,20},{28,0},{1,29},{... | collective-permute-start | bytes 786440 | tf_op jit(solution)/shard_map/ppermute | solution.py:372
  10.6 4.0 %copy-done = f32[2,80,128,128]{3,2,1,0:T(8,128)S(1)} copy-done((f32[2,80,128,128]{3,2,1,0:T(8,128)S(1)}, f32[2,80,128,128]{3,2,1,0:T(8,128)}, u32[]{:S(2)}) %copy-start) | copy-done | bytes 10485784
  16.4 4.9 %local.7.refs_3_ = f32[2,32,2048]{2,1,0:T(8,128)S(1)} custom-call(s32[2,80]{1,0:T(2,128)S(1)} %and_select_fusion.place_ref.refs_0_, bf16[2,16,256,640]{3,2,1,0:T(8,128)(2,1)S(1)} %prep.1.tiles_ref.refs_2_, f32[2,32,2048]{2,1,0:T(8,128)S(1)} %get-tuple-element.44.y_ref.refs_4_.refs_9_), custom_call_target="tpu_custom_call" | custom-call | flops 671088640 | bytes 1048576 | tf_op jit(solution)/shard_map/local/pallas_call | solution.py:41
  21.4 4.3 %finish_first.2 = (f32[2,32,2048]{2,1,0:T(8,128)S(1)}, f32[2,32,1024]{2,1,0:T(8,128)S(1)}, f32[2,32,1024]{2,1,0:T(8,128)S(1)}, f32[1,32,2048]{2,1,0:T(8,128)S(1)}, f32[1,32,2048]{2,1,0:T(8,128)S(1)}) custom-call(s32[2,80]{1,0:T(2,128)S(1)} %and_select_fusion.place_ref.refs_0_, s32[4]{0:T(128)S(1)} %pad_add_fusion.odd_ref.refs_1_, ...), custom_call_target="tpu_custom_call" | custom-call | flops 671088640 | bytes 3145728 | tf_op jit(solution)/shard_map/finish_first/pallas_call | solution.py:41
  27.4 2.6 %collective-permute-start.7 = (f32[1,32,2048]{2,1,0:T(8,128)S(1)}, f32[1,32,2048]{2,1,0:T(8,128)S(1)}, u32[]{:S(2)}, u32[]{:S(2)}) collective-permute-start(f32[1,32,2048]{2,1,0:T(8,128)S(1)} %get-tuple-element.53), channel_id=1, source_target_pairs={{0,28},{4,8},{8,4},{12,16},{16,12},{20,24},{24,20},{28,0},{1,29},{... | collective-permute-start | bytes 786440 | tf_op jit(solution)/shard_map/ppermute | solution.py:372
  29.9 4.9 %local.8.refs_3_ = f32[2,32,2048]{2,1,0:T(8,128)S(1)} custom-call(s32[2,80]{1,0:T(2,128)S(1)} %and_select_fusion.place_ref.refs_0_, bf16[2,16,256,640]{3,2,1,0:T(8,128)(2,1)S(1)} %prep.1.tiles_ref.refs_2_, f32[2,32,2048]{2,1,0:T(8,128)S(1)} %get-tuple-element.49.y_ref.refs_4_.refs_9_), custom_call_target="tpu_custom_call" | custom-call | flops 671088640 | bytes 1048576 | tf_op jit(solution)/shard_map/local/pallas_call | solution.py:41
  34.8 3.8 %collective-permute-done.4.refs_5_ = f32[2,32,1024]{2,1,0:T(8,128)S(1)} collective-permute-done((f32[2,32,1024]{2,1,0:T(8,128)S(1)}, f32[2,32,1024]{2,1,0:T(8,128)S(1)}, u32[]{:S(2)}, u32[]{:S(2)}) %collective-permute-start.4) | collective-permute-done | bytes 262176 | tf_op jit(solution)/shard_map/ppermute | solution.py:370
  38.6 4.3 %finish_step.2 = (f32[2,32,2048]{2,1,0:T(8,128)S(1)}, f32[2,32,1024]{2,1,0:T(8,128)S(1)}, f32[2,32,1024]{2,1,0:T(8,128)S(1)}, f32[1,32,2048]{2,1,0:T(8,128)S(1)}, f32[1,32,2048]{2,1,0:T(8,128)S(1)}) custom-call(s32[2,80]{1,0:T(2,128)S(1)} %and_select_fusion.place_ref.refs_0_, s32[4]{0:T(128)S(1)} %pad_add_fusion.odd_ref.refs_1_, ...), custom_call_target="tpu_custom_call" | custom-call | flops 671088640 | bytes 3145728 | tf_op jit(solution)/shard_map/finish_step/pallas_call | solution.py:41
  47.2 4.9 %local.9.refs_3_ = f32[2,32,2048]{2,1,0:T(8,128)S(1)} custom-call(s32[2,80]{1,0:T(2,128)S(1)} %and_select_fusion.place_ref.refs_0_, bf16[2,16,256,640]{3,2,1,0:T(8,128)(2,1)S(1)} %prep.1.tiles_ref.refs_2_, f32[2,32,2048]{2,1,0:T(8,128)S(1)} %get-tuple-element.54.y_ref.refs_4_), custom_call_target="tpu_custom_call" | custom-call | flops 671088640 | bytes 1048576 | tf_op jit(solution)/shard_map/local/pallas_call | solution.py:41
  52.1 3.7 %collective-permute-done.9.refs_6_ = f32[2,32,1024]{2,1,0:T(8,128)S(1)} collective-permute-done((f32[2,32,1024]{2,1,0:T(8,128)S(1)}, f32[2,32,1024]{2,1,0:T(8,128)S(1)}, u32[]{:S(2)}, u32[]{:S(2)}) %collective-permute-start.9) | collective-permute-done | bytes 262176 | tf_op jit(solution)/shard_map/ppermute | solution.py:371
  55.8 4.7 %finish_gram.1 = (f32[2,32,2048]{2,1,0:T(8,128)S(1)}, f32[2,32,1024]{2,1,0:T(8,128)S(1)}, f32[2,32,1024]{2,1,0:T(8,128)S(1)}, f32[1,32,2048]{2,1,0:T(8,128)S(1)}...) custom-call(s32[2,80]{1,0:T(2,128)S(1)} %and_select_fusion.place_ref.refs_0_, s32[4]{0:T(128)S(1)} %pad_add_fusion.odd_ref.refs_1_, ...), custom_call_target="tpu_custom_call" | custom-call | flops 671088640 | bytes 3145728 | tf_op jit(solution)/shard_map/finish_gram/pallas_call | solution.py:41
  61.5 2.5 %collective-permute-start.13 = (f32[2,32,1024]{2,1,0:T(8,128)S(1)}, f32[2,32,1024]{2,1,0:T(8,128)S(1)}, u32[]{:S(2)}, u32[]{:S(2)}) collective-permute-start(f32[2,32,1024]{2,1,0:T(8,128)S(1)} %get-tuple-element.61), channel_id=1, source_target_pairs={{0,3},{1,2},{2,1},{3,0},{4,7},{5,6},{6,5},{7,4},{8,11},{9,10},{10,... | collective-permute-start | bytes 786440 | tf_op jit(solution)/shard_map/ppermute | solution.py:371
  66.3 4.9 %local.10.refs_3_ = f32[2,32,2048]{2,1,0:T(8,128)S(1)} custom-call(s32[2,80]{1,0:T(2,128)S(1)} %and_select_fusion.place_ref.refs_0_, bf16[2,16,256,640]{3,2,1,0:T(8,128)(2,1)S(1)} %prep.1.tiles_ref.refs_2_, f32[2,32,2048]{2,1,0:T(8,128)S(1)} %get-tuple-element.59.y_ref.refs_4_.refs_9_), custom_call_target="tpu_custom_call" | custom-call | flops 671088640 | bytes 1048576 | tf_op jit(solution)/shard_map/local/pallas_call | solution.py:41
  71.2 3.5 %collective-permute-done.13.refs_6_ = f32[2,32,1024]{2,1,0:T(8,128)S(1)} collective-permute-done((f32[2,32,1024]{2,1,0:T(8,128)S(1)}, f32[2,32,1024]{2,1,0:T(8,128)S(1)}, u32[]{:S(2)}, u32[]{:S(2)}) %collective-permute-start.13) | collective-permute-done | bytes 262176 | tf_op jit(solution)/shard_map/ppermute | solution.py:371
  74.7 4.3 %finish_first.3 = (f32[2,32,2048]{2,1,0:T(8,128)S(1)}, f32[2,32,1024]{2,1,0:T(8,128)S(1)}, f32[2,32,1024]{2,1,0:T(8,128)S(1)}, f32[1,32,2048]{2,1,0:T(8,128)S(1)}, f32[1,32,2048]{2,1,0:T(8,128)S(1)}) custom-call(s32[2,80]{1,0:T(2,128)S(1)} %and_select_fusion.place_ref.refs_0_, s32[4]{0:T(128)S(1)} %pad_add_fusion.odd_ref.refs_1_, ...), custom_call_target="tpu_custom_call" | custom-call | flops 671088640 | bytes 3145728 | tf_op jit(solution)/shard_map/finish_first/pallas_call | solution.py:41
  79.7 2.6 %collective-permute-start.17 = (f32[2,32,1024]{2,1,0:T(8,128)S(1)}, f32[2,32,1024]{2,1,0:T(8,128)S(1)}, u32[]{:S(2)}, u32[]{:S(2)}) collective-permute-start(f32[2,32,1024]{2,1,0:T(8,128)S(1)} %get-tuple-element.66), channel_id=1, source_target_pairs={{0,3},{1,2},{2,1},{3,0},{4,7},{5,6},{6,5},{7,4},{8,11},{9,10},{10,... | collective-permute-start | bytes 786440 | tf_op jit(solution)/shard_map/ppermute | solution.py:371
  84.6 4.9 %local.11.refs_3_ = f32[2,32,2048]{2,1,0:T(8,128)S(1)} custom-call(s32[2,80]{1,0:T(2,128)S(1)} %and_select_fusion.place_ref.refs_0_, bf16[2,16,256,640]{3,2,1,0:T(8,128)(2,1)S(1)} %prep.1.tiles_ref.refs_2_, f32[2,32,2048]{2,1,0:T(8,128)S(1)} %get-tuple-element.64.y_ref.refs_4_.refs_9_), custom_call_target="tpu_custom_call" | custom-call | flops 671088640 | bytes 1048576 | tf_op jit(solution)/shard_map/local/pallas_call | solution.py:41
  89.5 3.0 %collective-permute-done.16.refs_5_ = f32[2,32,1024]{2,1,0:T(8,128)S(1)} collective-permute-done((f32[2,32,1024]{2,1,0:T(8,128)S(1)}, f32[2,32,1024]{2,1,0:T(8,128)S(1)}, u32[]{:S(2)}, u32[]{:S(2)}) %collective-permute-start.16) | collective-permute-done | bytes 262176 | tf_op jit(solution)/shard_map/ppermute | solution.py:370
  92.5 4.3 %finish_step.3 = (f32[2,32,2048]{2,1,0:T(8,128)S(1)}, f32[2,32,1024]{2,1,0:T(8,128)S(1)}, f32[2,32,1024]{2,1,0:T(8,128)S(1)}, f32[1,32,2048]{2,1,0:T(8,128)S(1)}, f32[1,32,2048]{2,1,0:T(8,128)S(1)}) custom-call(s32[2,80]{1,0:T(2,128)S(1)} %and_select_fusion.place_ref.refs_0_, s32[4]{0:T(128)S(1)} %pad_add_fusion.odd_ref.refs_1_, ...), custom_call_target="tpu_custom_call" | custom-call | flops 671088640 | bytes 3145728 | tf_op jit(solution)/shard_map/finish_step/pallas_call | solution.py:41
  103.2 5.4 %collective-permute-done.25 = f32[32,32]{1,0:T(8,128)S(1)} collective-permute-done((f32[32,32]{1,0:T(8,128)S(1)}, f32[32,32]{1,0:T(8,128)S(1)}, u32[]{:S(2)}, u32[]{:S(2)}) %collective-permute-start.25) | collective-permute-done | bytes 4128 | tf_op jit(solution)/shard_map/ppermute | solution.py:353
  109.6 2.7 %collective-permute-done.26 = f32[32,32]{1,0:T(8,128)S(1)} collective-permute-done((f32[32,32]{1,0:T(8,128)S(1)}, f32[32,32]{1,0:T(8,128)S(1)}, u32[]{:S(2)}, u32[]{:S(2)}) %collective-permute-start.26) | collective-permute-done | bytes 4128 | tf_op jit(solution)/shard_map/ppermute | solution.py:353
  112.8 3.3 %collective-permute-done.27 = f32[32,32]{1,0:T(8,128)S(1)} collective-permute-done((f32[32,32]{1,0:T(8,128)S(1)}, f32[32,32]{1,0:T(8,128)S(1)}, u32[]{:S(2)}, u32[]{:S(2)}) %collective-permute-start.27) | collective-permute-done | bytes 4128 | tf_op jit(solution)/shard_map/ppermute | solution.py:353
  116.9 3.9 %collective-permute-done.28 = f32[32,32]{1,0:T(8,128)S(1)} collective-permute-done((f32[32,32]{1,0:T(8,128)S(1)}, f32[32,32]{1,0:T(8,128)S(1)}, u32[]{:S(2)}, u32[]{:S(2)}) %collective-permute-start.28) | collective-permute-done | bytes 4128 | tf_op jit(solution)/shard_map/ppermute | solution.py:353
  120.8 3.7 %orth.2 = (f32[2,32,2048]{2,1,0:T(8,128)}, f32[32,32]{1,0:T(8,128)S(1)}) custom-call(f32[32,32]{1,0:T(8,128)S(1)} %add.73.gram_ref, f32[2,32,2048]{2,1,0:T(8,128)S(1)} %get-tuple-element.59.y_ref.refs_4_.refs_9_), custom_call_target="tpu_custom_call" | custom-call | flops 8388608 | bytes 1048576 | tf_op jit(solution)/shard_map/orth/pallas_call | solution.py:319
  124.5 4.9 %local.12.refs_3_ = f32[2,32,2048]{2,1,0:T(8,128)S(1)} custom-call(s32[2,80]{1,0:T(2,128)S(1)} %and_select_fusion.place_ref.refs_0_, bf16[2,16,256,640]{3,2,1,0:T(8,128)(2,1)S(1)} %prep.1.tiles_ref.refs_2_, f32[2,32,2048]{2,1,0:T(8,128)S(1)} %get-tuple-element.69.y_ref.refs_4_), custom_call_target="tpu_custom_call" | custom-call | flops 671088640 | bytes 1048576 | tf_op jit(solution)/shard_map/local/pallas_call | solution.py:41
  129.4 5.3 %finish_mixed.1 = (f32[2,32,2048]{2,1,0:T(8,128)S(1)}, f32[2,32,1024]{2,1,0:T(8,128)S(1)}, f32[2,32,1024]{2,1,0:T(8,128)S(1)}, f32[1,32,2048]{2,1,0:T(8,128)S(1)...) custom-call(s32[2,80]{1,0:T(2,128)S(1)} %and_select_fusion.place_ref.refs_0_, s32[4]{0:T(128)S(1)} %pad_add_fusion.odd_ref.refs_1_, ...), custom_call_target="tpu_custom_call" | custom-call | flops 671088640 | bytes 3145728 | tf_op jit(solution)/shard_map/finish_mixed/pallas_call | solution.py:41
  137.0 2.6 %collective-permute-start.37 = (f32[1,32,2048]{2,1,0:T(8,128)S(1)}, f32[1,32,2048]{2,1,0:T(8,128)S(1)}, u32[]{:S(2)}, u32[]{:S(2)}) collective-permute-start(f32[1,32,2048]{2,1,0:T(8,128)S(1)} %get-tuple-element.84), channel_id=1, source_target_pairs={{0,28},{4,8},{8,4},{12,16},{16,12},{20,24},{24,20},{28,0},{1,29},{... | collective-permute-start | bytes 786440 | tf_op jit(solution)/shard_map/ppermute | solution.py:372
  139.6 4.9 %local.13.refs_3_ = f32[2,32,2048]{2,1,0:T(8,128)S(1)} custom-call(s32[2,80]{1,0:T(2,128)S(1)} %and_select_fusion.place_ref.refs_0_, bf16[2,16,256,640]{3,2,1,0:T(8,128)(2,1)S(1)} %prep.1.tiles_ref.refs_2_, f32[2,32,2048]{2,1,0:T(8,128)S(1)} %get-tuple-element.77.y_ref.refs_4_), custom_call_target="tpu_custom_call" | custom-call | flops 671088640 | bytes 1048576 | tf_op jit(solution)/shard_map/local/pallas_call | solution.py:41
  146.1 4.6 %finish_image.1 = f32[32,32]{1,0:T(8,128)S(1)} custom-call(s32[2,80]{1,0:T(2,128)S(1)} %and_select_fusion.place_ref.refs_0_, s32[4]{0:T(128)S(1)} %pad_add_fusion.odd_ref.refs_1_, bf16[2,16,256,640]{3,2,1,0:T(8,128)(2,1)S(1)} %prep.1.tiles_ref.refs_2_, f32[2,32,2048]{2,1,0:T(8,128)S(1)} %local.13.refs_3_, ...), custom_call_target="tpu_custom_call" | custom-call | flops 671088640 | bytes 3145728 | tf_op jit(solution)/shard_map/finish_image/pallas_call | solution.py:41
  166.9 3.7 %orth.3 = (f32[2,32,2048]{2,1,0:T(8,128)}, f32[32,32]{1,0:T(8,128)S(1)}) custom-call(f32[32,32]{1,0:T(8,128)S(1)} %add.78.gram_ref, f32[2,32,2048]{2,1,0:T(8,128)S(1)} %get-tuple-element.77.y_ref.refs_4_), custom_call_target="tpu_custom_call" | custom-call | flops 8388608 | bytes 1048576 | tf_op jit(solution)/shard_map/orth/pallas_call | solution.py:319
  (96 shorter events, 45.4 us)
Async XLA Ops:
  2.4 18.9 %collective-permute-start = (f32[2,32,1024]{2,1,0:T(8,128)S(1)}, f32[2,32,1024]{2,1,0:T(8,128)S(1)}, u32[]{:S(2)}, u32[]{:S(2)}) collective-permute-start(f32[2,32,1024]{2,1,0:T(8,128)S(1)} %get-tuple-element.45), channel_id=1, source_target_pairs={{0,1},{1,0},{2,3},{3,2},{4,5},{5,4},{6,7},{7,6},{8,9},{9,8},{10,11... | collective-permute-start | bytes 786440 | tf_op jit(solution)/shard_map/ppermute | solution.py:370
  5.5 15.8 %collective-permute-start.1 = (f32[2,32,1024]{2,1,0:T(8,128)S(1)}, f32[2,32,1024]{2,1,0:T(8,128)S(1)}, u32[]{:S(2)}, u32[]{:S(2)}) collective-permute-start(f32[2,32,1024]{2,1,0:T(8,128)S(1)} %get-tuple-element.46), channel_id=1, source_target_pairs={{0,3},{1,2},{2,1},{3,0},{4,7},{5,6},{6,5},{7,4},{8,11},{9,10},{10,... | collective-permute-start | bytes 786440 | tf_op jit(solution)/shard_map/ppermute | solution.py:371
  8.0 13.3 %collective-permute-start.2 = (f32[1,32,2048]{2,1,0:T(8,128)S(1)}, f32[1,32,2048]{2,1,0:T(8,128)S(1)}, u32[]{:S(2)}, u32[]{:S(2)}) collective-permute-start(f32[1,32,2048]{2,1,0:T(8,128)S(1)} %get-tuple-element.47), channel_id=1, source_target_pairs={{0,4},{4,0},{8,12},{12,8},{16,20},{20,16},{24,28},{28,24},{1,5},{5... | collective-permute-start | bytes 786440 | tf_op jit(solution)/shard_map/ppermute | solution.py:373
  8.0 13.3 %collective-permute-start.3 = (f32[1,32,2048]{2,1,0:T(8,128)S(1)}, f32[1,32,2048]{2,1,0:T(8,128)S(1)}, u32[]{:S(2)}, u32[]{:S(2)}) collective-permute-start(f32[1,32,2048]{2,1,0:T(8,128)S(1)} %get-tuple-element.48), channel_id=1, source_target_pairs={{0,28},{4,8},{8,4},{12,16},{16,12},{20,24},{24,20},{28,0},{1,29},{... | collective-permute-start | bytes 786440 | tf_op jit(solution)/shard_map/ppermute | solution.py:372
  25.7 12.9 %collective-permute-start.4 = (f32[2,32,1024]{2,1,0:T(8,128)S(1)}, f32[2,32,1024]{2,1,0:T(8,128)S(1)}, u32[]{:S(2)}, u32[]{:S(2)}) collective-permute-start(f32[2,32,1024]{2,1,0:T(8,128)S(1)} %get-tuple-element.50), channel_id=1, source_target_pairs={{0,1},{1,0},{2,3},{3,2},{4,5},{5,4},{6,7},{7,6},{8,9},{9,8},{10,11... | collective-permute-start | bytes 786440 | tf_op jit(solution)/shard_map/ppermute | solution.py:370
  26.4 12.2 %collective-permute-start.5 = (f32[2,32,1024]{2,1,0:T(8,128)S(1)}, f32[2,32,1024]{2,1,0:T(8,128)S(1)}, u32[]{:S(2)}, u32[]{:S(2)}) collective-permute-start(f32[2,32,1024]{2,1,0:T(8,128)S(1)} %get-tuple-element.51), channel_id=1, source_target_pairs={{0,3},{1,2},{2,1},{3,0},{4,7},{5,6},{6,5},{7,4},{8,11},{9,10},{10,... | collective-permute-start | bytes 786440 | tf_op jit(solution)/shard_map/ppermute | solution.py:371
  27.3 11.3 %collective-permute-start.6 = (f32[1,32,2048]{2,1,0:T(8,128)S(1)}, f32[1,32,2048]{2,1,0:T(8,128)S(1)}, u32[]{:S(2)}, u32[]{:S(2)}) collective-permute-start(f32[1,32,2048]{2,1,0:T(8,128)S(1)} %get-tuple-element.52), channel_id=1, source_target_pairs={{0,4},{4,0},{8,12},{12,8},{16,20},{20,16},{24,28},{28,24},{1,5},{5... | collective-permute-start | bytes 786440 | tf_op jit(solution)/shard_map/ppermute | solution.py:373
  27.4 11.3 %collective-permute-start.7 = (f32[1,32,2048]{2,1,0:T(8,128)S(1)}, f32[1,32,2048]{2,1,0:T(8,128)S(1)}, u32[]{:S(2)}, u32[]{:S(2)}) collective-permute-start(f32[1,32,2048]{2,1,0:T(8,128)S(1)} %get-tuple-element.53), channel_id=1, source_target_pairs={{0,28},{4,8},{8,4},{12,16},{16,12},{20,24},{24,20},{28,0},{1,29},{... | collective-permute-start | bytes 786440 | tf_op jit(solution)/shard_map/ppermute | solution.py:372
  43.0 9.1 %collective-permute-start.8 = (f32[2,32,1024]{2,1,0:T(8,128)S(1)}, f32[2,32,1024]{2,1,0:T(8,128)S(1)}, u32[]{:S(2)}, u32[]{:S(2)}) collective-permute-start(f32[2,32,1024]{2,1,0:T(8,128)S(1)} %get-tuple-element.55), channel_id=1, source_target_pairs={{0,1},{1,0},{2,3},{3,2},{4,5},{5,4},{6,7},{7,6},{8,9},{9,8},{10,11... | collective-permute-start | bytes 786440 | tf_op jit(solution)/shard_map/ppermute | solution.py:370
  44.8 11.0 %collective-permute-start.9 = (f32[2,32,1024]{2,1,0:T(8,128)S(1)}, f32[2,32,1024]{2,1,0:T(8,128)S(1)}, u32[]{:S(2)}, u32[]{:S(2)}) collective-permute-start(f32[2,32,1024]{2,1,0:T(8,128)S(1)} %get-tuple-element.56), channel_id=1, source_target_pairs={{0,3},{1,2},{2,1},{3,0},{4,7},{5,6},{6,5},{7,4},{8,11},{9,10},{10,... | collective-permute-start | bytes 786440 | tf_op jit(solution)/shard_map/ppermute | solution.py:371
  45.6 10.2 %collective-permute-start.10 = (f32[1,32,2048]{2,1,0:T(8,128)S(1)}, f32[1,32,2048]{2,1,0:T(8,128)S(1)}, u32[]{:S(2)}, u32[]{:S(2)}) collective-permute-start(f32[1,32,2048]{2,1,0:T(8,128)S(1)} %get-tuple-element.57), channel_id=1, source_target_pairs={{0,4},{4,0},{8,12},{12,8},{16,20},{20,16},{24,28},{28,24},{1,5},{5... | collective-permute-start | bytes 786440 | tf_op jit(solution)/shard_map/ppermute | solution.py:373
  45.6 10.2 %collective-permute-start.11 = (f32[1,32,2048]{2,1,0:T(8,128)S(1)}, f32[1,32,2048]{2,1,0:T(8,128)S(1)}, u32[]{:S(2)}, u32[]{:S(2)}) collective-permute-start(f32[1,32,2048]{2,1,0:T(8,128)S(1)} %get-tuple-element.58), channel_id=1, source_target_pairs={{0,28},{4,8},{8,4},{12,16},{16,12},{20,24},{24,20},{28,0},{1,29},{... | collective-permute-start | bytes 786440 | tf_op jit(solution)/shard_map/ppermute | solution.py:372
  60.6 10.6 %collective-permute-start.12 = (f32[2,32,1024]{2,1,0:T(8,128)S(1)}, f32[2,32,1024]{2,1,0:T(8,128)S(1)}, u32[]{:S(2)}, u32[]{:S(2)}) collective-permute-start(f32[2,32,1024]{2,1,0:T(8,128)S(1)} %get-tuple-element.60), channel_id=1, source_target_pairs={{0,1},{1,0},{2,3},{3,2},{4,5},{5,4},{6,7},{7,6},{8,9},{9,8},{10,11... | collective-permute-start | bytes 786440 | tf_op jit(solution)/shard_map/ppermute | solution.py:370
  61.5 13.1 %collective-permute-start.13 = (f32[2,32,1024]{2,1,0:T(8,128)S(1)}, f32[2,32,1024]{2,1,0:T(8,128)S(1)}, u32[]{:S(2)}, u32[]{:S(2)}) collective-permute-start(f32[2,32,1024]{2,1,0:T(8,128)S(1)} %get-tuple-element.61), channel_id=1, source_target_pairs={{0,3},{1,2},{2,1},{3,0},{4,7},{5,6},{6,5},{7,4},{8,11},{9,10},{10,... | collective-permute-start | bytes 786440 | tf_op jit(solution)/shard_map/ppermute | solution.py:371
  64.0 10.6 %collective-permute-start.14 = (f32[1,32,2048]{2,1,0:T(8,128)S(1)}, f32[1,32,2048]{2,1,0:T(8,128)S(1)}, u32[]{:S(2)}, u32[]{:S(2)}) collective-permute-start(f32[1,32,2048]{2,1,0:T(8,128)S(1)} %get-tuple-element.62), channel_id=1, source_target_pairs={{0,4},{4,0},{8,12},{12,8},{16,20},{20,16},{24,28},{28,24},{1,5},{5... | collective-permute-start | bytes 786440 | tf_op jit(solution)/shard_map/ppermute | solution.py:373
  64.0 10.6 %collective-permute-start.15 = (f32[1,32,2048]{2,1,0:T(8,128)S(1)}, f32[1,32,2048]{2,1,0:T(8,128)S(1)}, u32[]{:S(2)}, u32[]{:S(2)}) collective-permute-start(f32[1,32,2048]{2,1,0:T(8,128)S(1)} %get-tuple-element.63), channel_id=1, source_target_pairs={{0,28},{4,8},{8,4},{12,16},{16,12},{20,24},{24,20},{28,0},{1,29},{... | collective-permute-start | bytes 786440 | tf_op jit(solution)/shard_map/ppermute | solution.py:372
  79.0 13.5 %collective-permute-start.16 = (f32[2,32,1024]{2,1,0:T(8,128)S(1)}, f32[2,32,1024]{2,1,0:T(8,128)S(1)}, u32[]{:S(2)}, u32[]{:S(2)}) collective-permute-start(f32[2,32,1024]{2,1,0:T(8,128)S(1)} %get-tuple-element.65), channel_id=1, source_target_pairs={{0,1},{1,0},{2,3},{3,2},{4,5},{5,4},{6,7},{7,6},{8,9},{9,8},{10,11... | collective-permute-start | bytes 786440 | tf_op jit(solution)/shard_map/ppermute | solution.py:370
  79.7 12.8 %collective-permute-start.17 = (f32[2,32,1024]{2,1,0:T(8,128)S(1)}, f32[2,32,1024]{2,1,0:T(8,128)S(1)}, u32[]{:S(2)}, u32[]{:S(2)}) collective-permute-start(f32[2,32,1024]{2,1,0:T(8,128)S(1)} %get-tuple-element.66), channel_id=1, source_target_pairs={{0,3},{1,2},{2,1},{3,0},{4,7},{5,6},{6,5},{7,4},{8,11},{9,10},{10,... | collective-permute-start | bytes 786440 | tf_op jit(solution)/shard_map/ppermute | solution.py:371
  82.3 10.2 %collective-permute-start.18 = (f32[1,32,2048]{2,1,0:T(8,128)S(1)}, f32[1,32,2048]{2,1,0:T(8,128)S(1)}, u32[]{:S(2)}, u32[]{:S(2)}) collective-permute-start(f32[1,32,2048]{2,1,0:T(8,128)S(1)} %get-tuple-element.67), channel_id=1, source_target_pairs={{0,4},{4,0},{8,12},{12,8},{16,20},{20,16},{24,28},{28,24},{1,5},{5... | collective-permute-start | bytes 786440 | tf_op jit(solution)/shard_map/ppermute | solution.py:373
  82.3 10.2 %collective-permute-start.19 = (f32[1,32,2048]{2,1,0:T(8,128)S(1)}, f32[1,32,2048]{2,1,0:T(8,128)S(1)}, u32[]{:S(2)}, u32[]{:S(2)}) collective-permute-start(f32[1,32,2048]{2,1,0:T(8,128)S(1)} %get-tuple-element.68), channel_id=1, source_target_pairs={{0,28},{4,8},{8,4},{12,16},{16,12},{20,24},{24,20},{28,0},{1,29},{... | collective-permute-start | bytes 786440 | tf_op jit(solution)/shard_map/ppermute | solution.py:372
  96.9 32.5 %collective-permute-start.20 = (f32[2,32,1024]{2,1,0:T(8,128)S(1)}, f32[2,32,1024]{2,1,0:T(8,128)S(1)}, u32[]{:S(2)}, u32[]{:S(2)}) collective-permute-start(f32[2,32,1024]{2,1,0:T(8,128)S(1)} %get-tuple-element.70), channel_id=1, source_target_pairs={{0,1},{1,0},{2,3},{3,2},{4,5},{5,4},{6,7},{7,6},{8,9},{9,8},{10,11... | collective-permute-start | bytes 786440 | tf_op jit(solution)/shard_map/ppermute | solution.py:370
  98.7 30.7 %collective-permute-start.21 = (f32[2,32,1024]{2,1,0:T(8,128)S(1)}, f32[2,32,1024]{2,1,0:T(8,128)S(1)}, u32[]{:S(2)}, u32[]{:S(2)}) collective-permute-start(f32[2,32,1024]{2,1,0:T(8,128)S(1)} %get-tuple-element.71), channel_id=1, source_target_pairs={{0,3},{1,2},{2,1},{3,0},{4,7},{5,6},{6,5},{7,4},{8,11},{9,10},{10,... | collective-permute-start | bytes 786440 | tf_op jit(solution)/shard_map/ppermute | solution.py:371
  99.8 29.6 %collective-permute-start.22 = (f32[1,32,2048]{2,1,0:T(8,128)S(1)}, f32[1,32,2048]{2,1,0:T(8,128)S(1)}, u32[]{:S(2)}, u32[]{:S(2)}) collective-permute-start(f32[1,32,2048]{2,1,0:T(8,128)S(1)} %get-tuple-element.72), channel_id=1, source_target_pairs={{0,4},{4,0},{8,12},{12,8},{16,20},{20,16},{24,28},{28,24},{1,5},{5... | collective-permute-start | bytes 786440 | tf_op jit(solution)/shard_map/ppermute | solution.py:373
  99.9 29.6 %collective-permute-start.23 = (f32[1,32,2048]{2,1,0:T(8,128)S(1)}, f32[1,32,2048]{2,1,0:T(8,128)S(1)}, u32[]{:S(2)}, u32[]{:S(2)}) collective-permute-start(f32[1,32,2048]{2,1,0:T(8,128)S(1)} %get-tuple-element.73), channel_id=1, source_target_pairs={{0,28},{4,8},{8,4},{12,16},{16,12},{20,24},{24,20},{28,0},{1,29},{... | collective-permute-start | bytes 786440 | tf_op jit(solution)/shard_map/ppermute | solution.py:372
  103.1 5.5 %collective-permute-start.25 = (f32[32,32]{1,0:T(8,128)S(1)}, f32[32,32]{1,0:T(8,128)S(1)}, u32[]{:S(2)}, u32[]{:S(2)}) collective-permute-start(f32[32,32]{1,0:T(8,128)S(1)} %add.69), channel_id=1, source_target_pairs={{0,8},{4,12},{8,0},{12,4},{16,24},{20,28},{24,16},{28,20},{1,9},{5... | collective-permute-start | bytes 12296 | tf_op jit(solution)/shard_map/ppermute | solution.py:353
  116.1 4.7 %collective-permute-start.28 = (f32[32,32]{1,0:T(8,128)S(1)}, f32[32,32]{1,0:T(8,128)S(1)}, u32[]{:S(2)}, u32[]{:S(2)}) collective-permute-start(f32[32,32]{1,0:T(8,128)S(1)} %add.72), channel_id=1, source_target_pairs={{0,2},{1,3},{2,0},{3,1},{4,6},{5,7},{6,4},{7,5},{8,10},{9,11},{10,... | collective-permute-start | bytes 12296 | tf_op jit(solution)/shard_map/ppermute | solution.py:353
  134.7 9.8 %collective-permute-start.34 = (f32[2,32,1024]{2,1,0:T(8,128)S(1)}, f32[2,32,1024]{2,1,0:T(8,128)S(1)}, u32[]{:S(2)}, u32[]{:S(2)}) collective-permute-start(f32[2,32,1024]{2,1,0:T(8,128)S(1)} %get-tuple-element.81), channel_id=1, source_target_pairs={{0,1},{1,0},{2,3},{3,2},{4,5},{5,4},{6,7},{7,6},{8,9},{9,8},{10,11... | collective-permute-start | bytes 786440 | tf_op jit(solution)/shard_map/ppermute | solution.py:370
  135.1 10.5 %collective-permute-start.35 = (f32[2,32,1024]{2,1,0:T(8,128)S(1)}, f32[2,32,1024]{2,1,0:T(8,128)S(1)}, u32[]{:S(2)}, u32[]{:S(2)}) collective-permute-start(f32[2,32,1024]{2,1,0:T(8,128)S(1)} %get-tuple-element.82), channel_id=1, source_target_pairs={{0,3},{1,2},{2,1},{3,0},{4,7},{5,6},{6,5},{7,4},{8,11},{9,10},{10,... | collective-permute-start | bytes 786440 | tf_op jit(solution)/shard_map/ppermute | solution.py:371
  137.0 8.7 %collective-permute-start.36 = (f32[1,32,2048]{2,1,0:T(8,128)S(1)}, f32[1,32,2048]{2,1,0:T(8,128)S(1)}, u32[]{:S(2)}, u32[]{:S(2)}) collective-permute-start(f32[1,32,2048]{2,1,0:T(8,128)S(1)} %get-tuple-element.83), channel_id=1, source_target_pairs={{0,4},{4,0},{8,12},{12,8},{16,20},{20,16},{24,28},{28,24},{1,5},{5... | collective-permute-start | bytes 786440 | tf_op jit(solution)/shard_map/ppermute | solution.py:373
  137.0 9.2 %collective-permute-start.37 = (f32[1,32,2048]{2,1,0:T(8,128)S(1)}, f32[1,32,2048]{2,1,0:T(8,128)S(1)}, u32[]{:S(2)}, u32[]{:S(2)}) collective-permute-start(f32[1,32,2048]{2,1,0:T(8,128)S(1)} %get-tuple-element.84), channel_id=1, source_target_pairs={{0,28},{4,8},{8,4},{12,16},{16,12},{20,24},{24,20},{28,0},{1,29},{... | collective-permute-start | bytes 786440 | tf_op jit(solution)/shard_map/ppermute | solution.py:372
  139.6 11.4 %collective-permute-start.29 = (f32[32,32]{1,0:T(8,128)S(1)}, f32[32,32]{1,0:T(8,128)S(1)}, u32[]{:S(2)}, u32[]{:S(2)}) collective-permute-start(f32[32,32]{1,0:T(8,128)S(1)} %get-tuple-element.76), channel_id=1, source_target_pairs={{0,4},{4,0},{8,12},{12,8},{16,20},{20,16},{24,28},{28,24},{1,5},{5... | collective-permute-start | bytes 12296 | tf_op jit(solution)/shard_map/ppermute | solution.py:353
  163.9 6.6 %collective-permute-start.42 = (f32[32,32]{1,0:T(8,128)S(1)}, f32[32,32]{1,0:T(8,128)S(1)}, u32[]{:S(2)}, u32[]{:S(2)}) collective-permute-start(f32[32,32]{1,0:T(8,128)S(1)} %add.82), channel_id=1, source_target_pairs={{0,2},{1,3},{2,0},{3,1},{4,6},{5,7},{6,4},{7,5},{8,10},{9,11},{10,... | collective-permute-start | bytes 12296 | tf_op jit(solution)/shard_map/ppermute | solution.py:353
  (14 other events, 44.6 us)

commit v3 on v2

v3 whole, which is shorter than its diff:
```python
import functools

import jax
import jax.numpy as jnp
from jax import lax
from jax.experimental import pallas as pl
from jax.experimental.pallas import tpu as pltpu
from jax.sharding import PartitionSpec as P

TILE = 128
TPR = 5
HB = 8
CENTER = 6.5
RADIUS = 3.5
INFLATION_FACTOR = 0.8
GROUP = 8

F32 = jnp.float32
BF16 = jnp.bfloat16
VM = pltpu.VMEM
NT = (((1,), (1,)), ((), ()))
NN = (((1,), (0,)), ((), ()))
WHOLE = pl.BlockSpec(memory_space=VM)
SCALARS = pl.BlockSpec(memory_space=pltpu.SMEM)


def near(x):
    return pltpu.with_memory_space_constraint(x, VM)


def split(x):
    high = x.astype(BF16)
    return high, (x - high.astype(F32)).astype(BF16)


def stacked(x):
    return jnp.concatenate(split(x), axis=0)


def call(kernel, ins, outs, scratch=(), specs=None, flops=0, moved=0, name=None, out_vmem=True):
    out_shape = [VM(s, d) if out_vmem else jax.ShapeDtypeStruct(s, d) for s, d in outs]
    return pl.pallas_call(
        kernel,
        out_shape=out_shape,
        in_specs=specs,
        out_specs=[WHOLE] * len(outs),
        scratch_shapes=list(scratch),
        name=name,
        cost_estimate=pl.CostEstimate(flops=flops, bytes_accessed=moved, transcendentals=0),
        compiler_params=pltpu.CompilerParams(vmem_limit_bytes=6 << 20),
    )(*ins)


def prep_kernel(tiles_ref, out_ref, buffer_ref, semaphores):
    slots, step = buffer_ref.shape[:2]
    chunks = tiles_ref.shape[0] // step

    def copy(c):
        slot = lax.rem(c, slots)
        return pltpu.make_async_copy(
            tiles_ref.at[pl.ds(c * step, step)], buffer_ref.at[slot], semaphores.at[slot]
        )

    for c in range(slots):
        copy(c).start()

    def chunk(c, carry):
        copy(c).wait()
        slot = lax.rem(c, slots)
        for n in range(step):
            high, low = split(buffer_ref[slot, n].T)
            out_ref[c * step + n, :, :TILE] = high
            out_ref[c * step + n, :, TILE:] = low

        @pl.when(c + slots < chunks)
        def _():
            copy(c + slots).start()

        return carry

    lax.fori_loop(0, chunks, chunk, 0)


def prep(tiles):
    tiles = tiles.reshape(-1, TILE, TILE)
    slots, step = 5, 16
    return pl.pallas_call(
        prep_kernel,
        out_shape=VM((tiles.shape[0], TILE, 2 * TILE), BF16),
        in_specs=[pl.BlockSpec(memory_space=pltpu.HBM)],
        out_specs=WHOLE,
        scratch_shapes=[VM((slots, step, TILE, TILE), F32), pltpu.SemaphoreType.DMA((slots,))],
        name="prep",
        cost_estimate=pl.CostEstimate(flops=0, bytes_accessed=4 * tiles.size, transcendentals=0),
        compiler_params=pltpu.CompilerParams(vmem_limit_bytes=8 << 20),
    )(pltpu.with_memory_space_constraint(tiles, pltpu.HBM))


class Layout:
    def __init__(self, slices, blocks):
        most = slices * blocks * ((TPR - 1 + 1) // 2)
        room = most + GROUP + 2
        self.rows = slices * blocks * TPR
        self.tiles = self.rows + room
        self.places = self.tiles + 2 * room
        self.groups = self.places + 2 * room
        self.flags = self.groups + 1
        self.size = -(-(self.flags + 4) // 128) * 128


def plan_kernel(blocks_all, columns_ref, flags_ref, out_ref):
    slices, count = columns_ref.shape
    blocks = count // TPR
    at = Layout(slices, blocks)
    for i in range(4):
        out_ref[at.flags + i] = flags_ref[i]
    first_block = flags_ref[4]
    left_at = jnp.where(flags_ref[0] == 0, HB, 0)
    right_at = -left_at - blocks
    here = slices * blocks
    zero = slices * 2 * HB

    def row(i, units):
        s, r = i // blocks, i % blocks
        out_ref[at.rows + units] = i
        out_ref[at.rows + units + 1] = i
        found = jnp.int32(0)
        for n in range(TPR):
            where = columns_ref[s, r * TPR + n] - first_block + HB
            where = jnp.where(where < 0, where + blocks_all, where)
            where = jnp.where(where >= blocks_all, where - blocks_all, where)
            left = where < HB
            right = where >= HB + blocks
            away = jnp.logical_or(left, right)
            out_ref[i * TPR + n] = jnp.where(away, here, s * blocks + where - HB)
            if n > 0:
                out_ref[at.tiles + 2 * units + found] = i * TPR + n
                out_ref[at.places + 2 * units + found] = (
                    s * 2 * HB + where + jnp.where(right, right_at, left_at)
                )
                found = found + away.astype(jnp.int32)
        out_ref[at.tiles + 2 * units + found] = i * TPR
        out_ref[at.places + 2 * units + found] = zero
        return units + (found + 1) // 2

    units = lax.fori_loop(0, slices * blocks, row, jnp.int32(0))
    for n in range(GROUP):
        out_ref[at.rows + units + n] = 0
        for k in range(2):
            out_ref[at.tiles + 2 * (units + n) + k] = 0
            out_ref[at.places + 2 * (units + n) + k] = zero
    out_ref[at.groups] = (units + GROUP - 1) // GROUP


def plan(columns, flags, blocks_all):
    slices, count = columns.shape
    size = Layout(slices, count // TPR).size
    return pl.pallas_call(
        functools.partial(plan_kernel, blocks_all),
        out_shape=jax.ShapeDtypeStruct((size,), jnp.int32),
        in_specs=[SCALARS, SCALARS],
        out_specs=SCALARS,
        name="plan",
        compiler_params=pltpu.CompilerParams(vmem_limit_bytes=1 << 20),
    )(columns, flags)


def edges(flags, y_ref, inner_ref, outer_ref, near_ref, far_ref):
    width = HB * TILE
    points = y_ref.shape[2]
    final = y_ref.shape[0] - 1
    head = lambda: y_ref[:, :, :width]
    tail = lambda: y_ref[:, :, points - width :]
    first = lambda: y_ref[:1]
    last = lambda: y_ref[final:]
    for axis, inner, outer, low, high in (
        (0, inner_ref, outer_ref, head, tail),
        (1, near_ref, far_ref, first, last),
    ):

        @pl.when(flags[axis] == 0)
        def _(inner=inner, outer=outer, low=low, high=high):
            inner[...] = high()
            outer[...] = low()

        @pl.when(flags[axis] != 0)
        def _(inner=inner, outer=outer, low=low, high=high):
            inner[...] = low()
            outer[...] = high()


def edge_shapes(shape):
    slices, width, points = shape
    side = (slices, width, HB * TILE)
    return [(shape, F32), (side, F32), (side, F32), ((1, width, points), F32), ((1, width, points), F32)]


def start_kernel(odd_ref, x_ref, y_ref, *edge_refs):
    y_ref[...] = x_ref[...]
    edges([odd_ref[0], odd_ref[1]], y_ref, *edge_refs)


def start(odd, block):
    return call(
        start_kernel,
        [odd, block],
        edge_shapes(block.shape),
        specs=[SCALARS, WHOLE],
        moved=16 * block.size,
        name="start",
    )


def fold(product, width):
    return product[:width, :TILE] + product[:width, TILE:] + product[width:, :TILE]


def product(halves, tiles, width):
    left = jnp.concatenate(halves, axis=1)
    right = jnp.concatenate(tiles, axis=0)
    return fold(lax.dot_general(left, right, NN, preferred_element_type=F32), width)


def local_kernel(mode, scale, plan_ref, tiles_ref, y_ref, *refs):
    if mode in ("step", "gram", "mixed"):
        previous_ref, out_ref, halves_ref = refs
    else:
        previous_ref, (out_ref, halves_ref) = None, refs
    slices, width, points = y_ref.shape
    blocks = points // TILE
    at = Layout(slices, blocks)
    for s in range(slices):
        for b in range(blocks):
            halves_ref[s * blocks + b] = stacked(y_ref[s, :, b * TILE : (b + 1) * TILE])
    halves_ref[slices * blocks] = jnp.zeros((2 * width, TILE), BF16)

    for s in range(slices):
        degree = 2.0
        if s == 0:
            degree = degree - jnp.where(plan_ref[at.flags + 2] != 0, 1.0, 0.0)
        if s == slices - 1:
            degree = degree - jnp.where(plan_ref[at.flags + 3] != 0, 1.0, 0.0)

        def row(r, carry, s=s, degree=degree):
            i = s * blocks + r
            halves = [halves_ref[plan_ref[i * TPR + n]] for n in range(TPR)]
            tiles = [tiles_ref[i * TPR + n] for n in range(TPR)]
            here = pl.ds(pl.multiple_of(r * TILE, TILE), TILE)
            y = y_ref[s, :, here]
            time = degree * y
            if s > 0:
                time = time - y_ref[s - 1, :, here]
            if s < slices - 1:
                time = time - y_ref[s + 1, :, here]
            image = product(halves, tiles, width) + INFLATION_FACTOR * time
            if mode != "image":
                image = (image - CENTER * y) * scale
            if previous_ref is not None:
                image = image - previous_ref[s, :, here]
            out_ref[s, :, here] = image
            return carry

        lax.fori_loop(0, blocks, row, 0, unroll=8)


def local_part(mode, scale, table, tiles, y, previous):
    slices, width, points = y.shape
    blocks = points // TILE
    ins = [table, near(tiles), near(y)] + ([] if previous is None else [near(previous)])
    return call(
        functools.partial(local_kernel, mode, scale),
        ins,
        [(y.shape, F32)],
        specs=[SCALARS] + [WHOLE] * (len(ins) - 1),
        scratch=[VM((slices * blocks + 1, 2 * width, TILE), BF16)],
        flops=2 * slices * blocks * TPR * 4 * width * TILE * TILE,
        moved=12 * y.size,
        name="local_" + mode,
    )[0]


def mix(matrix, y):
    high, low = split(matrix)
    y_high, y_low = split(y)
    left = jnp.concatenate([high, low, high], axis=1)
    right = jnp.concatenate([y_high, y_high, y_low], axis=0)
    return lax.dot_general(left, right, NN, preferred_element_type=F32)


def inner(left, right):
    width = left.shape[0]
    p = lax.dot_general(stacked(left), stacked(right), NT, preferred_element_type=F32)
    return (p[:width, :width] + p[width:, width:]) + (p[:width, width:] + p[width:, :width])


def finish_kernel(mode, scale, *refs):
    refs = list(refs)
    take = lambda n: [refs.pop(0) for _ in range(n)]
    plan_ref, tiles_ref, part_ref = take(3)
    inner_ref, outer_ref, near_ref, far_ref = take(4)
    y_ref = take(1)[0] if mode == "image" else None
    matrix_ref = take(1)[0] if mode == "mixed" else None
    if mode == "image":
        gram_ref, halves_ref, new_ref = refs
    else:
        new_ref, *edge_refs = take(5)
        gram_ref = take(1)[0] if mode in ("gram", "mixed") else None
        (halves_ref,) = refs
    slices, width, points = part_ref.shape
    blocks = points // TILE
    at = Layout(slices, blocks)
    for s in range(slices):
        for b in range(HB):
            to = s * 2 * HB + b
            halves_ref[to] = stacked(inner_ref[s, :, b * TILE : (b + 1) * TILE])
            halves_ref[to + HB] = stacked(outer_ref[s, :, b * TILE : (b + 1) * TILE])
    halves_ref[slices * 2 * HB] = jnp.zeros((2 * width, TILE), BF16)

    time_odd = plan_ref[at.flags + 1] != 0
    factor = INFLATION_FACTOR * scale
    for s in range(slices):
        image = part_ref[s]
        if s == 0:
            before = jnp.where(time_odd, near_ref[0], far_ref[0])
            image = image - jnp.where(plan_ref[at.flags + 2] != 0, 0.0, factor * before)
        if s == slices - 1:
            after = jnp.where(time_odd, far_ref[0], near_ref[0])
            image = image - jnp.where(plan_ref[at.flags + 3] != 0, 0.0, factor * after)
        new_ref[s] = image

    def group(g, carry):
        done = []
        for k in range(GROUP):
            u = g * GROUP + k
            halves = [halves_ref[plan_ref[at.places + 2 * u + j]] for j in range(2)]
            tiles = [plan_ref[at.tiles + 2 * u + j] for j in range(2)]
            tiles = [tiles_ref[t] for t in tiles]
            done.append((plan_ref[at.rows + u], product(halves, tiles, width)))
        for i, value in done:
            here = pl.ds(pl.multiple_of((i % blocks) * TILE, TILE), TILE)
            new_ref[i // blocks, :, here] += scale * value
        return carry

    lax.fori_loop(0, plan_ref[at.groups], group, 0)

    if mode == "mixed":
        for s in range(slices):
            new_ref[s] = mix(matrix_ref[...], new_ref[s])
    if mode != "image":
        edges([plan_ref[at.flags], plan_ref[at.flags + 1]], new_ref, *edge_refs)
    if gram_ref is not None:
        base_ref = y_ref if mode == "image" else new_ref
        total = inner(base_ref[0], new_ref[0])
        for s in range(1, slices):
            total = total + inner(base_ref[s], new_ref[s])
        gram_ref[...] = total


def finish(mode, scale, table, tiles, part, y, halo, matrix=None):
    slices, width, points = y.shape
    blocks = points // TILE
    ins = [table] + [near(v) for v in (tiles, part, *halo)]
    if mode == "image":
        ins.append(near(y))
    if matrix is not None:
        ins.append(near(matrix))
    outs = [] if mode == "image" else edge_shapes(y.shape)
    if mode in ("gram", "mixed", "image"):
        outs = outs + [((width, width), F32)]
    scratch = [VM((slices * 2 * HB + 1, 2 * width, TILE), BF16)]
    if mode == "image":
        scratch.append(VM(y.shape, F32))
    return call(
        functools.partial(finish_kernel, mode, scale),
        ins,
        outs,
        scratch=scratch,
        specs=[SCALARS] + [WHOLE] * (len(ins) - 1),
        flops=2 * slices * blocks * 2 * 4 * width * TILE * TILE,
        moved=24 * y.size,
        name="finish_" + mode,
    )


def inverse_factor(gram):
    width = gram.shape[0]
    rows = lax.broadcasted_iota(jnp.int32, (width, width), 0)
    columns = lax.broadcasted_iota(jnp.int32, (width, width), 1)
    inverse = (rows == columns).astype(F32)
    row_of = lax.broadcasted_iota(jnp.int32, (width, 1), 0)
    for j in range(width):
        root = lax.rsqrt(gram[j : j + 1, j : j + 1])
        gram_row = gram[j : j + 1, :] * root
        inverse_row = inverse[j : j + 1, :] * root
        column = jnp.where(row_of > j, gram[:, j : j + 1] * root, 0.0)
        gram = gram - column * gram_row
        inverse = jnp.where(row_of == j, inverse_row, inverse - column * inverse_row)
    return inverse


def orth_kernel(count, gram_ref, y_ref, out_ref, matrix_ref):
    matrix = inverse_factor(gram_ref[...] * (1.0 / count))
    matrix_ref[...] = matrix
    for s in range(y_ref.shape[0]):
        out_ref[s] = mix(matrix, y_ref[s])


def orth(gram, y, count):
    width = gram.shape[0]
    return pl.pallas_call(
        functools.partial(orth_kernel, float(count)),
        out_shape=[jax.ShapeDtypeStruct(y.shape, F32), VM((width, width), F32)],
        in_specs=[WHOLE, WHOLE],
        out_specs=[WHOLE, WHOLE],
        name="orth",
        cost_estimate=pl.CostEstimate(flops=2 * width * y.size, bytes_accessed=8 * y.size, transcendentals=0),
        compiler_params=pltpu.CompilerParams(vmem_limit_bytes=6 << 20),
    )(near(gram), near(y))


def ritz_kernel(count, matrix_ref, inner_ref, out_ref):
    high = lax.Precision.HIGHEST
    matrix = matrix_ref[...]
    half = lax.dot_general(matrix, inner_ref[...] * (1.0 / count), NN, precision=high, preferred_element_type=F32)
    out_ref[...] = lax.dot_general(half, matrix, NT, precision=high, preferred_element_type=F32)


def ritz(matrix, product, count):
    return call(
        functools.partial(ritz_kernel, float(count)),
        [near(matrix), near(product)],
        [(product.shape, F32)],
        specs=[WHOLE, WHOLE],
        name="ritz",
        moved=4 * product.size,
        out_vmem=False,
    )[0]


def stages_of(axis):
    count = lax.axis_size(axis)
    found, stride = [], 1
    if (count.bit_length() - 1) % 2:
        found, stride = [(axis, (1,))], 2
    while stride < count:
        found.append((axis, (stride, 2 * stride, 3 * stride)))
        stride *= 4
    return found


def add_over(value, stages):
    for axis, strides in stages:
        count = lax.axis_size(axis)
        others = [lax.ppermute(value, axis, [(i, i ^ k) for i in range(count)]) for k in strides]
        if len(others) == 1:
            value = value + others[0]
        else:
            value = (value + others[0]) + (others[1] + others[2])
    return value


def inner_pairs(axis):
    count = lax.axis_size(axis)
    return [(i, i ^ 1) for i in range(count)]


def outer_pairs(axis):
    count = lax.axis_size(axis)
    return [(i, (i + 1) % count if i % 2 else (i - 1) % count) for i in range(count)]


def exchange(edge):
    inner, outer, near_slice, far_slice = edge
    inner = lax.ppermute(inner, "space", inner_pairs("space"))
    outer = lax.ppermute(outer, "space", outer_pairs("space"))
    far_slice = lax.ppermute(far_slice, "tm", outer_pairs("tm"))
    near_slice = lax.ppermute(near_slice, "tm", inner_pairs("tm"))
    return inner, outer, near_slice, far_slice


def body(start_block, stiffness_tiles, tile_columns):
    slices, width, local_points = start_block.shape
    local_blocks = local_points // TILE
    blocks_all = lax.axis_size("space") * local_blocks
    count_all = slices * local_points * lax.axis_size("tm") * lax.axis_size("space")
    time_index = lax.axis_index("tm")
    ends = (time_index == 0, time_index == lax.axis_size("tm") - 1)
    space_index = lax.axis_index("space")
    odd = jnp.stack(
        [
            space_index % 2,
            time_index % 2,
            ends[0].astype(jnp.int32),
            ends[1].astype(jnp.int32),
            space_index * local_blocks,
        ]
    )

    y, *edge = start(odd, start_block)
    table = plan(tile_columns, odd, blocks_all)
    tiles = prep(stiffness_tiles)

    across, along = stages_of("space"), stages_of("tm")
    early, late = across + along[::-1], along + across
    share = -(-len(early) // 3)

    def apply(mode, scale, y, edge, previous=None, beside=None):
        halo = exchange(edge)
        part = local_part(mode, scale, table, tiles, y, previous)
        extra = beside() if beside else None
        if extra is not None:
            part, extra = lax.optimization_barrier((part, extra))
        matrix = extra if mode == "mixed" else None
        return finish(mode, scale, table, tiles, part, y, halo, matrix), extra

    (y1, *edge), _ = apply("first", 1.0 / RADIUS, y, edge)
    (y2, *edge), _ = apply("step", 2.0 / RADIUS, y1, edge, y)
    (filtered, *edge, gram), _ = apply("gram", 2.0 / RADIUS, y2, edge, y1)

    kept = {}

    def first_matrix():
        total = add_over(gram, early[2 * share :])
        kept["first"], matrix = orth(total, filtered, count_all)
        return matrix

    (y1, *edge), gram = apply(
        "first", 1.0 / RADIUS, filtered, edge, beside=lambda: add_over(gram, early[:share])
    )
    (y2, *edge), gram = apply(
        "step", 2.0 / RADIUS, y1, edge, filtered, beside=lambda: add_over(gram, early[share : 2 * share])
    )
    (second, *edge, gram_two), _ = apply("mixed", 2.0 / RADIUS, y2, edge, y1, beside=first_matrix)
    (inner_two,), gram_two = apply(
        "image", 1.0, second, edge, beside=lambda: add_over(gram_two, along)
    )
    ritz_basis, matrix = orth(add_over(gram_two, across), second, count_all)
    return ritz_basis, kept["first"], ritz(matrix, add_over(inner_two, late), count_all)


def solution(mesh):
    placed = (P("tm", None, "space"), P("tm", "space", None, None), P("tm", "space"))
    return jax.shard_map(
        body,
        mesh=mesh,
        in_specs=placed,
        out_specs=(P("tm", None, "space"), P("tm", None, "space"), P()),
        check_vma=False,
    )
```

time: 172 us -> 147 us (0.85)
  Pallas kernels: 76.8 us -> 54 us
  starting transfers between devices: 49.8 us -> 57.4 us
  waiting for transfers between devices: 38.8 us -> 32.4 us
  local copies, waits for them, and re-layouts: 5.05 us -> 1.81 us
    pallas_call x16, Pallas kernels: 67.7 us -> 38.8 us  [call(): pl.pallas_call(kernel, out_shape=out_shape, in_specs=specs, out_specs=[WH...]
    ppermute x15 -> x21, waiting for transfers between devices: 23 us -> 7.69 us  [add_over(): lax.ppermute(value, axis, [(i, i ^ k) for i in range(count)])]
    ppermute x15 -> x21, starting transfers between devices: 12 us -> 26.2 us  [add_over(): lax.ppermute(value, axis, [(i, i ^ k) for i in range(count)])]
    ppermute x7, starting transfers between devices: 15.9 us -> 9.03 us  [exchange(): far_slice = lax.ppermute(far_slice, 'tm', outer_pairs('tm'))]
    pallas_call x1 -> x2, Pallas kernels: 1.82 us -> 7.87 us  [the longest x1 4.8 us: prep(): pl.pallas_call(prep_kernel, out_shape=VM((tiles.shape[0], TILE, 2 * TILE)...]
    ppermute x7, waiting for transfers between devices: 8.41 us -> 13.9 us  [exchange(): outer = lax.ppermute(outer, 'space', outer_pairs('space'))]
    ppermute x7, waiting for transfers between devices: 6.87 us -> 10.8 us  [exchange(): inner = lax.ppermute(inner, 'space', inner_pairs('space'))]
    unnamed x6 -> x4, local copies, waits for them, and re-layouts: 5.05 us -> 1.72 us
  transfers between devices with their start and end apart: 43 -> 49, of which waited for: 18 -> 14; matrix products, arithmetic and copies ran while one was open for 0% -> 0% of each run, Pallas kernels for 28% -> 26%
where the time goes in v3:
time: 147 us
  starting transfers between devices  57.4 us (39%)
  Pallas kernels  54 us (37%)
  waiting for transfers between devices  32.4 us (22%)
  local copies, waits for them, and re-layouts  1.81 us (1%)
    pallas_call x16, Pallas kernels, call(): pl.pallas_call(kernel, out_shape=out_shape, in_specs=specs, out_specs=[WH...  38.8 us
    ppermute x21, starting transfers between devices, add_over(): lax.ppermute(value, axis, [(i, i ^ k) for i in range(count)])  26.2 us
    ppermute x7, waiting for transfers between devices, exchange(): outer = lax.ppermute(outer, 'space', outer_pairs('space'))  13.9 us
    ppermute x7, starting transfers between devices, exchange(): outer = lax.ppermute(outer, 'space', outer_pairs('space'))  12.9 us
    ppermute x7, waiting for transfers between devices, exchange(): inner = lax.ppermute(inner, 'space', inner_pairs('space'))  10.8 us
    ppermute x7, starting transfers between devices, exchange(): inner = lax.ppermute(inner, 'space', inner_pairs('space'))  9.2 us
    ppermute x7, starting transfers between devices, exchange(): far_slice = lax.ppermute(far_slice, 'tm', outer_pairs('tm'))  9.03 us
    ppermute x21, waiting for transfers between devices, add_over(): lax.ppermute(value, axis, [(i, i ^ k) for i in range(count)])  7.69 us
  transfers between devices with their start and end apart: 49, of which 14 were waited for; matrix products, arithmetic and copies ran while one was open for 0% of the time, Pallas kernels for 26%

profile of v3, /device:TPU:0, one launch (start us, length us, event | category | flops | bytes accessed | tf_op | source)
XLA Modules:
  0.0 146.6 jit_solution(10652166203117189123)
XLA Ops:
  2.4 3.1 %collective-permute-start = (f32[2,32,1024]{2,1,0:T(8,128)S(1)}, f32[2,32,1024]{2,1,0:T(8,128)S(1)}, u32[]{:S(2)}, u32[]{:S(2)}) collective-permute-start(f32[2,32,1024]{2,1,0:T(8,128)S(1)} %get-tuple-element.53), channel_id=1, source_target_pairs={{0,1},{1,0},{2,3},{3,2},{4,5},{5,4},{6,7},{7,6},{8,9},{9,8},{10,11... | collective-permute-start | bytes 786440 | tf_op jit(solution)/shard_map/ppermute | solution.py:474
  5.5 2.5 %collective-permute-start.1 = (f32[2,32,1024]{2,1,0:T(8,128)S(1)}, f32[2,32,1024]{2,1,0:T(8,128)S(1)}, u32[]{:S(2)}, u32[]{:S(2)}) collective-permute-start(f32[2,32,1024]{2,1,0:T(8,128)S(1)} %get-tuple-element.54), channel_id=1, source_target_pairs={{0,3},{1,2},{2,1},{3,0},{4,7},{5,6},{6,5},{7,4},{8,11},{9,10},{10,... | collective-permute-start | bytes 786440 | tf_op jit(solution)/shard_map/ppermute | solution.py:475
  8.0 2.6 %collective-permute-start.3 = (f32[1,32,2048]{2,1,0:T(8,128)S(1)}, f32[1,32,2048]{2,1,0:T(8,128)S(1)}, u32[]{:S(2)}, u32[]{:S(2)}) collective-permute-start(f32[1,32,2048]{2,1,0:T(8,128)S(1)} %get-tuple-element.56), channel_id=1, source_target_pairs={{0,28},{4,8},{8,4},{12,16},{16,12},{20,24},{24,20},{28,0},{1,29},{... | collective-permute-start | bytes 786440 | tf_op jit(solution)/shard_map/ppermute | solution.py:476
  11.2 3.1 %plan.1.plan_ref.refs_0_ = s32[640]{0:T(1024)S(1)} custom-call(s32[2,80]{1,0:T(2,128)S(1)} %copy-done.1, s32[5]{0:T(128)S(1)} %stack.31.flags_ref.odd_ref), custom_call_target="tpu_custom_call" | custom-call | tf_op jit(solution)/shard_map/plan/pallas_call | solution.py:158
  14.3 4.8 %prep.1.tiles_ref.refs_1_ = bf16[160,128,256]{2,1,0:T(8,128)(2,1)S(1)} custom-call(f32[160,128,128]{2,1,0:T(8,128)} %bitcast.6), custom_call_target="tpu_custom_call" | custom-call | bytes 10485760 | tf_op jit(solution)/shard_map/prep/pallas_call | solution.py:87
  19.1 3.0 %local_first.2.refs_2_ = f32[2,32,2048]{2,1,0:T(8,128)S(1)} custom-call(s32[640]{0:T(1024)S(1)} %plan.1.plan_ref.refs_0_, bf16[160,128,256]{2,1,0:T(8,128)(2,1)S(1)} %prep.1.tiles_ref.refs_1_, f32[2,32,2048]{2,1,0:T(8,128)S(1)} %get-tuple-element.52.y_ref.refs_0_), custom_call_target="tpu_custom_call" | custom-call | flops 671088640 | bytes 1572864 | tf_op jit(solution)/shard_map/local_first/pallas_call | solution.py:42
  27.3 3.0 %local_step.2.refs_2_ = f32[2,32,2048]{2,1,0:T(8,128)S(1)} custom-call(s32[640]{0:T(1024)S(1)} %plan.1.plan_ref.refs_0_, bf16[160,128,256]{2,1,0:T(8,128)(2,1)S(1)} %prep.1.tiles_ref.refs_1_, f32[2,32,2048]{2,1,0:T(8,128)S(1)} %get-tuple-element.57.y_ref.refs_0_, f32[2,32,2048]{2,1,0:T(8,128)S(1)} %get-tuple-element.52.y_ref.refs_0_), custom_call_target="tpu_custom_call" | custom-call | flops 671088640 | bytes 1572864 | tf_op jit(solution)/shard_map/local_step/pallas_call | solution.py:42
  30.4 6.8 %collective-permute-done.4.refs_3_ = f32[2,32,1024]{2,1,0:T(8,128)S(1)} collective-permute-done((f32[2,32,1024]{2,1,0:T(8,128)S(1)}, f32[2,32,1024]{2,1,0:T(8,128)S(1)}, u32[]{:S(2)}, u32[]{:S(2)}) %collective-permute-start.4) | collective-permute-done | bytes 262176 | tf_op jit(solution)/shard_map/ppermute | solution.py:474
  43.5 3.0 %local_gram.1.refs_2_ = f32[2,32,2048]{2,1,0:T(8,128)S(1)} custom-call(s32[640]{0:T(1024)S(1)} %plan.1.plan_ref.refs_0_, bf16[160,128,256]{2,1,0:T(8,128)(2,1)S(1)} %prep.1.tiles_ref.refs_1_, f32[2,32,2048]{2,1,0:T(8,128)S(1)} %get-tuple-element.62.y_ref, f32[2,32,2048]{2,1,0:T(8,128)S(1)} %get-tuple-element.57.y_ref.refs_0_), custom_call_target="tpu_custom_call" | custom-call | flops 671088640 | bytes 1572864 | tf_op jit(solution)/shard_map/local_gram/pallas_call | solution.py:42
  47.9 4.0 %collective-permute-done.9.refs_4_ = f32[2,32,1024]{2,1,0:T(8,128)S(1)} collective-permute-done((f32[2,32,1024]{2,1,0:T(8,128)S(1)}, f32[2,32,1024]{2,1,0:T(8,128)S(1)}, u32[]{:S(2)}, u32[]{:S(2)}) %collective-permute-start.9) | collective-permute-done | bytes 262176 | tf_op jit(solution)/shard_map/ppermute | solution.py:475
  52.0 2.5 %finish_gram.1 = (f32[2,32,2048]{2,1,0:T(8,128)S(1)}, f32[2,32,1024]{2,1,0:T(8,128)S(1)}, f32[2,32,1024]{2,1,0:T(8,128)S(1)}, f32[1,32,2048]{2,1,0:T(8,128)S(1)}...) custom-call(s32[640]{0:T(1024)S(1)} %plan.1.plan_ref.refs_0_, bf16[160,128,256]{2,1,0:T(8,128)(2,1)S(1)} %prep.1.tiles_ref.refs_1_, ...), custom_call_target="tpu_custom_call" | custom-call | flops 268435456 | bytes 3145728 | tf_op jit(solution)/shard_map/finish_gram/pallas_call | solution.py:42
  54.4 2.4 %collective-permute-start.14 = (f32[32,32]{1,0:T(8,128)S(1)}, f32[32,32]{1,0:T(8,128)S(1)}, u32[]{:S(2)}, u32[]{:S(2)}) collective-permute-start(f32[32,32]{1,0:T(8,128)S(1)} %get-tuple-element.68), channel_id=1, source_target_pairs={{0,3},{1,2},{2,1},{3,0},{4,7},{5,6},{6,5},{7,4},{8,11},{9,10},{10,... | collective-permute-start | bytes 12296 | tf_op jit(solution)/shard_map/ppermute | solution.py:454
  58.9 2.3 %collective-permute-start.16 = (f32[2,32,1024]{2,1,0:T(8,128)S(1)}, f32[2,32,1024]{2,1,0:T(8,128)S(1)}, u32[]{:S(2)}, u32[]{:S(2)}) collective-permute-start(f32[2,32,1024]{2,1,0:T(8,128)S(1)} %get-tuple-element.71), channel_id=1, source_target_pairs={{0,3},{1,2},{2,1},{3,0},{4,7},{5,6},{6,5},{7,4},{8,11},{9,10},{10,... | collective-permute-start | bytes 786440 | tf_op jit(solution)/shard_map/ppermute | solution.py:475
  61.6 2.5 %collective-permute-start.18 = (f32[1,32,2048]{2,1,0:T(8,128)S(1)}, f32[1,32,2048]{2,1,0:T(8,128)S(1)}, u32[]{:S(2)}, u32[]{:S(2)}) collective-permute-start(f32[1,32,2048]{2,1,0:T(8,128)S(1)} %get-tuple-element.73), channel_id=1, source_target_pairs={{0,28},{4,8},{8,4},{12,16},{16,12},{20,24},{24,20},{28,0},{1,29},{... | collective-permute-start | bytes 786440 | tf_op jit(solution)/shard_map/ppermute | solution.py:476
  64.1 3.0 %local_first.3.refs_2_ = f32[2,32,2048]{2,1,0:T(8,128)S(1)} custom-call(s32[640]{0:T(1024)S(1)} %plan.1.plan_ref.refs_0_, bf16[160,128,256]{2,1,0:T(8,128)(2,1)S(1)} %prep.1.tiles_ref.refs_1_, f32[2,32,2048]{2,1,0:T(8,128)S(1)} %get-tuple-element.67.y_ref.refs_0_), custom_call_target="tpu_custom_call" | custom-call | flops 671088640 | bytes 1572864 | tf_op jit(solution)/shard_map/local_first/pallas_call | solution.py:42
  69.7 2.7 %collective-permute-done.16.refs_4_ = f32[2,32,1024]{2,1,0:T(8,128)S(1)} collective-permute-done((f32[2,32,1024]{2,1,0:T(8,128)S(1)}, f32[2,32,1024]{2,1,0:T(8,128)S(1)}, u32[]{:S(2)}, u32[]{:S(2)}) %collective-permute-start.16) | collective-permute-done | bytes 262176 | tf_op jit(solution)/shard_map/ppermute | solution.py:475
  72.4 2.9 %collective-permute-start.19 = (f32[32,32]{1,0:T(8,128)S(1)}, f32[32,32]{1,0:T(8,128)S(1)}, u32[]{:S(2)}, u32[]{:S(2)}) collective-permute-start(f32[32,32]{1,0:T(8,128)S(1)} %add_add_fusion.5), channel_id=1, source_target_pairs={{0,8},{4,12},{8,0},{12,4},{16,24},{20,28},{24,16},{28,20},{1,9},{5... | collective-permute-start | bytes 12296 | tf_op jit(solution)/shard_map/ppermute | solution.py:454
  81.0 3.0 %local_step.3.refs_2_ = f32[2,32,2048]{2,1,0:T(8,128)S(1)} custom-call(s32[640]{0:T(1024)S(1)} %plan.1.plan_ref.refs_0_, bf16[160,128,256]{2,1,0:T(8,128)(2,1)S(1)} %prep.1.tiles_ref.refs_1_, f32[2,32,2048]{2,1,0:T(8,128)S(1)} %get-tuple-element.74.y_ref.refs_0_, f32[2,32,2048]{2,1,0:T(8,128)S(1)} %get-tuple-element.67.y_ref.refs_0_), custom_call_target="tpu_custom_call" | custom-call | flops 671088640 | bytes 1572864 | tf_op jit(solution)/shard_map/local_step/pallas_call | solution.py:42
  84.0 2.6 %collective-permute-done.22.refs_3_ = f32[2,32,1024]{2,1,0:T(8,128)S(1)} collective-permute-done((f32[2,32,1024]{2,1,0:T(8,128)S(1)}, f32[2,32,1024]{2,1,0:T(8,128)S(1)}, u32[]{:S(2)}, u32[]{:S(2)}) %collective-permute-start.22) | collective-permute-done | bytes 262176 | tf_op jit(solution)/shard_map/ppermute | solution.py:474
  86.6 3.1 %collective-permute-done.23.refs_4_ = f32[2,32,1024]{2,1,0:T(8,128)S(1)} collective-permute-done((f32[2,32,1024]{2,1,0:T(8,128)S(1)}, f32[2,32,1024]{2,1,0:T(8,128)S(1)}, u32[]{:S(2)}, u32[]{:S(2)}) %collective-permute-start.23) | collective-permute-done | bytes 262176 | tf_op jit(solution)/shard_map/ppermute | solution.py:475
  89.7 2.2 %finish_step.3 = (f32[2,32,2048]{2,1,0:T(8,128)S(1)}, f32[2,32,1024]{2,1,0:T(8,128)S(1)}, f32[2,32,1024]{2,1,0:T(8,128)S(1)}, f32[1,32,2048]{2,1,0:T(8,128)S(1)}, f32[1,32,2048]{2,1,0:T(8,128)S(1)}) custom-call(s32[640]{0:T(1024)S(1)} %plan.1.plan_ref.refs_0_, bf16[160,128,256]{2,1,0:T(8,128)(2,1)S(1)} %prep.1.tiles_ref.refs_1_, ...), custom_call_target="tpu_custom_call" | custom-call | flops 268435456 | bytes 3145728 | tf_op jit(solution)/shard_map/finish_step/pallas_call | solution.py:42
  92.7 2.6 %collective-permute-start.28 = (f32[2,32,1024]{2,1,0:T(8,128)S(1)}, f32[2,32,1024]{2,1,0:T(8,128)S(1)}, u32[]{:S(2)}, u32[]{:S(2)}) collective-permute-start(f32[2,32,1024]{2,1,0:T(8,128)S(1)} %get-tuple-element.86), channel_id=1, source_target_pairs={{0,3},{1,2},{2,1},{3,0},{4,7},{5,6},{6,5},{7,4},{8,11},{9,10},{10,... | collective-permute-start | bytes 786440 | tf_op jit(solution)/shard_map/ppermute | solution.py:475
  96.9 3.7 %orth.2 = (f32[2,32,2048]{2,1,0:T(8,128)}, f32[32,32]{1,0:T(8,128)S(1)}) custom-call(f32[32,32]{1,0:T(8,128)S(1)} %add.78.gram_ref, f32[2,32,2048]{2,1,0:T(8,128)S(1)} %get-tuple-element.67.y_ref.refs_0_), custom_call_target="tpu_custom_call" | custom-call | flops 8388608 | bytes 1048576 | tf_op jit(solution)/shard_map/orth/pallas_call | solution.py:410
  100.6 3.0 %local_mixed.1.refs_2_ = f32[2,32,2048]{2,1,0:T(8,128)S(1)} custom-call(s32[640]{0:T(1024)S(1)} %plan.1.plan_ref.refs_0_, bf16[160,128,256]{2,1,0:T(8,128)(2,1)S(1)} %prep.1.tiles_ref.refs_1_, f32[2,32,2048]{2,1,0:T(8,128)S(1)} %get-tuple-element.81.y_ref, f32[2,32,2048]{2,1,0:T(8,128)S(1)} %get-tuple-element.74.y_ref.refs_0_), custom_call_target="tpu_custom_call" | custom-call | flops 671088640 | bytes 1572864 | tf_op jit(solution)/shard_map/local_mixed/pallas_call | solution.py:42
  104.9 2.8 %finish_mixed.1 = (f32[2,32,2048]{2,1,0:T(8,128)S(1)}, f32[2,32,1024]{2,1,0:T(8,128)S(1)}, f32[2,32,1024]{2,1,0:T(8,128)S(1)}, f32[1,32,2048]{2,1,0:T(8,128)S(1)...) custom-call(s32[640]{0:T(1024)S(1)} %plan.1.plan_ref.refs_0_, bf16[160,128,256]{2,1,0:T(8,128)(2,1)S(1)} %prep.1.tiles_ref.refs_1_, ...), custom_call_target="tpu_custom_call" | custom-call | flops 268435456 | bytes 3145728 | tf_op jit(solution)/shard_map/finish_mixed/pallas_call | solution.py:42
  116.3 3.0 %local_image.1.refs_2_ = f32[2,32,2048]{2,1,0:T(8,128)S(1)} custom-call(s32[640]{0:T(1024)S(1)} %plan.1.plan_ref.refs_0_, bf16[160,128,256]{2,1,0:T(8,128)(2,1)S(1)} %prep.1.tiles_ref.refs_1_, f32[2,32,2048]{2,1,0:T(8,128)S(1)} %get-tuple-element.90.y_ref.refs_7_), custom_call_target="tpu_custom_call" | custom-call | flops 671088640 | bytes 1572864 | tf_op jit(solution)/shard_map/local_image/pallas_call | solution.py:42
  119.4 3.7 %collective-permute-done.32 = f32[32,32]{1,0:T(8,128)S(1)} collective-permute-done((f32[32,32]{1,0:T(8,128)S(1)}, f32[32,32]{1,0:T(8,128)S(1)}, u32[]{:S(2)}, u32[]{:S(2)}) %collective-permute-start.32) | collective-permute-done | bytes 4128 | tf_op jit(solution)/shard_map/ppermute | solution.py:454
  123.1 2.9 %collective-permute-done.39.refs_4_ = f32[2,32,1024]{2,1,0:T(8,128)S(1)} collective-permute-done((f32[2,32,1024]{2,1,0:T(8,128)S(1)}, f32[2,32,1024]{2,1,0:T(8,128)S(1)}, u32[]{:S(2)}, u32[]{:S(2)}) %collective-permute-start.39) | collective-permute-done | bytes 262176 | tf_op jit(solution)/shard_map/ppermute | solution.py:475
  126.0 2.4 %finish_image.1 = f32[32,32]{1,0:T(8,128)S(1)} custom-call(s32[640]{0:T(1024)S(1)} %plan.1.plan_ref.refs_0_, bf16[160,128,256]{2,1,0:T(8,128)(2,1)S(1)} %prep.1.tiles_ref.refs_1_, f32[2,32,2048]{2,1,0:T(8,128)S(1)} %local_image.1.refs_2_, f32[2,32,1024]{2,1,0:T(8,128)S(1)} %collective-permute-done.38.refs_3_, ...), custom_call_target="tpu_custom_call" | custom-call | flops 268435456 | bytes 3145728 | tf_op jit(solution)/shard_map/finish_image/pallas_call | solution.py:42
  135.2 2.3 %collective-permute-start.35 = (f32[32,32]{1,0:T(8,128)S(1)}, f32[32,32]{1,0:T(8,128)S(1)}, u32[]{:S(2)}, u32[]{:S(2)}) collective-permute-start(f32[32,32]{1,0:T(8,128)S(1)} %add_add_fusion.3), channel_id=1, source_target_pairs={{0,1},{1,0},{2,3},{3,2},{4,5},{5,4},{6,7},{7,6},{8,9},{9,8},{10,11... | collective-permute-start | bytes 12296 | tf_op jit(solution)/shard_map/ppermute | solution.py:454
  139.6 2.4 %collective-permute-start.46 = (f32[32,32]{1,0:T(8,128)S(1)}, f32[32,32]{1,0:T(8,128)S(1)}, u32[]{:S(2)}, u32[]{:S(2)}) collective-permute-start(f32[32,32]{1,0:T(8,128)S(1)} %add_add_fusion.1), channel_id=1, source_target_pairs={{0,1},{1,0},{2,3},{3,2},{4,5},{5,4},{6,7},{7,6},{8,9},{9,8},{10,11... | collective-permute-start | bytes 12296 | tf_op jit(solution)/shard_map/ppermute | solution.py:454
  142.0 3.7 %orth.3 = (f32[2,32,2048]{2,1,0:T(8,128)}, f32[32,32]{1,0:T(8,128)S(1)}) custom-call(f32[32,32]{1,0:T(8,128)S(1)} %add_add_fusion.2.gram_ref, f32[2,32,2048]{2,1,0:T(8,128)S(1)} %get-tuple-element.90.y_ref.refs_7_), custom_call_target="tpu_custom_call" | custom-call | flops 8388608 | bytes 1048576 | tf_op jit(solution)/shard_map/orth/pallas_call | solution.py:410
  (100 shorter events, 48.1 us)
Async XLA Ops:
  2.4 19.7 %collective-permute-start = (f32[2,32,1024]{2,1,0:T(8,128)S(1)}, f32[2,32,1024]{2,1,0:T(8,128)S(1)}, u32[]{:S(2)}, u32[]{:S(2)}) collective-permute-start(f32[2,32,1024]{2,1,0:T(8,128)S(1)} %get-tuple-element.53), channel_id=1, source_target_pairs={{0,1},{1,0},{2,3},{3,2},{4,5},{5,4},{6,7},{7,6},{8,9},{9,8},{10,11... | collective-permute-start | bytes 786440 | tf_op jit(solution)/shard_map/ppermute | solution.py:474
  5.5 16.7 %collective-permute-start.1 = (f32[2,32,1024]{2,1,0:T(8,128)S(1)}, f32[2,32,1024]{2,1,0:T(8,128)S(1)}, u32[]{:S(2)}, u32[]{:S(2)}) collective-permute-start(f32[2,32,1024]{2,1,0:T(8,128)S(1)} %get-tuple-element.54), channel_id=1, source_target_pairs={{0,3},{1,2},{2,1},{3,0},{4,7},{5,6},{6,5},{7,4},{8,11},{9,10},{10,... | collective-permute-start | bytes 786440 | tf_op jit(solution)/shard_map/ppermute | solution.py:475
  8.0 14.2 %collective-permute-start.2 = (f32[1,32,2048]{2,1,0:T(8,128)S(1)}, f32[1,32,2048]{2,1,0:T(8,128)S(1)}, u32[]{:S(2)}, u32[]{:S(2)}) collective-permute-start(f32[1,32,2048]{2,1,0:T(8,128)S(1)} %get-tuple-element.55), channel_id=1, source_target_pairs={{0,4},{4,0},{8,12},{12,8},{16,20},{20,16},{24,28},{28,24},{1,5},{5... | collective-permute-start | bytes 786440 | tf_op jit(solution)/shard_map/ppermute | solution.py:477
  8.0 14.2 %collective-permute-start.3 = (f32[1,32,2048]{2,1,0:T(8,128)S(1)}, f32[1,32,2048]{2,1,0:T(8,128)S(1)}, u32[]{:S(2)}, u32[]{:S(2)}) collective-permute-start(f32[1,32,2048]{2,1,0:T(8,128)S(1)} %get-tuple-element.56), channel_id=1, source_target_pairs={{0,28},{4,8},{8,4},{12,16},{16,12},{20,24},{24,20},{28,0},{1,29},{... | collective-permute-start | bytes 786440 | tf_op jit(solution)/shard_map/ppermute | solution.py:476
  24.3 12.9 %collective-permute-start.4 = (f32[2,32,1024]{2,1,0:T(8,128)S(1)}, f32[2,32,1024]{2,1,0:T(8,128)S(1)}, u32[]{:S(2)}, u32[]{:S(2)}) collective-permute-start(f32[2,32,1024]{2,1,0:T(8,128)S(1)} %get-tuple-element.58), channel_id=1, source_target_pairs={{0,1},{1,0},{2,3},{3,2},{4,5},{5,4},{6,7},{7,6},{8,9},{9,8},{10,11... | collective-permute-start | bytes 786440 | tf_op jit(solution)/shard_map/ppermute | solution.py:474
  25.0 12.2 %collective-permute-start.5 = (f32[2,32,1024]{2,1,0:T(8,128)S(1)}, f32[2,32,1024]{2,1,0:T(8,128)S(1)}, u32[]{:S(2)}, u32[]{:S(2)}) collective-permute-start(f32[2,32,1024]{2,1,0:T(8,128)S(1)} %get-tuple-element.59), channel_id=1, source_target_pairs={{0,3},{1,2},{2,1},{3,0},{4,7},{5,6},{6,5},{7,4},{8,11},{9,10},{10,... | collective-permute-start | bytes 786440 | tf_op jit(solution)/shard_map/ppermute | solution.py:475
  25.9 11.3 %collective-permute-start.6 = (f32[1,32,2048]{2,1,0:T(8,128)S(1)}, f32[1,32,2048]{2,1,0:T(8,128)S(1)}, u32[]{:S(2)}, u32[]{:S(2)}) collective-permute-start(f32[1,32,2048]{2,1,0:T(8,128)S(1)} %get-tuple-element.60), channel_id=1, source_target_pairs={{0,4},{4,0},{8,12},{12,8},{16,20},{20,16},{24,28},{28,24},{1,5},{5... | collective-permute-start | bytes 786440 | tf_op jit(solution)/shard_map/ppermute | solution.py:477
  25.9 11.3 %collective-permute-start.7 = (f32[1,32,2048]{2,1,0:T(8,128)S(1)}, f32[1,32,2048]{2,1,0:T(8,128)S(1)}, u32[]{:S(2)}, u32[]{:S(2)}) collective-permute-start(f32[1,32,2048]{2,1,0:T(8,128)S(1)} %get-tuple-element.61), channel_id=1, source_target_pairs={{0,28},{4,8},{8,4},{12,16},{16,12},{20,24},{24,20},{28,0},{1,29},{... | collective-permute-start | bytes 786440 | tf_op jit(solution)/shard_map/ppermute | solution.py:476
  39.3 8.7 %collective-permute-start.8 = (f32[2,32,1024]{2,1,0:T(8,128)S(1)}, f32[2,32,1024]{2,1,0:T(8,128)S(1)}, u32[]{:S(2)}, u32[]{:S(2)}) collective-permute-start(f32[2,32,1024]{2,1,0:T(8,128)S(1)} %get-tuple-element.63), channel_id=1, source_target_pairs={{0,1},{1,0},{2,3},{3,2},{4,5},{5,4},{6,7},{7,6},{8,9},{9,8},{10,11... | collective-permute-start | bytes 786440 | tf_op jit(solution)/shard_map/ppermute | solution.py:474
  41.1 10.9 %collective-permute-start.9 = (f32[2,32,1024]{2,1,0:T(8,128)S(1)}, f32[2,32,1024]{2,1,0:T(8,128)S(1)}, u32[]{:S(2)}, u32[]{:S(2)}) collective-permute-start(f32[2,32,1024]{2,1,0:T(8,128)S(1)} %get-tuple-element.64), channel_id=1, source_target_pairs={{0,3},{1,2},{2,1},{3,0},{4,7},{5,6},{6,5},{7,4},{8,11},{9,10},{10,... | collective-permute-start | bytes 786440 | tf_op jit(solution)/shard_map/ppermute | solution.py:475
  41.9 10.1 %collective-permute-start.10 = (f32[1,32,2048]{2,1,0:T(8,128)S(1)}, f32[1,32,2048]{2,1,0:T(8,128)S(1)}, u32[]{:S(2)}, u32[]{:S(2)}) collective-permute-start(f32[1,32,2048]{2,1,0:T(8,128)S(1)} %get-tuple-element.65), channel_id=1, source_target_pairs={{0,4},{4,0},{8,12},{12,8},{16,20},{20,16},{24,28},{28,24},{1,5},{5... | collective-permute-start | bytes 786440 | tf_op jit(solution)/shard_map/ppermute | solution.py:477
  41.9 10.1 %collective-permute-start.11 = (f32[1,32,2048]{2,1,0:T(8,128)S(1)}, f32[1,32,2048]{2,1,0:T(8,128)S(1)}, u32[]{:S(2)}, u32[]{:S(2)}) collective-permute-start(f32[1,32,2048]{2,1,0:T(8,128)S(1)} %get-tuple-element.66), channel_id=1, source_target_pairs={{0,28},{4,8},{8,4},{12,16},{16,12},{20,24},{24,20},{28,0},{1,29},{... | collective-permute-start | bytes 786440 | tf_op jit(solution)/shard_map/ppermute | solution.py:476
  56.9 10.2 %collective-permute-start.12 = (f32[32,32]{1,0:T(8,128)S(1)}, f32[32,32]{1,0:T(8,128)S(1)}, u32[]{:S(2)}, u32[]{:S(2)}) collective-permute-start(f32[32,32]{1,0:T(8,128)S(1)} %get-tuple-element.68), channel_id=1, source_target_pairs={{0,1},{1,0},{2,3},{3,2},{4,5},{5,4},{6,7},{7,6},{8,9},{9,8},{10,11... | collective-permute-start | bytes 12296 | tf_op jit(solution)/shard_map/ppermute | solution.py:454
  58.9 9.3 %collective-permute-start.15 = (f32[2,32,1024]{2,1,0:T(8,128)S(1)}, f32[2,32,1024]{2,1,0:T(8,128)S(1)}, u32[]{:S(2)}, u32[]{:S(2)}) collective-permute-start(f32[2,32,1024]{2,1,0:T(8,128)S(1)} %get-tuple-element.70), channel_id=1, source_target_pairs={{0,1},{1,0},{2,3},{3,2},{4,5},{5,4},{6,7},{7,6},{8,9},{9,8},{10,11... | collective-permute-start | bytes 786440 | tf_op jit(solution)/shard_map/ppermute | solution.py:474
  58.9 13.4 %collective-permute-start.16 = (f32[2,32,1024]{2,1,0:T(8,128)S(1)}, f32[2,32,1024]{2,1,0:T(8,128)S(1)}, u32[]{:S(2)}, u32[]{:S(2)}) collective-permute-start(f32[2,32,1024]{2,1,0:T(8,128)S(1)} %get-tuple-element.71), channel_id=1, source_target_pairs={{0,3},{1,2},{2,1},{3,0},{4,7},{5,6},{6,5},{7,4},{8,11},{9,10},{10,... | collective-permute-start | bytes 786440 | tf_op jit(solution)/shard_map/ppermute | solution.py:475
  61.2 14.0 %collective-permute-start.17 = (f32[1,32,2048]{2,1,0:T(8,128)S(1)}, f32[1,32,2048]{2,1,0:T(8,128)S(1)}, u32[]{:S(2)}, u32[]{:S(2)}) collective-permute-start(f32[1,32,2048]{2,1,0:T(8,128)S(1)} %get-tuple-element.72), channel_id=1, source_target_pairs={{0,4},{4,0},{8,12},{12,8},{16,20},{20,16},{24,28},{28,24},{1,5},{5... | collective-permute-start | bytes 786440 | tf_op jit(solution)/shard_map/ppermute | solution.py:477
  61.6 13.7 %collective-permute-start.18 = (f32[1,32,2048]{2,1,0:T(8,128)S(1)}, f32[1,32,2048]{2,1,0:T(8,128)S(1)}, u32[]{:S(2)}, u32[]{:S(2)}) collective-permute-start(f32[1,32,2048]{2,1,0:T(8,128)S(1)} %get-tuple-element.73), channel_id=1, source_target_pairs={{0,28},{4,8},{8,4},{12,16},{16,12},{20,24},{24,20},{28,0},{1,29},{... | collective-permute-start | bytes 786440 | tf_op jit(solution)/shard_map/ppermute | solution.py:476
  67.1 13.7 %collective-permute-start.21 = (f32[32,32]{1,0:T(8,128)S(1)}, f32[32,32]{1,0:T(8,128)S(1)}, u32[]{:S(2)}, u32[]{:S(2)}) collective-permute-start(f32[32,32]{1,0:T(8,128)S(1)} %add_add_fusion.5), channel_id=1, source_target_pairs={{0,24},{4,28},{8,16},{12,20},{16,8},{20,12},{24,0},{28,4},{1,25},{... | collective-permute-start | bytes 12296 | tf_op jit(solution)/shard_map/ppermute | solution.py:454
  68.2 12.6 %collective-permute-start.20 = (f32[32,32]{1,0:T(8,128)S(1)}, f32[32,32]{1,0:T(8,128)S(1)}, u32[]{:S(2)}, u32[]{:S(2)}) collective-permute-start(f32[32,32]{1,0:T(8,128)S(1)} %add_add_fusion.5), channel_id=1, source_target_pairs={{0,16},{4,20},{8,24},{12,28},{16,0},{20,4},{24,8},{28,12},{1,17},{... | collective-permute-start | bytes 12296 | tf_op jit(solution)/shard_map/ppermute | solution.py:454
  72.4 8.6 %collective-permute-start.19 = (f32[32,32]{1,0:T(8,128)S(1)}, f32[32,32]{1,0:T(8,128)S(1)}, u32[]{:S(2)}, u32[]{:S(2)}) collective-permute-start(f32[32,32]{1,0:T(8,128)S(1)} %add_add_fusion.5), channel_id=1, source_target_pairs={{0,8},{4,12},{8,0},{12,4},{16,24},{20,28},{24,16},{28,20},{1,9},{5... | collective-permute-start | bytes 12296 | tf_op jit(solution)/shard_map/ppermute | solution.py:454
  77.3 9.2 %collective-permute-start.22 = (f32[2,32,1024]{2,1,0:T(8,128)S(1)}, f32[2,32,1024]{2,1,0:T(8,128)S(1)}, u32[]{:S(2)}, u32[]{:S(2)}) collective-permute-start(f32[2,32,1024]{2,1,0:T(8,128)S(1)} %get-tuple-element.77), channel_id=1, source_target_pairs={{0,1},{1,0},{2,3},{3,2},{4,5},{5,4},{6,7},{7,6},{8,9},{9,8},{10,11... | collective-permute-start | bytes 786440 | tf_op jit(solution)/shard_map/ppermute | solution.py:474
  78.8 10.9 %collective-permute-start.23 = (f32[2,32,1024]{2,1,0:T(8,128)S(1)}, f32[2,32,1024]{2,1,0:T(8,128)S(1)}, u32[]{:S(2)}, u32[]{:S(2)}) collective-permute-start(f32[2,32,1024]{2,1,0:T(8,128)S(1)} %get-tuple-element.78), channel_id=1, source_target_pairs={{0,3},{1,2},{2,1},{3,0},{4,7},{5,6},{6,5},{7,4},{8,11},{9,10},{10,... | collective-permute-start | bytes 786440 | tf_op jit(solution)/shard_map/ppermute | solution.py:475
  80.8 8.9 %collective-permute-start.24 = (f32[1,32,2048]{2,1,0:T(8,128)S(1)}, f32[1,32,2048]{2,1,0:T(8,128)S(1)}, u32[]{:S(2)}, u32[]{:S(2)}) collective-permute-start(f32[1,32,2048]{2,1,0:T(8,128)S(1)} %get-tuple-element.79), channel_id=1, source_target_pairs={{0,4},{4,0},{8,12},{12,8},{16,20},{20,16},{24,28},{28,24},{1,5},{5... | collective-permute-start | bytes 786440 | tf_op jit(solution)/shard_map/ppermute | solution.py:477
  80.9 8.9 %collective-permute-start.25 = (f32[1,32,2048]{2,1,0:T(8,128)S(1)}, f32[1,32,2048]{2,1,0:T(8,128)S(1)}, u32[]{:S(2)}, u32[]{:S(2)}) collective-permute-start(f32[1,32,2048]{2,1,0:T(8,128)S(1)} %get-tuple-element.80), channel_id=1, source_target_pairs={{0,28},{4,8},{8,4},{12,16},{16,12},{20,24},{24,20},{28,0},{1,29},{... | collective-permute-start | bytes 786440 | tf_op jit(solution)/shard_map/ppermute | solution.py:476
  92.0 11.7 %collective-permute-start.27 = (f32[2,32,1024]{2,1,0:T(8,128)S(1)}, f32[2,32,1024]{2,1,0:T(8,128)S(1)}, u32[]{:S(2)}, u32[]{:S(2)}) collective-permute-start(f32[2,32,1024]{2,1,0:T(8,128)S(1)} %get-tuple-element.85), channel_id=1, source_target_pairs={{0,1},{1,0},{2,3},{3,2},{4,5},{5,4},{6,7},{7,6},{8,9},{9,8},{10,11... | collective-permute-start | bytes 786440 | tf_op jit(solution)/shard_map/ppermute | solution.py:474
  92.7 12.2 %collective-permute-start.28 = (f32[2,32,1024]{2,1,0:T(8,128)S(1)}, f32[2,32,1024]{2,1,0:T(8,128)S(1)}, u32[]{:S(2)}, u32[]{:S(2)}) collective-permute-start(f32[2,32,1024]{2,1,0:T(8,128)S(1)} %get-tuple-element.86), channel_id=1, source_target_pairs={{0,3},{1,2},{2,1},{3,0},{4,7},{5,6},{6,5},{7,4},{8,11},{9,10},{10,... | collective-permute-start | bytes 786440 | tf_op jit(solution)/shard_map/ppermute | solution.py:475
  95.4 9.5 %collective-permute-start.29 = (f32[1,32,2048]{2,1,0:T(8,128)S(1)}, f32[1,32,2048]{2,1,0:T(8,128)S(1)}, u32[]{:S(2)}, u32[]{:S(2)}) collective-permute-start(f32[1,32,2048]{2,1,0:T(8,128)S(1)} %get-tuple-element.87), channel_id=1, source_target_pairs={{0,4},{4,0},{8,12},{12,8},{16,20},{20,16},{24,28},{28,24},{1,5},{5... | collective-permute-start | bytes 786440 | tf_op jit(solution)/shard_map/ppermute | solution.py:477
  95.4 9.5 %collective-permute-start.30 = (f32[1,32,2048]{2,1,0:T(8,128)S(1)}, f32[1,32,2048]{2,1,0:T(8,128)S(1)}, u32[]{:S(2)}, u32[]{:S(2)}) collective-permute-start(f32[1,32,2048]{2,1,0:T(8,128)S(1)} %get-tuple-element.88), channel_id=1, source_target_pairs={{0,28},{4,8},{8,4},{12,16},{16,12},{20,24},{24,20},{28,0},{1,29},{... | collective-permute-start | bytes 786440 | tf_op jit(solution)/shard_map/ppermute | solution.py:476
  111.1 12.0 %collective-permute-start.38 = (f32[2,32,1024]{2,1,0:T(8,128)S(1)}, f32[2,32,1024]{2,1,0:T(8,128)S(1)}, u32[]{:S(2)}, u32[]{:S(2)}) collective-permute-start(f32[2,32,1024]{2,1,0:T(8,128)S(1)} %get-tuple-element.97), channel_id=1, source_target_pairs={{0,1},{1,0},{2,3},{3,2},{4,5},{5,4},{6,7},{7,6},{8,9},{9,8},{10,11... | collective-permute-start | bytes 786440 | tf_op jit(solution)/shard_map/ppermute | solution.py:474
  112.5 13.5 %collective-permute-start.39 = (f32[2,32,1024]{2,1,0:T(8,128)S(1)}, f32[2,32,1024]{2,1,0:T(8,128)S(1)}, u32[]{:S(2)}, u32[]{:S(2)}) collective-permute-start(f32[2,32,1024]{2,1,0:T(8,128)S(1)} %get-tuple-element.98), channel_id=1, source_target_pairs={{0,3},{1,2},{2,1},{3,0},{4,7},{5,6},{6,5},{7,4},{8,11},{9,10},{10,... | collective-permute-start | bytes 786440 | tf_op jit(solution)/shard_map/ppermute | solution.py:475
  114.2 11.8 %collective-permute-start.40 = (f32[1,32,2048]{2,1,0:T(8,128)S(1)}, f32[1,32,2048]{2,1,0:T(8,128)S(1)}, u32[]{:S(2)}, u32[]{:S(2)}) collective-permute-start(f32[1,32,2048]{2,1,0:T(8,128)S(1)} %get-tuple-element.99), channel_id=1, source_target_pairs={{0,4},{4,0},{8,12},{12,8},{16,20},{20,16},{24,28},{28,24},{1,5},{5... | collective-permute-start | bytes 786440 | tf_op jit(solution)/shard_map/ppermute | solution.py:477
  114.2 11.8 %collective-permute-start.41 = (f32[1,32,2048]{2,1,0:T(8,128)S(1)}, f32[1,32,2048]{2,1,0:T(8,128)S(1)}, u32[]{:S(2)}, u32[]{:S(2)}) collective-permute-start(f32[1,32,2048]{2,1,0:T(8,128)S(1)} %get-tuple-element.100), channel_id=1, source_target_pairs={{0,28},{4,8},{8,4},{12,16},{16,12},{20,24},{24,20},{28,0},{1,29},{... | collective-permute-start | bytes 786440 | tf_op jit(solution)/shard_map/ppermute | solution.py:476
  (19 other events, 93.6 us)

commit v4 on v3

--- a/solution.py
+++ b/solution.py
@@ -143,7 +143,7 @@
         out_ref[at.places + 2 * units + found] = zero
         return units + (found + 1) // 2
 
-    units = lax.fori_loop(0, slices * blocks, row, jnp.int32(0))
+    units = lax.fori_loop(0, slices * blocks, row, jnp.int32(0), unroll=4)
     for n in range(GROUP):
         out_ref[at.rows + units + n] = 0
         for k in range(2):
@@ -222,7 +222,7 @@
 
 
 def local_kernel(mode, scale, plan_ref, tiles_ref, y_ref, *refs):
-    if mode in ("step", "gram", "mixed"):
+    if mode in ("step", "gram"):
         previous_ref, out_ref, halves_ref = refs
     else:
         previous_ref, (out_ref, halves_ref) = None, refs
@@ -298,13 +298,11 @@
     take = lambda n: [refs.pop(0) for _ in range(n)]
     plan_ref, tiles_ref, part_ref = take(3)
     inner_ref, outer_ref, near_ref, far_ref = take(4)
-    y_ref = take(1)[0] if mode == "image" else None
-    matrix_ref = take(1)[0] if mode == "mixed" else None
     if mode == "image":
-        gram_ref, halves_ref, new_ref = refs
+        y_ref, matrix_ref, mixed_ref, gram_ref, halves_ref, new_ref = refs
     else:
         new_ref, *edge_refs = take(5)
-        gram_ref = take(1)[0] if mode in ("gram", "mixed") else None
+        gram_ref = take(1)[0] if mode == "gram" else None
         (halves_ref,) = refs
     slices, width, points = part_ref.shape
     blocks = points // TILE
@@ -343,17 +341,20 @@
 
     lax.fori_loop(0, plan_ref[at.groups], group, 0)
 
-    if mode == "mixed":
-        for s in range(slices):
-            new_ref[s] = mix(matrix_ref[...], new_ref[s])
     if mode != "image":
         edges([plan_ref[at.flags], plan_ref[at.flags + 1]], new_ref, *edge_refs)
-    if gram_ref is not None:
-        base_ref = y_ref if mode == "image" else new_ref
-        total = inner(base_ref[0], new_ref[0])
-        for s in range(1, slices):
-            total = total + inner(base_ref[s], new_ref[s])
-        gram_ref[...] = total
+    if mode == "gram":
+        gram_ref[...] = sum(inner(new_ref[s], new_ref[s]) for s in range(slices))
+    if mode == "image":
+        matrix = matrix_ref[...]
+        first, second = 0.0, 0.0
+        for s in range(slices):
+            mixed = mix(matrix, y_ref[s])
+            mixed_ref[s] = mixed
+            first = first + inner(mixed, mixed)
+            second = second + inner(mixed, mix(matrix, new_ref[s]))
+        gram_ref[:width] = first
+        gram_ref[width:] = second
 
 
 def finish(mode, scale, table, tiles, part, y, halo, matrix=None):
@@ -361,11 +362,11 @@
     blocks = points // TILE
     ins = [table] + [near(v) for v in (tiles, part, *halo)]
     if mode == "image":
-        ins.append(near(y))
-    if matrix is not None:
-        ins.append(near(matrix))
-    outs = [] if mode == "image" else edge_shapes(y.shape)
-    if mode in ("gram", "mixed", "image"):
+        ins += [near(y), near(matrix)]
+        outs = [(y.shape, F32), ((2 * width, width), F32)]
+    else:
+        outs = edge_shapes(y.shape)
+    if mode == "gram":
         outs = outs + [((width, width), F32)]
     scratch = [VM((slices * 2 * HB + 1, 2 * width, TILE), BF16)]
     if mode == "image":
@@ -398,43 +399,63 @@
     return inverse
 
 
-def orth_kernel(count, gram_ref, y_ref, out_ref, matrix_ref):
-    matrix = inverse_factor(gram_ref[...] * (1.0 / count))
-    matrix_ref[...] = matrix
+def factor_kernel(count, gram_ref, out_ref):
+    out_ref[...] = inverse_factor(gram_ref[...] * (1.0 / count))
+
+
+def factor(gram, count):
+    return call(
+        functools.partial(factor_kernel, float(count)),
+        [near(gram)],
+        [(gram.shape, F32)],
+        specs=[WHOLE],
+        flops=40000 * gram.size,
+        moved=8 * gram.size,
+        name="factor",
+    )[0]
+
+
+def basis_kernel(matrix_ref, y_ref, out_ref):
     for s in range(y_ref.shape[0]):
-        out_ref[s] = mix(matrix, y_ref[s])
-
-
-def orth(gram, y, count):
-    width = gram.shape[0]
-    return pl.pallas_call(
-        functools.partial(orth_kernel, float(count)),
-        out_shape=[jax.ShapeDtypeStruct(y.shape, F32), VM((width, width), F32)],
-        in_specs=[WHOLE, WHOLE],
-        out_specs=[WHOLE, WHOLE],
-        name="orth",
-        cost_estimate=pl.CostEstimate(flops=2 * width * y.size, bytes_accessed=8 * y.size, transcendentals=0),
-        compiler_params=pltpu.CompilerParams(vmem_limit_bytes=6 << 20),
-    )(near(gram), near(y))
-
-
-def ritz_kernel(count, matrix_ref, inner_ref, out_ref):
-    high = lax.Precision.HIGHEST
-    matrix = matrix_ref[...]
-    half = lax.dot_general(matrix, inner_ref[...] * (1.0 / count), NN, precision=high, preferred_element_type=F32)
-    out_ref[...] = lax.dot_general(half, matrix, NT, precision=high, preferred_element_type=F32)
-
-
-def ritz(matrix, product, count):
+        out_ref[s] = mix(matrix_ref[...], y_ref[s])
+
+
+def basis(matrix, y):
     return call(
-        functools.partial(ritz_kernel, float(count)),
-        [near(matrix), near(product)],
-        [(product.shape, F32)],
-        specs=[WHOLE, WHOLE],
-        name="ritz",
-        moved=4 * product.size,
+        basis_kernel,
+        [near(matrix), near(y)],
+        [(y.shape, F32)],
+        specs=[WHOLE] * 2,
+        flops=2 * matrix.shape[0] * y.size,
+        moved=8 * y.size,
+        name="basis",
         out_vmem=False,
     )[0]
+
+
+def close_kernel(count, sums_ref, y_ref, basis_ref, ritz_ref):
+    high = lax.Precision.HIGHEST
+    width = sums_ref.shape[1]
+    matrix = inverse_factor(sums_ref[:width] * (1.0 / count))
+    projected = sums_ref[width:] * (1.0 / count)
+    for s in range(y_ref.shape[0]):
+        basis_ref[s] = mix(matrix, y_ref[s])
+    half = lax.dot_general(matrix, projected, NN, precision=high, preferred_element_type=F32)
+    ritz_ref[...] = lax.dot_general(half, matrix, NT, precision=high, preferred_element_type=F32)
+
+
+def close(sums, y, count):
+    width = sums.shape[1]
+    return call(
+        functools.partial(close_kernel, float(count)),
+        [near(sums), near(y)],
+        [(y.shape, F32), ((width, width), F32)],
+        specs=[WHOLE] * 2,
+        flops=2 * width * y.size,
+        moved=8 * y.size,
+        name="close",
+        out_vmem=False,
+    )
 
 
 def stages_of(axis):
@@ -446,6 +467,10 @@
         found.append((axis, (stride, 2 * stride, 3 * stride)))
         stride *= 4
     return found
+
+
+def pairs_of(axis):
+    return [(axis, (1 << k,)) for k in range((lax.axis_size(axis) - 1).bit_length())]
 
 
 def add_over(value, stages):
@@ -500,42 +525,36 @@
     table = plan(tile_columns, odd, blocks_all)
     tiles = prep(stiffness_tiles)
 
-    across, along = stages_of("space"), stages_of("tm")
-    early, late = across + along[::-1], along + across
-    share = -(-len(early) // 3)
+    across, along = pairs_of("space"), pairs_of("tm")
+    half = -(-len(across) // 2)
+    early = [along[:1] + across[:half], across[half:], along[1:-1], along[-1:]]
 
     def apply(mode, scale, y, edge, previous=None, beside=None):
         halo = exchange(edge)
         part = local_part(mode, scale, table, tiles, y, previous)
-        extra = beside() if beside else None
-        if extra is not None:
-            part, extra = lax.optimization_barrier((part, extra))
-        matrix = extra if mode == "mixed" else None
-        return finish(mode, scale, table, tiles, part, y, halo, matrix), extra
+        extra = None
+        if beside is not None:
+            part, extra = lax.optimization_barrier((part, beside[0]))
+            part, extra = lax.optimization_barrier((part, beside[1](extra)))
+        return finish(mode, scale, table, tiles, part, y, halo, extra), extra
 
     (y1, *edge), _ = apply("first", 1.0 / RADIUS, y, edge)
     (y2, *edge), _ = apply("step", 2.0 / RADIUS, y1, edge, y)
     (filtered, *edge, gram), _ = apply("gram", 2.0 / RADIUS, y2, edge, y1)
 
-    kept = {}
-
-    def first_matrix():
-        total = add_over(gram, early[2 * share :])
-        kept["first"], matrix = orth(total, filtered, count_all)
-        return matrix
-
-    (y1, *edge), gram = apply(
-        "first", 1.0 / RADIUS, filtered, edge, beside=lambda: add_over(gram, early[:share])
+    def stage(n):
+        return lambda gram: add_over(gram, early[n])
+
+    (y1, *edge), gram = apply("first", 1.0 / RADIUS, filtered, edge, None, (gram, stage(0)))
+    (y2, *edge), gram = apply("step", 2.0 / RADIUS, y1, edge, filtered, (gram, stage(1)))
+    (y3, *edge), gram = apply("step", 2.0 / RADIUS, y2, edge, y1, (gram, stage(2)))
+    (second, sums), matrix = apply(
+        "image", 1.0, y3, edge, None, (gram, lambda gram: factor(stage(3)(gram), count_all))
     )
-    (y2, *edge), gram = apply(
-        "step", 2.0 / RADIUS, y1, edge, filtered, beside=lambda: add_over(gram, early[share : 2 * share])
-    )
-    (second, *edge, gram_two), _ = apply("mixed", 2.0 / RADIUS, y2, edge, y1, beside=first_matrix)
-    (inner_two,), gram_two = apply(
-        "image", 1.0, second, edge, beside=lambda: add_over(gram_two, along)
-    )
-    ritz_basis, matrix = orth(add_over(gram_two, across), second, count_all)
-    return ritz_basis, kept["first"], ritz(matrix, add_over(inner_two, late), count_all)
+    first_basis = basis(matrix, filtered)
+    sums = add_over(sums, stages_of("tm") + stages_of("space"))
+    ritz_basis, ritz_matrix = close(sums, second, count_all)
+    return ritz_basis, first_basis, ritz_matrix
 
 
 def solution(mesh):

time: 147 us -> 141 us (0.959)
  starting transfers between devices: 57.4 us -> 50.3 us
  waiting for transfers between devices: 32.4 us -> 34.3 us
    ppermute x21 -> x12, waiting for transfers between devices: 7.69 us -> 22.9 us  [add_over(): lax.ppermute(value, axis, [(i, i ^ k) for i in range(count)])]
    ppermute x21 -> x12, starting transfers between devices: 26.2 us -> 12.5 us  [add_over(): lax.ppermute(value, axis, [(i, i ^ k) for i in range(count)])]
    ppermute x7, starting transfers between devices: 9.03 us -> 19.5 us  [exchange(): far_slice = lax.ppermute(far_slice, 'tm', outer_pairs('tm'))]
    ppermute x7, waiting for transfers between devices: 13.9 us -> 4.8 us  [exchange(): outer = lax.ppermute(outer, 'space', outer_pairs('space'))]
    pallas_call x2 -> x0, Pallas kernels: 7.36 us -> none  [orth(): pl.pallas_call(functools.partial(orth_kernel, float(count)), out_shape=[j...]
    pallas_call x16 -> x18, Pallas kernels: 38.8 us -> 45.1 us  [call(): pl.pallas_call(kernel, out_shape=out_shape, in_specs=specs, out_specs=[WH...]
    ppermute x7, waiting for transfers between devices: 10.8 us -> 6.5 us  [exchange(): inner = lax.ppermute(inner, 'space', inner_pairs('space'))]
    ppermute x7, starting transfers between devices: 12.9 us -> 10.1 us  [exchange(): outer = lax.ppermute(outer, 'space', outer_pairs('space'))]
  transfers between devices with their start and end apart: 49 -> 40, of which waited for: 14 -> 16; matrix products, arithmetic and copies ran while one was open for 0% -> 0% of each run, Pallas kernels for 26% -> 23%
where the time goes in v4:
time: 141 us; the launch traced here: 140 us
  Pallas kernels  52.9 us (38%)
  starting transfers between devices  50.3 us (36%)
  waiting for transfers between devices  34.3 us (24%)
  local copies, waits for them, and re-layouts  1.81 us (1%)
    pallas_call x18, Pallas kernels, call(): pl.pallas_call(kernel, out_shape=out_shape, in_specs=specs, out_specs=[WH...  45.1 us
    ppermute x12, waiting for transfers between devices, add_over(): lax.ppermute(value, axis, [(i, i ^ k) for i in range(count)])  22.9 us
    ppermute x7, starting transfers between devices, exchange(): far_slice = lax.ppermute(far_slice, 'tm', outer_pairs('tm'))  19.5 us
    ppermute x12, starting transfers between devices, add_over(): lax.ppermute(value, axis, [(i, i ^ k) for i in range(count)])  12.5 us
    ppermute x7, starting transfers between devices, exchange(): outer = lax.ppermute(outer, 'space', outer_pairs('space'))  10.1 us
    ppermute x7, starting transfers between devices, exchange(): inner = lax.ppermute(inner, 'space', inner_pairs('space'))  8.23 us
    ppermute x7, waiting for transfers between devices, exchange(): inner = lax.ppermute(inner, 'space', inner_pairs('space'))  6.5 us
    ppermute x7, waiting for transfers between devices, exchange(): outer = lax.ppermute(outer, 'space', outer_pairs('space'))  4.8 us
  transfers between devices with their start and end apart: 40, of which 16 were waited for; matrix products, arithmetic and copies ran while one was open for 0% of the time, Pallas kernels for 23%

profile of v4, /device:TPU:0, one launch (start us, length us, event | category | flops | bytes accessed | tf_op | source)
XLA Modules:
  0.0 140.3 jit_solution(2223709265066264924)
XLA Ops:
  2.4 3.1 %collective-permute-start = (f32[2,32,1024]{2,1,0:T(8,128)S(1)}, f32[2,32,1024]{2,1,0:T(8,128)S(1)}, u32[]{:S(2)}, u32[]{:S(2)}) collective-permute-start(f32[2,32,1024]{2,1,0:T(8,128)S(1)} %get-tuple-element.60), channel_id=1, source_target_pairs={{0,1},{1,0},{2,3},{3,2},{4,5},{5,4},{6,7},{7,6},{8,9},{9,8},{10,11... | collective-permute-start | bytes 786440 | tf_op jit(solution)/shard_map/ppermute | solution.py:499
  5.5 2.5 %collective-permute-start.1 = (f32[2,32,1024]{2,1,0:T(8,128)S(1)}, f32[2,32,1024]{2,1,0:T(8,128)S(1)}, u32[]{:S(2)}, u32[]{:S(2)}) collective-permute-start(f32[2,32,1024]{2,1,0:T(8,128)S(1)} %get-tuple-element.61), channel_id=1, source_target_pairs={{0,3},{1,2},{2,1},{3,0},{4,7},{5,6},{6,5},{7,4},{8,11},{9,10},{10,... | collective-permute-start | bytes 786440 | tf_op jit(solution)/shard_map/ppermute | solution.py:500
  8.0 2.6 %collective-permute-start.3 = (f32[1,32,2048]{2,1,0:T(8,128)S(1)}, f32[1,32,2048]{2,1,0:T(8,128)S(1)}, u32[]{:S(2)}, u32[]{:S(2)}) collective-permute-start(f32[1,32,2048]{2,1,0:T(8,128)S(1)} %get-tuple-element.63), channel_id=1, source_target_pairs={{0,28},{4,8},{8,4},{12,16},{16,12},{20,24},{24,20},{28,0},{1,29},{... | collective-permute-start | bytes 786440 | tf_op jit(solution)/shard_map/ppermute | solution.py:501
  11.2 3.0 %plan.1.plan_ref.refs_0_ = s32[640]{0:T(1024)S(1)} custom-call(s32[2,80]{1,0:T(2,128)S(1)} %copy-done.1, s32[5]{0:T(128)S(1)} %stack.31.flags_ref.odd_ref), custom_call_target="tpu_custom_call" | custom-call | tf_op jit(solution)/shard_map/plan/pallas_call | solution.py:158
  14.3 4.8 %prep.1.tiles_ref.refs_1_ = bf16[160,128,256]{2,1,0:T(8,128)(2,1)S(1)} custom-call(f32[160,128,128]{2,1,0:T(8,128)} %bitcast.6), custom_call_target="tpu_custom_call" | custom-call | bytes 10485760 | tf_op jit(solution)/shard_map/prep/pallas_call | solution.py:87
  19.1 3.0 %local_first.2.refs_2_ = f32[2,32,2048]{2,1,0:T(8,128)S(1)} custom-call(s32[640]{0:T(1024)S(1)} %plan.1.plan_ref.refs_0_, bf16[160,128,256]{2,1,0:T(8,128)(2,1)S(1)} %prep.1.tiles_ref.refs_1_, f32[2,32,2048]{2,1,0:T(8,128)S(1)} %get-tuple-element.59.y_ref.refs_0_), custom_call_target="tpu_custom_call" | custom-call | flops 671088640 | bytes 1572864 | tf_op jit(solution)/shard_map/local_first/pallas_call | solution.py:42
  25.5 2.1 %collective-permute-start.7 = (f32[1,32,2048]{2,1,0:T(8,128)S(1)}, f32[1,32,2048]{2,1,0:T(8,128)S(1)}, u32[]{:S(2)}, u32[]{:S(2)}) collective-permute-start(f32[1,32,2048]{2,1,0:T(8,128)S(1)} %get-tuple-element.68), channel_id=1, source_target_pairs={{0,28},{4,8},{8,4},{12,16},{16,12},{20,24},{24,20},{28,0},{1,29},{... | collective-permute-start | bytes 786440 | tf_op jit(solution)/shard_map/ppermute | solution.py:501
  27.7 3.0 %local_step.3.refs_2_ = f32[2,32,2048]{2,1,0:T(8,128)S(1)} custom-call(s32[640]{0:T(1024)S(1)} %plan.1.plan_ref.refs_0_, bf16[160,128,256]{2,1,0:T(8,128)(2,1)S(1)} %prep.1.tiles_ref.refs_1_, f32[2,32,2048]{2,1,0:T(8,128)S(1)} %get-tuple-element.64.y_ref.refs_0_, f32[2,32,2048]{2,1,0:T(8,128)S(1)} %get-tuple-element.59.y_ref.refs_0_), custom_call_target="tpu_custom_call" | custom-call | flops 671088640 | bytes 1572864 | tf_op jit(solution)/shard_map/local_step/pallas_call | solution.py:42
  30.7 6.1 %collective-permute-done.4.refs_3_ = f32[2,32,1024]{2,1,0:T(8,128)S(1)} collective-permute-done((f32[2,32,1024]{2,1,0:T(8,128)S(1)}, f32[2,32,1024]{2,1,0:T(8,128)S(1)}, u32[]{:S(2)}, u32[]{:S(2)}) %collective-permute-start.4) | collective-permute-done | bytes 262176 | tf_op jit(solution)/shard_map/ppermute | solution.py:499
  41.3 2.7 %collective-permute-start.11 = (f32[1,32,2048]{2,1,0:T(8,128)S(1)}, f32[1,32,2048]{2,1,0:T(8,128)S(1)}, u32[]{:S(2)}, u32[]{:S(2)}) collective-permute-start(f32[1,32,2048]{2,1,0:T(8,128)S(1)} %get-tuple-element.73), channel_id=1, source_target_pairs={{0,28},{4,8},{8,4},{12,16},{16,12},{20,24},{24,20},{28,0},{1,29},{... | collective-permute-start | bytes 786440 | tf_op jit(solution)/shard_map/ppermute | solution.py:501
  43.9 3.0 %local_gram.1.refs_2_ = f32[2,32,2048]{2,1,0:T(8,128)S(1)} custom-call(s32[640]{0:T(1024)S(1)} %plan.1.plan_ref.refs_0_, bf16[160,128,256]{2,1,0:T(8,128)(2,1)S(1)} %prep.1.tiles_ref.refs_1_, f32[2,32,2048]{2,1,0:T(8,128)S(1)} %get-tuple-element.69.y_ref, f32[2,32,2048]{2,1,0:T(8,128)S(1)} %get-tuple-element.64.y_ref.refs_0_), custom_call_target="tpu_custom_call" | custom-call | flops 671088640 | bytes 1572864 | tf_op jit(solution)/shard_map/local_gram/pallas_call | solution.py:42
  47.3 4.3 %collective-permute-done.9.refs_4_ = f32[2,32,1024]{2,1,0:T(8,128)S(1)} collective-permute-done((f32[2,32,1024]{2,1,0:T(8,128)S(1)}, f32[2,32,1024]{2,1,0:T(8,128)S(1)}, u32[]{:S(2)}, u32[]{:S(2)}) %collective-permute-start.9) | collective-permute-done | bytes 262176 | tf_op jit(solution)/shard_map/ppermute | solution.py:500
  51.6 2.5 %finish_gram.1 = (f32[2,32,2048]{2,1,0:T(8,128)S(1)}, f32[2,32,1024]{2,1,0:T(8,128)S(1)}, f32[2,32,1024]{2,1,0:T(8,128)S(1)}, f32[1,32,2048]{2,1,0:T(8,128)S(1)}...) custom-call(s32[640]{0:T(1024)S(1)} %plan.1.plan_ref.refs_0_, bf16[160,128,256]{2,1,0:T(8,128)(2,1)S(1)} %prep.1.tiles_ref.refs_1_, ...), custom_call_target="tpu_custom_call" | custom-call | flops 268435456 | bytes 3145728 | tf_op jit(solution)/shard_map/finish_gram/pallas_call | solution.py:42
  57.0 3.2 %collective-permute-start.17 = (f32[1,32,2048]{2,1,0:T(8,128)S(1)}, f32[1,32,2048]{2,1,0:T(8,128)S(1)}, u32[]{:S(2)}, u32[]{:S(2)}) collective-permute-start(f32[1,32,2048]{2,1,0:T(8,128)S(1)} %get-tuple-element.82), channel_id=1, source_target_pairs={{0,28},{4,8},{8,4},{12,16},{16,12},{20,24},{24,20},{28,0},{1,29},{... | collective-permute-start | bytes 786440 | tf_op jit(solution)/shard_map/ppermute | solution.py:501
  60.2 3.0 %local_first.3.refs_2_ = f32[2,32,2048]{2,1,0:T(8,128)S(1)} custom-call(s32[640]{0:T(1024)S(1)} %plan.1.plan_ref.refs_0_, bf16[160,128,256]{2,1,0:T(8,128)(2,1)S(1)} %prep.1.tiles_ref.refs_1_, f32[2,32,2048]{2,1,0:T(8,128)S(1)} %get-tuple-element.74.y_ref.refs_0_), custom_call_target="tpu_custom_call" | custom-call | flops 671088640 | bytes 1572864 | tf_op jit(solution)/shard_map/local_first/pallas_call | solution.py:42
  65.2 3.7 %collective-permute-done.13 = f32[32,32]{1,0:T(8,128)S(1)} collective-permute-done((f32[32,32]{1,0:T(8,128)S(1)}, f32[32,32]{1,0:T(8,128)S(1)}, u32[]{:S(2)}, u32[]{:S(2)}) %collective-permute-start.13) | collective-permute-done | bytes 4128 | tf_op jit(solution)/shard_map/ppermute | solution.py:479
  69.0 2.1 %finish_first.3 = (f32[2,32,2048]{2,1,0:T(8,128)S(1)}, f32[2,32,1024]{2,1,0:T(8,128)S(1)}, f32[2,32,1024]{2,1,0:T(8,128)S(1)}, f32[1,32,2048]{2,1,0:T(8,128)S(1)}, f32[1,32,2048]{2,1,0:T(8,128)S(1)}) custom-call(s32[640]{0:T(1024)S(1)} %plan.1.plan_ref.refs_0_, bf16[160,128,256]{2,1,0:T(8,128)(2,1)S(1)} %prep.1.tiles_ref.refs_1_, ...), custom_call_target="tpu_custom_call" | custom-call | flops 268435456 | bytes 3145728 | tf_op jit(solution)/shard_map/finish_first/pallas_call | solution.py:42
  72.8 2.9 %collective-permute-start.22 = (f32[1,32,2048]{2,1,0:T(8,128)S(1)}, f32[1,32,2048]{2,1,0:T(8,128)S(1)}, u32[]{:S(2)}, u32[]{:S(2)}) collective-permute-start(f32[1,32,2048]{2,1,0:T(8,128)S(1)} %get-tuple-element.91), channel_id=1, source_target_pairs={{0,28},{4,8},{8,4},{12,16},{16,12},{20,24},{24,20},{28,0},{1,29},{... | collective-permute-start | bytes 786440 | tf_op jit(solution)/shard_map/ppermute | solution.py:501
  75.7 3.0 %local_step.4.refs_2_ = f32[2,32,2048]{2,1,0:T(8,128)S(1)} custom-call(s32[640]{0:T(1024)S(1)} %plan.1.plan_ref.refs_0_, bf16[160,128,256]{2,1,0:T(8,128)(2,1)S(1)} %prep.1.tiles_ref.refs_1_, f32[2,32,2048]{2,1,0:T(8,128)S(1)} %get-tuple-element.83.y_ref.refs_0_, f32[2,32,2048]{2,1,0:T(8,128)S(1)} %get-tuple-element.74.y_ref.refs_0_), custom_call_target="tpu_custom_call" | custom-call | flops 671088640 | bytes 1572864 | tf_op jit(solution)/shard_map/local_step/pallas_call | solution.py:42
  79.8 5.9 %collective-permute-done.18 = f32[32,32]{1,0:T(8,128)S(1)} collective-permute-done((f32[32,32]{1,0:T(8,128)S(1)}, f32[32,32]{1,0:T(8,128)S(1)}, u32[]{:S(2)}, u32[]{:S(2)}) %collective-permute-start.18) | collective-permute-done | bytes 4128 | tf_op jit(solution)/shard_map/ppermute | solution.py:479
  89.1 3.6 %collective-permute-start.27 = (f32[1,32,2048]{2,1,0:T(8,128)S(1)}, f32[1,32,2048]{2,1,0:T(8,128)S(1)}, u32[]{:S(2)}, u32[]{:S(2)}) collective-permute-start(f32[1,32,2048]{2,1,0:T(8,128)S(1)} %get-tuple-element.100), channel_id=1, source_target_pairs={{0,28},{4,8},{8,4},{12,16},{16,12},{20,24},{24,20},{28,0},{1,29},{... | collective-permute-start | bytes 786440 | tf_op jit(solution)/shard_map/ppermute | solution.py:501
  92.6 3.0 %local_step.5.refs_2_ = f32[2,32,2048]{2,1,0:T(8,128)S(1)} custom-call(s32[640]{0:T(1024)S(1)} %plan.1.plan_ref.refs_0_, bf16[160,128,256]{2,1,0:T(8,128)(2,1)S(1)} %prep.1.tiles_ref.refs_1_, f32[2,32,2048]{2,1,0:T(8,128)S(1)} %get-tuple-element.92.y_ref, f32[2,32,2048]{2,1,0:T(8,128)S(1)} %get-tuple-element.83.y_ref.refs_0_), custom_call_target="tpu_custom_call" | custom-call | flops 671088640 | bytes 1572864 | tf_op jit(solution)/shard_map/local_step/pallas_call | solution.py:42
  96.2 4.2 %collective-permute-done.23 = f32[32,32]{1,0:T(8,128)S(1)} collective-permute-done((f32[32,32]{1,0:T(8,128)S(1)}, f32[32,32]{1,0:T(8,128)S(1)}, u32[]{:S(2)}, u32[]{:S(2)}) %collective-permute-start.23) | collective-permute-done | bytes 4128 | tf_op jit(solution)/shard_map/ppermute | solution.py:479
  101.0 2.2 %finish_step.5 = (f32[2,32,2048]{2,1,0:T(8,128)S(1)}, f32[2,32,1024]{2,1,0:T(8,128)S(1)}, f32[2,32,1024]{2,1,0:T(8,128)S(1)}, f32[1,32,2048]{2,1,0:T(8,128)S(1)}, f32[1,32,2048]{2,1,0:T(8,128)S(1)}) custom-call(s32[640]{0:T(1024)S(1)} %plan.1.plan_ref.refs_0_, bf16[160,128,256]{2,1,0:T(8,128)(2,1)S(1)} %prep.1.tiles_ref.refs_1_, ...), custom_call_target="tpu_custom_call" | custom-call | flops 268435456 | bytes 3145728 | tf_op jit(solution)/shard_map/finish_step/pallas_call | solution.py:42
  104.2 2.1 %collective-permute-start.30 = (f32[2,32,1024]{2,1,0:T(8,128)S(1)}, f32[2,32,1024]{2,1,0:T(8,128)S(1)}, u32[]{:S(2)}, u32[]{:S(2)}) collective-permute-start(f32[2,32,1024]{2,1,0:T(8,128)S(1)} %get-tuple-element.107), channel_id=1, source_target_pairs={{0,3},{1,2},{2,1},{3,0},{4,7},{5,6},{6,5},{7,4},{8,11},{9,10},{10,... | collective-permute-start | bytes 786440 | tf_op jit(solution)/shard_map/ppermute | solution.py:500
  106.3 2.5 %collective-permute-start.32 = (f32[1,32,2048]{2,1,0:T(8,128)S(1)}, f32[1,32,2048]{2,1,0:T(8,128)S(1)}, u32[]{:S(2)}, u32[]{:S(2)}) collective-permute-start(f32[1,32,2048]{2,1,0:T(8,128)S(1)} %get-tuple-element.109), channel_id=1, source_target_pairs={{0,28},{4,8},{8,4},{12,16},{16,12},{20,24},{24,20},{28,0},{1,29},{... | collective-permute-start | bytes 786440 | tf_op jit(solution)/shard_map/ppermute | solution.py:501
  108.8 3.0 %local_image.1.refs_2_ = f32[2,32,2048]{2,1,0:T(8,128)S(1)} custom-call(s32[640]{0:T(1024)S(1)} %plan.1.plan_ref.refs_0_, bf16[160,128,256]{2,1,0:T(8,128)(2,1)S(1)} %prep.1.tiles_ref.refs_1_, f32[2,32,2048]{2,1,0:T(8,128)S(1)} %get-tuple-element.101.y_ref.refs_7_), custom_call_target="tpu_custom_call" | custom-call | flops 671088640 | bytes 1572864 | tf_op jit(solution)/shard_map/local_image/pallas_call | solution.py:42
  115.7 2.6 %factor.1.refs_8_.matrix_ref = f32[32,32]{1,0:T(8,128)S(1)} custom-call(f32[32,32]{1,0:T(8,128)S(1)} %add.49.gram_ref), custom_call_target="tpu_custom_call" | custom-call | flops 40960000 | bytes 8192 | tf_op jit(solution)/shard_map/factor/pallas_call | solution.py:42
  118.3 2.9 %finish_image.1 = (f32[2,32,2048]{2,1,0:T(8,128)S(1)}, f32[64,32]{1,0:T(8,128)S(1)}) custom-call(s32[640]{0:T(1024)S(1)} %plan.1.plan_ref.refs_0_, bf16[160,128,256]{2,1,0:T(8,128)(2,1)S(1)} %prep.1.tiles_ref.refs_1_, f32[2,32,2048]{2,1,0:T(8,128)S(1)} %local_image.1.refs_2_, f32[2,32,1024]{2,1,0:T(8,128)S(1)} %collective-permute-done.29.refs_3_, ...), custom_call_target="tpu_custom_call" | custom-call | flops 268435456 | bytes 3145728 | tf_op jit(solution)/shard_map/finish_image/pallas_call | solution.py:42
  123.7 2.3 %collective-permute-start.35 = (f32[64,32]{1,0:T(8,128)S(1)}, f32[64,32]{1,0:T(8,128)S(1)}, u32[]{:S(2)}, u32[]{:S(2)}) collective-permute-start(f32[64,32]{1,0:T(8,128)S(1)} %add.50), channel_id=1, source_target_pairs={{0,16},{4,20},{8,24},{12,28},{16,0},{20,4},{24,8},{28,12},{1,17},{... | collective-permute-start | bytes 24584 | tf_op jit(solution)/shard_map/ppermute | solution.py:479
  131.4 2.9 %collective-permute-start.37 = (f32[64,32]{1,0:T(8,128)S(1)}, f32[64,32]{1,0:T(8,128)S(1)}, u32[]{:S(2)}, u32[]{:S(2)}) collective-permute-start(f32[64,32]{1,0:T(8,128)S(1)} %add_add_fusion.1), channel_id=1, source_target_pairs={{0,1},{1,0},{2,3},{3,2},{4,5},{5,4},{6,7},{7,6},{8,9},{9,8},{10,11... | collective-permute-start | bytes 24584 | tf_op jit(solution)/shard_map/ppermute | solution.py:479
  136.6 3.7 %close.1 = (f32[2,32,2048]{2,1,0:T(8,128)}, f32[32,32]{1,0:T(8,128)}) custom-call(f32[64,32]{1,0:T(8,128)S(1)} %add_add_fusion.sums_ref, f32[2,32,2048]{2,1,0:T(8,128)S(1)} %get-tuple-element.112.y_ref), custom_call_target="tpu_custom_call" | custom-call | flops 8388608 | bytes 1048576 | tf_op jit(solution)/shard_map/close/pallas_call | solution.py:42
  (81 shorter events, 37.7 us)
Async XLA Ops:
  2.4 19.7 %collective-permute-start = (f32[2,32,1024]{2,1,0:T(8,128)S(1)}, f32[2,32,1024]{2,1,0:T(8,128)S(1)}, u32[]{:S(2)}, u32[]{:S(2)}) collective-permute-start(f32[2,32,1024]{2,1,0:T(8,128)S(1)} %get-tuple-element.60), channel_id=1, source_target_pairs={{0,1},{1,0},{2,3},{3,2},{4,5},{5,4},{6,7},{7,6},{8,9},{9,8},{10,11... | collective-permute-start | bytes 786440 | tf_op jit(solution)/shard_map/ppermute | solution.py:499
  5.5 16.6 %collective-permute-start.1 = (f32[2,32,1024]{2,1,0:T(8,128)S(1)}, f32[2,32,1024]{2,1,0:T(8,128)S(1)}, u32[]{:S(2)}, u32[]{:S(2)}) collective-permute-start(f32[2,32,1024]{2,1,0:T(8,128)S(1)} %get-tuple-element.61), channel_id=1, source_target_pairs={{0,3},{1,2},{2,1},{3,0},{4,7},{5,6},{6,5},{7,4},{8,11},{9,10},{10,... | collective-permute-start | bytes 786440 | tf_op jit(solution)/shard_map/ppermute | solution.py:500
  8.0 14.1 %collective-permute-start.2 = (f32[1,32,2048]{2,1,0:T(8,128)S(1)}, f32[1,32,2048]{2,1,0:T(8,128)S(1)}, u32[]{:S(2)}, u32[]{:S(2)}) collective-permute-start(f32[1,32,2048]{2,1,0:T(8,128)S(1)} %get-tuple-element.62), channel_id=1, source_target_pairs={{0,4},{4,0},{8,12},{12,8},{16,20},{20,16},{24,28},{28,24},{1,5},{5... | collective-permute-start | bytes 786440 | tf_op jit(solution)/shard_map/ppermute | solution.py:502
  8.0 14.1 %collective-permute-start.3 = (f32[1,32,2048]{2,1,0:T(8,128)S(1)}, f32[1,32,2048]{2,1,0:T(8,128)S(1)}, u32[]{:S(2)}, u32[]{:S(2)}) collective-permute-start(f32[1,32,2048]{2,1,0:T(8,128)S(1)} %get-tuple-element.63), channel_id=1, source_target_pairs={{0,28},{4,8},{8,4},{12,16},{16,12},{20,24},{24,20},{28,0},{1,29},{... | collective-permute-start | bytes 786440 | tf_op jit(solution)/shard_map/ppermute | solution.py:501
  24.2 12.6 %collective-permute-start.4 = (f32[2,32,1024]{2,1,0:T(8,128)S(1)}, f32[2,32,1024]{2,1,0:T(8,128)S(1)}, u32[]{:S(2)}, u32[]{:S(2)}) collective-permute-start(f32[2,32,1024]{2,1,0:T(8,128)S(1)} %get-tuple-element.65), channel_id=1, source_target_pairs={{0,1},{1,0},{2,3},{3,2},{4,5},{5,4},{6,7},{7,6},{8,9},{9,8},{10,11... | collective-permute-start | bytes 786440 | tf_op jit(solution)/shard_map/ppermute | solution.py:499
  24.9 11.9 %collective-permute-start.5 = (f32[2,32,1024]{2,1,0:T(8,128)S(1)}, f32[2,32,1024]{2,1,0:T(8,128)S(1)}, u32[]{:S(2)}, u32[]{:S(2)}) collective-permute-start(f32[2,32,1024]{2,1,0:T(8,128)S(1)} %get-tuple-element.66), channel_id=1, source_target_pairs={{0,3},{1,2},{2,1},{3,0},{4,7},{5,6},{6,5},{7,4},{8,11},{9,10},{10,... | collective-permute-start | bytes 786440 | tf_op jit(solution)/shard_map/ppermute | solution.py:500
  25.5 11.3 %collective-permute-start.6 = (f32[1,32,2048]{2,1,0:T(8,128)S(1)}, f32[1,32,2048]{2,1,0:T(8,128)S(1)}, u32[]{:S(2)}, u32[]{:S(2)}) collective-permute-start(f32[1,32,2048]{2,1,0:T(8,128)S(1)} %get-tuple-element.67), channel_id=1, source_target_pairs={{0,4},{4,0},{8,12},{12,8},{16,20},{20,16},{24,28},{28,24},{1,5},{5... | collective-permute-start | bytes 786440 | tf_op jit(solution)/shard_map/ppermute | solution.py:502
  25.5 11.3 %collective-permute-start.7 = (f32[1,32,2048]{2,1,0:T(8,128)S(1)}, f32[1,32,2048]{2,1,0:T(8,128)S(1)}, u32[]{:S(2)}, u32[]{:S(2)}) collective-permute-start(f32[1,32,2048]{2,1,0:T(8,128)S(1)} %get-tuple-element.68), channel_id=1, source_target_pairs={{0,28},{4,8},{8,4},{12,16},{16,12},{20,24},{24,20},{28,0},{1,29},{... | collective-permute-start | bytes 786440 | tf_op jit(solution)/shard_map/ppermute | solution.py:501
  38.9 8.4 %collective-permute-start.8 = (f32[2,32,1024]{2,1,0:T(8,128)S(1)}, f32[2,32,1024]{2,1,0:T(8,128)S(1)}, u32[]{:S(2)}, u32[]{:S(2)}) collective-permute-start(f32[2,32,1024]{2,1,0:T(8,128)S(1)} %get-tuple-element.70), channel_id=1, source_target_pairs={{0,1},{1,0},{2,3},{3,2},{4,5},{5,4},{6,7},{7,6},{8,9},{9,8},{10,11... | collective-permute-start | bytes 786440 | tf_op jit(solution)/shard_map/ppermute | solution.py:499
  40.7 10.9 %collective-permute-start.9 = (f32[2,32,1024]{2,1,0:T(8,128)S(1)}, f32[2,32,1024]{2,1,0:T(8,128)S(1)}, u32[]{:S(2)}, u32[]{:S(2)}) collective-permute-start(f32[2,32,1024]{2,1,0:T(8,128)S(1)} %get-tuple-element.71), channel_id=1, source_target_pairs={{0,3},{1,2},{2,1},{3,0},{4,7},{5,6},{6,5},{7,4},{8,11},{9,10},{10,... | collective-permute-start | bytes 786440 | tf_op jit(solution)/shard_map/ppermute | solution.py:500
  41.3 10.4 %collective-permute-start.10 = (f32[1,32,2048]{2,1,0:T(8,128)S(1)}, f32[1,32,2048]{2,1,0:T(8,128)S(1)}, u32[]{:S(2)}, u32[]{:S(2)}) collective-permute-start(f32[1,32,2048]{2,1,0:T(8,128)S(1)} %get-tuple-element.72), channel_id=1, source_target_pairs={{0,4},{4,0},{8,12},{12,8},{16,20},{20,16},{24,28},{28,24},{1,5},{5... | collective-permute-start | bytes 786440 | tf_op jit(solution)/shard_map/ppermute | solution.py:502
  41.3 10.4 %collective-permute-start.11 = (f32[1,32,2048]{2,1,0:T(8,128)S(1)}, f32[1,32,2048]{2,1,0:T(8,128)S(1)}, u32[]{:S(2)}, u32[]{:S(2)}) collective-permute-start(f32[1,32,2048]{2,1,0:T(8,128)S(1)} %get-tuple-element.73), channel_id=1, source_target_pairs={{0,28},{4,8},{8,4},{12,16},{16,12},{20,24},{24,20},{28,0},{1,29},{... | collective-permute-start | bytes 786440 | tf_op jit(solution)/shard_map/ppermute | solution.py:501
  54.1 14.9 %collective-permute-start.14 = (f32[2,32,1024]{2,1,0:T(8,128)S(1)}, f32[2,32,1024]{2,1,0:T(8,128)S(1)}, u32[]{:S(2)}, u32[]{:S(2)}) collective-permute-start(f32[2,32,1024]{2,1,0:T(8,128)S(1)} %get-tuple-element.79), channel_id=1, source_target_pairs={{0,1},{1,0},{2,3},{3,2},{4,5},{5,4},{6,7},{7,6},{8,9},{9,8},{10,11... | collective-permute-start | bytes 786440 | tf_op jit(solution)/shard_map/ppermute | solution.py:499
  55.2 13.7 %collective-permute-start.15 = (f32[2,32,1024]{2,1,0:T(8,128)S(1)}, f32[2,32,1024]{2,1,0:T(8,128)S(1)}, u32[]{:S(2)}, u32[]{:S(2)}) collective-permute-start(f32[2,32,1024]{2,1,0:T(8,128)S(1)} %get-tuple-element.80), channel_id=1, source_target_pairs={{0,3},{1,2},{2,1},{3,0},{4,7},{5,6},{6,5},{7,4},{8,11},{9,10},{10,... | collective-permute-start | bytes 786440 | tf_op jit(solution)/shard_map/ppermute | solution.py:500
  57.0 11.9 %collective-permute-start.16 = (f32[1,32,2048]{2,1,0:T(8,128)S(1)}, f32[1,32,2048]{2,1,0:T(8,128)S(1)}, u32[]{:S(2)}, u32[]{:S(2)}) collective-permute-start(f32[1,32,2048]{2,1,0:T(8,128)S(1)} %get-tuple-element.81), channel_id=1, source_target_pairs={{0,4},{4,0},{8,12},{12,8},{16,20},{20,16},{24,28},{28,24},{1,5},{5... | collective-permute-start | bytes 786440 | tf_op jit(solution)/shard_map/ppermute | solution.py:502
  57.0 11.9 %collective-permute-start.17 = (f32[1,32,2048]{2,1,0:T(8,128)S(1)}, f32[1,32,2048]{2,1,0:T(8,128)S(1)}, u32[]{:S(2)}, u32[]{:S(2)}) collective-permute-start(f32[1,32,2048]{2,1,0:T(8,128)S(1)} %get-tuple-element.82), channel_id=1, source_target_pairs={{0,28},{4,8},{8,4},{12,16},{16,12},{20,24},{24,20},{28,0},{1,29},{... | collective-permute-start | bytes 786440 | tf_op jit(solution)/shard_map/ppermute | solution.py:501
  71.0 14.7 %collective-permute-start.19 = (f32[2,32,1024]{2,1,0:T(8,128)S(1)}, f32[2,32,1024]{2,1,0:T(8,128)S(1)}, u32[]{:S(2)}, u32[]{:S(2)}) collective-permute-start(f32[2,32,1024]{2,1,0:T(8,128)S(1)} %get-tuple-element.88), channel_id=1, source_target_pairs={{0,1},{1,0},{2,3},{3,2},{4,5},{5,4},{6,7},{7,6},{8,9},{9,8},{10,11... | collective-permute-start | bytes 786440 | tf_op jit(solution)/shard_map/ppermute | solution.py:499
  71.1 14.6 %collective-permute-start.20 = (f32[2,32,1024]{2,1,0:T(8,128)S(1)}, f32[2,32,1024]{2,1,0:T(8,128)S(1)}, u32[]{:S(2)}, u32[]{:S(2)}) collective-permute-start(f32[2,32,1024]{2,1,0:T(8,128)S(1)} %get-tuple-element.89), channel_id=1, source_target_pairs={{0,3},{1,2},{2,1},{3,0},{4,7},{5,6},{6,5},{7,4},{8,11},{9,10},{10,... | collective-permute-start | bytes 786440 | tf_op jit(solution)/shard_map/ppermute | solution.py:500
  72.8 12.9 %collective-permute-start.21 = (f32[1,32,2048]{2,1,0:T(8,128)S(1)}, f32[1,32,2048]{2,1,0:T(8,128)S(1)}, u32[]{:S(2)}, u32[]{:S(2)}) collective-permute-start(f32[1,32,2048]{2,1,0:T(8,128)S(1)} %get-tuple-element.90), channel_id=1, source_target_pairs={{0,4},{4,0},{8,12},{12,8},{16,20},{20,16},{24,28},{28,24},{1,5},{5... | collective-permute-start | bytes 786440 | tf_op jit(solution)/shard_map/ppermute | solution.py:502
  72.8 12.9 %collective-permute-start.22 = (f32[1,32,2048]{2,1,0:T(8,128)S(1)}, f32[1,32,2048]{2,1,0:T(8,128)S(1)}, u32[]{:S(2)}, u32[]{:S(2)}) collective-permute-start(f32[1,32,2048]{2,1,0:T(8,128)S(1)} %get-tuple-element.91), channel_id=1, source_target_pairs={{0,28},{4,8},{8,4},{12,16},{16,12},{20,24},{24,20},{28,0},{1,29},{... | collective-permute-start | bytes 786440 | tf_op jit(solution)/shard_map/ppermute | solution.py:501
  78.8 7.0 %collective-permute-start.18 = (f32[32,32]{1,0:T(8,128)S(1)}, f32[32,32]{1,0:T(8,128)S(1)}, u32[]{:S(2)}, u32[]{:S(2)}) collective-permute-start(f32[32,32]{1,0:T(8,128)S(1)} %add.46), channel_id=1, source_target_pairs={{0,2},{1,3},{2,0},{3,1},{4,6},{5,7},{6,4},{7,5},{8,10},{9,11},{10,... | collective-permute-start | bytes 12296 | tf_op jit(solution)/shard_map/ppermute | solution.py:479
  87.8 12.6 %collective-permute-start.24 = (f32[2,32,1024]{2,1,0:T(8,128)S(1)}, f32[2,32,1024]{2,1,0:T(8,128)S(1)}, u32[]{:S(2)}, u32[]{:S(2)}) collective-permute-start(f32[2,32,1024]{2,1,0:T(8,128)S(1)} %get-tuple-element.97), channel_id=1, source_target_pairs={{0,1},{1,0},{2,3},{3,2},{4,5},{5,4},{6,7},{7,6},{8,9},{9,8},{10,11... | collective-permute-start | bytes 786440 | tf_op jit(solution)/shard_map/ppermute | solution.py:499
  88.2 12.7 %collective-permute-start.25 = (f32[2,32,1024]{2,1,0:T(8,128)S(1)}, f32[2,32,1024]{2,1,0:T(8,128)S(1)}, u32[]{:S(2)}, u32[]{:S(2)}) collective-permute-start(f32[2,32,1024]{2,1,0:T(8,128)S(1)} %get-tuple-element.98), channel_id=1, source_target_pairs={{0,3},{1,2},{2,1},{3,0},{4,7},{5,6},{6,5},{7,4},{8,11},{9,10},{10,... | collective-permute-start | bytes 786440 | tf_op jit(solution)/shard_map/ppermute | solution.py:500
  89.1 11.9 %collective-permute-start.26 = (f32[1,32,2048]{2,1,0:T(8,128)S(1)}, f32[1,32,2048]{2,1,0:T(8,128)S(1)}, u32[]{:S(2)}, u32[]{:S(2)}) collective-permute-start(f32[1,32,2048]{2,1,0:T(8,128)S(1)} %get-tuple-element.99), channel_id=1, source_target_pairs={{0,4},{4,0},{8,12},{12,8},{16,20},{20,16},{24,28},{28,24},{1,5},{5... | collective-permute-start | bytes 786440 | tf_op jit(solution)/shard_map/ppermute | solution.py:502
  89.1 11.9 %collective-permute-start.27 = (f32[1,32,2048]{2,1,0:T(8,128)S(1)}, f32[1,32,2048]{2,1,0:T(8,128)S(1)}, u32[]{:S(2)}, u32[]{:S(2)}) collective-permute-start(f32[1,32,2048]{2,1,0:T(8,128)S(1)} %get-tuple-element.100), channel_id=1, source_target_pairs={{0,28},{4,8},{8,4},{12,16},{16,12},{20,24},{24,20},{28,0},{1,29},{... | collective-permute-start | bytes 786440 | tf_op jit(solution)/shard_map/ppermute | solution.py:501
  103.2 15.1 %collective-permute-start.29 = (f32[2,32,1024]{2,1,0:T(8,128)S(1)}, f32[2,32,1024]{2,1,0:T(8,128)S(1)}, u32[]{:S(2)}, u32[]{:S(2)}) collective-permute-start(f32[2,32,1024]{2,1,0:T(8,128)S(1)} %get-tuple-element.106), channel_id=1, source_target_pairs={{0,1},{1,0},{2,3},{3,2},{4,5},{5,4},{6,7},{7,6},{8,9},{9,8},{10,11... | collective-permute-start | bytes 786440 | tf_op jit(solution)/shard_map/ppermute | solution.py:499
  104.2 14.1 %collective-permute-start.30 = (f32[2,32,1024]{2,1,0:T(8,128)S(1)}, f32[2,32,1024]{2,1,0:T(8,128)S(1)}, u32[]{:S(2)}, u32[]{:S(2)}) collective-permute-start(f32[2,32,1024]{2,1,0:T(8,128)S(1)} %get-tuple-element.107), channel_id=1, source_target_pairs={{0,3},{1,2},{2,1},{3,0},{4,7},{5,6},{6,5},{7,4},{8,11},{9,10},{10,... | collective-permute-start | bytes 786440 | tf_op jit(solution)/shard_map/ppermute | solution.py:500
  106.3 11.9 %collective-permute-start.31 = (f32[1,32,2048]{2,1,0:T(8,128)S(1)}, f32[1,32,2048]{2,1,0:T(8,128)S(1)}, u32[]{:S(2)}, u32[]{:S(2)}) collective-permute-start(f32[1,32,2048]{2,1,0:T(8,128)S(1)} %get-tuple-element.108), channel_id=1, source_target_pairs={{0,4},{4,0},{8,12},{12,8},{16,20},{20,16},{24,28},{28,24},{1,5},{5... | collective-permute-start | bytes 786440 | tf_op jit(solution)/shard_map/ppermute | solution.py:502
  106.3 12.0 %collective-permute-start.32 = (f32[1,32,2048]{2,1,0:T(8,128)S(1)}, f32[1,32,2048]{2,1,0:T(8,128)S(1)}, u32[]{:S(2)}, u32[]{:S(2)}) collective-permute-start(f32[1,32,2048]{2,1,0:T(8,128)S(1)} %get-tuple-element.109), channel_id=1, source_target_pairs={{0,28},{4,8},{8,4},{12,16},{16,12},{20,24},{24,20},{28,0},{1,29},{... | collective-permute-start | bytes 786440 | tf_op jit(solution)/shard_map/ppermute | solution.py:501
  129.9 5.8 %collective-permute-start.39 = (f32[64,32]{1,0:T(8,128)S(1)}, f32[64,32]{1,0:T(8,128)S(1)}, u32[]{:S(2)}, u32[]{:S(2)}) collective-permute-start(f32[64,32]{1,0:T(8,128)S(1)} %add_add_fusion.1), channel_id=1, source_target_pairs={{0,3},{1,2},{2,1},{3,0},{4,7},{5,6},{6,5},{7,4},{8,11},{9,10},{10,... | collective-permute-start | bytes 24584 | tf_op jit(solution)/shard_map/ppermute | solution.py:479
  131.4 5.0 %collective-permute-start.38 = (f32[64,32]{1,0:T(8,128)S(1)}, f32[64,32]{1,0:T(8,128)S(1)}, u32[]{:S(2)}, u32[]{:S(2)}) collective-permute-start(f32[64,32]{1,0:T(8,128)S(1)} %add_add_fusion.1), channel_id=1, source_target_pairs={{0,2},{1,3},{2,0},{3,1},{4,6},{5,7},{6,4},{7,5},{8,10},{9,11},{10,... | collective-permute-start | bytes 24584 | tf_op jit(solution)/shard_map/ppermute | solution.py:479
  131.4 5.2 %collective-permute-start.37 = (f32[64,32]{1,0:T(8,128)S(1)}, f32[64,32]{1,0:T(8,128)S(1)}, u32[]{:S(2)}, u32[]{:S(2)}) collective-permute-start(f32[64,32]{1,0:T(8,128)S(1)} %add_add_fusion.1), channel_id=1, source_target_pairs={{0,1},{1,0},{2,3},{3,2},{4,5},{5,4},{6,7},{7,6},{8,9},{9,8},{10,11... | collective-permute-start | bytes 24584 | tf_op jit(solution)/shard_map/ppermute | solution.py:479
  (10 other events, 30.2 us)

commit v5 on v4

--- a/solution.py
+++ b/solution.py
@@ -293,6 +293,18 @@
     return (p[:width, :width] + p[width:, width:]) + (p[:width, width:] + p[width:, :width])
 
 
+def folded(*matrices):
+    width = matrices[0].shape[0]
+    rows = width * width * len(matrices) // TILE
+    flat = jnp.concatenate(matrices, axis=0)
+    return jnp.concatenate([flat[i : i + rows] for i in range(0, flat.shape[0], rows)], axis=1)
+
+
+def unfolded(block, width):
+    flat = jnp.concatenate([block[:, i : i + width] for i in range(0, TILE, width)], axis=0)
+    return [flat[i : i + width] for i in range(0, flat.shape[0], width)]
+
+
 def finish_kernel(mode, scale, *refs):
     refs = list(refs)
     take = lambda n: [refs.pop(0) for _ in range(n)]
@@ -344,7 +356,7 @@
     if mode != "image":
         edges([plan_ref[at.flags], plan_ref[at.flags + 1]], new_ref, *edge_refs)
     if mode == "gram":
-        gram_ref[...] = sum(inner(new_ref[s], new_ref[s]) for s in range(slices))
+        gram_ref[...] = folded(sum(inner(new_ref[s], new_ref[s]) for s in range(slices)))
     if mode == "image":
         matrix = matrix_ref[...]
         first, second = 0.0, 0.0
@@ -353,8 +365,7 @@
             mixed_ref[s] = mixed
             first = first + inner(mixed, mixed)
             second = second + inner(mixed, mix(matrix, new_ref[s]))
-        gram_ref[:width] = first
-        gram_ref[width:] = second
+        gram_ref[...] = folded(first, second)
 
 
 def finish(mode, scale, table, tiles, part, y, halo, matrix=None):
@@ -363,11 +374,11 @@
     ins = [table] + [near(v) for v in (tiles, part, *halo)]
     if mode == "image":
         ins += [near(y), near(matrix)]
-        outs = [(y.shape, F32), ((2 * width, width), F32)]
+        outs = [(y.shape, F32), ((2 * width * width // TILE, TILE), F32)]
     else:
         outs = edge_shapes(y.shape)
     if mode == "gram":
-        outs = outs + [((width, width), F32)]
+        outs = outs + [((width * width // TILE, TILE), F32)]
     scratch = [VM((slices * 2 * HB + 1, 2 * width, TILE), BF16)]
     if mode == "image":
         scratch.append(VM(y.shape, F32))
@@ -400,14 +411,15 @@
 
 
 def factor_kernel(count, gram_ref, out_ref):
-    out_ref[...] = inverse_factor(gram_ref[...] * (1.0 / count))
-
-
-def factor(gram, count):
+    (gram,) = unfolded(gram_ref[...] * (1.0 / count), out_ref.shape[0])
+    out_ref[...] = inverse_factor(gram)
+
+
+def factor(gram, width, count):
     return call(
         functools.partial(factor_kernel, float(count)),
         [near(gram)],
-        [(gram.shape, F32)],
+        [((width, width), F32)],
         specs=[WHOLE],
         flops=40000 * gram.size,
         moved=8 * gram.size,
@@ -435,9 +447,8 @@
 
 def close_kernel(count, sums_ref, y_ref, basis_ref, ritz_ref):
     high = lax.Precision.HIGHEST
-    width = sums_ref.shape[1]
-    matrix = inverse_factor(sums_ref[:width] * (1.0 / count))
-    projected = sums_ref[width:] * (1.0 / count)
+    gram, projected = unfolded(sums_ref[...] * (1.0 / count), ritz_ref.shape[0])
+    matrix = inverse_factor(gram)
     for s in range(y_ref.shape[0]):
         basis_ref[s] = mix(matrix, y_ref[s])
     half = lax.dot_general(matrix, projected, NN, precision=high, preferred_element_type=F32)
@@ -445,7 +456,7 @@
 
 
 def close(sums, y, count):
-    width = sums.shape[1]
+    width = y.shape[1]
     return call(
         functools.partial(close_kernel, float(count)),
         [near(sums), near(y)],
@@ -549,7 +560,7 @@
     (y2, *edge), gram = apply("step", 2.0 / RADIUS, y1, edge, filtered, (gram, stage(1)))
     (y3, *edge), gram = apply("step", 2.0 / RADIUS, y2, edge, y1, (gram, stage(2)))
     (second, sums), matrix = apply(
-        "image", 1.0, y3, edge, None, (gram, lambda gram: factor(stage(3)(gram), count_all))
+        "image", 1.0, y3, edge, None, (gram, lambda gram: factor(stage(3)(gram), width, count_all))
     )
     first_basis = basis(matrix, filtered)
     sums = add_over(sums, stages_of("tm") + stages_of("space"))

time: 141 us -> 139 us (0.986)
  Pallas kernels: 52.9 us -> 51.1 us
    ppermute x7, starting transfers between devices: 19.5 us -> 15.5 us  [exchange(): far_slice = lax.ppermute(far_slice, 'tm', outer_pairs('tm'))]
    ppermute x7, starting transfers between devices: 10.1 us -> 13.1 us  [exchange(): outer = lax.ppermute(outer, 'space', outer_pairs('space'))]
    ppermute x12, waiting for transfers between devices: 22.9 us -> 20.6 us  [add_over(): lax.ppermute(value, axis, [(i, i ^ k) for i in range(count)])]
    pallas_call x18, Pallas kernels: 45.1 us -> 43.3 us  [call(): pl.pallas_call(kernel, out_shape=out_shape, in_specs=specs, out_specs=[WH...]
    ppermute x7, waiting for transfers between devices: 6.5 us -> 8.23 us  [exchange(): inner = lax.ppermute(inner, 'space', inner_pairs('space'))]
  transfers between devices with their start and end apart: 40 -> 40, of which waited for: 16 -> 15; matrix products, arithmetic and copies ran while one was open for 0% -> 0% of each run, Pallas kernels for 23% -> 24%
where the time goes in v5:
time: 139 us; the launch traced here: 137 us
  Pallas kernels  51.1 us (37%)
  starting transfers between devices  49.7 us (36%)
  waiting for transfers between devices  33.8 us (24%)
  local copies, waits for them, and re-layouts  1.81 us (1%)
    pallas_call x18, Pallas kernels, call(): pl.pallas_call(kernel, out_shape=out_shape, in_specs=specs, out_specs=[WH...  43.3 us
    ppermute x12, waiting for transfers between devices, add_over(): lax.ppermute(value, axis, [(i, i ^ k) for i in range(count)])  20.6 us
    ppermute x7, starting transfers between devices, exchange(): far_slice = lax.ppermute(far_slice, 'tm', outer_pairs('tm'))  15.5 us
    ppermute x7, starting transfers between devices, exchange(): outer = lax.ppermute(outer, 'space', outer_pairs('space'))  13.1 us
    ppermute x12, starting transfers between devices, add_over(): lax.ppermute(value, axis, [(i, i ^ k) for i in range(count)])  11.6 us
    ppermute x7, starting transfers between devices, exchange(): inner = lax.ppermute(inner, 'space', inner_pairs('space'))  9.54 us
    ppermute x7, waiting for transfers between devices, exchange(): inner = lax.ppermute(inner, 'space', inner_pairs('space'))  8.23 us
    ppermute x7, waiting for transfers between devices, exchange(): outer = lax.ppermute(outer, 'space', outer_pairs('space'))  4.94 us
  transfers between devices with their start and end apart: 40, of which 15 were waited for; matrix products, arithmetic and copies ran while one was open for 0% of the time, Pallas kernels for 24%

profile of v5, /device:TPU:0, one launch (start us, length us, event | category | flops | bytes accessed | tf_op | source)
XLA Modules:
  0.0 137.3 jit_solution(735003859684257449)
XLA Ops:
  2.4 3.1 %collective-permute-start = (f32[2,32,1024]{2,1,0:T(8,128)S(1)}, f32[2,32,1024]{2,1,0:T(8,128)S(1)}, u32[]{:S(2)}, u32[]{:S(2)}) collective-permute-start(f32[2,32,1024]{2,1,0:T(8,128)S(1)} %get-tuple-element.60), channel_id=1, source_target_pairs={{0,1},{1,0},{2,3},{3,2},{4,5},{5,4},{6,7},{7,6},{8,9},{9,8},{10,11... | collective-permute-start | bytes 786440 | tf_op jit(solution)/shard_map/ppermute | solution.py:510
  5.5 2.5 %collective-permute-start.1 = (f32[2,32,1024]{2,1,0:T(8,128)S(1)}, f32[2,32,1024]{2,1,0:T(8,128)S(1)}, u32[]{:S(2)}, u32[]{:S(2)}) collective-permute-start(f32[2,32,1024]{2,1,0:T(8,128)S(1)} %get-tuple-element.61), channel_id=1, source_target_pairs={{0,3},{1,2},{2,1},{3,0},{4,7},{5,6},{6,5},{7,4},{8,11},{9,10},{10,... | collective-permute-start | bytes 786440 | tf_op jit(solution)/shard_map/ppermute | solution.py:511
  8.0 2.6 %collective-permute-start.3 = (f32[1,32,2048]{2,1,0:T(8,128)S(1)}, f32[1,32,2048]{2,1,0:T(8,128)S(1)}, u32[]{:S(2)}, u32[]{:S(2)}) collective-permute-start(f32[1,32,2048]{2,1,0:T(8,128)S(1)} %get-tuple-element.63), channel_id=1, source_target_pairs={{0,28},{4,8},{8,4},{12,16},{16,12},{20,24},{24,20},{28,0},{1,29},{... | collective-permute-start | bytes 786440 | tf_op jit(solution)/shard_map/ppermute | solution.py:512
  11.2 3.0 %plan.1.plan_ref.refs_0_ = s32[640]{0:T(1024)S(1)} custom-call(s32[2,80]{1,0:T(2,128)S(1)} %copy-done.1, s32[5]{0:T(128)S(1)} %stack.31.flags_ref.odd_ref), custom_call_target="tpu_custom_call" | custom-call | tf_op jit(solution)/shard_map/plan/pallas_call | solution.py:158
  14.3 4.8 %prep.1.tiles_ref.refs_1_ = bf16[160,128,256]{2,1,0:T(8,128)(2,1)S(1)} custom-call(f32[160,128,128]{2,1,0:T(8,128)} %bitcast.6), custom_call_target="tpu_custom_call" | custom-call | bytes 10485760 | tf_op jit(solution)/shard_map/prep/pallas_call | solution.py:87
  19.1 3.1 %local_first.2.refs_2_ = f32[2,32,2048]{2,1,0:T(8,128)S(1)} custom-call(s32[640]{0:T(1024)S(1)} %plan.1.plan_ref.refs_0_, bf16[160,128,256]{2,1,0:T(8,128)(2,1)S(1)} %prep.1.tiles_ref.refs_1_, f32[2,32,2048]{2,1,0:T(8,128)S(1)} %get-tuple-element.59.y_ref.refs_0_), custom_call_target="tpu_custom_call" | custom-call | flops 671088640 | bytes 1572864 | tf_op jit(solution)/shard_map/local_first/pallas_call | solution.py:42
  25.7 1.9 %collective-permute-start.7 = (f32[1,32,2048]{2,1,0:T(8,128)S(1)}, f32[1,32,2048]{2,1,0:T(8,128)S(1)}, u32[]{:S(2)}, u32[]{:S(2)}) collective-permute-start(f32[1,32,2048]{2,1,0:T(8,128)S(1)} %get-tuple-element.68), channel_id=1, source_target_pairs={{0,28},{4,8},{8,4},{12,16},{16,12},{20,24},{24,20},{28,0},{1,29},{... | collective-permute-start | bytes 786440 | tf_op jit(solution)/shard_map/ppermute | solution.py:512
  27.7 3.0 %local_step.3.refs_2_ = f32[2,32,2048]{2,1,0:T(8,128)S(1)} custom-call(s32[640]{0:T(1024)S(1)} %plan.1.plan_ref.refs_0_, bf16[160,128,256]{2,1,0:T(8,128)(2,1)S(1)} %prep.1.tiles_ref.refs_1_, f32[2,32,2048]{2,1,0:T(8,128)S(1)} %get-tuple-element.64.y_ref.refs_0_, f32[2,32,2048]{2,1,0:T(8,128)S(1)} %get-tuple-element.59.y_ref.refs_0_), custom_call_target="tpu_custom_call" | custom-call | flops 671088640 | bytes 1572864 | tf_op jit(solution)/shard_map/local_step/pallas_call | solution.py:42
  30.7 6.5 %collective-permute-done.4.refs_3_ = f32[2,32,1024]{2,1,0:T(8,128)S(1)} collective-permute-done((f32[2,32,1024]{2,1,0:T(8,128)S(1)}, f32[2,32,1024]{2,1,0:T(8,128)S(1)}, u32[]{:S(2)}, u32[]{:S(2)}) %collective-permute-start.4) | collective-permute-done | bytes 262176 | tf_op jit(solution)/shard_map/ppermute | solution.py:510
  39.0 1.8 %collective-permute-start.8 = (f32[2,32,1024]{2,1,0:T(8,128)S(1)}, f32[2,32,1024]{2,1,0:T(8,128)S(1)}, u32[]{:S(2)}, u32[]{:S(2)}) collective-permute-start(f32[2,32,1024]{2,1,0:T(8,128)S(1)} %get-tuple-element.70), channel_id=1, source_target_pairs={{0,1},{1,0},{2,3},{3,2},{4,5},{5,4},{6,7},{7,6},{8,9},{9,8},{10,11... | collective-permute-start | bytes 786440 | tf_op jit(solution)/shard_map/ppermute | solution.py:510
  43.5 3.1 %local_gram.1.refs_2_ = f32[2,32,2048]{2,1,0:T(8,128)S(1)} custom-call(s32[640]{0:T(1024)S(1)} %plan.1.plan_ref.refs_0_, bf16[160,128,256]{2,1,0:T(8,128)(2,1)S(1)} %prep.1.tiles_ref.refs_1_, f32[2,32,2048]{2,1,0:T(8,128)S(1)} %get-tuple-element.69.y_ref, f32[2,32,2048]{2,1,0:T(8,128)S(1)} %get-tuple-element.64.y_ref.refs_0_), custom_call_target="tpu_custom_call" | custom-call | flops 671088640 | bytes 1572864 | tf_op jit(solution)/shard_map/local_gram/pallas_call | solution.py:42
  48.3 3.5 %collective-permute-done.9.refs_4_ = f32[2,32,1024]{2,1,0:T(8,128)S(1)} collective-permute-done((f32[2,32,1024]{2,1,0:T(8,128)S(1)}, f32[2,32,1024]{2,1,0:T(8,128)S(1)}, u32[]{:S(2)}, u32[]{:S(2)}) %collective-permute-start.9) | collective-permute-done | bytes 262176 | tf_op jit(solution)/shard_map/ppermute | solution.py:511
  51.8 2.2 %finish_gram.1 = (f32[2,32,2048]{2,1,0:T(8,128)S(1)}, f32[2,32,1024]{2,1,0:T(8,128)S(1)}, f32[2,32,1024]{2,1,0:T(8,128)S(1)}, f32[1,32,2048]{2,1,0:T(8,128)S(1)}...) custom-call(s32[640]{0:T(1024)S(1)} %plan.1.plan_ref.refs_0_, bf16[160,128,256]{2,1,0:T(8,128)(2,1)S(1)} %prep.1.tiles_ref.refs_1_, ...), custom_call_target="tpu_custom_call" | custom-call | flops 268435456 | bytes 3145728 | tf_op jit(solution)/shard_map/finish_gram/pallas_call | solution.py:42
  55.2 2.3 %collective-permute-start.15 = (f32[2,32,1024]{2,1,0:T(8,128)S(1)}, f32[2,32,1024]{2,1,0:T(8,128)S(1)}, u32[]{:S(2)}, u32[]{:S(2)}) collective-permute-start(f32[2,32,1024]{2,1,0:T(8,128)S(1)} %get-tuple-element.80), channel_id=1, source_target_pairs={{0,3},{1,2},{2,1},{3,0},{4,7},{5,6},{6,5},{7,4},{8,11},{9,10},{10,... | collective-permute-start | bytes 786440 | tf_op jit(solution)/shard_map/ppermute | solution.py:511
  57.5 3.1 %collective-permute-start.17 = (f32[1,32,2048]{2,1,0:T(8,128)S(1)}, f32[1,32,2048]{2,1,0:T(8,128)S(1)}, u32[]{:S(2)}, u32[]{:S(2)}) collective-permute-start(f32[1,32,2048]{2,1,0:T(8,128)S(1)} %get-tuple-element.82), channel_id=1, source_target_pairs={{0,28},{4,8},{8,4},{12,16},{16,12},{20,24},{24,20},{28,0},{1,29},{... | collective-permute-start | bytes 786440 | tf_op jit(solution)/shard_map/ppermute | solution.py:512
  60.6 3.1 %local_first.3.refs_2_ = f32[2,32,2048]{2,1,0:T(8,128)S(1)} custom-call(s32[640]{0:T(1024)S(1)} %plan.1.plan_ref.refs_0_, bf16[160,128,256]{2,1,0:T(8,128)(2,1)S(1)} %prep.1.tiles_ref.refs_1_, f32[2,32,2048]{2,1,0:T(8,128)S(1)} %get-tuple-element.74.y_ref.refs_0_), custom_call_target="tpu_custom_call" | custom-call | flops 671088640 | bytes 1572864 | tf_op jit(solution)/shard_map/local_first/pallas_call | solution.py:42
  65.2 3.3 %collective-permute-done.13 = f32[8,128]{1,0:T(8,128)S(1)} collective-permute-done((f32[8,128]{1,0:T(8,128)S(1)}, f32[8,128]{1,0:T(8,128)S(1)}, u32[]{:S(2)}, u32[]{:S(2)}) %collective-permute-start.13) | collective-permute-done | bytes 4128 | tf_op jit(solution)/shard_map/ppermute | solution.py:490
  71.4 2.1 %collective-permute-start.20 = (f32[2,32,1024]{2,1,0:T(8,128)S(1)}, f32[2,32,1024]{2,1,0:T(8,128)S(1)}, u32[]{:S(2)}, u32[]{:S(2)}) collective-permute-start(f32[2,32,1024]{2,1,0:T(8,128)S(1)} %get-tuple-element.89), channel_id=1, source_target_pairs={{0,3},{1,2},{2,1},{3,0},{4,7},{5,6},{6,5},{7,4},{8,11},{9,10},{10,... | collective-permute-start | bytes 786440 | tf_op jit(solution)/shard_map/ppermute | solution.py:511
  73.5 2.3 %collective-permute-start.22 = (f32[1,32,2048]{2,1,0:T(8,128)S(1)}, f32[1,32,2048]{2,1,0:T(8,128)S(1)}, u32[]{:S(2)}, u32[]{:S(2)}) collective-permute-start(f32[1,32,2048]{2,1,0:T(8,128)S(1)} %get-tuple-element.91), channel_id=1, source_target_pairs={{0,28},{4,8},{8,4},{12,16},{16,12},{20,24},{24,20},{28,0},{1,29},{... | collective-permute-start | bytes 786440 | tf_op jit(solution)/shard_map/ppermute | solution.py:512
  75.8 3.1 %local_step.4.refs_2_ = f32[2,32,2048]{2,1,0:T(8,128)S(1)} custom-call(s32[640]{0:T(1024)S(1)} %plan.1.plan_ref.refs_0_, bf16[160,128,256]{2,1,0:T(8,128)(2,1)S(1)} %prep.1.tiles_ref.refs_1_, f32[2,32,2048]{2,1,0:T(8,128)S(1)} %get-tuple-element.83.y_ref.refs_0_, f32[2,32,2048]{2,1,0:T(8,128)S(1)} %get-tuple-element.74.y_ref.refs_0_), custom_call_target="tpu_custom_call" | custom-call | flops 671088640 | bytes 1572864 | tf_op jit(solution)/shard_map/local_step/pallas_call | solution.py:42
  80.2 5.3 %collective-permute-done.18 = f32[8,128]{1,0:T(8,128)S(1)} collective-permute-done((f32[8,128]{1,0:T(8,128)S(1)}, f32[8,128]{1,0:T(8,128)S(1)}, u32[]{:S(2)}, u32[]{:S(2)}) %collective-permute-start.18) | collective-permute-done | bytes 4128 | tf_op jit(solution)/shard_map/ppermute | solution.py:490
  89.3 2.4 %collective-permute-start.27 = (f32[1,32,2048]{2,1,0:T(8,128)S(1)}, f32[1,32,2048]{2,1,0:T(8,128)S(1)}, u32[]{:S(2)}, u32[]{:S(2)}) collective-permute-start(f32[1,32,2048]{2,1,0:T(8,128)S(1)} %get-tuple-element.100), channel_id=1, source_target_pairs={{0,28},{4,8},{8,4},{12,16},{16,12},{20,24},{24,20},{28,0},{1,29},{... | collective-permute-start | bytes 786440 | tf_op jit(solution)/shard_map/ppermute | solution.py:512
  91.8 3.1 %local_step.5.refs_2_ = f32[2,32,2048]{2,1,0:T(8,128)S(1)} custom-call(s32[640]{0:T(1024)S(1)} %plan.1.plan_ref.refs_0_, bf16[160,128,256]{2,1,0:T(8,128)(2,1)S(1)} %prep.1.tiles_ref.refs_1_, f32[2,32,2048]{2,1,0:T(8,128)S(1)} %get-tuple-element.92.y_ref, f32[2,32,2048]{2,1,0:T(8,128)S(1)} %get-tuple-element.83.y_ref.refs_0_), custom_call_target="tpu_custom_call" | custom-call | flops 671088640 | bytes 1572864 | tf_op jit(solution)/shard_map/local_step/pallas_call | solution.py:42
  95.4 4.0 %collective-permute-done.23 = f32[8,128]{1,0:T(8,128)S(1)} collective-permute-done((f32[8,128]{1,0:T(8,128)S(1)}, f32[8,128]{1,0:T(8,128)S(1)}, u32[]{:S(2)}, u32[]{:S(2)}) %collective-permute-start.23) | collective-permute-done | bytes 4128 | tf_op jit(solution)/shard_map/ppermute | solution.py:490
  100.8 1.9 %finish_step.5 = (f32[2,32,2048]{2,1,0:T(8,128)S(1)}, f32[2,32,1024]{2,1,0:T(8,128)S(1)}, f32[2,32,1024]{2,1,0:T(8,128)S(1)}, f32[1,32,2048]{2,1,0:T(8,128)S(1)}, f32[1,32,2048]{2,1,0:T(8,128)S(1)}) custom-call(s32[640]{0:T(1024)S(1)} %plan.1.plan_ref.refs_0_, bf16[160,128,256]{2,1,0:T(8,128)(2,1)S(1)} %prep.1.tiles_ref.refs_1_, ...), custom_call_target="tpu_custom_call" | custom-call | flops 268435456 | bytes 3145728 | tf_op jit(solution)/shard_map/finish_step/pallas_call | solution.py:42
  103.9 2.4 %collective-permute-start.30 = (f32[2,32,1024]{2,1,0:T(8,128)S(1)}, f32[2,32,1024]{2,1,0:T(8,128)S(1)}, u32[]{:S(2)}, u32[]{:S(2)}) collective-permute-start(f32[2,32,1024]{2,1,0:T(8,128)S(1)} %get-tuple-element.107), channel_id=1, source_target_pairs={{0,3},{1,2},{2,1},{3,0},{4,7},{5,6},{6,5},{7,4},{8,11},{9,10},{10,... | collective-permute-start | bytes 786440 | tf_op jit(solution)/shard_map/ppermute | solution.py:511
  108.0 3.0 %local_image.1.refs_2_ = f32[2,32,2048]{2,1,0:T(8,128)S(1)} custom-call(s32[640]{0:T(1024)S(1)} %plan.1.plan_ref.refs_0_, bf16[160,128,256]{2,1,0:T(8,128)(2,1)S(1)} %prep.1.tiles_ref.refs_1_, f32[2,32,2048]{2,1,0:T(8,128)S(1)} %get-tuple-element.101.y_ref.refs_7_), custom_call_target="tpu_custom_call" | custom-call | flops 671088640 | bytes 1572864 | tf_op jit(solution)/shard_map/local_image/pallas_call | solution.py:42
  112.5 2.3 %collective-permute-done.28 = f32[8,128]{1,0:T(8,128)S(1)} collective-permute-done((f32[8,128]{1,0:T(8,128)S(1)}, f32[8,128]{1,0:T(8,128)S(1)}, u32[]{:S(2)}, u32[]{:S(2)}) %collective-permute-start.28) | collective-permute-done | bytes 4128 | tf_op jit(solution)/shard_map/ppermute | solution.py:490
  114.8 2.6 %factor.1.refs_8_.matrix_ref = f32[32,32]{1,0:T(8,128)S(1)} custom-call(f32[8,128]{1,0:T(8,128)S(1)} %add.49.gram_ref), custom_call_target="tpu_custom_call" | custom-call | flops 40960000 | bytes 8192 | tf_op jit(solution)/shard_map/factor/pallas_call | solution.py:42
  117.4 2.7 %finish_image.1 = (f32[2,32,2048]{2,1,0:T(8,128)S(1)}, f32[16,128]{1,0:T(8,128)S(1)}) custom-call(s32[640]{0:T(1024)S(1)} %plan.1.plan_ref.refs_0_, bf16[160,128,256]{2,1,0:T(8,128)(2,1)S(1)} %prep.1.tiles_ref.refs_1_, f32[2,32,2048]{2,1,0:T(8,128)S(1)} %local_image.1.refs_2_, f32[2,32,1024]{2,1,0:T(8,128)S(1)} %collective-permute-done.29.refs_3_, ...), custom_call_target="tpu_custom_call" | custom-call | flops 268435456 | bytes 3145728 | tf_op jit(solution)/shard_map/finish_image/pallas_call | solution.py:42
  128.9 3.0 %collective-permute-start.37 = (f32[16,128]{1,0:T(8,128)S(1)}, f32[16,128]{1,0:T(8,128)S(1)}, u32[]{:S(2)}, u32[]{:S(2)}) collective-permute-start(f32[16,128]{1,0:T(8,128)S(1)} %add_add_fusion.1), channel_id=1, source_target_pairs={{0,1},{1,0},{2,3},{3,2},{4,5},{5,4},{6,7},{7,6},{8,9},{9,8},{10,11... | collective-permute-start | bytes 24584 | tf_op jit(solution)/shard_map/ppermute | solution.py:490
  133.6 3.7 %close.1 = (f32[2,32,2048]{2,1,0:T(8,128)}, f32[32,32]{1,0:T(8,128)}) custom-call(f32[16,128]{1,0:T(8,128)S(1)} %add_add_fusion.sums_ref, f32[2,32,2048]{2,1,0:T(8,128)S(1)} %get-tuple-element.112.y_ref), custom_call_target="tpu_custom_call" | custom-call | flops 8388608 | bytes 1048576 | tf_op jit(solution)/shard_map/close/pallas_call | solution.py:42
  (81 shorter events, 39.6 us)
Async XLA Ops:
  2.4 19.7 %collective-permute-start = (f32[2,32,1024]{2,1,0:T(8,128)S(1)}, f32[2,32,1024]{2,1,0:T(8,128)S(1)}, u32[]{:S(2)}, u32[]{:S(2)}) collective-permute-start(f32[2,32,1024]{2,1,0:T(8,128)S(1)} %get-tuple-element.60), channel_id=1, source_target_pairs={{0,1},{1,0},{2,3},{3,2},{4,5},{5,4},{6,7},{7,6},{8,9},{9,8},{10,11... | collective-permute-start | bytes 786440 | tf_op jit(solution)/shard_map/ppermute | solution.py:510
  5.5 16.6 %collective-permute-start.1 = (f32[2,32,1024]{2,1,0:T(8,128)S(1)}, f32[2,32,1024]{2,1,0:T(8,128)S(1)}, u32[]{:S(2)}, u32[]{:S(2)}) collective-permute-start(f32[2,32,1024]{2,1,0:T(8,128)S(1)} %get-tuple-element.61), channel_id=1, source_target_pairs={{0,3},{1,2},{2,1},{3,0},{4,7},{5,6},{6,5},{7,4},{8,11},{9,10},{10,... | collective-permute-start | bytes 786440 | tf_op jit(solution)/shard_map/ppermute | solution.py:511
  8.0 14.2 %collective-permute-start.2 = (f32[1,32,2048]{2,1,0:T(8,128)S(1)}, f32[1,32,2048]{2,1,0:T(8,128)S(1)}, u32[]{:S(2)}, u32[]{:S(2)}) collective-permute-start(f32[1,32,2048]{2,1,0:T(8,128)S(1)} %get-tuple-element.62), channel_id=1, source_target_pairs={{0,4},{4,0},{8,12},{12,8},{16,20},{20,16},{24,28},{28,24},{1,5},{5... | collective-permute-start | bytes 786440 | tf_op jit(solution)/shard_map/ppermute | solution.py:513
  8.0 14.2 %collective-permute-start.3 = (f32[1,32,2048]{2,1,0:T(8,128)S(1)}, f32[1,32,2048]{2,1,0:T(8,128)S(1)}, u32[]{:S(2)}, u32[]{:S(2)}) collective-permute-start(f32[1,32,2048]{2,1,0:T(8,128)S(1)} %get-tuple-element.63), channel_id=1, source_target_pairs={{0,28},{4,8},{8,4},{12,16},{16,12},{20,24},{24,20},{28,0},{1,29},{... | collective-permute-start | bytes 786440 | tf_op jit(solution)/shard_map/ppermute | solution.py:512
  23.9 13.2 %collective-permute-start.4 = (f32[2,32,1024]{2,1,0:T(8,128)S(1)}, f32[2,32,1024]{2,1,0:T(8,128)S(1)}, u32[]{:S(2)}, u32[]{:S(2)}) collective-permute-start(f32[2,32,1024]{2,1,0:T(8,128)S(1)} %get-tuple-element.65), channel_id=1, source_target_pairs={{0,1},{1,0},{2,3},{3,2},{4,5},{5,4},{6,7},{7,6},{8,9},{9,8},{10,11... | collective-permute-start | bytes 786440 | tf_op jit(solution)/shard_map/ppermute | solution.py:510
  24.7 12.5 %collective-permute-start.5 = (f32[2,32,1024]{2,1,0:T(8,128)S(1)}, f32[2,32,1024]{2,1,0:T(8,128)S(1)}, u32[]{:S(2)}, u32[]{:S(2)}) collective-permute-start(f32[2,32,1024]{2,1,0:T(8,128)S(1)} %get-tuple-element.66), channel_id=1, source_target_pairs={{0,3},{1,2},{2,1},{3,0},{4,7},{5,6},{6,5},{7,4},{8,11},{9,10},{10,... | collective-permute-start | bytes 786440 | tf_op jit(solution)/shard_map/ppermute | solution.py:511
  25.7 11.5 %collective-permute-start.6 = (f32[1,32,2048]{2,1,0:T(8,128)S(1)}, f32[1,32,2048]{2,1,0:T(8,128)S(1)}, u32[]{:S(2)}, u32[]{:S(2)}) collective-permute-start(f32[1,32,2048]{2,1,0:T(8,128)S(1)} %get-tuple-element.67), channel_id=1, source_target_pairs={{0,4},{4,0},{8,12},{12,8},{16,20},{20,16},{24,28},{28,24},{1,5},{5... | collective-permute-start | bytes 786440 | tf_op jit(solution)/shard_map/ppermute | solution.py:513
  25.7 11.5 %collective-permute-start.7 = (f32[1,32,2048]{2,1,0:T(8,128)S(1)}, f32[1,32,2048]{2,1,0:T(8,128)S(1)}, u32[]{:S(2)}, u32[]{:S(2)}) collective-permute-start(f32[1,32,2048]{2,1,0:T(8,128)S(1)} %get-tuple-element.68), channel_id=1, source_target_pairs={{0,28},{4,8},{8,4},{12,16},{16,12},{20,24},{24,20},{28,0},{1,29},{... | collective-permute-start | bytes 786440 | tf_op jit(solution)/shard_map/ppermute | solution.py:512
  39.0 9.3 %collective-permute-start.8 = (f32[2,32,1024]{2,1,0:T(8,128)S(1)}, f32[2,32,1024]{2,1,0:T(8,128)S(1)}, u32[]{:S(2)}, u32[]{:S(2)}) collective-permute-start(f32[2,32,1024]{2,1,0:T(8,128)S(1)} %get-tuple-element.70), channel_id=1, source_target_pairs={{0,1},{1,0},{2,3},{3,2},{4,5},{5,4},{6,7},{7,6},{8,9},{9,8},{10,11... | collective-permute-start | bytes 786440 | tf_op jit(solution)/shard_map/ppermute | solution.py:510
  40.8 11.1 %collective-permute-start.9 = (f32[2,32,1024]{2,1,0:T(8,128)S(1)}, f32[2,32,1024]{2,1,0:T(8,128)S(1)}, u32[]{:S(2)}, u32[]{:S(2)}) collective-permute-start(f32[2,32,1024]{2,1,0:T(8,128)S(1)} %get-tuple-element.71), channel_id=1, source_target_pairs={{0,3},{1,2},{2,1},{3,0},{4,7},{5,6},{6,5},{7,4},{8,11},{9,10},{10,... | collective-permute-start | bytes 786440 | tf_op jit(solution)/shard_map/ppermute | solution.py:511
  42.1 9.7 %collective-permute-start.10 = (f32[1,32,2048]{2,1,0:T(8,128)S(1)}, f32[1,32,2048]{2,1,0:T(8,128)S(1)}, u32[]{:S(2)}, u32[]{:S(2)}) collective-permute-start(f32[1,32,2048]{2,1,0:T(8,128)S(1)} %get-tuple-element.72), channel_id=1, source_target_pairs={{0,4},{4,0},{8,12},{12,8},{16,20},{20,16},{24,28},{28,24},{1,5},{5... | collective-permute-start | bytes 786440 | tf_op jit(solution)/shard_map/ppermute | solution.py:513
  42.1 9.7 %collective-permute-start.11 = (f32[1,32,2048]{2,1,0:T(8,128)S(1)}, f32[1,32,2048]{2,1,0:T(8,128)S(1)}, u32[]{:S(2)}, u32[]{:S(2)}) collective-permute-start(f32[1,32,2048]{2,1,0:T(8,128)S(1)} %get-tuple-element.73), channel_id=1, source_target_pairs={{0,28},{4,8},{8,4},{12,16},{16,12},{20,24},{24,20},{28,0},{1,29},{... | collective-permute-start | bytes 786440 | tf_op jit(solution)/shard_map/ppermute | solution.py:512
  54.0 14.4 %collective-permute-start.14 = (f32[2,32,1024]{2,1,0:T(8,128)S(1)}, f32[2,32,1024]{2,1,0:T(8,128)S(1)}, u32[]{:S(2)}, u32[]{:S(2)}) collective-permute-start(f32[2,32,1024]{2,1,0:T(8,128)S(1)} %get-tuple-element.79), channel_id=1, source_target_pairs={{0,1},{1,0},{2,3},{3,2},{4,5},{5,4},{6,7},{7,6},{8,9},{9,8},{10,11... | collective-permute-start | bytes 786440 | tf_op jit(solution)/shard_map/ppermute | solution.py:510
  55.2 13.3 %collective-permute-start.15 = (f32[2,32,1024]{2,1,0:T(8,128)S(1)}, f32[2,32,1024]{2,1,0:T(8,128)S(1)}, u32[]{:S(2)}, u32[]{:S(2)}) collective-permute-start(f32[2,32,1024]{2,1,0:T(8,128)S(1)} %get-tuple-element.80), channel_id=1, source_target_pairs={{0,3},{1,2},{2,1},{3,0},{4,7},{5,6},{6,5},{7,4},{8,11},{9,10},{10,... | collective-permute-start | bytes 786440 | tf_op jit(solution)/shard_map/ppermute | solution.py:511
  57.5 11.0 %collective-permute-start.16 = (f32[1,32,2048]{2,1,0:T(8,128)S(1)}, f32[1,32,2048]{2,1,0:T(8,128)S(1)}, u32[]{:S(2)}, u32[]{:S(2)}) collective-permute-start(f32[1,32,2048]{2,1,0:T(8,128)S(1)} %get-tuple-element.81), channel_id=1, source_target_pairs={{0,4},{4,0},{8,12},{12,8},{16,20},{20,16},{24,28},{28,24},{1,5},{5... | collective-permute-start | bytes 786440 | tf_op jit(solution)/shard_map/ppermute | solution.py:513
  57.5 11.0 %collective-permute-start.17 = (f32[1,32,2048]{2,1,0:T(8,128)S(1)}, f32[1,32,2048]{2,1,0:T(8,128)S(1)}, u32[]{:S(2)}, u32[]{:S(2)}) collective-permute-start(f32[1,32,2048]{2,1,0:T(8,128)S(1)} %get-tuple-element.82), channel_id=1, source_target_pairs={{0,28},{4,8},{8,4},{12,16},{16,12},{20,24},{24,20},{28,0},{1,29},{... | collective-permute-start | bytes 786440 | tf_op jit(solution)/shard_map/ppermute | solution.py:512
  70.3 15.3 %collective-permute-start.19 = (f32[2,32,1024]{2,1,0:T(8,128)S(1)}, f32[2,32,1024]{2,1,0:T(8,128)S(1)}, u32[]{:S(2)}, u32[]{:S(2)}) collective-permute-start(f32[2,32,1024]{2,1,0:T(8,128)S(1)} %get-tuple-element.88), channel_id=1, source_target_pairs={{0,1},{1,0},{2,3},{3,2},{4,5},{5,4},{6,7},{7,6},{8,9},{9,8},{10,11... | collective-permute-start | bytes 786440 | tf_op jit(solution)/shard_map/ppermute | solution.py:510
  71.4 14.2 %collective-permute-start.20 = (f32[2,32,1024]{2,1,0:T(8,128)S(1)}, f32[2,32,1024]{2,1,0:T(8,128)S(1)}, u32[]{:S(2)}, u32[]{:S(2)}) collective-permute-start(f32[2,32,1024]{2,1,0:T(8,128)S(1)} %get-tuple-element.89), channel_id=1, source_target_pairs={{0,3},{1,2},{2,1},{3,0},{4,7},{5,6},{6,5},{7,4},{8,11},{9,10},{10,... | collective-permute-start | bytes 786440 | tf_op jit(solution)/shard_map/ppermute | solution.py:511
  73.5 12.1 %collective-permute-start.21 = (f32[1,32,2048]{2,1,0:T(8,128)S(1)}, f32[1,32,2048]{2,1,0:T(8,128)S(1)}, u32[]{:S(2)}, u32[]{:S(2)}) collective-permute-start(f32[1,32,2048]{2,1,0:T(8,128)S(1)} %get-tuple-element.90), channel_id=1, source_target_pairs={{0,4},{4,0},{8,12},{12,8},{16,20},{20,16},{24,28},{28,24},{1,5},{5... | collective-permute-start | bytes 786440 | tf_op jit(solution)/shard_map/ppermute | solution.py:513
  73.5 12.1 %collective-permute-start.22 = (f32[1,32,2048]{2,1,0:T(8,128)S(1)}, f32[1,32,2048]{2,1,0:T(8,128)S(1)}, u32[]{:S(2)}, u32[]{:S(2)}) collective-permute-start(f32[1,32,2048]{2,1,0:T(8,128)S(1)} %get-tuple-element.91), channel_id=1, source_target_pairs={{0,28},{4,8},{8,4},{12,16},{16,12},{20,24},{24,20},{28,0},{1,29},{... | collective-permute-start | bytes 786440 | tf_op jit(solution)/shard_map/ppermute | solution.py:512
  78.8 6.7 %collective-permute-start.18 = (f32[8,128]{1,0:T(8,128)S(1)}, f32[8,128]{1,0:T(8,128)S(1)}, u32[]{:S(2)}, u32[]{:S(2)}) collective-permute-start(f32[8,128]{1,0:T(8,128)S(1)} %add.46), channel_id=1, source_target_pairs={{0,2},{1,3},{2,0},{3,1},{4,6},{5,7},{6,4},{7,5},{8,10},{9,11},{10,... | collective-permute-start | bytes 12296 | tf_op jit(solution)/shard_map/ppermute | solution.py:490
  87.3 12.1 %collective-permute-start.24 = (f32[2,32,1024]{2,1,0:T(8,128)S(1)}, f32[2,32,1024]{2,1,0:T(8,128)S(1)}, u32[]{:S(2)}, u32[]{:S(2)}) collective-permute-start(f32[2,32,1024]{2,1,0:T(8,128)S(1)} %get-tuple-element.97), channel_id=1, source_target_pairs={{0,1},{1,0},{2,3},{3,2},{4,5},{5,4},{6,7},{7,6},{8,9},{9,8},{10,11... | collective-permute-start | bytes 786440 | tf_op jit(solution)/shard_map/ppermute | solution.py:510
  87.9 12.9 %collective-permute-start.25 = (f32[2,32,1024]{2,1,0:T(8,128)S(1)}, f32[2,32,1024]{2,1,0:T(8,128)S(1)}, u32[]{:S(2)}, u32[]{:S(2)}) collective-permute-start(f32[2,32,1024]{2,1,0:T(8,128)S(1)} %get-tuple-element.98), channel_id=1, source_target_pairs={{0,3},{1,2},{2,1},{3,0},{4,7},{5,6},{6,5},{7,4},{8,11},{9,10},{10,... | collective-permute-start | bytes 786440 | tf_op jit(solution)/shard_map/ppermute | solution.py:511
  89.3 11.5 %collective-permute-start.26 = (f32[1,32,2048]{2,1,0:T(8,128)S(1)}, f32[1,32,2048]{2,1,0:T(8,128)S(1)}, u32[]{:S(2)}, u32[]{:S(2)}) collective-permute-start(f32[1,32,2048]{2,1,0:T(8,128)S(1)} %get-tuple-element.99), channel_id=1, source_target_pairs={{0,4},{4,0},{8,12},{12,8},{16,20},{20,16},{24,28},{28,24},{1,5},{5... | collective-permute-start | bytes 786440 | tf_op jit(solution)/shard_map/ppermute | solution.py:513
  89.3 11.5 %collective-permute-start.27 = (f32[1,32,2048]{2,1,0:T(8,128)S(1)}, f32[1,32,2048]{2,1,0:T(8,128)S(1)}, u32[]{:S(2)}, u32[]{:S(2)}) collective-permute-start(f32[1,32,2048]{2,1,0:T(8,128)S(1)} %get-tuple-element.100), channel_id=1, source_target_pairs={{0,28},{4,8},{8,4},{12,16},{16,12},{20,24},{24,20},{28,0},{1,29},{... | collective-permute-start | bytes 786440 | tf_op jit(solution)/shard_map/ppermute | solution.py:512
  102.8 14.6 %collective-permute-start.29 = (f32[2,32,1024]{2,1,0:T(8,128)S(1)}, f32[2,32,1024]{2,1,0:T(8,128)S(1)}, u32[]{:S(2)}, u32[]{:S(2)}) collective-permute-start(f32[2,32,1024]{2,1,0:T(8,128)S(1)} %get-tuple-element.106), channel_id=1, source_target_pairs={{0,1},{1,0},{2,3},{3,2},{4,5},{5,4},{6,7},{7,6},{8,9},{9,8},{10,11... | collective-permute-start | bytes 786440 | tf_op jit(solution)/shard_map/ppermute | solution.py:510
  103.9 13.5 %collective-permute-start.30 = (f32[2,32,1024]{2,1,0:T(8,128)S(1)}, f32[2,32,1024]{2,1,0:T(8,128)S(1)}, u32[]{:S(2)}, u32[]{:S(2)}) collective-permute-start(f32[2,32,1024]{2,1,0:T(8,128)S(1)} %get-tuple-element.107), channel_id=1, source_target_pairs={{0,3},{1,2},{2,1},{3,0},{4,7},{5,6},{6,5},{7,4},{8,11},{9,10},{10,... | collective-permute-start | bytes 786440 | tf_op jit(solution)/shard_map/ppermute | solution.py:511
  106.2 11.2 %collective-permute-start.31 = (f32[1,32,2048]{2,1,0:T(8,128)S(1)}, f32[1,32,2048]{2,1,0:T(8,128)S(1)}, u32[]{:S(2)}, u32[]{:S(2)}) collective-permute-start(f32[1,32,2048]{2,1,0:T(8,128)S(1)} %get-tuple-element.108), channel_id=1, source_target_pairs={{0,4},{4,0},{8,12},{12,8},{16,20},{20,16},{24,28},{28,24},{1,5},{5... | collective-permute-start | bytes 786440 | tf_op jit(solution)/shard_map/ppermute | solution.py:513
  106.2 11.2 %collective-permute-start.32 = (f32[1,32,2048]{2,1,0:T(8,128)S(1)}, f32[1,32,2048]{2,1,0:T(8,128)S(1)}, u32[]{:S(2)}, u32[]{:S(2)}) collective-permute-start(f32[1,32,2048]{2,1,0:T(8,128)S(1)} %get-tuple-element.109), channel_id=1, source_target_pairs={{0,28},{4,8},{8,4},{12,16},{16,12},{20,24},{24,20},{28,0},{1,29},{... | collective-permute-start | bytes 786440 | tf_op jit(solution)/shard_map/ppermute | solution.py:512
  127.5 5.5 %collective-permute-start.39 = (f32[16,128]{1,0:T(8,128)S(1)}, f32[16,128]{1,0:T(8,128)S(1)}, u32[]{:S(2)}, u32[]{:S(2)}) collective-permute-start(f32[16,128]{1,0:T(8,128)S(1)} %add_add_fusion.1), channel_id=1, source_target_pairs={{0,3},{1,2},{2,1},{3,0},{4,7},{5,6},{6,5},{7,4},{8,11},{9,10},{10,... | collective-permute-start | bytes 24584 | tf_op jit(solution)/shard_map/ppermute | solution.py:490
  128.5 4.7 %collective-permute-start.38 = (f32[16,128]{1,0:T(8,128)S(1)}, f32[16,128]{1,0:T(8,128)S(1)}, u32[]{:S(2)}, u32[]{:S(2)}) collective-permute-start(f32[16,128]{1,0:T(8,128)S(1)} %add_add_fusion.1), channel_id=1, source_target_pairs={{0,2},{1,3},{2,0},{3,1},{4,6},{5,7},{6,4},{7,5},{8,10},{9,11},{10,... | collective-permute-start | bytes 24584 | tf_op jit(solution)/shard_map/ppermute | solution.py:490
  128.9 4.7 %collective-permute-start.37 = (f32[16,128]{1,0:T(8,128)S(1)}, f32[16,128]{1,0:T(8,128)S(1)}, u32[]{:S(2)}, u32[]{:S(2)}) collective-permute-start(f32[16,128]{1,0:T(8,128)S(1)} %add_add_fusion.1), channel_id=1, source_target_pairs={{0,1},{1,0},{2,3},{3,2},{4,5},{5,4},{6,7},{7,6},{8,9},{9,8},{10,11... | collective-permute-start | bytes 24584 | tf_op jit(solution)/shard_map/ppermute | solution.py:490
  (10 other events, 27.9 us)

commit v6 on v5

--- a/solution.py
+++ b/solution.py
@@ -13,7 +13,7 @@
 CENTER = 6.5
 RADIUS = 3.5
 INFLATION_FACTOR = 0.8
-GROUP = 8
+GROUP = 12
 
 F32 = jnp.float32
 BF16 = jnp.bfloat16
@@ -157,7 +157,7 @@
     size = Layout(slices, count // TPR).size
     return pl.pallas_call(
         functools.partial(plan_kernel, blocks_all),
-        out_shape=jax.ShapeDtypeStruct((size,), jnp.int32),
+        out_shape=pltpu.SMEM((size,), jnp.int32),
         in_specs=[SCALARS, SCALARS],
         out_specs=SCALARS,
         name="plan",
@@ -260,7 +260,7 @@
             out_ref[s, :, here] = image
             return carry
 
-        lax.fori_loop(0, blocks, row, 0, unroll=8)
+        lax.fori_loop(0, blocks, row, 0, unroll=16)
 
 
 def local_part(mode, scale, table, tiles, y, previous):
@@ -396,18 +396,19 @@
 
 def inverse_factor(gram):
     width = gram.shape[0]
-    rows = lax.broadcasted_iota(jnp.int32, (width, width), 0)
-    columns = lax.broadcasted_iota(jnp.int32, (width, width), 1)
+    square = (width, width)
+    rows = lax.broadcasted_iota(jnp.int32, square, 0)
+    columns = lax.broadcasted_iota(jnp.int32, square, 1)
     inverse = (rows == columns).astype(F32)
-    row_of = lax.broadcasted_iota(jnp.int32, (width, 1), 0)
-    for j in range(width):
-        root = lax.rsqrt(gram[j : j + 1, j : j + 1])
-        gram_row = gram[j : j + 1, :] * root
-        inverse_row = inverse[j : j + 1, :] * root
-        column = jnp.where(row_of > j, gram[:, j : j + 1] * root, 0.0)
-        gram = gram - column * gram_row
-        inverse = jnp.where(row_of == j, inverse_row, inverse - column * inverse_row)
-    return inverse
+    column = jnp.broadcast_to(gram[:, :1], square)
+    for j in range(width - 1):
+        following = jnp.broadcast_to(gram[:, j + 1 : j + 2], square)
+        scaled = jnp.where(rows > j, column, 0.0) * (1.0 / column[j : j + 1])
+        gram = gram - scaled * gram[j : j + 1]
+        inverse = inverse - scaled * inverse[j : j + 1]
+        column = following - scaled * column[j + 1 : j + 2]
+    pivots = jnp.sum(jnp.where(rows == columns, gram, 0.0), axis=1, keepdims=True)
+    return inverse * lax.rsqrt(pivots)
 
 
 def factor_kernel(count, gram_ref, out_ref):

time: 139 us -> 131 us (0.942); the launches traced: 137 us -> 131 us
  Pallas kernels: 51.1 us -> 39 us
  waiting for transfers between devices: 33.8 us -> 38.2 us
    pallas_call x18, Pallas kernels: 43.3 us -> 31.8 us  [call(): pl.pallas_call(kernel, out_shape=out_shape, in_specs=specs, out_specs=[WH...]
    ppermute x12, waiting for transfers between devices: 20.6 us -> 24.2 us  [add_over(): lax.ppermute(value, axis, [(i, i ^ k) for i in range(count)])]
    ppermute x7, starting transfers between devices: 13.1 us -> 15.9 us  [exchange(): outer = lax.ppermute(outer, 'space', outer_pairs('space'))]
    ppermute x7, starting transfers between devices: 9.54 us -> 6.99 us  [exchange(): inner = lax.ppermute(inner, 'space', inner_pairs('space'))]
    ppermute x7, waiting for transfers between devices: 4.94 us -> 6.74 us  [exchange(): outer = lax.ppermute(outer, 'space', outer_pairs('space'))]
  transfers between devices with their start and end apart: 40 -> 40, of which waited for: 15 -> 15; matrix products, arithmetic and copies ran while one was open for 0% -> 0% of each run, Pallas kernels for 24% -> 18%
where the time goes in v6:
time: 131 us
  starting transfers between devices  50.7 us (39%)
  Pallas kernels  39 us (30%)
  waiting for transfers between devices  38.2 us (29%)
  local copies, waits for them, and re-layouts  1.81 us (1%)
    pallas_call x18, Pallas kernels, call(): pl.pallas_call(kernel, out_shape=out_shape, in_specs=specs, out_specs=[WH...  31.8 us
    ppermute x12, waiting for transfers between devices, add_over(): lax.ppermute(value, axis, [(i, i ^ k) for i in range(count)])  24.2 us
    ppermute x7, starting transfers between devices, exchange(): outer = lax.ppermute(outer, 'space', outer_pairs('space'))  15.9 us
    ppermute x7, starting transfers between devices, exchange(): far_slice = lax.ppermute(far_slice, 'tm', outer_pairs('tm'))  15.3 us
    ppermute x12, starting transfers between devices, add_over(): lax.ppermute(value, axis, [(i, i ^ k) for i in range(count)])  12.5 us
    ppermute x7, waiting for transfers between devices, exchange(): inner = lax.ppermute(inner, 'space', inner_pairs('space'))  7.26 us
    ppermute x7, starting transfers between devices, exchange(): inner = lax.ppermute(inner, 'space', inner_pairs('space'))  6.99 us
    ppermute x7, waiting for transfers between devices, exchange(): outer = lax.ppermute(outer, 'space', outer_pairs('space'))  6.74 us
  transfers between devices with their start and end apart: 40, of which 15 were waited for; matrix products, arithmetic and copies ran while one was open for 0% of the time, Pallas kernels for 18%

profile of v6, /device:TPU:0, one launch (start us, length us, event | category | flops | bytes accessed | tf_op | source)
XLA Modules:
  0.0 130.7 jit_solution(7047607744361174203)
XLA Ops:
  2.4 3.1 %collective-permute-start = (f32[2,32,1024]{2,1,0:T(8,128)S(1)}, f32[2,32,1024]{2,1,0:T(8,128)S(1)}, u32[]{:S(2)}, u32[]{:S(2)}) collective-permute-start(f32[2,32,1024]{2,1,0:T(8,128)S(1)} %get-tuple-element.60), channel_id=1, source_target_pairs={{0,1},{1,0},{2,3},{3,2},{4,5},{5,4},{6,7},{7,6},{8,9},{9,8},{10,11... | collective-permute-start | bytes 786440 | tf_op jit(solution)/shard_map/ppermute | solution.py:511
  5.5 2.5 %collective-permute-start.1 = (f32[2,32,1024]{2,1,0:T(8,128)S(1)}, f32[2,32,1024]{2,1,0:T(8,128)S(1)}, u32[]{:S(2)}, u32[]{:S(2)}) collective-permute-start(f32[2,32,1024]{2,1,0:T(8,128)S(1)} %get-tuple-element.61), channel_id=1, source_target_pairs={{0,3},{1,2},{2,1},{3,0},{4,7},{5,6},{6,5},{7,4},{8,11},{9,10},{10,... | collective-permute-start | bytes 786440 | tf_op jit(solution)/shard_map/ppermute | solution.py:512
  8.0 2.6 %collective-permute-start.3 = (f32[1,32,2048]{2,1,0:T(8,128)S(1)}, f32[1,32,2048]{2,1,0:T(8,128)S(1)}, u32[]{:S(2)}, u32[]{:S(2)}) collective-permute-start(f32[1,32,2048]{2,1,0:T(8,128)S(1)} %get-tuple-element.63), channel_id=1, source_target_pairs={{0,28},{4,8},{8,4},{12,16},{16,12},{20,24},{24,20},{28,0},{1,29},{... | collective-permute-start | bytes 786440 | tf_op jit(solution)/shard_map/ppermute | solution.py:513
  11.2 2.4 %plan.1.plan_ref.refs_0_ = s32[640]{0:T(1024)S(4)} custom-call(s32[2,80]{1,0:T(2,128)S(1)} %copy-done.1, s32[5]{0:T(128)S(1)} %stack.31.flags_ref.odd_ref), custom_call_target="tpu_custom_call" | custom-call | tf_op jit(solution)/shard_map/plan/pallas_call | solution.py:158
  13.7 4.8 %prep.1.tiles_ref.refs_1_ = bf16[160,128,256]{2,1,0:T(8,128)(2,1)S(1)} custom-call(f32[160,128,128]{2,1,0:T(8,128)} %bitcast.6), custom_call_target="tpu_custom_call" | custom-call | bytes 10485760 | tf_op jit(solution)/shard_map/prep/pallas_call | solution.py:87
  18.5 2.1 %local_first.2.refs_2_ = f32[2,32,2048]{2,1,0:T(8,128)S(1)} custom-call(s32[640]{0:T(1024)S(4)} %plan.1.plan_ref.refs_0_, bf16[160,128,256]{2,1,0:T(8,128)(2,1)S(1)} %prep.1.tiles_ref.refs_1_, f32[2,32,2048]{2,1,0:T(8,128)S(1)} %get-tuple-element.59.y_ref.refs_0_), custom_call_target="tpu_custom_call" | custom-call | flops 671088640 | bytes 1572864 | tf_op jit(solution)/shard_map/local_first/pallas_call | solution.py:42
  22.4 2.1 %collective-permute-start.5 = (f32[2,32,1024]{2,1,0:T(8,128)S(1)}, f32[2,32,1024]{2,1,0:T(8,128)S(1)}, u32[]{:S(2)}, u32[]{:S(2)}) collective-permute-start(f32[2,32,1024]{2,1,0:T(8,128)S(1)} %get-tuple-element.66), channel_id=1, source_target_pairs={{0,3},{1,2},{2,1},{3,0},{4,7},{5,6},{6,5},{7,4},{8,11},{9,10},{10,... | collective-permute-start | bytes 786440 | tf_op jit(solution)/shard_map/ppermute | solution.py:512
  24.5 2.6 %collective-permute-start.7 = (f32[1,32,2048]{2,1,0:T(8,128)S(1)}, f32[1,32,2048]{2,1,0:T(8,128)S(1)}, u32[]{:S(2)}, u32[]{:S(2)}) collective-permute-start(f32[1,32,2048]{2,1,0:T(8,128)S(1)} %get-tuple-element.68), channel_id=1, source_target_pairs={{0,28},{4,8},{8,4},{12,16},{16,12},{20,24},{24,20},{28,0},{1,29},{... | collective-permute-start | bytes 786440 | tf_op jit(solution)/shard_map/ppermute | solution.py:513
  27.0 2.1 %local_step.3.refs_2_ = f32[2,32,2048]{2,1,0:T(8,128)S(1)} custom-call(s32[640]{0:T(1024)S(4)} %plan.1.plan_ref.refs_0_, bf16[160,128,256]{2,1,0:T(8,128)(2,1)S(1)} %prep.1.tiles_ref.refs_1_, f32[2,32,2048]{2,1,0:T(8,128)S(1)} %get-tuple-element.64.y_ref.refs_0_, f32[2,32,2048]{2,1,0:T(8,128)S(1)} %get-tuple-element.59.y_ref.refs_0_), custom_call_target="tpu_custom_call" | custom-call | flops 671088640 | bytes 1572864 | tf_op jit(solution)/shard_map/local_step/pallas_call | solution.py:42
  29.1 5.8 %collective-permute-done.4.refs_3_ = f32[2,32,1024]{2,1,0:T(8,128)S(1)} collective-permute-done((f32[2,32,1024]{2,1,0:T(8,128)S(1)}, f32[2,32,1024]{2,1,0:T(8,128)S(1)}, u32[]{:S(2)}, u32[]{:S(2)}) %collective-permute-start.4) | collective-permute-done | bytes 262176 | tf_op jit(solution)/shard_map/ppermute | solution.py:511
  38.7 2.5 %collective-permute-start.11 = (f32[1,32,2048]{2,1,0:T(8,128)S(1)}, f32[1,32,2048]{2,1,0:T(8,128)S(1)}, u32[]{:S(2)}, u32[]{:S(2)}) collective-permute-start(f32[1,32,2048]{2,1,0:T(8,128)S(1)} %get-tuple-element.73), channel_id=1, source_target_pairs={{0,28},{4,8},{8,4},{12,16},{16,12},{20,24},{24,20},{28,0},{1,29},{... | collective-permute-start | bytes 786440 | tf_op jit(solution)/shard_map/ppermute | solution.py:513
  41.2 2.1 %local_gram.1.refs_2_ = f32[2,32,2048]{2,1,0:T(8,128)S(1)} custom-call(s32[640]{0:T(1024)S(4)} %plan.1.plan_ref.refs_0_, bf16[160,128,256]{2,1,0:T(8,128)(2,1)S(1)} %prep.1.tiles_ref.refs_1_, f32[2,32,2048]{2,1,0:T(8,128)S(1)} %get-tuple-element.69.y_ref, f32[2,32,2048]{2,1,0:T(8,128)S(1)} %get-tuple-element.64.y_ref.refs_0_), custom_call_target="tpu_custom_call" | custom-call | flops 671088640 | bytes 1572864 | tf_op jit(solution)/shard_map/local_gram/pallas_call | solution.py:42
  44.6 5.0 %collective-permute-done.9.refs_4_ = f32[2,32,1024]{2,1,0:T(8,128)S(1)} collective-permute-done((f32[2,32,1024]{2,1,0:T(8,128)S(1)}, f32[2,32,1024]{2,1,0:T(8,128)S(1)}, u32[]{:S(2)}, u32[]{:S(2)}) %collective-permute-start.9) | collective-permute-done | bytes 262176 | tf_op jit(solution)/shard_map/ppermute | solution.py:512
  52.3 2.8 %collective-permute-start.15 = (f32[2,32,1024]{2,1,0:T(8,128)S(1)}, f32[2,32,1024]{2,1,0:T(8,128)S(1)}, u32[]{:S(2)}, u32[]{:S(2)}) collective-permute-start(f32[2,32,1024]{2,1,0:T(8,128)S(1)} %get-tuple-element.80), channel_id=1, source_target_pairs={{0,3},{1,2},{2,1},{3,0},{4,7},{5,6},{6,5},{7,4},{8,11},{9,10},{10,... | collective-permute-start | bytes 786440 | tf_op jit(solution)/shard_map/ppermute | solution.py:512
  55.6 2.0 %local_first.3.refs_2_ = f32[2,32,2048]{2,1,0:T(8,128)S(1)} custom-call(s32[640]{0:T(1024)S(4)} %plan.1.plan_ref.refs_0_, bf16[160,128,256]{2,1,0:T(8,128)(2,1)S(1)} %prep.1.tiles_ref.refs_1_, f32[2,32,2048]{2,1,0:T(8,128)S(1)} %get-tuple-element.74.y_ref.refs_0_), custom_call_target="tpu_custom_call" | custom-call | flops 671088640 | bytes 1572864 | tf_op jit(solution)/shard_map/local_first/pallas_call | solution.py:42
  57.6 2.2 %collective-permute-start.12 = (f32[8,128]{1,0:T(8,128)S(1)}, f32[8,128]{1,0:T(8,128)S(1)}, u32[]{:S(2)}, u32[]{:S(2)}) collective-permute-start(f32[8,128]{1,0:T(8,128)S(1)} %get-tuple-element.77), channel_id=1, source_target_pairs={{0,4},{4,0},{8,12},{12,8},{16,20},{20,16},{24,28},{28,24},{1,5},{5... | collective-permute-start | bytes 12296 | tf_op jit(solution)/shard_map/ppermute | solution.py:491
  60.6 3.9 %collective-permute-done.13 = f32[8,128]{1,0:T(8,128)S(1)} collective-permute-done((f32[8,128]{1,0:T(8,128)S(1)}, f32[8,128]{1,0:T(8,128)S(1)}, u32[]{:S(2)}, u32[]{:S(2)}) %collective-permute-start.13) | collective-permute-done | bytes 4128 | tf_op jit(solution)/shard_map/ppermute | solution.py:491
  66.7 3.0 %collective-permute-start.20 = (f32[2,32,1024]{2,1,0:T(8,128)S(1)}, f32[2,32,1024]{2,1,0:T(8,128)S(1)}, u32[]{:S(2)}, u32[]{:S(2)}) collective-permute-start(f32[2,32,1024]{2,1,0:T(8,128)S(1)} %get-tuple-element.89), channel_id=1, source_target_pairs={{0,3},{1,2},{2,1},{3,0},{4,7},{5,6},{6,5},{7,4},{8,11},{9,10},{10,... | collective-permute-start | bytes 786440 | tf_op jit(solution)/shard_map/ppermute | solution.py:512
  69.7 2.5 %collective-permute-start.22 = (f32[1,32,2048]{2,1,0:T(8,128)S(1)}, f32[1,32,2048]{2,1,0:T(8,128)S(1)}, u32[]{:S(2)}, u32[]{:S(2)}) collective-permute-start(f32[1,32,2048]{2,1,0:T(8,128)S(1)} %get-tuple-element.91), channel_id=1, source_target_pairs={{0,28},{4,8},{8,4},{12,16},{16,12},{20,24},{24,20},{28,0},{1,29},{... | collective-permute-start | bytes 786440 | tf_op jit(solution)/shard_map/ppermute | solution.py:513
  72.1 2.0 %local_step.4.refs_2_ = f32[2,32,2048]{2,1,0:T(8,128)S(1)} custom-call(s32[640]{0:T(1024)S(4)} %plan.1.plan_ref.refs_0_, bf16[160,128,256]{2,1,0:T(8,128)(2,1)S(1)} %prep.1.tiles_ref.refs_1_, f32[2,32,2048]{2,1,0:T(8,128)S(1)} %get-tuple-element.83.y_ref.refs_0_, f32[2,32,2048]{2,1,0:T(8,128)S(1)} %get-tuple-element.74.y_ref.refs_0_), custom_call_target="tpu_custom_call" | custom-call | flops 671088640 | bytes 1572864 | tf_op jit(solution)/shard_map/local_step/pallas_call | solution.py:42
  74.4 6.9 %collective-permute-done.18 = f32[8,128]{1,0:T(8,128)S(1)} collective-permute-done((f32[8,128]{1,0:T(8,128)S(1)}, f32[8,128]{1,0:T(8,128)S(1)}, u32[]{:S(2)}, u32[]{:S(2)}) %collective-permute-start.18) | collective-permute-done | bytes 4128 | tf_op jit(solution)/shard_map/ppermute | solution.py:491
  83.0 2.4 %collective-permute-start.25 = (f32[2,32,1024]{2,1,0:T(8,128)S(1)}, f32[2,32,1024]{2,1,0:T(8,128)S(1)}, u32[]{:S(2)}, u32[]{:S(2)}) collective-permute-start(f32[2,32,1024]{2,1,0:T(8,128)S(1)} %get-tuple-element.98), channel_id=1, source_target_pairs={{0,3},{1,2},{2,1},{3,0},{4,7},{5,6},{6,5},{7,4},{8,11},{9,10},{10,... | collective-permute-start | bytes 786440 | tf_op jit(solution)/shard_map/ppermute | solution.py:512
  85.4 2.4 %collective-permute-start.27 = (f32[1,32,2048]{2,1,0:T(8,128)S(1)}, f32[1,32,2048]{2,1,0:T(8,128)S(1)}, u32[]{:S(2)}, u32[]{:S(2)}) collective-permute-start(f32[1,32,2048]{2,1,0:T(8,128)S(1)} %get-tuple-element.100), channel_id=1, source_target_pairs={{0,28},{4,8},{8,4},{12,16},{16,12},{20,24},{24,20},{28,0},{1,29},{... | collective-permute-start | bytes 786440 | tf_op jit(solution)/shard_map/ppermute | solution.py:513
  87.8 2.1 %local_step.5.refs_2_ = f32[2,32,2048]{2,1,0:T(8,128)S(1)} custom-call(s32[640]{0:T(1024)S(4)} %plan.1.plan_ref.refs_0_, bf16[160,128,256]{2,1,0:T(8,128)(2,1)S(1)} %prep.1.tiles_ref.refs_1_, f32[2,32,2048]{2,1,0:T(8,128)S(1)} %get-tuple-element.92.y_ref, f32[2,32,2048]{2,1,0:T(8,128)S(1)} %get-tuple-element.83.y_ref.refs_0_), custom_call_target="tpu_custom_call" | custom-call | flops 671088640 | bytes 1572864 | tf_op jit(solution)/shard_map/local_step/pallas_call | solution.py:42
  90.0 4.6 %collective-permute-done.23 = f32[8,128]{1,0:T(8,128)S(1)} collective-permute-done((f32[8,128]{1,0:T(8,128)S(1)}, f32[8,128]{1,0:T(8,128)S(1)}, u32[]{:S(2)}, u32[]{:S(2)}) %collective-permute-start.23) | collective-permute-done | bytes 4128 | tf_op jit(solution)/shard_map/ppermute | solution.py:491
  98.7 2.3 %collective-permute-start.30 = (f32[2,32,1024]{2,1,0:T(8,128)S(1)}, f32[2,32,1024]{2,1,0:T(8,128)S(1)}, u32[]{:S(2)}, u32[]{:S(2)}) collective-permute-start(f32[2,32,1024]{2,1,0:T(8,128)S(1)} %get-tuple-element.107), channel_id=1, source_target_pairs={{0,3},{1,2},{2,1},{3,0},{4,7},{5,6},{6,5},{7,4},{8,11},{9,10},{10,... | collective-permute-start | bytes 786440 | tf_op jit(solution)/shard_map/ppermute | solution.py:512
  101.0 2.3 %collective-permute-start.32 = (f32[1,32,2048]{2,1,0:T(8,128)S(1)}, f32[1,32,2048]{2,1,0:T(8,128)S(1)}, u32[]{:S(2)}, u32[]{:S(2)}) collective-permute-start(f32[1,32,2048]{2,1,0:T(8,128)S(1)} %get-tuple-element.109), channel_id=1, source_target_pairs={{0,28},{4,8},{8,4},{12,16},{16,12},{20,24},{24,20},{28,0},{1,29},{... | collective-permute-start | bytes 786440 | tf_op jit(solution)/shard_map/ppermute | solution.py:513
  106.5 2.6 %collective-permute-done.28 = f32[8,128]{1,0:T(8,128)S(1)} collective-permute-done((f32[8,128]{1,0:T(8,128)S(1)}, f32[8,128]{1,0:T(8,128)S(1)}, u32[]{:S(2)}, u32[]{:S(2)}) %collective-permute-start.28) | collective-permute-done | bytes 4128 | tf_op jit(solution)/shard_map/ppermute | solution.py:491
  110.5 2.4 %finish_image.1 = (f32[2,32,2048]{2,1,0:T(8,128)S(1)}, f32[16,128]{1,0:T(8,128)S(1)}) custom-call(s32[640]{0:T(1024)S(4)} %plan.1.plan_ref.refs_0_, bf16[160,128,256]{2,1,0:T(8,128)(2,1)S(1)} %prep.1.tiles_ref.refs_1_, f32[2,32,2048]{2,1,0:T(8,128)S(1)} %local_image.1.refs_2_, f32[2,32,1024]{2,1,0:T(8,128)S(1)} %collective-permute-done.29.refs_3_, ...), custom_call_target="tpu_custom_call" | custom-call | flops 268435456 | bytes 3145728 | tf_op jit(solution)/shard_map/finish_image/pallas_call | solution.py:42
  114.1 2.7 %collective-permute-start.36 = (f32[16,128]{1,0:T(8,128)S(1)}, f32[16,128]{1,0:T(8,128)S(1)}, u32[]{:S(2)}, u32[]{:S(2)}) collective-permute-start(f32[16,128]{1,0:T(8,128)S(1)} %add.50), channel_id=1, source_target_pairs={{0,24},{4,28},{8,16},{12,20},{16,8},{20,12},{24,0},{28,4},{1,25},{... | collective-permute-start | bytes 24584 | tf_op jit(solution)/shard_map/ppermute | solution.py:491
  122.9 3.7 %collective-permute-start.37 = (f32[16,128]{1,0:T(8,128)S(1)}, f32[16,128]{1,0:T(8,128)S(1)}, u32[]{:S(2)}, u32[]{:S(2)}) collective-permute-start(f32[16,128]{1,0:T(8,128)S(1)} %add_add_fusion.1), channel_id=1, source_target_pairs={{0,1},{1,0},{2,3},{3,2},{4,5},{5,4},{6,7},{7,6},{8,9},{9,8},{10,11... | collective-permute-start | bytes 24584 | tf_op jit(solution)/shard_map/ppermute | solution.py:491
  128.2 2.5 %close.1 = (f32[2,32,2048]{2,1,0:T(8,128)}, f32[32,32]{1,0:T(8,128)}) custom-call(f32[16,128]{1,0:T(8,128)S(1)} %add_add_fusion.sums_ref, f32[2,32,2048]{2,1,0:T(8,128)S(1)} %get-tuple-element.112.y_ref), custom_call_target="tpu_custom_call" | custom-call | flops 8388608 | bytes 1048576 | tf_op jit(solution)/shard_map/close/pallas_call | solution.py:42
  (81 shorter events, 34.9 us)
Async XLA Ops:
  2.4 18.1 %collective-permute-start = (f32[2,32,1024]{2,1,0:T(8,128)S(1)}, f32[2,32,1024]{2,1,0:T(8,128)S(1)}, u32[]{:S(2)}, u32[]{:S(2)}) collective-permute-start(f32[2,32,1024]{2,1,0:T(8,128)S(1)} %get-tuple-element.60), channel_id=1, source_target_pairs={{0,1},{1,0},{2,3},{3,2},{4,5},{5,4},{6,7},{7,6},{8,9},{9,8},{10,11... | collective-permute-start | bytes 786440 | tf_op jit(solution)/shard_map/ppermute | solution.py:511
  5.5 15.0 %collective-permute-start.1 = (f32[2,32,1024]{2,1,0:T(8,128)S(1)}, f32[2,32,1024]{2,1,0:T(8,128)S(1)}, u32[]{:S(2)}, u32[]{:S(2)}) collective-permute-start(f32[2,32,1024]{2,1,0:T(8,128)S(1)} %get-tuple-element.61), channel_id=1, source_target_pairs={{0,3},{1,2},{2,1},{3,0},{4,7},{5,6},{6,5},{7,4},{8,11},{9,10},{10,... | collective-permute-start | bytes 786440 | tf_op jit(solution)/shard_map/ppermute | solution.py:512
  8.0 12.5 %collective-permute-start.2 = (f32[1,32,2048]{2,1,0:T(8,128)S(1)}, f32[1,32,2048]{2,1,0:T(8,128)S(1)}, u32[]{:S(2)}, u32[]{:S(2)}) collective-permute-start(f32[1,32,2048]{2,1,0:T(8,128)S(1)} %get-tuple-element.62), channel_id=1, source_target_pairs={{0,4},{4,0},{8,12},{12,8},{16,20},{20,16},{24,28},{28,24},{1,5},{5... | collective-permute-start | bytes 786440 | tf_op jit(solution)/shard_map/ppermute | solution.py:514
  8.0 12.6 %collective-permute-start.3 = (f32[1,32,2048]{2,1,0:T(8,128)S(1)}, f32[1,32,2048]{2,1,0:T(8,128)S(1)}, u32[]{:S(2)}, u32[]{:S(2)}) collective-permute-start(f32[1,32,2048]{2,1,0:T(8,128)S(1)} %get-tuple-element.63), channel_id=1, source_target_pairs={{0,28},{4,8},{8,4},{12,16},{16,12},{20,24},{24,20},{28,0},{1,29},{... | collective-permute-start | bytes 786440 | tf_op jit(solution)/shard_map/ppermute | solution.py:513
  22.0 12.9 %collective-permute-start.4 = (f32[2,32,1024]{2,1,0:T(8,128)S(1)}, f32[2,32,1024]{2,1,0:T(8,128)S(1)}, u32[]{:S(2)}, u32[]{:S(2)}) collective-permute-start(f32[2,32,1024]{2,1,0:T(8,128)S(1)} %get-tuple-element.65), channel_id=1, source_target_pairs={{0,1},{1,0},{2,3},{3,2},{4,5},{5,4},{6,7},{7,6},{8,9},{9,8},{10,11... | collective-permute-start | bytes 786440 | tf_op jit(solution)/shard_map/ppermute | solution.py:511
  22.4 12.6 %collective-permute-start.5 = (f32[2,32,1024]{2,1,0:T(8,128)S(1)}, f32[2,32,1024]{2,1,0:T(8,128)S(1)}, u32[]{:S(2)}, u32[]{:S(2)}) collective-permute-start(f32[2,32,1024]{2,1,0:T(8,128)S(1)} %get-tuple-element.66), channel_id=1, source_target_pairs={{0,3},{1,2},{2,1},{3,0},{4,7},{5,6},{6,5},{7,4},{8,11},{9,10},{10,... | collective-permute-start | bytes 786440 | tf_op jit(solution)/shard_map/ppermute | solution.py:512
  24.5 10.5 %collective-permute-start.6 = (f32[1,32,2048]{2,1,0:T(8,128)S(1)}, f32[1,32,2048]{2,1,0:T(8,128)S(1)}, u32[]{:S(2)}, u32[]{:S(2)}) collective-permute-start(f32[1,32,2048]{2,1,0:T(8,128)S(1)} %get-tuple-element.67), channel_id=1, source_target_pairs={{0,4},{4,0},{8,12},{12,8},{16,20},{20,16},{24,28},{28,24},{1,5},{5... | collective-permute-start | bytes 786440 | tf_op jit(solution)/shard_map/ppermute | solution.py:514
  24.5 10.5 %collective-permute-start.7 = (f32[1,32,2048]{2,1,0:T(8,128)S(1)}, f32[1,32,2048]{2,1,0:T(8,128)S(1)}, u32[]{:S(2)}, u32[]{:S(2)}) collective-permute-start(f32[1,32,2048]{2,1,0:T(8,128)S(1)} %get-tuple-element.68), channel_id=1, source_target_pairs={{0,28},{4,8},{8,4},{12,16},{16,12},{20,24},{24,20},{28,0},{1,29},{... | collective-permute-start | bytes 786440 | tf_op jit(solution)/shard_map/ppermute | solution.py:513
  36.4 8.2 %collective-permute-start.8 = (f32[2,32,1024]{2,1,0:T(8,128)S(1)}, f32[2,32,1024]{2,1,0:T(8,128)S(1)}, u32[]{:S(2)}, u32[]{:S(2)}) collective-permute-start(f32[2,32,1024]{2,1,0:T(8,128)S(1)} %get-tuple-element.70), channel_id=1, source_target_pairs={{0,1},{1,0},{2,3},{3,2},{4,5},{5,4},{6,7},{7,6},{8,9},{9,8},{10,11... | collective-permute-start | bytes 786440 | tf_op jit(solution)/shard_map/ppermute | solution.py:511
  37.8 11.9 %collective-permute-start.9 = (f32[2,32,1024]{2,1,0:T(8,128)S(1)}, f32[2,32,1024]{2,1,0:T(8,128)S(1)}, u32[]{:S(2)}, u32[]{:S(2)}) collective-permute-start(f32[2,32,1024]{2,1,0:T(8,128)S(1)} %get-tuple-element.71), channel_id=1, source_target_pairs={{0,3},{1,2},{2,1},{3,0},{4,7},{5,6},{6,5},{7,4},{8,11},{9,10},{10,... | collective-permute-start | bytes 786440 | tf_op jit(solution)/shard_map/ppermute | solution.py:512
  38.7 11.0 %collective-permute-start.10 = (f32[1,32,2048]{2,1,0:T(8,128)S(1)}, f32[1,32,2048]{2,1,0:T(8,128)S(1)}, u32[]{:S(2)}, u32[]{:S(2)}) collective-permute-start(f32[1,32,2048]{2,1,0:T(8,128)S(1)} %get-tuple-element.72), channel_id=1, source_target_pairs={{0,4},{4,0},{8,12},{12,8},{16,20},{20,16},{24,28},{28,24},{1,5},{5... | collective-permute-start | bytes 786440 | tf_op jit(solution)/shard_map/ppermute | solution.py:514
  38.7 11.0 %collective-permute-start.11 = (f32[1,32,2048]{2,1,0:T(8,128)S(1)}, f32[1,32,2048]{2,1,0:T(8,128)S(1)}, u32[]{:S(2)}, u32[]{:S(2)}) collective-permute-start(f32[1,32,2048]{2,1,0:T(8,128)S(1)} %get-tuple-element.73), channel_id=1, source_target_pairs={{0,28},{4,8},{8,4},{12,16},{16,12},{20,24},{24,20},{28,0},{1,29},{... | collective-permute-start | bytes 786440 | tf_op jit(solution)/shard_map/ppermute | solution.py:513
  51.6 12.9 %collective-permute-start.14 = (f32[2,32,1024]{2,1,0:T(8,128)S(1)}, f32[2,32,1024]{2,1,0:T(8,128)S(1)}, u32[]{:S(2)}, u32[]{:S(2)}) collective-permute-start(f32[2,32,1024]{2,1,0:T(8,128)S(1)} %get-tuple-element.79), channel_id=1, source_target_pairs={{0,1},{1,0},{2,3},{3,2},{4,5},{5,4},{6,7},{7,6},{8,9},{9,8},{10,11... | collective-permute-start | bytes 786440 | tf_op jit(solution)/shard_map/ppermute | solution.py:511
  52.3 12.4 %collective-permute-start.15 = (f32[2,32,1024]{2,1,0:T(8,128)S(1)}, f32[2,32,1024]{2,1,0:T(8,128)S(1)}, u32[]{:S(2)}, u32[]{:S(2)}) collective-permute-start(f32[2,32,1024]{2,1,0:T(8,128)S(1)} %get-tuple-element.80), channel_id=1, source_target_pairs={{0,3},{1,2},{2,1},{3,0},{4,7},{5,6},{6,5},{7,4},{8,11},{9,10},{10,... | collective-permute-start | bytes 786440 | tf_op jit(solution)/shard_map/ppermute | solution.py:512
  55.0 9.7 %collective-permute-start.16 = (f32[1,32,2048]{2,1,0:T(8,128)S(1)}, f32[1,32,2048]{2,1,0:T(8,128)S(1)}, u32[]{:S(2)}, u32[]{:S(2)}) collective-permute-start(f32[1,32,2048]{2,1,0:T(8,128)S(1)} %get-tuple-element.81), channel_id=1, source_target_pairs={{0,4},{4,0},{8,12},{12,8},{16,20},{20,16},{24,28},{28,24},{1,5},{5... | collective-permute-start | bytes 786440 | tf_op jit(solution)/shard_map/ppermute | solution.py:514
  55.0 9.7 %collective-permute-start.17 = (f32[1,32,2048]{2,1,0:T(8,128)S(1)}, f32[1,32,2048]{2,1,0:T(8,128)S(1)}, u32[]{:S(2)}, u32[]{:S(2)}) collective-permute-start(f32[1,32,2048]{2,1,0:T(8,128)S(1)} %get-tuple-element.82), channel_id=1, source_target_pairs={{0,28},{4,8},{8,4},{12,16},{16,12},{20,24},{24,20},{28,0},{1,29},{... | collective-permute-start | bytes 786440 | tf_op jit(solution)/shard_map/ppermute | solution.py:513
  66.3 15.0 %collective-permute-start.19 = (f32[2,32,1024]{2,1,0:T(8,128)S(1)}, f32[2,32,1024]{2,1,0:T(8,128)S(1)}, u32[]{:S(2)}, u32[]{:S(2)}) collective-permute-start(f32[2,32,1024]{2,1,0:T(8,128)S(1)} %get-tuple-element.88), channel_id=1, source_target_pairs={{0,1},{1,0},{2,3},{3,2},{4,5},{5,4},{6,7},{7,6},{8,9},{9,8},{10,11... | collective-permute-start | bytes 786440 | tf_op jit(solution)/shard_map/ppermute | solution.py:511
  66.7 14.7 %collective-permute-start.20 = (f32[2,32,1024]{2,1,0:T(8,128)S(1)}, f32[2,32,1024]{2,1,0:T(8,128)S(1)}, u32[]{:S(2)}, u32[]{:S(2)}) collective-permute-start(f32[2,32,1024]{2,1,0:T(8,128)S(1)} %get-tuple-element.89), channel_id=1, source_target_pairs={{0,3},{1,2},{2,1},{3,0},{4,7},{5,6},{6,5},{7,4},{8,11},{9,10},{10,... | collective-permute-start | bytes 786440 | tf_op jit(solution)/shard_map/ppermute | solution.py:512
  69.7 11.7 %collective-permute-start.21 = (f32[1,32,2048]{2,1,0:T(8,128)S(1)}, f32[1,32,2048]{2,1,0:T(8,128)S(1)}, u32[]{:S(2)}, u32[]{:S(2)}) collective-permute-start(f32[1,32,2048]{2,1,0:T(8,128)S(1)} %get-tuple-element.90), channel_id=1, source_target_pairs={{0,4},{4,0},{8,12},{12,8},{16,20},{20,16},{24,28},{28,24},{1,5},{5... | collective-permute-start | bytes 786440 | tf_op jit(solution)/shard_map/ppermute | solution.py:514
  69.7 11.7 %collective-permute-start.22 = (f32[1,32,2048]{2,1,0:T(8,128)S(1)}, f32[1,32,2048]{2,1,0:T(8,128)S(1)}, u32[]{:S(2)}, u32[]{:S(2)}) collective-permute-start(f32[1,32,2048]{2,1,0:T(8,128)S(1)} %get-tuple-element.91), channel_id=1, source_target_pairs={{0,28},{4,8},{8,4},{12,16},{16,12},{20,24},{24,20},{28,0},{1,29},{... | collective-permute-start | bytes 786440 | tf_op jit(solution)/shard_map/ppermute | solution.py:513
  74.2 7.2 %collective-permute-start.18 = (f32[8,128]{1,0:T(8,128)S(1)}, f32[8,128]{1,0:T(8,128)S(1)}, u32[]{:S(2)}, u32[]{:S(2)}) collective-permute-start(f32[8,128]{1,0:T(8,128)S(1)} %add.46), channel_id=1, source_target_pairs={{0,2},{1,3},{2,0},{3,1},{4,6},{5,7},{6,4},{7,5},{8,10},{9,11},{10,... | collective-permute-start | bytes 12296 | tf_op jit(solution)/shard_map/ppermute | solution.py:491
  82.8 11.7 %collective-permute-start.24 = (f32[2,32,1024]{2,1,0:T(8,128)S(1)}, f32[2,32,1024]{2,1,0:T(8,128)S(1)}, u32[]{:S(2)}, u32[]{:S(2)}) collective-permute-start(f32[2,32,1024]{2,1,0:T(8,128)S(1)} %get-tuple-element.97), channel_id=1, source_target_pairs={{0,1},{1,0},{2,3},{3,2},{4,5},{5,4},{6,7},{7,6},{8,9},{9,8},{10,11... | collective-permute-start | bytes 786440 | tf_op jit(solution)/shard_map/ppermute | solution.py:511
  83.0 13.2 %collective-permute-start.25 = (f32[2,32,1024]{2,1,0:T(8,128)S(1)}, f32[2,32,1024]{2,1,0:T(8,128)S(1)}, u32[]{:S(2)}, u32[]{:S(2)}) collective-permute-start(f32[2,32,1024]{2,1,0:T(8,128)S(1)} %get-tuple-element.98), channel_id=1, source_target_pairs={{0,3},{1,2},{2,1},{3,0},{4,7},{5,6},{6,5},{7,4},{8,11},{9,10},{10,... | collective-permute-start | bytes 786440 | tf_op jit(solution)/shard_map/ppermute | solution.py:512
  85.4 10.8 %collective-permute-start.26 = (f32[1,32,2048]{2,1,0:T(8,128)S(1)}, f32[1,32,2048]{2,1,0:T(8,128)S(1)}, u32[]{:S(2)}, u32[]{:S(2)}) collective-permute-start(f32[1,32,2048]{2,1,0:T(8,128)S(1)} %get-tuple-element.99), channel_id=1, source_target_pairs={{0,4},{4,0},{8,12},{12,8},{16,20},{20,16},{24,28},{28,24},{1,5},{5... | collective-permute-start | bytes 786440 | tf_op jit(solution)/shard_map/ppermute | solution.py:514
  85.4 10.8 %collective-permute-start.27 = (f32[1,32,2048]{2,1,0:T(8,128)S(1)}, f32[1,32,2048]{2,1,0:T(8,128)S(1)}, u32[]{:S(2)}, u32[]{:S(2)}) collective-permute-start(f32[1,32,2048]{2,1,0:T(8,128)S(1)} %get-tuple-element.100), channel_id=1, source_target_pairs={{0,28},{4,8},{8,4},{12,16},{16,12},{20,24},{24,20},{28,0},{1,29},{... | collective-permute-start | bytes 786440 | tf_op jit(solution)/shard_map/ppermute | solution.py:513
  97.6 12.9 %collective-permute-start.29 = (f32[2,32,1024]{2,1,0:T(8,128)S(1)}, f32[2,32,1024]{2,1,0:T(8,128)S(1)}, u32[]{:S(2)}, u32[]{:S(2)}) collective-permute-start(f32[2,32,1024]{2,1,0:T(8,128)S(1)} %get-tuple-element.106), channel_id=1, source_target_pairs={{0,1},{1,0},{2,3},{3,2},{4,5},{5,4},{6,7},{7,6},{8,9},{9,8},{10,11... | collective-permute-start | bytes 786440 | tf_op jit(solution)/shard_map/ppermute | solution.py:511
  98.7 11.8 %collective-permute-start.30 = (f32[2,32,1024]{2,1,0:T(8,128)S(1)}, f32[2,32,1024]{2,1,0:T(8,128)S(1)}, u32[]{:S(2)}, u32[]{:S(2)}) collective-permute-start(f32[2,32,1024]{2,1,0:T(8,128)S(1)} %get-tuple-element.107), channel_id=1, source_target_pairs={{0,3},{1,2},{2,1},{3,0},{4,7},{5,6},{6,5},{7,4},{8,11},{9,10},{10,... | collective-permute-start | bytes 786440 | tf_op jit(solution)/shard_map/ppermute | solution.py:512
  101.0 9.5 %collective-permute-start.31 = (f32[1,32,2048]{2,1,0:T(8,128)S(1)}, f32[1,32,2048]{2,1,0:T(8,128)S(1)}, u32[]{:S(2)}, u32[]{:S(2)}) collective-permute-start(f32[1,32,2048]{2,1,0:T(8,128)S(1)} %get-tuple-element.108), channel_id=1, source_target_pairs={{0,4},{4,0},{8,12},{12,8},{16,20},{20,16},{24,28},{28,24},{1,5},{5... | collective-permute-start | bytes 786440 | tf_op jit(solution)/shard_map/ppermute | solution.py:514
  101.0 9.5 %collective-permute-start.32 = (f32[1,32,2048]{2,1,0:T(8,128)S(1)}, f32[1,32,2048]{2,1,0:T(8,128)S(1)}, u32[]{:S(2)}, u32[]{:S(2)}) collective-permute-start(f32[1,32,2048]{2,1,0:T(8,128)S(1)} %get-tuple-element.109), channel_id=1, source_target_pairs={{0,28},{4,8},{8,4},{12,16},{16,12},{20,24},{24,20},{28,0},{1,29},{... | collective-permute-start | bytes 786440 | tf_op jit(solution)/shard_map/ppermute | solution.py:513
  122.2 5.5 %collective-permute-start.39 = (f32[16,128]{1,0:T(8,128)S(1)}, f32[16,128]{1,0:T(8,128)S(1)}, u32[]{:S(2)}, u32[]{:S(2)}) collective-permute-start(f32[16,128]{1,0:T(8,128)S(1)} %add_add_fusion.1), channel_id=1, source_target_pairs={{0,3},{1,2},{2,1},{3,0},{4,7},{5,6},{6,5},{7,4},{8,11},{9,10},{10,... | collective-permute-start | bytes 24584 | tf_op jit(solution)/shard_map/ppermute | solution.py:491
  122.4 5.3 %collective-permute-start.38 = (f32[16,128]{1,0:T(8,128)S(1)}, f32[16,128]{1,0:T(8,128)S(1)}, u32[]{:S(2)}, u32[]{:S(2)}) collective-permute-start(f32[16,128]{1,0:T(8,128)S(1)} %add_add_fusion.1), channel_id=1, source_target_pairs={{0,2},{1,3},{2,0},{3,1},{4,6},{5,7},{6,4},{7,5},{8,10},{9,11},{10,... | collective-permute-start | bytes 24584 | tf_op jit(solution)/shard_map/ppermute | solution.py:491
  122.9 5.3 %collective-permute-start.37 = (f32[16,128]{1,0:T(8,128)S(1)}, f32[16,128]{1,0:T(8,128)S(1)}, u32[]{:S(2)}, u32[]{:S(2)}) collective-permute-start(f32[16,128]{1,0:T(8,128)S(1)} %add_add_fusion.1), channel_id=1, source_target_pairs={{0,1},{1,0},{2,3},{3,2},{4,5},{5,4},{6,7},{7,6},{8,9},{9,8},{10,11... | collective-permute-start | bytes 24584 | tf_op jit(solution)/shard_map/ppermute | solution.py:491
  (10 other events, 30.1 us)

commit v7 on v6

v7 whole, which is shorter than its diff:
```python
import functools

import jax
import jax.numpy as jnp
from jax import lax
from jax.experimental import pallas as pl
from jax.experimental.pallas import tpu as pltpu
from jax.sharding import PartitionSpec as P

TILE = 128
TPR = 5
HB = 8
CENTER = 6.5
RADIUS = 3.5
INFLATION_FACTOR = 0.8
GROUP = 8

F32 = jnp.float32
BF16 = jnp.bfloat16
VM = pltpu.VMEM
NT = (((1,), (1,)), ((), ()))
NN = (((1,), (0,)), ((), ()))
WHOLE = pl.BlockSpec(memory_space=VM)
SCALARS = pl.BlockSpec(memory_space=pltpu.SMEM)


def near(x):
    return pltpu.with_memory_space_constraint(x, VM)


def split(x):
    high = x.astype(BF16)
    return high, (x - high.astype(F32)).astype(BF16)


def stacked(x):
    return jnp.concatenate(split(x), axis=0)


def call(kernel, ins, outs, scratch=(), specs=None, flops=0, moved=0, name=None, out_vmem=True, aliases=None):
    out_shape = [VM(s, d) if out_vmem else jax.ShapeDtypeStruct(s, d) for s, d in outs]
    return pl.pallas_call(
        kernel,
        out_shape=out_shape,
        in_specs=specs,
        out_specs=[WHOLE] * len(outs),
        scratch_shapes=list(scratch),
        name=name,
        input_output_aliases=aliases or {},
        cost_estimate=pl.CostEstimate(flops=flops, bytes_accessed=moved, transcendentals=0),
        compiler_params=pltpu.CompilerParams(vmem_limit_bytes=6 << 20),
    )(*ins)


def prep_kernel(tiles_ref, out_ref, buffer_ref, semaphores):
    slots, step = buffer_ref.shape[:2]
    chunks = tiles_ref.shape[0] // step

    def copy(c):
        slot = lax.rem(c, slots)
        return pltpu.make_async_copy(
            tiles_ref.at[pl.ds(c * step, step)], buffer_ref.at[slot], semaphores.at[slot]
        )

    for c in range(slots):
        copy(c).start()

    def chunk(c, carry):
        copy(c).wait()
        slot = lax.rem(c, slots)
        for n in range(step):
            high, low = split(buffer_ref[slot, n].T)
            out_ref[c * step + n, :, :TILE] = high
            out_ref[c * step + n, :, TILE:] = low

        @pl.when(c + slots < chunks)
        def _():
            copy(c + slots).start()

        return carry

    lax.fori_loop(0, chunks, chunk, 0)


def prep(tiles):
    tiles = tiles.reshape(-1, TILE, TILE)
    slots, step = 5, 16
    return pl.pallas_call(
        prep_kernel,
        out_shape=VM((tiles.shape[0], TILE, 2 * TILE), BF16),
        in_specs=[pl.BlockSpec(memory_space=pltpu.HBM)],
        out_specs=WHOLE,
        scratch_shapes=[VM((slots, step, TILE, TILE), F32), pltpu.SemaphoreType.DMA((slots,))],
        name="prep",
        cost_estimate=pl.CostEstimate(flops=0, bytes_accessed=4 * tiles.size, transcendentals=0),
        compiler_params=pltpu.CompilerParams(vmem_limit_bytes=8 << 20),
    )(pltpu.with_memory_space_constraint(tiles, pltpu.HBM))


class Layout:
    def __init__(self, slices, blocks):
        self.half = blocks // 2
        self.room = slices * self.half * (TPR // 2) + GROUP + 2
        self.rows = slices * blocks * TPR
        self.tiles = self.rows + 2 * self.room
        self.places = self.tiles + 4 * self.room
        self.groups = self.places + 4 * self.room
        self.flags = self.groups + 2
        self.size = -(-(self.flags + 4) // 128) * 128


def plan_kernel(blocks_all, columns_ref, flags_ref, out_ref):
    slices, count = columns_ref.shape
    blocks = count // TPR
    at = Layout(slices, blocks)
    for i in range(4):
        out_ref[at.flags + i] = flags_ref[i]
    first_block = flags_ref[4]
    here = slices * blocks
    zero = slices * HB
    for side in range(2):
        rows = at.rows + side * at.room
        tiles = at.tiles + side * 2 * at.room
        places = at.places + side * 2 * at.room
        units = jnp.int32(0)
        for s in range(slices):

            def row(k, units, s=s, side=side, rows=rows, tiles=tiles, places=places):
                r = side * at.half + k
                i = s * blocks + r
                out_ref[rows + units] = s * at.half + k
                out_ref[rows + units + 1] = s * at.half + k
                found = jnp.int32(0)
                for n in range(TPR):
                    where = columns_ref[s, r * TPR + n] - first_block + HB
                    where = jnp.where(where < 0, where + blocks_all, where)
                    where = jnp.where(where >= blocks_all, where - blocks_all, where)
                    away = where >= HB + blocks if side else where < HB
                    out_ref[i * TPR + n] = jnp.where(away, here, s * blocks + where - HB)
                    if n > 0:
                        out_ref[tiles + 2 * units + found] = i * TPR + n
                        out_ref[places + 2 * units + found] = s * HB + where - side * (HB + blocks)
                        found = found + away.astype(jnp.int32)
                out_ref[tiles + 2 * units + found] = i * TPR
                out_ref[places + 2 * units + found] = zero
                return units + (found + 1) // 2

            units = lax.fori_loop(0, at.half, row, units, unroll=4)
        for n in range(GROUP):
            out_ref[rows + units + n] = 0
            for k in range(2):
                out_ref[tiles + 2 * (units + n) + k] = 0
                out_ref[places + 2 * (units + n) + k] = zero
        out_ref[at.groups + side] = (units + GROUP - 1) // GROUP


def plan(columns, flags, blocks_all):
    slices, count = columns.shape
    size = Layout(slices, count // TPR).size
    return pl.pallas_call(
        functools.partial(plan_kernel, blocks_all),
        out_shape=pltpu.SMEM((size,), jnp.int32),
        in_specs=[SCALARS, SCALARS],
        out_specs=SCALARS,
        name="plan",
        compiler_params=pltpu.CompilerParams(vmem_limit_bytes=1 << 20),
    )(columns, flags)


def slice_ends(odd, left_ref, right_ref, near_ref, far_ref):
    half = left_ref.shape[2]
    last = left_ref.shape[0] - 1

    def fill(ref, s):
        ref[0, :, :half] = left_ref[s]
        ref[0, :, half:] = right_ref[s]

    @pl.when(odd == 0)
    def _():
        fill(near_ref, last)
        fill(far_ref, 0)

    @pl.when(odd != 0)
    def _():
        fill(near_ref, 0)
        fill(far_ref, last)


def start_kernel(odd_ref, x_ref, left_ref, right_ref, near_ref, far_ref):
    half = left_ref.shape[2]
    left_ref[...] = x_ref[:, :, :half]
    right_ref[...] = x_ref[:, :, half:]
    slice_ends(odd_ref[1], left_ref, right_ref, near_ref, far_ref)


def start(odd, block):
    slices, width, points = block.shape
    half = ((slices, width, points // 2), F32)
    whole = ((1, width, points), F32)
    return call(
        start_kernel,
        [odd, block],
        [half, half, whole, whole],
        specs=[SCALARS, WHOLE],
        moved=16 * block.size,
        name="start",
    )


def fold(product, width):
    return product[:width, :TILE] + product[:width, TILE:] + product[width:, :TILE]


def product(halves, tiles, width):
    left = jnp.concatenate(halves, axis=1)
    right = jnp.concatenate(tiles, axis=0)
    return fold(lax.dot_general(left, right, NN, preferred_element_type=F32), width)


def local_kernel(mode, scale, plan_ref, tiles_ref, *refs):
    y_refs, refs = refs[:2], refs[2:]
    previous_refs, (left_ref, right_ref, halves_ref) = refs[:-3], refs[-3:]
    slices, width, points = left_ref.shape
    half = points // TILE
    blocks = 2 * half
    at = Layout(slices, blocks)
    for s in range(slices):
        for b in range(blocks):
            k = b % half
            halves_ref[s * blocks + b] = stacked(y_refs[b // half][s, :, k * TILE : (k + 1) * TILE])
    halves_ref[slices * blocks] = jnp.zeros((2 * width, TILE), BF16)

    for s in range(slices):
        degree = 2.0
        if s == 0:
            degree = degree - jnp.where(plan_ref[at.flags + 2] != 0, 1.0, 0.0)
        if s == slices - 1:
            degree = degree - jnp.where(plan_ref[at.flags + 3] != 0, 1.0, 0.0)
        for side, out_ref in enumerate((left_ref, right_ref)):

            def row(k, carry, s=s, side=side, out_ref=out_ref, degree=degree):
                i = s * blocks + side * half + k
                halves = [halves_ref[plan_ref[i * TPR + n]] for n in range(TPR)]
                tiles = [tiles_ref[i * TPR + n] for n in range(TPR)]
                here = pl.ds(pl.multiple_of(k * TILE, TILE), TILE)
                y_ref = y_refs[side]
                y = y_ref[s, :, here]
                time = degree * y
                if s > 0:
                    time = time - y_ref[s - 1, :, here]
                if s < slices - 1:
                    time = time - y_ref[s + 1, :, here]
                image = product(halves, tiles, width) + INFLATION_FACTOR * time
                if mode != "image":
                    image = (image - CENTER * y) * scale
                if previous_refs:
                    image = image - previous_refs[side][s, :, here]
                out_ref[s, :, here] = image
                return carry

            lax.fori_loop(0, half, row, 0, unroll=8)


def local_part(mode, scale, table, tiles, ys, previous):
    slices, width, points = ys[0].shape
    rows = 2 * slices * points // TILE
    ins = [table, near(tiles)] + [near(y) for y in ys] + [near(y) for y in previous or ()]
    return call(
        functools.partial(local_kernel, mode, scale),
        ins,
        [(ys[0].shape, F32)] * 2,
        specs=[SCALARS] + [WHOLE] * (len(ins) - 1),
        scratch=[VM((rows + 1, 2 * width, TILE), BF16)],
        flops=2 * rows * TPR * 4 * width * TILE * TILE,
        moved=24 * ys[0].size,
        name="local_" + mode,
    )


def mix(matrix, y):
    high, low = split(matrix)
    y_high, y_low = split(y)
    left = jnp.concatenate([high, low, high], axis=1)
    right = jnp.concatenate([y_high, y_high, y_low], axis=0)
    return lax.dot_general(left, right, NN, preferred_element_type=F32)


def inner(left, right):
    width = left.shape[0]
    p = lax.dot_general(stacked(left), stacked(right), NT, preferred_element_type=F32)
    return (p[:width, :width] + p[width:, width:]) + (p[:width, width:] + p[width:, :width])


def side_kernel(side, second, mode, scale, plan_ref, tiles_ref, part_ref, halo_ref, near_ref, far_ref, *refs):
    refs = list(refs)
    halves_ref = refs.pop()
    slices, width, points = part_ref.shape
    half = points // TILE
    at = Layout(slices, 2 * half)
    inputs = 0
    if second:
        inputs = 4 if mode == "image" else 1
    given, (new_ref, *out_refs) = refs[:inputs], refs[inputs:]
    for s in range(slices):
        for b in range(HB):
            halves_ref[s * HB + b] = stacked(halo_ref[s, :, b * TILE : (b + 1) * TILE])
    halves_ref[slices * HB] = jnp.zeros((2 * width, TILE), BF16)

    here = slice(side * points, (side + 1) * points)
    time_odd = plan_ref[at.flags + 1] != 0
    factor = INFLATION_FACTOR * scale
    for s in range(slices):
        image = part_ref[s]
        if s == 0:
            before = jnp.where(time_odd, near_ref[0, :, here], far_ref[0, :, here])
            image = image - jnp.where(plan_ref[at.flags + 2] != 0, 0.0, factor * before)
        if s == slices - 1:
            after = jnp.where(time_odd, far_ref[0, :, here], near_ref[0, :, here])
            image = image - jnp.where(plan_ref[at.flags + 3] != 0, 0.0, factor * after)
        new_ref[s] = image

    rows = at.rows + side * at.room
    tiles_at = at.tiles + side * 2 * at.room
    places = at.places + side * 2 * at.room

    def group(g, carry):
        done = []
        for k in range(GROUP):
            u = g * GROUP + k
            halves = [halves_ref[plan_ref[places + 2 * u + j]] for j in range(2)]
            tiles = [tiles_ref[plan_ref[tiles_at + 2 * u + j]] for j in range(2)]
            done.append((plan_ref[rows + u], product(halves, tiles, width)))
        for i, value in done:
            to = pl.ds(pl.multiple_of((i % half) * TILE, TILE), TILE)
            new_ref[i // half, :, to] += scale * value
        return carry

    lax.fori_loop(0, plan_ref[at.groups + side], group, 0)

    pair = (lambda other: (new_ref, other)) if side == 0 else (lambda other: (other, new_ref))
    if second and mode == "image":
        image_ref, left_ref, right_ref, matrix_ref = given
        mixed_ref, gram_ref = out_refs
        matrix = matrix_ref[...]
        gram, product_sum = 0.0, 0.0
        images = pair(image_ref)
        for s in range(slices):
            for k, y_ref in enumerate((left_ref, right_ref)):
                mixed = mix(matrix, y_ref[s])
                mixed_ref[s, :, k * points : (k + 1) * points] = mixed
                gram = gram + inner(mixed, mixed)
                product_sum = product_sum + inner(mixed, mix(matrix, images[k][s]))
        gram_ref[...] = folded(gram, product_sum)
    elif second:
        slice_ends(plan_ref[at.flags + 1], *pair(given[0]), *out_refs[:2])
        out_refs = out_refs[2:]
        if mode == "gram":
            gram = sum(inner(y[s], y[s]) for y in (given[0], new_ref) for s in range(slices))
            gram_ref = out_refs.pop(0)
            gram_ref[...] = folded(gram)
    if mode != "image" and out_refs:
        side_points = HB * TILE
        start = points - side_points if side else 0
        out_refs[0][...] = new_ref[:, :, start : start + side_points]


def folded(*matrices):
    width = matrices[0].shape[0]
    rows = width * width * len(matrices) // TILE
    flat = jnp.concatenate(matrices, axis=0)
    return jnp.concatenate([flat[i : i + rows] for i in range(0, flat.shape[0], rows)], axis=1)


def unfolded(block, width):
    rows = block.shape[0]
    flat = jnp.concatenate([block[:, i : i + width] for i in range(0, TILE, width)], axis=0)
    return [flat[i : i + width] for i in range(0, flat.shape[0], width)]


def finish(side, second, mode, scale, table, tiles, part, halo, ends, given=()):
    slices, width, points = part.shape
    ins = [table] + [near(v) for v in (tiles, part, halo, *ends, *given)]
    outs = [(part.shape, F32)]
    whole = (slices, width, 2 * points)
    if second and mode == "image":
        outs += [(whole, F32), ((2 * width * width // TILE, TILE), F32)]
    elif second:
        outs += [((1, width, 2 * points), F32)] * 2
        if mode == "gram":
            outs.append(((width * width // TILE, TILE), F32))
    if mode != "image" and points != HB * TILE:
        outs.append(((slices, width, HB * TILE), F32))
    return call(
        functools.partial(side_kernel, side, second, mode, scale),
        ins,
        outs,
        scratch=[VM((slices * HB + 1, 2 * width, TILE), BF16)],
        specs=[SCALARS] + [WHOLE] * (len(ins) - 1),
        flops=2 * slices * points * 4 * width * TILE * 2,
        moved=24 * part.size,
        name=("left_", "right_")[side] + mode,
        aliases={2: 0},
    )


def inverse_factor(gram):
    width = gram.shape[0]
    square = (width, width)
    rows = lax.broadcasted_iota(jnp.int32, square, 0)
    columns = lax.broadcasted_iota(jnp.int32, square, 1)
    inverse = (rows == columns).astype(F32)
    column = jnp.broadcast_to(gram[:, :1], square)
    for j in range(width - 1):
        following = jnp.broadcast_to(gram[:, j + 1 : j + 2], square)
        scaled = jnp.where(rows > j, column, 0.0) * (1.0 / column[j : j + 1])
        gram = gram - scaled * gram[j : j + 1]
        inverse = inverse - scaled * inverse[j : j + 1]
        column = following - scaled * column[j + 1 : j + 2]
    pivots = jnp.sum(jnp.where(rows == columns, gram, 0.0), axis=1, keepdims=True)
    return inverse * lax.rsqrt(pivots)


def factor_kernel(count, gram_ref, out_ref):
    (gram,) = unfolded(gram_ref[...] * (1.0 / count), out_ref.shape[0])
    out_ref[...] = inverse_factor(gram)


def factor(gram, width, count):
    return call(
        functools.partial(factor_kernel, float(count)),
        [near(gram)],
        [((width, width), F32)],
        specs=[WHOLE],
        flops=40000 * gram.size,
        moved=8 * gram.size,
        name="factor",
    )[0]


def basis_kernel(matrix_ref, left_ref, right_ref, out_ref):
    half = left_ref.shape[2]
    for s in range(left_ref.shape[0]):
        out_ref[s, :, :half] = mix(matrix_ref[...], left_ref[s])
        out_ref[s, :, half:] = mix(matrix_ref[...], right_ref[s])


def basis(matrix, ys):
    slices, width, half = ys[0].shape
    return call(
        basis_kernel,
        [near(matrix)] + [near(y) for y in ys],
        [((slices, width, 2 * half), F32)],
        specs=[WHOLE] * 3,
        flops=4 * width * ys[0].size,
        moved=16 * ys[0].size,
        name="basis",
        out_vmem=False,
    )[0]


def close_kernel(count, sums_ref, y_ref, basis_ref, ritz_ref):
    high = lax.Precision.HIGHEST
    gram, projected = unfolded(sums_ref[...] * (1.0 / count), ritz_ref.shape[0])
    matrix = inverse_factor(gram)
    for s in range(y_ref.shape[0]):
        basis_ref[s] = mix(matrix, y_ref[s])
    half = lax.dot_general(matrix, projected, NN, precision=high, preferred_element_type=F32)
    ritz_ref[...] = lax.dot_general(half, matrix, NT, precision=high, preferred_element_type=F32)


def close(sums, y, count):
    width = y.shape[1]
    return call(
        functools.partial(close_kernel, float(count)),
        [near(sums), near(y)],
        [(y.shape, F32), ((width, width), F32)],
        specs=[WHOLE] * 2,
        flops=2 * width * y.size,
        moved=8 * y.size,
        name="close",
        out_vmem=False,
    )


def stages_of(axis):
    count = lax.axis_size(axis)
    found, stride = [], 1
    if (count.bit_length() - 1) % 2:
        found, stride = [(axis, (1,))], 2
    while stride < count:
        found.append((axis, (stride, 2 * stride, 3 * stride)))
        stride *= 4
    return found


def pairs_of(axis):
    return [(axis, (1 << k,)) for k in range((lax.axis_size(axis) - 1).bit_length())]


def add_over(value, stages):
    for axis, strides in stages:
        count = lax.axis_size(axis)
        others = [lax.ppermute(value, axis, [(i, i ^ k) for i in range(count)]) for k in strides]
        if len(others) == 1:
            value = value + others[0]
        else:
            value = (value + others[0]) + (others[1] + others[2])
    return value


def inner_pairs(axis):
    count = lax.axis_size(axis)
    return [(i, i ^ 1) for i in range(count)]


def outer_pairs(axis):
    count = lax.axis_size(axis)
    return [(i, (i + 1) % count if i % 2 else (i - 1) % count) for i in range(count)]


def body(start_block, stiffness_tiles, tile_columns):
    slices, width, local_points = start_block.shape
    local_blocks = local_points // TILE
    blocks_all = lax.axis_size("space") * local_blocks
    count_all = slices * local_points * lax.axis_size("tm") * lax.axis_size("space")
    time_index = lax.axis_index("tm")
    ends = (time_index == 0, time_index == lax.axis_size("tm") - 1)
    space_index = lax.axis_index("space")
    odd = jnp.stack(
        [
            space_index % 2,
            time_index % 2,
            ends[0].astype(jnp.int32),
            ends[1].astype(jnp.int32),
            space_index * local_blocks,
        ]
    )

    left, right, *ends = start(odd, start_block)
    side = HB * TILE
    half = left.shape[2]
    state = ((left, right), ends, (left[:, :, :side], right[:, :, half - side :]))
    table = plan(tile_columns, odd, blocks_all)
    tiles = prep(stiffness_tiles)

    across, along = pairs_of("space"), pairs_of("tm")
    early = [along[:-1], across[:1], across[1:], along[-1:]]
    ring = lax.axis_size("space")
    up = [(i, (i + 1) % ring) for i in range(ring)]
    down = [((i + 1) % ring, i) for i in range(ring)]

    def step(mode, scale, first, state, previous=None, beside=None):
        halves, ends, sides = state
        halos = [None, None]
        for side in (first, 1 - first):
            pairs = down if side == 1 else up
            halos[side] = lax.ppermute(sides[1 - side], "space", pairs)
        far_slice = lax.ppermute(ends[1], "tm", outer_pairs("tm"))
        near_slice = lax.ppermute(ends[0], "tm", inner_pairs("tm"))
        ends = (near_slice, far_slice)
        parts = local_part(mode, scale, table, tiles, halves, previous)
        extra = None
        if beside is not None:
            parts, extra = lax.optimization_barrier((parts, beside[0]))
            extra = beside[1](extra)
        news, sends = [None, None], [None, None]
        new, *own = finish(first, False, mode, scale, table, tiles, parts[first], halos[first], ends)
        news[first], sends[first] = new, own[0] if own else new
        given = (new, *halves, extra) if mode == "image" else (new,)
        last = 1 - first
        part, _ = lax.optimization_barrier((parts[last], halos[first]))
        if beside is not None:
            part, extra = lax.optimization_barrier((part, extra))
        new, *rest = finish(last, True, mode, scale, table, tiles, part, halos[last], ends, given)
        if mode == "image":
            return rest[0], rest[1], extra
        ends, rest = rest[:2], rest[2:]
        gram = rest.pop(0) if mode == "gram" else None
        news[last], sends[last] = new, rest[0] if rest else new
        return (tuple(news), ends, sends), gram, extra

    def stage(n):
        return lambda gram: add_over(gram, early[n])

    state0 = state
    state1, _, _ = step("first", 1.0 / RADIUS, 0, state0)
    state2, _, _ = step("step", 2.0 / RADIUS, 1, state1, state0[0])
    filtered, gram, _ = step("gram", 2.0 / RADIUS, 0, state2, state1[0])
    state1, _, gram = step("first", 1.0 / RADIUS, 1, filtered, None, (gram, stage(0)))
    state2, _, gram = step("step", 2.0 / RADIUS, 0, state1, filtered[0], (gram, stage(1)))
    state3, _, gram = step("step", 2.0 / RADIUS, 1, state2, state1[0], (gram, stage(2)))
    second, sums, matrix = step(
        "image", 1.0, 0, state3, None, (gram, lambda gram: factor(stage(3)(gram), width, count_all))
    )
    first_basis = basis(matrix, filtered[0])
    sums = add_over(sums, stages_of("tm") + stages_of("space"))
    ritz_basis, ritz_matrix = close(sums, second, count_all)
    return ritz_basis, first_basis, ritz_matrix


def solution(mesh):
    placed = (P("tm", None, "space"), P("tm", "space", None, None), P("tm", "space"))
    return jax.shard_map(
        body,
        mesh=mesh,
        in_specs=placed,
        out_specs=(P("tm", None, "space"), P("tm", None, "space"), P()),
        check_vma=False,
    )
```

time: 131 us -> 125 us (0.954)
  starting transfers between devices: 50.7 us -> 45.1 us
    ppermute x28, starting transfers between devices: 38.3 us -> 33.6 us  [the longest x14 22.2 us: step(): halos[side] = lax.ppermute(sides[1 - side], 'space', pairs)]
    pallas_call x18 -> x25, Pallas kernels: 31.8 us -> 33 us  [call(): pl.pallas_call(kernel, out_shape=out_shape, in_specs=specs, out_specs=[WH...]
  transfers between devices with their start and end apart: 40 -> 40, of which waited for: 15 -> 17; matrix products, arithmetic and copies ran while one was open for 0% -> 0% of each run, Pallas kernels for 18% -> 28%
where the time goes in v7:
time: 125 us
  starting transfers between devices  45.1 us (36%)
  Pallas kernels  39.7 us (32%)
  waiting for transfers between devices  37.1 us (30%)
  local copies, waits for them, and re-layouts  1.81 us (1%)
    pallas_call x25, Pallas kernels, call(): pl.pallas_call(kernel, out_shape=out_shape, in_specs=specs, out_specs=[WH...  33 us
    ppermute x12, waiting for transfers between devices, add_over(): lax.ppermute(value, axis, [(i, i ^ k) for i in range(count)])  23.9 us
    ppermute x14, starting transfers between devices, step(): halos[side] = lax.ppermute(sides[1 - side], 'space', pairs)  22.2 us
    ppermute x12, starting transfers between devices, add_over(): lax.ppermute(value, axis, [(i, i ^ k) for i in range(count)])  11.5 us
    ppermute x7, starting transfers between devices, step(): far_slice = lax.ppermute(ends[1], 'tm', outer_pairs('tm'))  11 us
    ppermute x14, waiting for transfers between devices, step(): halos[side] = lax.ppermute(sides[1 - side], 'space', pairs)  9.31 us
    pallas_call x1, Pallas kernels, prep(): pl.pallas_call(prep_kernel, out_shape=VM((tiles.shape[0], TILE, 2 * TILE)...  4.8 us
    ppermute x7, waiting for transfers between devices, step(): far_slice = lax.ppermute(ends[1], 'tm', outer_pairs('tm'))  3.85 us
  transfers between devices with their start and end apart: 40, of which 17 were waited for; matrix products, arithmetic and copies ran while one was open for 0% of the time, Pallas kernels for 28%

profile of v7, /device:TPU:0, one launch (start us, length us, event | category | flops | bytes accessed | tf_op | source)
XLA Modules:
  0.0 124.6 jit_solution(15641496458053528355)
XLA Ops:
  2.4 3.1 %collective-permute-start = (f32[2,32,1024]{2,1,0:T(8,128)S(1)}, f32[2,32,1024]{2,1,0:T(8,128)S(1)}, u32[]{:S(2)}, u32[]{:S(2)}) collective-permute-start(f32[2,32,1024]{2,1,0:T(8,128)S(1)} %get-tuple-element.72.refs_1_.refs_3_), channel_id=1, source_target_pairs={{0,1},{1,2},{2,3},{3,0},{4,5},{5,6},{6,7},{7,4},{8,9},{9,10},{10,1... | collective-permute-start | bytes 786440 | tf_op jit(solution)/shard_map/ppermute | solution.py:557
  5.5 2.6 %collective-permute-start.2 = (f32[1,32,2048]{2,1,0:T(8,128)S(1)}, f32[1,32,2048]{2,1,0:T(8,128)S(1)}, u32[]{:S(2)}, u32[]{:S(2)}) collective-permute-start(f32[1,32,2048]{2,1,0:T(8,128)S(1)} %get-tuple-element.75), channel_id=1, source_target_pairs={{0,28},{4,8},{8,4},{12,16},{16,12},{20,24},{24,20},{28,0},{1,29},{... | collective-permute-start | bytes 786440 | tf_op jit(solution)/shard_map/ppermute | solution.py:558
  8.0 2.2 %collective-permute-start.3 = (f32[2,32,1024]{2,1,0:T(8,128)S(1)}, f32[2,32,1024]{2,1,0:T(8,128)S(1)}, u32[]{:S(2)}, u32[]{:S(2)}) collective-permute-start(f32[2,32,1024]{2,1,0:T(8,128)S(1)} %get-tuple-element.71.refs_0_.refs_2_), channel_id=1, source_target_pairs={{1,0},{2,1},{3,2},{0,3},{5,4},{6,5},{7,6},{4,7},{9,8},{10,9},{11,1... | collective-permute-start | bytes 786440 | tf_op jit(solution)/shard_map/ppermute | solution.py:557
  11.0 1.9 %plan.1.plan_ref = s32[640]{0:T(1024)S(4)} custom-call(s32[2,80]{1,0:T(2,128)S(1)} %copy-done.1, s32[5]{0:T(128)S(1)} %stack.31.flags_ref.odd_ref), custom_call_target="tpu_custom_call" | custom-call | tf_op jit(solution)/shard_map/plan/pallas_call | solution.py:160
  12.9 4.8 %prep.1.tiles_ref = bf16[160,128,256]{2,1,0:T(8,128)(2,1)S(1)} custom-call(f32[160,128,128]{2,1,0:T(8,128)} %bitcast.6), custom_call_target="tpu_custom_call" | custom-call | bytes 10485760 | tf_op jit(solution)/shard_map/prep/pallas_call | solution.py:88
  17.7 2.1 %local_first.2 = (f32[2,32,1024]{2,1,0:T(8,128)S(1)}, f32[2,32,1024]{2,1,0:T(8,128)S(1)}) custom-call(s32[640]{0:T(1024)S(4)} %plan.1.plan_ref, bf16[160,128,256]{2,1,0:T(8,128)(2,1)S(1)} %prep.1.tiles_ref, f32[2,32,1024]{2,1,0:T(8,128)S(1)} %get-tuple-element.71.refs_0_.refs_2_, f32[2,32,1024]{2,1,0:T(8,128)S(1)} %get-tuple-element.72.refs_1_.refs_3_), custom_call_target="tpu_custom_call" | custom-call | flops 671088640 | bytes 1572864 | tf_op jit(solution)/shard_map/local_first/pallas_call | solution.py:42
  20.6 1.9 %collective-permute-start.4 = (f32[2,32,1024]{2,1,0:T(8,128)S(1)}, f32[2,32,1024]{2,1,0:T(8,128)S(1)}, u32[]{:S(2)}, u32[]{:S(2)}) collective-permute-start(f32[2,32,1024]{2,1,0:T(8,128)S(1)} %left_first.2.refs_0_.refs_2_), channel_id=1, source_target_pairs={{1,0},{2,1},{3,2},{0,3},{5,4},{6,5},{7,6},{4,7},{9,8},{10,9},{11,1... | collective-permute-start | bytes 786440 | tf_op jit(solution)/shard_map/ppermute | solution.py:557
  23.3 2.1 %collective-permute-start.7 = (f32[1,32,2048]{2,1,0:T(8,128)S(1)}, f32[1,32,2048]{2,1,0:T(8,128)S(1)}, u32[]{:S(2)}, u32[]{:S(2)}) collective-permute-start(f32[1,32,2048]{2,1,0:T(8,128)S(1)} %get-tuple-element.82), channel_id=1, source_target_pairs={{0,28},{4,8},{8,4},{12,16},{16,12},{20,24},{24,20},{28,0},{1,29},{... | collective-permute-start | bytes 786440 | tf_op jit(solution)/shard_map/ppermute | solution.py:558
  25.4 2.1 %local_step.3 = (f32[2,32,1024]{2,1,0:T(8,128)S(1)}, f32[2,32,1024]{2,1,0:T(8,128)S(1)}) custom-call(s32[640]{0:T(1024)S(4)} %plan.1.plan_ref, bf16[160,128,256]{2,1,0:T(8,128)(2,1)S(1)} %prep.1.tiles_ref, f32[2,32,1024]{2,1,0:T(8,128)S(1)} %left_first.2.refs_0_.refs_2_, f32[2,32,1024]{2,1,0:T(8,128)S(1)} %get-tuple-element.78.refs_1_.refs_3_, ...), custom_call_target="tpu_custom_call" | custom-call | flops 671088640 | bytes 1572864 | tf_op jit(solution)/shard_map/local_step/pallas_call | solution.py:42
  29.0 3.7 %collective-permute-done.7.far_ref = f32[1,32,2048]{2,1,0:T(8,128)S(1)} collective-permute-done((f32[1,32,2048]{2,1,0:T(8,128)S(1)}, f32[1,32,2048]{2,1,0:T(8,128)S(1)}, u32[]{:S(2)}, u32[]{:S(2)}) %collective-permute-start.7) | collective-permute-done | bytes 262176 | tf_op jit(solution)/shard_map/ppermute | solution.py:558
  37.1 2.2 %collective-permute-start.11 = (f32[2,32,1024]{2,1,0:T(8,128)S(1)}, f32[2,32,1024]{2,1,0:T(8,128)S(1)}, u32[]{:S(2)}, u32[]{:S(2)}) collective-permute-start(f32[2,32,1024]{2,1,0:T(8,128)S(1)} %get-tuple-element.84.refs_0_), channel_id=1, source_target_pairs={{1,0},{2,1},{3,2},{0,3},{5,4},{6,5},{7,6},{4,7},{9,8},{10,9},{11,1... | collective-permute-start | bytes 786440 | tf_op jit(solution)/shard_map/ppermute | solution.py:557
  39.3 2.1 %local_gram.1 = (f32[2,32,1024]{2,1,0:T(8,128)S(1)}, f32[2,32,1024]{2,1,0:T(8,128)S(1)}) custom-call(s32[640]{0:T(1024)S(4)} %plan.1.plan_ref, bf16[160,128,256]{2,1,0:T(8,128)(2,1)S(1)} %prep.1.tiles_ref, f32[2,32,1024]{2,1,0:T(8,128)S(1)} %get-tuple-element.84.refs_0_, f32[2,32,1024]{2,1,0:T(8,128)S(1)} %right_step.3.refs_0_.refs_1_, ...), custom_call_target="tpu_custom_call" | custom-call | flops 671088640 | bytes 1572864 | tf_op jit(solution)/shard_map/local_gram/pallas_call | solution.py:42
  41.4 3.1 %collective-permute-done.8.halo_ref = f32[2,32,1024]{2,1,0:T(8,128)S(1)} collective-permute-done((f32[2,32,1024]{2,1,0:T(8,128)S(1)}, f32[2,32,1024]{2,1,0:T(8,128)S(1)}, u32[]{:S(2)}, u32[]{:S(2)}) %collective-permute-start.8) | collective-permute-done | bytes 262176 | tf_op jit(solution)/shard_map/ppermute | solution.py:557
  45.2 3.0 %collective-permute-start.12 = (f32[2,32,1024]{2,1,0:T(8,128)S(1)}, f32[2,32,1024]{2,1,0:T(8,128)S(1)}, u32[]{:S(2)}, u32[]{:S(2)}) collective-permute-start(f32[2,32,1024]{2,1,0:T(8,128)S(1)} %left_gram.1.refs_0_.refs_2_.left_ref), channel_id=1, source_target_pairs={{1,0},{2,1},{3,2},{0,3},{5,4},{6,5},{7,6},{4,7},{9,8},{10,9},{11,1... | collective-permute-start | bytes 786440 | tf_op jit(solution)/shard_map/ppermute | solution.py:557
  52.5 2.1 %local_first.3 = (f32[2,32,1024]{2,1,0:T(8,128)S(1)}, f32[2,32,1024]{2,1,0:T(8,128)S(1)}) custom-call(s32[640]{0:T(1024)S(4)} %plan.1.plan_ref, bf16[160,128,256]{2,1,0:T(8,128)(2,1)S(1)} %prep.1.tiles_ref, f32[2,32,1024]{2,1,0:T(8,128)S(1)} %left_gram.1.refs_0_.refs_2_.left_ref, f32[2,32,1024]{2,1,0:T(8,128)S(1)} %get-tuple-element.90.refs_1_.refs_3_.right_ref), custom_call_target="tpu_custom_call" | custom-call | flops 671088640 | bytes 1572864 | tf_op jit(solution)/shard_map/local_first/pallas_call | solution.py:42
  56.4 3.2 %collective-permute-done.14 = f32[8,128]{1,0:T(8,128)S(1)} collective-permute-done((f32[8,128]{1,0:T(8,128)S(1)}, f32[8,128]{1,0:T(8,128)S(1)}, u32[]{:S(2)}, u32[]{:S(2)}) %collective-permute-start.14) | collective-permute-done | bytes 4128 | tf_op jit(solution)/shard_map/ppermute | solution.py:503
  62.0 2.1 %collective-permute-start.20 = (f32[1,32,2048]{2,1,0:T(8,128)S(1)}, f32[1,32,2048]{2,1,0:T(8,128)S(1)}, u32[]{:S(2)}, u32[]{:S(2)}) collective-permute-start(f32[1,32,2048]{2,1,0:T(8,128)S(1)} %get-tuple-element.107), channel_id=1, source_target_pairs={{0,28},{4,8},{8,4},{12,16},{16,12},{20,24},{24,20},{28,0},{1,29},{... | collective-permute-start | bytes 786440 | tf_op jit(solution)/shard_map/ppermute | solution.py:558
  64.2 2.0 %collective-permute-start.22 = (f32[2,32,1024]{2,1,0:T(8,128)S(1)}, f32[2,32,1024]{2,1,0:T(8,128)S(1)}, u32[]{:S(2)}, u32[]{:S(2)}) collective-permute-start(f32[2,32,1024]{2,1,0:T(8,128)S(1)} %get-tuple-element.101.refs_0_.refs_2_), channel_id=1, source_target_pairs={{1,0},{2,1},{3,2},{0,3},{5,4},{6,5},{7,6},{4,7},{9,8},{10,9},{11,1... | collective-permute-start | bytes 786440 | tf_op jit(solution)/shard_map/ppermute | solution.py:557
  66.2 2.1 %local_step.4 = (f32[2,32,1024]{2,1,0:T(8,128)S(1)}, f32[2,32,1024]{2,1,0:T(8,128)S(1)}) custom-call(s32[640]{0:T(1024)S(4)} %plan.1.plan_ref, bf16[160,128,256]{2,1,0:T(8,128)(2,1)S(1)} %prep.1.tiles_ref, f32[2,32,1024]{2,1,0:T(8,128)S(1)} %get-tuple-element.101.refs_0_.refs_2_, f32[2,32,1024]{2,1,0:T(8,128)S(1)} %right_first.3.refs_0_.refs_1_.refs_3_, ...), custom_call_target="tpu_custom_call" | custom-call | flops 671088640 | bytes 1572864 | tf_op jit(solution)/shard_map/local_step/pallas_call | solution.py:42
  68.4 7.8 %collective-permute-done.21 = f32[8,128]{1,0:T(8,128)S(1)} collective-permute-done((f32[8,128]{1,0:T(8,128)S(1)}, f32[8,128]{1,0:T(8,128)S(1)}, u32[]{:S(2)}, u32[]{:S(2)}) %collective-permute-start.21) | collective-permute-done | bytes 4128 | tf_op jit(solution)/shard_map/ppermute | solution.py:503
  78.5 2.0 %collective-permute-start.25 = (f32[2,32,1024]{2,1,0:T(8,128)S(1)}, f32[2,32,1024]{2,1,0:T(8,128)S(1)}, u32[]{:S(2)}, u32[]{:S(2)}) collective-permute-start(f32[2,32,1024]{2,1,0:T(8,128)S(1)} %get-tuple-element.112.refs_1_), channel_id=1, source_target_pairs={{0,1},{1,2},{2,3},{3,0},{4,5},{5,6},{6,7},{7,4},{8,9},{9,10},{10,1... | collective-permute-start | bytes 786440 | tf_op jit(solution)/shard_map/ppermute | solution.py:557
  80.5 2.1 %local_step.5 = (f32[2,32,1024]{2,1,0:T(8,128)S(1)}, f32[2,32,1024]{2,1,0:T(8,128)S(1)}) custom-call(s32[640]{0:T(1024)S(4)} %plan.1.plan_ref, bf16[160,128,256]{2,1,0:T(8,128)(2,1)S(1)} %prep.1.tiles_ref, f32[2,32,1024]{2,1,0:T(8,128)S(1)} %left_step.4.refs_0_, f32[2,32,1024]{2,1,0:T(8,128)S(1)} %get-tuple-element.112.refs_1_, ...), custom_call_target="tpu_custom_call" | custom-call | flops 671088640 | bytes 1572864 | tf_op jit(solution)/shard_map/local_step/pallas_call | solution.py:42
  83.6 5.2 %collective-permute-done.24 = f32[8,128]{1,0:T(8,128)S(1)} collective-permute-done((f32[8,128]{1,0:T(8,128)S(1)}, f32[8,128]{1,0:T(8,128)S(1)}, u32[]{:S(2)}, u32[]{:S(2)}) %collective-permute-start.24) | collective-permute-done | bytes 4128 | tf_op jit(solution)/shard_map/ppermute | solution.py:503
  88.8 2.2 %collective-permute-done.23.halo_ref = f32[2,32,1024]{2,1,0:T(8,128)S(1)} collective-permute-done((f32[2,32,1024]{2,1,0:T(8,128)S(1)}, f32[2,32,1024]{2,1,0:T(8,128)S(1)}, u32[]{:S(2)}, u32[]{:S(2)}) %collective-permute-start.23) | collective-permute-done | bytes 262176 | tf_op jit(solution)/shard_map/ppermute | solution.py:557
  93.6 3.7 %collective-permute-start.30 = (f32[2,32,1024]{2,1,0:T(8,128)S(1)}, f32[2,32,1024]{2,1,0:T(8,128)S(1)}, u32[]{:S(2)}, u32[]{:S(2)}) collective-permute-start(f32[2,32,1024]{2,1,0:T(8,128)S(1)} %get-tuple-element.123.refs_0_.refs_1_), channel_id=1, source_target_pairs={{1,0},{2,1},{3,2},{0,3},{5,4},{6,5},{7,6},{4,7},{9,8},{10,9},{11,1... | collective-permute-start | bytes 786440 | tf_op jit(solution)/shard_map/ppermute | solution.py:557
  97.3 2.1 %local_image.1 = (f32[2,32,1024]{2,1,0:T(8,128)S(1)}, f32[2,32,1024]{2,1,0:T(8,128)S(1)}) custom-call(s32[640]{0:T(1024)S(4)} %plan.1.plan_ref, bf16[160,128,256]{2,1,0:T(8,128)(2,1)S(1)} %prep.1.tiles_ref, f32[2,32,1024]{2,1,0:T(8,128)S(1)} %get-tuple-element.123.refs_0_.refs_1_, f32[2,32,1024]{2,1,0:T(8,128)S(1)} %right_step.5.refs_0_.refs_1_.refs_2_), custom_call_target="tpu_custom_call" | custom-call | flops 671088640 | bytes 1572864 | tf_op jit(solution)/shard_map/local_image/pallas_call | solution.py:42
  99.5 1.8 %collective-permute-start.29 = (f32[8,128]{1,0:T(8,128)S(1)}, f32[8,128]{1,0:T(8,128)S(1)}, u32[]{:S(2)}, u32[]{:S(2)}) collective-permute-start(f32[8,128]{1,0:T(8,128)S(1)} %add.48), channel_id=1, source_target_pairs={{0,16},{4,20},{8,24},{12,28},{16,0},{20,4},{24,8},{28,12},{1,17},{... | collective-permute-start | bytes 12296 | tf_op jit(solution)/shard_map/ppermute | solution.py:503
  101.2 1.9 %collective-permute-done.29 = f32[8,128]{1,0:T(8,128)S(1)} collective-permute-done((f32[8,128]{1,0:T(8,128)S(1)}, f32[8,128]{1,0:T(8,128)S(1)}, u32[]{:S(2)}, u32[]{:S(2)}) %collective-permute-start.29) | collective-permute-done | bytes 4128 | tf_op jit(solution)/shard_map/ppermute | solution.py:503
  106.1 2.2 %right_image.1 = (f32[2,32,1024]{2,1,0:T(8,128)S(1)}, f32[2,32,2048]{2,1,0:T(8,128)S(1)}, f32[16,128]{1,0:T(8,128)S(1)}) custom-call(s32[640]{0:T(1024)S(4)} %plan.1.plan_ref, bf16[160,128,256]{2,1,0:T(8,128)(2,1)S(1)} %prep.1.tiles_ref, f32[2,32,1024]{2,1,0:T(8,128)S(1)} %get-tuple-element.130.part_ref, ...), custom_call_target="tpu_custom_call", output_to_operand_aliasing={{0}: (2, {})} | custom-call | flops 134217728 | bytes 1572864 | tf_op jit(solution)/shard_map/right_image/pallas_call | solution.py:42
  115.7 1.9 %collective-permute-start.39 = (f32[16,128]{1,0:T(8,128)S(1)}, f32[16,128]{1,0:T(8,128)S(1)}, u32[]{:S(2)}, u32[]{:S(2)}) collective-permute-start(f32[16,128]{1,0:T(8,128)S(1)} %add_add_fusion.1), channel_id=1, source_target_pairs={{0,3},{1,2},{2,1},{3,0},{4,7},{5,6},{6,5},{7,4},{8,11},{9,10},{10,... | collective-permute-start | bytes 24584 | tf_op jit(solution)/shard_map/ppermute | solution.py:503
  117.7 2.4 %collective-permute-start.37 = (f32[16,128]{1,0:T(8,128)S(1)}, f32[16,128]{1,0:T(8,128)S(1)}, u32[]{:S(2)}, u32[]{:S(2)}) collective-permute-start(f32[16,128]{1,0:T(8,128)S(1)} %add_add_fusion.1), channel_id=1, source_target_pairs={{0,1},{1,0},{2,3},{3,2},{4,5},{5,4},{6,7},{7,6},{8,9},{9,8},{10,11... | collective-permute-start | bytes 24584 | tf_op jit(solution)/shard_map/ppermute | solution.py:503
  122.1 2.5 %close.1 = (f32[2,32,2048]{2,1,0:T(8,128)}, f32[32,32]{1,0:T(8,128)}) custom-call(f32[16,128]{1,0:T(8,128)S(1)} %add_add_fusion.sums_ref, f32[2,32,2048]{2,1,0:T(8,128)S(1)} %get-tuple-element.135.y_ref), custom_call_target="tpu_custom_call" | custom-call | flops 8388608 | bytes 1048576 | tf_op jit(solution)/shard_map/close/pallas_call | solution.py:42
  (88 shorter events, 37.5 us)
Async XLA Ops:
  2.4 17.4 %collective-permute-start = (f32[2,32,1024]{2,1,0:T(8,128)S(1)}, f32[2,32,1024]{2,1,0:T(8,128)S(1)}, u32[]{:S(2)}, u32[]{:S(2)}) collective-permute-start(f32[2,32,1024]{2,1,0:T(8,128)S(1)} %get-tuple-element.72.refs_1_.refs_3_), channel_id=1, source_target_pairs={{0,1},{1,2},{2,3},{3,0},{4,5},{5,6},{6,7},{7,4},{8,9},{9,10},{10,1... | collective-permute-start | bytes 786440 | tf_op jit(solution)/shard_map/ppermute | solution.py:557
  5.5 14.3 %collective-permute-start.1 = (f32[1,32,2048]{2,1,0:T(8,128)S(1)}, f32[1,32,2048]{2,1,0:T(8,128)S(1)}, u32[]{:S(2)}, u32[]{:S(2)}) collective-permute-start(f32[1,32,2048]{2,1,0:T(8,128)S(1)} %get-tuple-element.74), channel_id=1, source_target_pairs={{0,4},{4,0},{8,12},{12,8},{16,20},{20,16},{24,28},{28,24},{1,5},{5... | collective-permute-start | bytes 786440 | tf_op jit(solution)/shard_map/ppermute | solution.py:559
  5.5 14.3 %collective-permute-start.2 = (f32[1,32,2048]{2,1,0:T(8,128)S(1)}, f32[1,32,2048]{2,1,0:T(8,128)S(1)}, u32[]{:S(2)}, u32[]{:S(2)}) collective-permute-start(f32[1,32,2048]{2,1,0:T(8,128)S(1)} %get-tuple-element.75), channel_id=1, source_target_pairs={{0,28},{4,8},{8,4},{12,16},{16,12},{20,24},{24,20},{28,0},{1,29},{... | collective-permute-start | bytes 786440 | tf_op jit(solution)/shard_map/ppermute | solution.py:558
  8.0 14.4 %collective-permute-start.3 = (f32[2,32,1024]{2,1,0:T(8,128)S(1)}, f32[2,32,1024]{2,1,0:T(8,128)S(1)}, u32[]{:S(2)}, u32[]{:S(2)}) collective-permute-start(f32[2,32,1024]{2,1,0:T(8,128)S(1)} %get-tuple-element.71.refs_0_.refs_2_), channel_id=1, source_target_pairs={{1,0},{2,1},{3,2},{0,3},{5,4},{6,5},{7,6},{4,7},{9,8},{10,9},{11,1... | collective-permute-start | bytes 786440 | tf_op jit(solution)/shard_map/ppermute | solution.py:557
  20.6 8.4 %collective-permute-start.4 = (f32[2,32,1024]{2,1,0:T(8,128)S(1)}, f32[2,32,1024]{2,1,0:T(8,128)S(1)}, u32[]{:S(2)}, u32[]{:S(2)}) collective-permute-start(f32[2,32,1024]{2,1,0:T(8,128)S(1)} %left_first.2.refs_0_.refs_2_), channel_id=1, source_target_pairs={{1,0},{2,1},{3,2},{0,3},{5,4},{6,5},{7,6},{4,7},{9,8},{10,9},{11,1... | collective-permute-start | bytes 786440 | tf_op jit(solution)/shard_map/ppermute | solution.py:557
  23.2 5.8 %collective-permute-start.6 = (f32[1,32,2048]{2,1,0:T(8,128)S(1)}, f32[1,32,2048]{2,1,0:T(8,128)S(1)}, u32[]{:S(2)}, u32[]{:S(2)}) collective-permute-start(f32[1,32,2048]{2,1,0:T(8,128)S(1)} %get-tuple-element.81), channel_id=1, source_target_pairs={{0,4},{4,0},{8,12},{12,8},{16,20},{20,16},{24,28},{28,24},{1,5},{5... | collective-permute-start | bytes 786440 | tf_op jit(solution)/shard_map/ppermute | solution.py:559
  23.3 9.4 %collective-permute-start.7 = (f32[1,32,2048]{2,1,0:T(8,128)S(1)}, f32[1,32,2048]{2,1,0:T(8,128)S(1)}, u32[]{:S(2)}, u32[]{:S(2)}) collective-permute-start(f32[1,32,2048]{2,1,0:T(8,128)S(1)} %get-tuple-element.82), channel_id=1, source_target_pairs={{0,28},{4,8},{8,4},{12,16},{16,12},{20,24},{24,20},{28,0},{1,29},{... | collective-permute-start | bytes 786440 | tf_op jit(solution)/shard_map/ppermute | solution.py:558
  25.4 9.1 %collective-permute-start.5 = (f32[2,32,1024]{2,1,0:T(8,128)S(1)}, f32[2,32,1024]{2,1,0:T(8,128)S(1)}, u32[]{:S(2)}, u32[]{:S(2)}) collective-permute-start(f32[2,32,1024]{2,1,0:T(8,128)S(1)} %get-tuple-element.78.refs_1_.refs_3_), channel_id=1, source_target_pairs={{0,1},{1,2},{2,3},{3,0},{4,5},{5,6},{6,7},{7,4},{8,9},{9,10},{10,1... | collective-permute-start | bytes 786440 | tf_op jit(solution)/shard_map/ppermute | solution.py:557
  33.4 11.1 %collective-permute-start.8 = (f32[2,32,1024]{2,1,0:T(8,128)S(1)}, f32[2,32,1024]{2,1,0:T(8,128)S(1)}, u32[]{:S(2)}, u32[]{:S(2)}) collective-permute-start(f32[2,32,1024]{2,1,0:T(8,128)S(1)} %right_step.3.refs_0_.refs_1_), channel_id=1, source_target_pairs={{0,1},{1,2},{2,3},{3,0},{4,5},{5,6},{6,7},{7,4},{8,9},{9,10},{10,1... | collective-permute-start | bytes 786440 | tf_op jit(solution)/shard_map/ppermute | solution.py:557
  35.3 9.2 %collective-permute-start.9 = (f32[1,32,2048]{2,1,0:T(8,128)S(1)}, f32[1,32,2048]{2,1,0:T(8,128)S(1)}, u32[]{:S(2)}, u32[]{:S(2)}) collective-permute-start(f32[1,32,2048]{2,1,0:T(8,128)S(1)} %get-tuple-element.86), channel_id=1, source_target_pairs={{0,4},{4,0},{8,12},{12,8},{16,20},{20,16},{24,28},{28,24},{1,5},{5... | collective-permute-start | bytes 786440 | tf_op jit(solution)/shard_map/ppermute | solution.py:559
  35.4 9.1 %collective-permute-start.10 = (f32[1,32,2048]{2,1,0:T(8,128)S(1)}, f32[1,32,2048]{2,1,0:T(8,128)S(1)}, u32[]{:S(2)}, u32[]{:S(2)}) collective-permute-start(f32[1,32,2048]{2,1,0:T(8,128)S(1)} %get-tuple-element.87), channel_id=1, source_target_pairs={{0,28},{4,8},{8,4},{12,16},{16,12},{20,24},{24,20},{28,0},{1,29},{... | collective-permute-start | bytes 786440 | tf_op jit(solution)/shard_map/ppermute | solution.py:558
  37.1 12.0 %collective-permute-start.11 = (f32[2,32,1024]{2,1,0:T(8,128)S(1)}, f32[2,32,1024]{2,1,0:T(8,128)S(1)}, u32[]{:S(2)}, u32[]{:S(2)}) collective-permute-start(f32[2,32,1024]{2,1,0:T(8,128)S(1)} %get-tuple-element.84.refs_0_), channel_id=1, source_target_pairs={{1,0},{2,1},{3,2},{0,3},{5,4},{6,5},{7,6},{4,7},{9,8},{10,9},{11,1... | collective-permute-start | bytes 786440 | tf_op jit(solution)/shard_map/ppermute | solution.py:557
  45.2 14.4 %collective-permute-start.12 = (f32[2,32,1024]{2,1,0:T(8,128)S(1)}, f32[2,32,1024]{2,1,0:T(8,128)S(1)}, u32[]{:S(2)}, u32[]{:S(2)}) collective-permute-start(f32[2,32,1024]{2,1,0:T(8,128)S(1)} %left_gram.1.refs_0_.refs_2_.left_ref), channel_id=1, source_target_pairs={{1,0},{2,1},{3,2},{0,3},{5,4},{6,5},{7,6},{4,7},{9,8},{10,9},{11,1... | collective-permute-start | bytes 786440 | tf_op jit(solution)/shard_map/ppermute | solution.py:557
  50.4 9.3 %collective-permute-start.16 = (f32[1,32,2048]{2,1,0:T(8,128)S(1)}, f32[1,32,2048]{2,1,0:T(8,128)S(1)}, u32[]{:S(2)}, u32[]{:S(2)}) collective-permute-start(f32[1,32,2048]{2,1,0:T(8,128)S(1)} %get-tuple-element.98), channel_id=1, source_target_pairs={{0,4},{4,0},{8,12},{12,8},{16,20},{20,16},{24,28},{28,24},{1,5},{5... | collective-permute-start | bytes 786440 | tf_op jit(solution)/shard_map/ppermute | solution.py:559
  50.4 9.4 %collective-permute-start.17 = (f32[1,32,2048]{2,1,0:T(8,128)S(1)}, f32[1,32,2048]{2,1,0:T(8,128)S(1)}, u32[]{:S(2)}, u32[]{:S(2)}) collective-permute-start(f32[1,32,2048]{2,1,0:T(8,128)S(1)} %get-tuple-element.99), channel_id=1, source_target_pairs={{0,28},{4,8},{8,4},{12,16},{16,12},{20,24},{24,20},{28,0},{1,29},{... | collective-permute-start | bytes 786440 | tf_op jit(solution)/shard_map/ppermute | solution.py:558
  51.9 9.2 %collective-permute-start.15 = (f32[2,32,1024]{2,1,0:T(8,128)S(1)}, f32[2,32,1024]{2,1,0:T(8,128)S(1)}, u32[]{:S(2)}, u32[]{:S(2)}) collective-permute-start(f32[2,32,1024]{2,1,0:T(8,128)S(1)} %get-tuple-element.90.refs_1_.refs_3_.right_ref), channel_id=1, source_target_pairs={{0,1},{1,2},{2,3},{3,0},{4,5},{5,6},{6,7},{7,4},{8,9},{9,10},{10,1... | collective-permute-start | bytes 786440 | tf_op jit(solution)/shard_map/ppermute | solution.py:557
  60.5 15.7 %collective-permute-start.18 = (f32[2,32,1024]{2,1,0:T(8,128)S(1)}, f32[2,32,1024]{2,1,0:T(8,128)S(1)}, u32[]{:S(2)}, u32[]{:S(2)}) collective-permute-start(f32[2,32,1024]{2,1,0:T(8,128)S(1)} %right_first.3.refs_0_.refs_1_.refs_3_), channel_id=1, source_target_pairs={{0,1},{1,2},{2,3},{3,0},{4,5},{5,6},{6,7},{7,4},{8,9},{9,10},{10,1... | collective-permute-start | bytes 786440 | tf_op jit(solution)/shard_map/ppermute | solution.py:557
  62.0 14.2 %collective-permute-start.19 = (f32[1,32,2048]{2,1,0:T(8,128)S(1)}, f32[1,32,2048]{2,1,0:T(8,128)S(1)}, u32[]{:S(2)}, u32[]{:S(2)}) collective-permute-start(f32[1,32,2048]{2,1,0:T(8,128)S(1)} %get-tuple-element.106), channel_id=1, source_target_pairs={{0,4},{4,0},{8,12},{12,8},{16,20},{20,16},{24,28},{28,24},{1,5},{5... | collective-permute-start | bytes 786440 | tf_op jit(solution)/shard_map/ppermute | solution.py:559
  62.0 14.2 %collective-permute-start.20 = (f32[1,32,2048]{2,1,0:T(8,128)S(1)}, f32[1,32,2048]{2,1,0:T(8,128)S(1)}, u32[]{:S(2)}, u32[]{:S(2)}) collective-permute-start(f32[1,32,2048]{2,1,0:T(8,128)S(1)} %get-tuple-element.107), channel_id=1, source_target_pairs={{0,28},{4,8},{8,4},{12,16},{16,12},{20,24},{24,20},{28,0},{1,29},{... | collective-permute-start | bytes 786440 | tf_op jit(solution)/shard_map/ppermute | solution.py:558
  64.2 13.4 %collective-permute-start.22 = (f32[2,32,1024]{2,1,0:T(8,128)S(1)}, f32[2,32,1024]{2,1,0:T(8,128)S(1)}, u32[]{:S(2)}, u32[]{:S(2)}) collective-permute-start(f32[2,32,1024]{2,1,0:T(8,128)S(1)} %get-tuple-element.101.refs_0_.refs_2_), channel_id=1, source_target_pairs={{1,0},{2,1},{3,2},{0,3},{5,4},{6,5},{7,6},{4,7},{9,8},{10,9},{11,1... | collective-permute-start | bytes 786440 | tf_op jit(solution)/shard_map/ppermute | solution.py:557
  68.4 7.8 %collective-permute-start.21 = (f32[8,128]{1,0:T(8,128)S(1)}, f32[8,128]{1,0:T(8,128)S(1)}, u32[]{:S(2)}, u32[]{:S(2)}) collective-permute-start(f32[8,128]{1,0:T(8,128)S(1)} %add.46), channel_id=1, source_target_pairs={{0,1},{1,0},{2,3},{3,2},{4,5},{5,4},{6,7},{7,6},{8,9},{9,8},{10,11... | collective-permute-start | bytes 12296 | tf_op jit(solution)/shard_map/ppermute | solution.py:503
  77.0 14.0 %collective-permute-start.23 = (f32[2,32,1024]{2,1,0:T(8,128)S(1)}, f32[2,32,1024]{2,1,0:T(8,128)S(1)}, u32[]{:S(2)}, u32[]{:S(2)}) collective-permute-start(f32[2,32,1024]{2,1,0:T(8,128)S(1)} %left_step.4.refs_0_), channel_id=1, source_target_pairs={{1,0},{2,1},{3,2},{0,3},{5,4},{6,5},{7,6},{4,7},{9,8},{10,9},{11,1... | collective-permute-start | bytes 786440 | tf_op jit(solution)/shard_map/ppermute | solution.py:557
  78.4 12.6 %collective-permute-start.26 = (f32[1,32,2048]{2,1,0:T(8,128)S(1)}, f32[1,32,2048]{2,1,0:T(8,128)S(1)}, u32[]{:S(2)}, u32[]{:S(2)}) collective-permute-start(f32[1,32,2048]{2,1,0:T(8,128)S(1)} %get-tuple-element.120), channel_id=1, source_target_pairs={{0,4},{4,0},{8,12},{12,8},{16,20},{20,16},{24,28},{28,24},{1,5},{5... | collective-permute-start | bytes 786440 | tf_op jit(solution)/shard_map/ppermute | solution.py:559
  78.4 12.5 %collective-permute-start.27 = (f32[1,32,2048]{2,1,0:T(8,128)S(1)}, f32[1,32,2048]{2,1,0:T(8,128)S(1)}, u32[]{:S(2)}, u32[]{:S(2)}) collective-permute-start(f32[1,32,2048]{2,1,0:T(8,128)S(1)} %get-tuple-element.121), channel_id=1, source_target_pairs={{0,28},{4,8},{8,4},{12,16},{16,12},{20,24},{24,20},{28,0},{1,29},{... | collective-permute-start | bytes 786440 | tf_op jit(solution)/shard_map/ppermute | solution.py:558
  78.5 13.3 %collective-permute-start.25 = (f32[2,32,1024]{2,1,0:T(8,128)S(1)}, f32[2,32,1024]{2,1,0:T(8,128)S(1)}, u32[]{:S(2)}, u32[]{:S(2)}) collective-permute-start(f32[2,32,1024]{2,1,0:T(8,128)S(1)} %get-tuple-element.112.refs_1_), channel_id=1, source_target_pairs={{0,1},{1,2},{2,3},{3,0},{4,5},{5,6},{6,7},{7,4},{8,9},{9,10},{10,1... | collective-permute-start | bytes 786440 | tf_op jit(solution)/shard_map/ppermute | solution.py:557
  82.6 6.2 %collective-permute-start.24 = (f32[8,128]{1,0:T(8,128)S(1)}, f32[8,128]{1,0:T(8,128)S(1)}, u32[]{:S(2)}, u32[]{:S(2)}) collective-permute-start(f32[8,128]{1,0:T(8,128)S(1)} %add.47), channel_id=1, source_target_pairs={{0,2},{1,3},{2,0},{3,1},{4,6},{5,7},{6,4},{7,5},{8,10},{9,11},{10,... | collective-permute-start | bytes 12296 | tf_op jit(solution)/shard_map/ppermute | solution.py:503
  91.7 12.8 %collective-permute-start.28 = (f32[2,32,1024]{2,1,0:T(8,128)S(1)}, f32[2,32,1024]{2,1,0:T(8,128)S(1)}, u32[]{:S(2)}, u32[]{:S(2)}) collective-permute-start(f32[2,32,1024]{2,1,0:T(8,128)S(1)} %right_step.5.refs_0_.refs_1_.refs_2_), channel_id=1, source_target_pairs={{0,1},{1,2},{2,3},{3,0},{4,5},{5,6},{6,7},{7,4},{8,9},{9,10},{10,1... | collective-permute-start | bytes 786440 | tf_op jit(solution)/shard_map/ppermute | solution.py:557
  92.6 12.0 %collective-permute-start.31 = (f32[1,32,2048]{2,1,0:T(8,128)S(1)}, f32[1,32,2048]{2,1,0:T(8,128)S(1)}, u32[]{:S(2)}, u32[]{:S(2)}) collective-permute-start(f32[1,32,2048]{2,1,0:T(8,128)S(1)} %get-tuple-element.131), channel_id=1, source_target_pairs={{0,4},{4,0},{8,12},{12,8},{16,20},{20,16},{24,28},{28,24},{1,5},{5... | collective-permute-start | bytes 786440 | tf_op jit(solution)/shard_map/ppermute | solution.py:559
  92.6 11.9 %collective-permute-start.32 = (f32[1,32,2048]{2,1,0:T(8,128)S(1)}, f32[1,32,2048]{2,1,0:T(8,128)S(1)}, u32[]{:S(2)}, u32[]{:S(2)}) collective-permute-start(f32[1,32,2048]{2,1,0:T(8,128)S(1)} %get-tuple-element.132), channel_id=1, source_target_pairs={{0,28},{4,8},{8,4},{12,16},{16,12},{20,24},{24,20},{28,0},{1,29},{... | collective-permute-start | bytes 786440 | tf_op jit(solution)/shard_map/ppermute | solution.py:558
  93.6 12.5 %collective-permute-start.30 = (f32[2,32,1024]{2,1,0:T(8,128)S(1)}, f32[2,32,1024]{2,1,0:T(8,128)S(1)}, u32[]{:S(2)}, u32[]{:S(2)}) collective-permute-start(f32[2,32,1024]{2,1,0:T(8,128)S(1)} %get-tuple-element.123.refs_0_.refs_1_), channel_id=1, source_target_pairs={{1,0},{2,1},{3,2},{0,3},{5,4},{6,5},{7,6},{4,7},{9,8},{10,9},{11,1... | collective-permute-start | bytes 786440 | tf_op jit(solution)/shard_map/ppermute | solution.py:557
  109.5 4.6 %collective-permute-start.36 = (f32[16,128]{1,0:T(8,128)S(1)}, f32[16,128]{1,0:T(8,128)S(1)}, u32[]{:S(2)}, u32[]{:S(2)}) collective-permute-start(f32[16,128]{1,0:T(8,128)S(1)} %add.50), channel_id=1, source_target_pairs={{0,24},{4,28},{8,16},{12,20},{16,8},{20,12},{24,0},{28,4},{1,25},{... | collective-permute-start | bytes 24584 | tf_op jit(solution)/shard_map/ppermute | solution.py:503
  115.7 5.5 %collective-permute-start.39 = (f32[16,128]{1,0:T(8,128)S(1)}, f32[16,128]{1,0:T(8,128)S(1)}, u32[]{:S(2)}, u32[]{:S(2)}) collective-permute-start(f32[16,128]{1,0:T(8,128)S(1)} %add_add_fusion.1), channel_id=1, source_target_pairs={{0,3},{1,2},{2,1},{3,0},{4,7},{5,6},{6,5},{7,4},{8,11},{9,10},{10,... | collective-permute-start | bytes 24584 | tf_op jit(solution)/shard_map/ppermute | solution.py:503
  (10 other events, 28.0 us)

commit v8 on v7

--- a/solution.py
+++ b/solution.py
@@ -544,7 +544,7 @@
     tiles = prep(stiffness_tiles)
 
     across, along = pairs_of("space"), pairs_of("tm")
-    early = [along[:-1], across[:1], across[1:], along[-1:]]
+    early = [along[:-1], along[-1:], across[:1], across[1:]]
     ring = lax.axis_size("space")
     up = [(i, (i + 1) % ring) for i in range(ring)]
     down = [((i + 1) % ring, i) for i in range(ring)]

time: 125 us -> 124 us (level)
  waiting for transfers between devices: 37.1 us -> 34.6 us
  starting transfers between devices: 45.1 us -> 46.7 us
    ppermute x14, waiting for transfers between devices: 9.31 us -> 7.04 us  [step(): halos[side] = lax.ppermute(sides[1 - side], 'space', pairs)]
    ppermute x7, starting transfers between devices: 11 us -> 12.4 us  [step(): far_slice = lax.ppermute(ends[1], 'tm', outer_pairs('tm'))]
  transfers between devices with their start and end apart: 40 -> 40, of which waited for: 17 -> 18; matrix products, arithmetic and copies ran while one was open for 0% -> 0% of each run, Pallas kernels for 28% -> 28%
where the time goes in v8:
time: 124 us
  starting transfers between devices  46.7 us (38%)
  Pallas kernels  39.7 us (32%)
  waiting for transfers between devices  34.6 us (28%)
  local copies, waits for them, and re-layouts  1.81 us (1%)
    pallas_call x25, Pallas kernels, call(): pl.pallas_call(kernel, out_shape=out_shape, in_specs=specs, out_specs=[WH...  33 us
    ppermute x12, waiting for transfers between devices, add_over(): lax.ppermute(value, axis, [(i, i ^ k) for i in range(count)])  23.6 us
    ppermute x14, starting transfers between devices, step(): halos[side] = lax.ppermute(sides[1 - side], 'space', pairs)  22.8 us
    ppermute x7, starting transfers between devices, step(): far_slice = lax.ppermute(ends[1], 'tm', outer_pairs('tm'))  12.4 us
    ppermute x12, starting transfers between devices, add_over(): lax.ppermute(value, axis, [(i, i ^ k) for i in range(count)])  11.2 us
    ppermute x14, waiting for transfers between devices, step(): halos[side] = lax.ppermute(sides[1 - side], 'space', pairs)  7.04 us
    pallas_call x1, Pallas kernels, prep(): pl.pallas_call(prep_kernel, out_shape=VM((tiles.shape[0], TILE, 2 * TILE)...  4.8 us
    ppermute x7, waiting for transfers between devices, step(): far_slice = lax.ppermute(ends[1], 'tm', outer_pairs('tm'))  3.91 us
  transfers between devices with their start and end apart: 40, of which 18 were waited for; matrix products, arithmetic and copies ran while one was open for 0% of the time, Pallas kernels for 28%

profile of v8, /device:TPU:0, one launch (start us, length us, event | category | flops | bytes accessed | tf_op | source)
XLA Modules:
  0.0 123.8 jit_solution(3323394396795603058)
XLA Ops:
  2.4 3.1 %collective-permute-start = (f32[2,32,1024]{2,1,0:T(8,128)S(1)}, f32[2,32,1024]{2,1,0:T(8,128)S(1)}, u32[]{:S(2)}, u32[]{:S(2)}) collective-permute-start(f32[2,32,1024]{2,1,0:T(8,128)S(1)} %get-tuple-element.72.refs_1_.refs_3_), channel_id=1, source_target_pairs={{0,1},{1,2},{2,3},{3,0},{4,5},{5,6},{6,7},{7,4},{8,9},{9,10},{10,1... | collective-permute-start | bytes 786440 | tf_op jit(solution)/shard_map/ppermute | solution.py:557
  5.5 2.6 %collective-permute-start.2 = (f32[1,32,2048]{2,1,0:T(8,128)S(1)}, f32[1,32,2048]{2,1,0:T(8,128)S(1)}, u32[]{:S(2)}, u32[]{:S(2)}) collective-permute-start(f32[1,32,2048]{2,1,0:T(8,128)S(1)} %get-tuple-element.75), channel_id=1, source_target_pairs={{0,28},{4,8},{8,4},{12,16},{16,12},{20,24},{24,20},{28,0},{1,29},{... | collective-permute-start | bytes 786440 | tf_op jit(solution)/shard_map/ppermute | solution.py:558
  8.0 2.2 %collective-permute-start.3 = (f32[2,32,1024]{2,1,0:T(8,128)S(1)}, f32[2,32,1024]{2,1,0:T(8,128)S(1)}, u32[]{:S(2)}, u32[]{:S(2)}) collective-permute-start(f32[2,32,1024]{2,1,0:T(8,128)S(1)} %get-tuple-element.71.refs_0_.refs_2_), channel_id=1, source_target_pairs={{1,0},{2,1},{3,2},{0,3},{5,4},{6,5},{7,6},{4,7},{9,8},{10,9},{11,1... | collective-permute-start | bytes 786440 | tf_op jit(solution)/shard_map/ppermute | solution.py:557
  11.0 1.9 %plan.1.plan_ref = s32[640]{0:T(1024)S(4)} custom-call(s32[2,80]{1,0:T(2,128)S(1)} %copy-done.1, s32[5]{0:T(128)S(1)} %stack.31.flags_ref.odd_ref), custom_call_target="tpu_custom_call" | custom-call | tf_op jit(solution)/shard_map/plan/pallas_call | solution.py:160
  12.9 4.8 %prep.1.tiles_ref = bf16[160,128,256]{2,1,0:T(8,128)(2,1)S(1)} custom-call(f32[160,128,128]{2,1,0:T(8,128)} %bitcast.6), custom_call_target="tpu_custom_call" | custom-call | bytes 10485760 | tf_op jit(solution)/shard_map/prep/pallas_call | solution.py:88
  17.7 2.1 %local_first.2 = (f32[2,32,1024]{2,1,0:T(8,128)S(1)}, f32[2,32,1024]{2,1,0:T(8,128)S(1)}) custom-call(s32[640]{0:T(1024)S(4)} %plan.1.plan_ref, bf16[160,128,256]{2,1,0:T(8,128)(2,1)S(1)} %prep.1.tiles_ref, f32[2,32,1024]{2,1,0:T(8,128)S(1)} %get-tuple-element.71.refs_0_.refs_2_, f32[2,32,1024]{2,1,0:T(8,128)S(1)} %get-tuple-element.72.refs_1_.refs_3_), custom_call_target="tpu_custom_call" | custom-call | flops 671088640 | bytes 1572864 | tf_op jit(solution)/shard_map/local_first/pallas_call | solution.py:42
  20.6 1.9 %collective-permute-start.4 = (f32[2,32,1024]{2,1,0:T(8,128)S(1)}, f32[2,32,1024]{2,1,0:T(8,128)S(1)}, u32[]{:S(2)}, u32[]{:S(2)}) collective-permute-start(f32[2,32,1024]{2,1,0:T(8,128)S(1)} %left_first.2.refs_0_.refs_2_), channel_id=1, source_target_pairs={{1,0},{2,1},{3,2},{0,3},{5,4},{6,5},{7,6},{4,7},{9,8},{10,9},{11,1... | collective-permute-start | bytes 786440 | tf_op jit(solution)/shard_map/ppermute | solution.py:557
  23.3 2.1 %collective-permute-start.7 = (f32[1,32,2048]{2,1,0:T(8,128)S(1)}, f32[1,32,2048]{2,1,0:T(8,128)S(1)}, u32[]{:S(2)}, u32[]{:S(2)}) collective-permute-start(f32[1,32,2048]{2,1,0:T(8,128)S(1)} %get-tuple-element.82), channel_id=1, source_target_pairs={{0,28},{4,8},{8,4},{12,16},{16,12},{20,24},{24,20},{28,0},{1,29},{... | collective-permute-start | bytes 786440 | tf_op jit(solution)/shard_map/ppermute | solution.py:558
  25.4 2.1 %local_step.3 = (f32[2,32,1024]{2,1,0:T(8,128)S(1)}, f32[2,32,1024]{2,1,0:T(8,128)S(1)}) custom-call(s32[640]{0:T(1024)S(4)} %plan.1.plan_ref, bf16[160,128,256]{2,1,0:T(8,128)(2,1)S(1)} %prep.1.tiles_ref, f32[2,32,1024]{2,1,0:T(8,128)S(1)} %left_first.2.refs_0_.refs_2_, f32[2,32,1024]{2,1,0:T(8,128)S(1)} %get-tuple-element.78.refs_1_.refs_3_, ...), custom_call_target="tpu_custom_call" | custom-call | flops 671088640 | bytes 1572864 | tf_op jit(solution)/shard_map/local_step/pallas_call | solution.py:42
  29.0 3.7 %collective-permute-done.7.far_ref = f32[1,32,2048]{2,1,0:T(8,128)S(1)} collective-permute-done((f32[1,32,2048]{2,1,0:T(8,128)S(1)}, f32[1,32,2048]{2,1,0:T(8,128)S(1)}, u32[]{:S(2)}, u32[]{:S(2)}) %collective-permute-start.7) | collective-permute-done | bytes 262176 | tf_op jit(solution)/shard_map/ppermute | solution.py:558
  35.4 2.0 %collective-permute-start.10 = (f32[1,32,2048]{2,1,0:T(8,128)S(1)}, f32[1,32,2048]{2,1,0:T(8,128)S(1)}, u32[]{:S(2)}, u32[]{:S(2)}) collective-permute-start(f32[1,32,2048]{2,1,0:T(8,128)S(1)} %get-tuple-element.87), channel_id=1, source_target_pairs={{0,28},{4,8},{8,4},{12,16},{16,12},{20,24},{24,20},{28,0},{1,29},{... | collective-permute-start | bytes 786440 | tf_op jit(solution)/shard_map/ppermute | solution.py:558
  37.4 1.9 %collective-permute-start.11 = (f32[2,32,1024]{2,1,0:T(8,128)S(1)}, f32[2,32,1024]{2,1,0:T(8,128)S(1)}, u32[]{:S(2)}, u32[]{:S(2)}) collective-permute-start(f32[2,32,1024]{2,1,0:T(8,128)S(1)} %get-tuple-element.84.refs_0_), channel_id=1, source_target_pairs={{1,0},{2,1},{3,2},{0,3},{5,4},{6,5},{7,6},{4,7},{9,8},{10,9},{11,1... | collective-permute-start | bytes 786440 | tf_op jit(solution)/shard_map/ppermute | solution.py:557
  39.3 2.1 %local_gram.1 = (f32[2,32,1024]{2,1,0:T(8,128)S(1)}, f32[2,32,1024]{2,1,0:T(8,128)S(1)}) custom-call(s32[640]{0:T(1024)S(4)} %plan.1.plan_ref, bf16[160,128,256]{2,1,0:T(8,128)(2,1)S(1)} %prep.1.tiles_ref, f32[2,32,1024]{2,1,0:T(8,128)S(1)} %get-tuple-element.84.refs_0_, f32[2,32,1024]{2,1,0:T(8,128)S(1)} %right_step.3.refs_0_.refs_1_, ...), custom_call_target="tpu_custom_call" | custom-call | flops 671088640 | bytes 1572864 | tf_op jit(solution)/shard_map/local_gram/pallas_call | solution.py:42
  41.4 3.1 %collective-permute-done.8.halo_ref = f32[2,32,1024]{2,1,0:T(8,128)S(1)} collective-permute-done((f32[2,32,1024]{2,1,0:T(8,128)S(1)}, f32[2,32,1024]{2,1,0:T(8,128)S(1)}, u32[]{:S(2)}, u32[]{:S(2)}) %collective-permute-start.8) | collective-permute-done | bytes 262176 | tf_op jit(solution)/shard_map/ppermute | solution.py:557
  45.2 3.0 %collective-permute-start.12 = (f32[2,32,1024]{2,1,0:T(8,128)S(1)}, f32[2,32,1024]{2,1,0:T(8,128)S(1)}, u32[]{:S(2)}, u32[]{:S(2)}) collective-permute-start(f32[2,32,1024]{2,1,0:T(8,128)S(1)} %left_gram.1.refs_0_.refs_2_.left_ref), channel_id=1, source_target_pairs={{1,0},{2,1},{3,2},{0,3},{5,4},{6,5},{7,6},{4,7},{9,8},{10,9},{11,1... | collective-permute-start | bytes 786440 | tf_op jit(solution)/shard_map/ppermute | solution.py:557
  52.5 2.1 %local_first.3 = (f32[2,32,1024]{2,1,0:T(8,128)S(1)}, f32[2,32,1024]{2,1,0:T(8,128)S(1)}) custom-call(s32[640]{0:T(1024)S(4)} %plan.1.plan_ref, bf16[160,128,256]{2,1,0:T(8,128)(2,1)S(1)} %prep.1.tiles_ref, f32[2,32,1024]{2,1,0:T(8,128)S(1)} %left_gram.1.refs_0_.refs_2_.left_ref, f32[2,32,1024]{2,1,0:T(8,128)S(1)} %get-tuple-element.90.refs_1_.refs_3_.right_ref), custom_call_target="tpu_custom_call" | custom-call | flops 671088640 | bytes 1572864 | tf_op jit(solution)/shard_map/local_first/pallas_call | solution.py:42
  56.4 3.2 %collective-permute-done.14 = f32[8,128]{1,0:T(8,128)S(1)} collective-permute-done((f32[8,128]{1,0:T(8,128)S(1)}, f32[8,128]{1,0:T(8,128)S(1)}, u32[]{:S(2)}, u32[]{:S(2)}) %collective-permute-start.14) | collective-permute-done | bytes 4128 | tf_op jit(solution)/shard_map/ppermute | solution.py:503
  62.0 2.5 %collective-permute-start.20 = (f32[1,32,2048]{2,1,0:T(8,128)S(1)}, f32[1,32,2048]{2,1,0:T(8,128)S(1)}, u32[]{:S(2)}, u32[]{:S(2)}) collective-permute-start(f32[1,32,2048]{2,1,0:T(8,128)S(1)} %get-tuple-element.107), channel_id=1, source_target_pairs={{0,28},{4,8},{8,4},{12,16},{16,12},{20,24},{24,20},{28,0},{1,29},{... | collective-permute-start | bytes 786440 | tf_op jit(solution)/shard_map/ppermute | solution.py:558
  64.5 1.7 %collective-permute-start.22 = (f32[2,32,1024]{2,1,0:T(8,128)S(1)}, f32[2,32,1024]{2,1,0:T(8,128)S(1)}, u32[]{:S(2)}, u32[]{:S(2)}) collective-permute-start(f32[2,32,1024]{2,1,0:T(8,128)S(1)} %get-tuple-element.101.refs_0_.refs_2_), channel_id=1, source_target_pairs={{1,0},{2,1},{3,2},{0,3},{5,4},{6,5},{7,6},{4,7},{9,8},{10,9},{11,1... | collective-permute-start | bytes 786440 | tf_op jit(solution)/shard_map/ppermute | solution.py:557
  66.2 2.1 %local_step.4 = (f32[2,32,1024]{2,1,0:T(8,128)S(1)}, f32[2,32,1024]{2,1,0:T(8,128)S(1)}) custom-call(s32[640]{0:T(1024)S(4)} %plan.1.plan_ref, bf16[160,128,256]{2,1,0:T(8,128)(2,1)S(1)} %prep.1.tiles_ref, f32[2,32,1024]{2,1,0:T(8,128)S(1)} %get-tuple-element.101.refs_0_.refs_2_, f32[2,32,1024]{2,1,0:T(8,128)S(1)} %right_first.3.refs_0_.refs_1_.refs_3_, ...), custom_call_target="tpu_custom_call" | custom-call | flops 671088640 | bytes 1572864 | tf_op jit(solution)/shard_map/local_step/pallas_call | solution.py:42
  69.3 2.7 %collective-permute-done.21 = f32[8,128]{1,0:T(8,128)S(1)} collective-permute-done((f32[8,128]{1,0:T(8,128)S(1)}, f32[8,128]{1,0:T(8,128)S(1)}, u32[]{:S(2)}, u32[]{:S(2)}) %collective-permute-start.21) | collective-permute-done | bytes 4128 | tf_op jit(solution)/shard_map/ppermute | solution.py:503
  72.8 2.8 %collective-permute-start.23 = (f32[2,32,1024]{2,1,0:T(8,128)S(1)}, f32[2,32,1024]{2,1,0:T(8,128)S(1)}, u32[]{:S(2)}, u32[]{:S(2)}) collective-permute-start(f32[2,32,1024]{2,1,0:T(8,128)S(1)} %left_step.4.refs_0_), channel_id=1, source_target_pairs={{1,0},{2,1},{3,2},{0,3},{5,4},{6,5},{7,6},{4,7},{9,8},{10,9},{11,1... | collective-permute-start | bytes 786440 | tf_op jit(solution)/shard_map/ppermute | solution.py:557
  78.4 2.1 %local_step.5 = (f32[2,32,1024]{2,1,0:T(8,128)S(1)}, f32[2,32,1024]{2,1,0:T(8,128)S(1)}) custom-call(s32[640]{0:T(1024)S(4)} %plan.1.plan_ref, bf16[160,128,256]{2,1,0:T(8,128)(2,1)S(1)} %prep.1.tiles_ref, f32[2,32,1024]{2,1,0:T(8,128)S(1)} %left_step.4.refs_0_, f32[2,32,1024]{2,1,0:T(8,128)S(1)} %get-tuple-element.112.refs_1_, ...), custom_call_target="tpu_custom_call" | custom-call | flops 671088640 | bytes 1572864 | tf_op jit(solution)/shard_map/local_step/pallas_call | solution.py:42
  81.2 5.5 %collective-permute-done.24 = f32[8,128]{1,0:T(8,128)S(1)} collective-permute-done((f32[8,128]{1,0:T(8,128)S(1)}, f32[8,128]{1,0:T(8,128)S(1)}, u32[]{:S(2)}, u32[]{:S(2)}) %collective-permute-start.24) | collective-permute-done | bytes 4128 | tf_op jit(solution)/shard_map/ppermute | solution.py:503
  87.5 2.5 %collective-permute-start.28 = (f32[2,32,1024]{2,1,0:T(8,128)S(1)}, f32[2,32,1024]{2,1,0:T(8,128)S(1)}, u32[]{:S(2)}, u32[]{:S(2)}) collective-permute-start(f32[2,32,1024]{2,1,0:T(8,128)S(1)} %right_step.5.refs_0_.refs_1_.refs_2_), channel_id=1, source_target_pairs={{0,1},{1,2},{2,3},{3,0},{4,5},{5,6},{6,7},{7,4},{8,9},{9,10},{10,1... | collective-permute-start | bytes 786440 | tf_op jit(solution)/shard_map/ppermute | solution.py:557
  91.9 1.8 %collective-permute-start.30 = (f32[2,32,1024]{2,1,0:T(8,128)S(1)}, f32[2,32,1024]{2,1,0:T(8,128)S(1)}, u32[]{:S(2)}, u32[]{:S(2)}) collective-permute-start(f32[2,32,1024]{2,1,0:T(8,128)S(1)} %get-tuple-element.123.refs_0_.refs_1_), channel_id=1, source_target_pairs={{1,0},{2,1},{3,2},{0,3},{5,4},{6,5},{7,6},{4,7},{9,8},{10,9},{11,1... | collective-permute-start | bytes 786440 | tf_op jit(solution)/shard_map/ppermute | solution.py:557
  93.7 2.1 %local_image.1 = (f32[2,32,1024]{2,1,0:T(8,128)S(1)}, f32[2,32,1024]{2,1,0:T(8,128)S(1)}) custom-call(s32[640]{0:T(1024)S(4)} %plan.1.plan_ref, bf16[160,128,256]{2,1,0:T(8,128)(2,1)S(1)} %prep.1.tiles_ref, f32[2,32,1024]{2,1,0:T(8,128)S(1)} %get-tuple-element.123.refs_0_.refs_1_, f32[2,32,1024]{2,1,0:T(8,128)S(1)} %right_step.5.refs_0_.refs_1_.refs_2_), custom_call_target="tpu_custom_call" | custom-call | flops 671088640 | bytes 1572864 | tf_op jit(solution)/shard_map/local_image/pallas_call | solution.py:42
  96.8 7.2 %collective-permute-done.29 = f32[8,128]{1,0:T(8,128)S(1)} collective-permute-done((f32[8,128]{1,0:T(8,128)S(1)}, f32[8,128]{1,0:T(8,128)S(1)}, u32[]{:S(2)}, u32[]{:S(2)}) %collective-permute-start.29) | collective-permute-done | bytes 4128 | tf_op jit(solution)/shard_map/ppermute | solution.py:503
  106.3 2.2 %right_image.1 = (f32[2,32,1024]{2,1,0:T(8,128)S(1)}, f32[2,32,2048]{2,1,0:T(8,128)S(1)}, f32[16,128]{1,0:T(8,128)S(1)}) custom-call(s32[640]{0:T(1024)S(4)} %plan.1.plan_ref, bf16[160,128,256]{2,1,0:T(8,128)(2,1)S(1)} %prep.1.tiles_ref, f32[2,32,1024]{2,1,0:T(8,128)S(1)} %get-tuple-element.130.part_ref, ...), custom_call_target="tpu_custom_call", output_to_operand_aliasing={{0}: (2, {})} | custom-call | flops 134217728 | bytes 1572864 | tf_op jit(solution)/shard_map/right_image/pallas_call | solution.py:42
  111.6 1.6 %collective-permute-start.34 = (f32[16,128]{1,0:T(8,128)S(1)}, f32[16,128]{1,0:T(8,128)S(1)}, u32[]{:S(2)}, u32[]{:S(2)}) collective-permute-start(f32[16,128]{1,0:T(8,128)S(1)} %add.50), channel_id=1, source_target_pairs={{0,8},{4,12},{8,0},{12,4},{16,24},{20,28},{24,16},{28,20},{1,9},{5... | collective-permute-start | bytes 24584 | tf_op jit(solution)/shard_map/ppermute | solution.py:503
  117.6 2.0 %collective-permute-start.37 = (f32[16,128]{1,0:T(8,128)S(1)}, f32[16,128]{1,0:T(8,128)S(1)}, u32[]{:S(2)}, u32[]{:S(2)}) collective-permute-start(f32[16,128]{1,0:T(8,128)S(1)} %add_add_fusion.1), channel_id=1, source_target_pairs={{0,1},{1,0},{2,3},{3,2},{4,5},{5,4},{6,7},{7,6},{8,9},{9,8},{10,11... | collective-permute-start | bytes 24584 | tf_op jit(solution)/shard_map/ppermute | solution.py:503
  121.3 2.5 %close.1 = (f32[2,32,2048]{2,1,0:T(8,128)}, f32[32,32]{1,0:T(8,128)}) custom-call(f32[16,128]{1,0:T(8,128)S(1)} %add_add_fusion.sums_ref, f32[2,32,2048]{2,1,0:T(8,128)S(1)} %get-tuple-element.135.y_ref), custom_call_target="tpu_custom_call" | custom-call | flops 8388608 | bytes 1048576 | tf_op jit(solution)/shard_map/close/pallas_call | solution.py:42
  (88 shorter events, 37.6 us)
Async XLA Ops:
  2.4 17.4 %collective-permute-start = (f32[2,32,1024]{2,1,0:T(8,128)S(1)}, f32[2,32,1024]{2,1,0:T(8,128)S(1)}, u32[]{:S(2)}, u32[]{:S(2)}) collective-permute-start(f32[2,32,1024]{2,1,0:T(8,128)S(1)} %get-tuple-element.72.refs_1_.refs_3_), channel_id=1, source_target_pairs={{0,1},{1,2},{2,3},{3,0},{4,5},{5,6},{6,7},{7,4},{8,9},{9,10},{10,1... | collective-permute-start | bytes 786440 | tf_op jit(solution)/shard_map/ppermute | solution.py:557
  5.5 14.3 %collective-permute-start.1 = (f32[1,32,2048]{2,1,0:T(8,128)S(1)}, f32[1,32,2048]{2,1,0:T(8,128)S(1)}, u32[]{:S(2)}, u32[]{:S(2)}) collective-permute-start(f32[1,32,2048]{2,1,0:T(8,128)S(1)} %get-tuple-element.74), channel_id=1, source_target_pairs={{0,4},{4,0},{8,12},{12,8},{16,20},{20,16},{24,28},{28,24},{1,5},{5... | collective-permute-start | bytes 786440 | tf_op jit(solution)/shard_map/ppermute | solution.py:559
  5.5 14.3 %collective-permute-start.2 = (f32[1,32,2048]{2,1,0:T(8,128)S(1)}, f32[1,32,2048]{2,1,0:T(8,128)S(1)}, u32[]{:S(2)}, u32[]{:S(2)}) collective-permute-start(f32[1,32,2048]{2,1,0:T(8,128)S(1)} %get-tuple-element.75), channel_id=1, source_target_pairs={{0,28},{4,8},{8,4},{12,16},{16,12},{20,24},{24,20},{28,0},{1,29},{... | collective-permute-start | bytes 786440 | tf_op jit(solution)/shard_map/ppermute | solution.py:558
  8.0 14.4 %collective-permute-start.3 = (f32[2,32,1024]{2,1,0:T(8,128)S(1)}, f32[2,32,1024]{2,1,0:T(8,128)S(1)}, u32[]{:S(2)}, u32[]{:S(2)}) collective-permute-start(f32[2,32,1024]{2,1,0:T(8,128)S(1)} %get-tuple-element.71.refs_0_.refs_2_), channel_id=1, source_target_pairs={{1,0},{2,1},{3,2},{0,3},{5,4},{6,5},{7,6},{4,7},{9,8},{10,9},{11,1... | collective-permute-start | bytes 786440 | tf_op jit(solution)/shard_map/ppermute | solution.py:557
  20.6 8.4 %collective-permute-start.4 = (f32[2,32,1024]{2,1,0:T(8,128)S(1)}, f32[2,32,1024]{2,1,0:T(8,128)S(1)}, u32[]{:S(2)}, u32[]{:S(2)}) collective-permute-start(f32[2,32,1024]{2,1,0:T(8,128)S(1)} %left_first.2.refs_0_.refs_2_), channel_id=1, source_target_pairs={{1,0},{2,1},{3,2},{0,3},{5,4},{6,5},{7,6},{4,7},{9,8},{10,9},{11,1... | collective-permute-start | bytes 786440 | tf_op jit(solution)/shard_map/ppermute | solution.py:557
  23.2 5.8 %collective-permute-start.6 = (f32[1,32,2048]{2,1,0:T(8,128)S(1)}, f32[1,32,2048]{2,1,0:T(8,128)S(1)}, u32[]{:S(2)}, u32[]{:S(2)}) collective-permute-start(f32[1,32,2048]{2,1,0:T(8,128)S(1)} %get-tuple-element.81), channel_id=1, source_target_pairs={{0,4},{4,0},{8,12},{12,8},{16,20},{20,16},{24,28},{28,24},{1,5},{5... | collective-permute-start | bytes 786440 | tf_op jit(solution)/shard_map/ppermute | solution.py:559
  23.3 9.4 %collective-permute-start.7 = (f32[1,32,2048]{2,1,0:T(8,128)S(1)}, f32[1,32,2048]{2,1,0:T(8,128)S(1)}, u32[]{:S(2)}, u32[]{:S(2)}) collective-permute-start(f32[1,32,2048]{2,1,0:T(8,128)S(1)} %get-tuple-element.82), channel_id=1, source_target_pairs={{0,28},{4,8},{8,4},{12,16},{16,12},{20,24},{24,20},{28,0},{1,29},{... | collective-permute-start | bytes 786440 | tf_op jit(solution)/shard_map/ppermute | solution.py:558
  25.4 9.1 %collective-permute-start.5 = (f32[2,32,1024]{2,1,0:T(8,128)S(1)}, f32[2,32,1024]{2,1,0:T(8,128)S(1)}, u32[]{:S(2)}, u32[]{:S(2)}) collective-permute-start(f32[2,32,1024]{2,1,0:T(8,128)S(1)} %get-tuple-element.78.refs_1_.refs_3_), channel_id=1, source_target_pairs={{0,1},{1,2},{2,3},{3,0},{4,5},{5,6},{6,7},{7,4},{8,9},{9,10},{10,1... | collective-permute-start | bytes 786440 | tf_op jit(solution)/shard_map/ppermute | solution.py:557
  33.4 11.1 %collective-permute-start.8 = (f32[2,32,1024]{2,1,0:T(8,128)S(1)}, f32[2,32,1024]{2,1,0:T(8,128)S(1)}, u32[]{:S(2)}, u32[]{:S(2)}) collective-permute-start(f32[2,32,1024]{2,1,0:T(8,128)S(1)} %right_step.3.refs_0_.refs_1_), channel_id=1, source_target_pairs={{0,1},{1,2},{2,3},{3,0},{4,5},{5,6},{6,7},{7,4},{8,9},{9,10},{10,1... | collective-permute-start | bytes 786440 | tf_op jit(solution)/shard_map/ppermute | solution.py:557
  35.3 9.2 %collective-permute-start.9 = (f32[1,32,2048]{2,1,0:T(8,128)S(1)}, f32[1,32,2048]{2,1,0:T(8,128)S(1)}, u32[]{:S(2)}, u32[]{:S(2)}) collective-permute-start(f32[1,32,2048]{2,1,0:T(8,128)S(1)} %get-tuple-element.86), channel_id=1, source_target_pairs={{0,4},{4,0},{8,12},{12,8},{16,20},{20,16},{24,28},{28,24},{1,5},{5... | collective-permute-start | bytes 786440 | tf_op jit(solution)/shard_map/ppermute | solution.py:559
  35.4 9.1 %collective-permute-start.10 = (f32[1,32,2048]{2,1,0:T(8,128)S(1)}, f32[1,32,2048]{2,1,0:T(8,128)S(1)}, u32[]{:S(2)}, u32[]{:S(2)}) collective-permute-start(f32[1,32,2048]{2,1,0:T(8,128)S(1)} %get-tuple-element.87), channel_id=1, source_target_pairs={{0,28},{4,8},{8,4},{12,16},{16,12},{20,24},{24,20},{28,0},{1,29},{... | collective-permute-start | bytes 786440 | tf_op jit(solution)/shard_map/ppermute | solution.py:558
  37.4 11.7 %collective-permute-start.11 = (f32[2,32,1024]{2,1,0:T(8,128)S(1)}, f32[2,32,1024]{2,1,0:T(8,128)S(1)}, u32[]{:S(2)}, u32[]{:S(2)}) collective-permute-start(f32[2,32,1024]{2,1,0:T(8,128)S(1)} %get-tuple-element.84.refs_0_), channel_id=1, source_target_pairs={{1,0},{2,1},{3,2},{0,3},{5,4},{6,5},{7,6},{4,7},{9,8},{10,9},{11,1... | collective-permute-start | bytes 786440 | tf_op jit(solution)/shard_map/ppermute | solution.py:557
  45.2 14.4 %collective-permute-start.12 = (f32[2,32,1024]{2,1,0:T(8,128)S(1)}, f32[2,32,1024]{2,1,0:T(8,128)S(1)}, u32[]{:S(2)}, u32[]{:S(2)}) collective-permute-start(f32[2,32,1024]{2,1,0:T(8,128)S(1)} %left_gram.1.refs_0_.refs_2_.left_ref), channel_id=1, source_target_pairs={{1,0},{2,1},{3,2},{0,3},{5,4},{6,5},{7,6},{4,7},{9,8},{10,9},{11,1... | collective-permute-start | bytes 786440 | tf_op jit(solution)/shard_map/ppermute | solution.py:557
  50.4 9.2 %collective-permute-start.16 = (f32[1,32,2048]{2,1,0:T(8,128)S(1)}, f32[1,32,2048]{2,1,0:T(8,128)S(1)}, u32[]{:S(2)}, u32[]{:S(2)}) collective-permute-start(f32[1,32,2048]{2,1,0:T(8,128)S(1)} %get-tuple-element.98), channel_id=1, source_target_pairs={{0,4},{4,0},{8,12},{12,8},{16,20},{20,16},{24,28},{28,24},{1,5},{5... | collective-permute-start | bytes 786440 | tf_op jit(solution)/shard_map/ppermute | solution.py:559
  50.4 9.4 %collective-permute-start.17 = (f32[1,32,2048]{2,1,0:T(8,128)S(1)}, f32[1,32,2048]{2,1,0:T(8,128)S(1)}, u32[]{:S(2)}, u32[]{:S(2)}) collective-permute-start(f32[1,32,2048]{2,1,0:T(8,128)S(1)} %get-tuple-element.99), channel_id=1, source_target_pairs={{0,28},{4,8},{8,4},{12,16},{16,12},{20,24},{24,20},{28,0},{1,29},{... | collective-permute-start | bytes 786440 | tf_op jit(solution)/shard_map/ppermute | solution.py:558
  51.9 9.3 %collective-permute-start.15 = (f32[2,32,1024]{2,1,0:T(8,128)S(1)}, f32[2,32,1024]{2,1,0:T(8,128)S(1)}, u32[]{:S(2)}, u32[]{:S(2)}) collective-permute-start(f32[2,32,1024]{2,1,0:T(8,128)S(1)} %get-tuple-element.90.refs_1_.refs_3_.right_ref), channel_id=1, source_target_pairs={{0,1},{1,2},{2,3},{3,0},{4,5},{5,6},{6,7},{7,4},{8,9},{9,10},{10,1... | collective-permute-start | bytes 786440 | tf_op jit(solution)/shard_map/ppermute | solution.py:557
  60.6 11.4 %collective-permute-start.18 = (f32[2,32,1024]{2,1,0:T(8,128)S(1)}, f32[2,32,1024]{2,1,0:T(8,128)S(1)}, u32[]{:S(2)}, u32[]{:S(2)}) collective-permute-start(f32[2,32,1024]{2,1,0:T(8,128)S(1)} %right_first.3.refs_0_.refs_1_.refs_3_), channel_id=1, source_target_pairs={{0,1},{1,2},{2,3},{3,0},{4,5},{5,6},{6,7},{7,4},{8,9},{9,10},{10,1... | collective-permute-start | bytes 786440 | tf_op jit(solution)/shard_map/ppermute | solution.py:557
  62.0 10.1 %collective-permute-start.19 = (f32[1,32,2048]{2,1,0:T(8,128)S(1)}, f32[1,32,2048]{2,1,0:T(8,128)S(1)}, u32[]{:S(2)}, u32[]{:S(2)}) collective-permute-start(f32[1,32,2048]{2,1,0:T(8,128)S(1)} %get-tuple-element.106), channel_id=1, source_target_pairs={{0,4},{4,0},{8,12},{12,8},{16,20},{20,16},{24,28},{28,24},{1,5},{5... | collective-permute-start | bytes 786440 | tf_op jit(solution)/shard_map/ppermute | solution.py:559
  62.0 10.0 %collective-permute-start.20 = (f32[1,32,2048]{2,1,0:T(8,128)S(1)}, f32[1,32,2048]{2,1,0:T(8,128)S(1)}, u32[]{:S(2)}, u32[]{:S(2)}) collective-permute-start(f32[1,32,2048]{2,1,0:T(8,128)S(1)} %get-tuple-element.107), channel_id=1, source_target_pairs={{0,28},{4,8},{8,4},{12,16},{16,12},{20,24},{24,20},{28,0},{1,29},{... | collective-permute-start | bytes 786440 | tf_op jit(solution)/shard_map/ppermute | solution.py:558
  64.5 11.7 %collective-permute-start.22 = (f32[2,32,1024]{2,1,0:T(8,128)S(1)}, f32[2,32,1024]{2,1,0:T(8,128)S(1)}, u32[]{:S(2)}, u32[]{:S(2)}) collective-permute-start(f32[2,32,1024]{2,1,0:T(8,128)S(1)} %get-tuple-element.101.refs_0_.refs_2_), channel_id=1, source_target_pairs={{1,0},{2,1},{3,2},{0,3},{5,4},{6,5},{7,6},{4,7},{9,8},{10,9},{11,1... | collective-permute-start | bytes 786440 | tf_op jit(solution)/shard_map/ppermute | solution.py:557
  72.8 14.0 %collective-permute-start.23 = (f32[2,32,1024]{2,1,0:T(8,128)S(1)}, f32[2,32,1024]{2,1,0:T(8,128)S(1)}, u32[]{:S(2)}, u32[]{:S(2)}) collective-permute-start(f32[2,32,1024]{2,1,0:T(8,128)S(1)} %left_step.4.refs_0_), channel_id=1, source_target_pairs={{1,0},{2,1},{3,2},{0,3},{5,4},{6,5},{7,6},{4,7},{9,8},{10,9},{11,1... | collective-permute-start | bytes 786440 | tf_op jit(solution)/shard_map/ppermute | solution.py:557
  77.0 9.8 %collective-permute-start.26 = (f32[1,32,2048]{2,1,0:T(8,128)S(1)}, f32[1,32,2048]{2,1,0:T(8,128)S(1)}, u32[]{:S(2)}, u32[]{:S(2)}) collective-permute-start(f32[1,32,2048]{2,1,0:T(8,128)S(1)} %get-tuple-element.120), channel_id=1, source_target_pairs={{0,4},{4,0},{8,12},{12,8},{16,20},{20,16},{24,28},{28,24},{1,5},{5... | collective-permute-start | bytes 786440 | tf_op jit(solution)/shard_map/ppermute | solution.py:559
  77.1 9.7 %collective-permute-start.27 = (f32[1,32,2048]{2,1,0:T(8,128)S(1)}, f32[1,32,2048]{2,1,0:T(8,128)S(1)}, u32[]{:S(2)}, u32[]{:S(2)}) collective-permute-start(f32[1,32,2048]{2,1,0:T(8,128)S(1)} %get-tuple-element.121), channel_id=1, source_target_pairs={{0,28},{4,8},{8,4},{12,16},{16,12},{20,24},{24,20},{28,0},{1,29},{... | collective-permute-start | bytes 786440 | tf_op jit(solution)/shard_map/ppermute | solution.py:558
  77.9 12.2 %collective-permute-start.25 = (f32[2,32,1024]{2,1,0:T(8,128)S(1)}, f32[2,32,1024]{2,1,0:T(8,128)S(1)}, u32[]{:S(2)}, u32[]{:S(2)}) collective-permute-start(f32[2,32,1024]{2,1,0:T(8,128)S(1)} %get-tuple-element.112.refs_1_), channel_id=1, source_target_pairs={{0,1},{1,2},{2,3},{3,0},{4,5},{5,6},{6,7},{7,4},{8,9},{9,10},{10,1... | collective-permute-start | bytes 786440 | tf_op jit(solution)/shard_map/ppermute | solution.py:557
  80.5 6.2 %collective-permute-start.24 = (f32[8,128]{1,0:T(8,128)S(1)}, f32[8,128]{1,0:T(8,128)S(1)}, u32[]{:S(2)}, u32[]{:S(2)}) collective-permute-start(f32[8,128]{1,0:T(8,128)S(1)} %add.47), channel_id=1, source_target_pairs={{0,1},{1,0},{2,3},{3,2},{4,5},{5,4},{6,7},{7,6},{8,9},{9,8},{10,11... | collective-permute-start | bytes 12296 | tf_op jit(solution)/shard_map/ppermute | solution.py:503
  87.5 17.9 %collective-permute-start.28 = (f32[2,32,1024]{2,1,0:T(8,128)S(1)}, f32[2,32,1024]{2,1,0:T(8,128)S(1)}, u32[]{:S(2)}, u32[]{:S(2)}) collective-permute-start(f32[2,32,1024]{2,1,0:T(8,128)S(1)} %right_step.5.refs_0_.refs_1_.refs_2_), channel_id=1, source_target_pairs={{0,1},{1,2},{2,3},{3,0},{4,5},{5,6},{6,7},{7,4},{8,9},{9,10},{10,1... | collective-permute-start | bytes 786440 | tf_op jit(solution)/shard_map/ppermute | solution.py:557
  90.8 14.6 %collective-permute-start.31 = (f32[1,32,2048]{2,1,0:T(8,128)S(1)}, f32[1,32,2048]{2,1,0:T(8,128)S(1)}, u32[]{:S(2)}, u32[]{:S(2)}) collective-permute-start(f32[1,32,2048]{2,1,0:T(8,128)S(1)} %get-tuple-element.131), channel_id=1, source_target_pairs={{0,4},{4,0},{8,12},{12,8},{16,20},{20,16},{24,28},{28,24},{1,5},{5... | collective-permute-start | bytes 786440 | tf_op jit(solution)/shard_map/ppermute | solution.py:559
  90.9 14.6 %collective-permute-start.32 = (f32[1,32,2048]{2,1,0:T(8,128)S(1)}, f32[1,32,2048]{2,1,0:T(8,128)S(1)}, u32[]{:S(2)}, u32[]{:S(2)}) collective-permute-start(f32[1,32,2048]{2,1,0:T(8,128)S(1)} %get-tuple-element.132), channel_id=1, source_target_pairs={{0,28},{4,8},{8,4},{12,16},{16,12},{20,24},{24,20},{28,0},{1,29},{... | collective-permute-start | bytes 786440 | tf_op jit(solution)/shard_map/ppermute | solution.py:558
  91.9 14.3 %collective-permute-start.30 = (f32[2,32,1024]{2,1,0:T(8,128)S(1)}, f32[2,32,1024]{2,1,0:T(8,128)S(1)}, u32[]{:S(2)}, u32[]{:S(2)}) collective-permute-start(f32[2,32,1024]{2,1,0:T(8,128)S(1)} %get-tuple-element.123.refs_0_.refs_1_), channel_id=1, source_target_pairs={{1,0},{2,1},{3,2},{0,3},{5,4},{6,5},{7,6},{4,7},{9,8},{10,9},{11,1... | collective-permute-start | bytes 786440 | tf_op jit(solution)/shard_map/ppermute | solution.py:557
  95.8 8.2 %collective-permute-start.29 = (f32[8,128]{1,0:T(8,128)S(1)}, f32[8,128]{1,0:T(8,128)S(1)}, u32[]{:S(2)}, u32[]{:S(2)}) collective-permute-start(f32[8,128]{1,0:T(8,128)S(1)} %add.48), channel_id=1, source_target_pairs={{0,2},{1,3},{2,0},{3,1},{4,6},{5,7},{6,4},{7,5},{8,10},{9,11},{10,... | collective-permute-start | bytes 12296 | tf_op jit(solution)/shard_map/ppermute | solution.py:503
  109.7 4.5 %collective-permute-start.36 = (f32[16,128]{1,0:T(8,128)S(1)}, f32[16,128]{1,0:T(8,128)S(1)}, u32[]{:S(2)}, u32[]{:S(2)}) collective-permute-start(f32[16,128]{1,0:T(8,128)S(1)} %add.50), channel_id=1, source_target_pairs={{0,24},{4,28},{8,16},{12,20},{16,8},{20,12},{24,0},{28,4},{1,25},{... | collective-permute-start | bytes 24584 | tf_op jit(solution)/shard_map/ppermute | solution.py:503
  115.2 5.5 %collective-permute-start.39 = (f32[16,128]{1,0:T(8,128)S(1)}, f32[16,128]{1,0:T(8,128)S(1)}, u32[]{:S(2)}, u32[]{:S(2)}) collective-permute-start(f32[16,128]{1,0:T(8,128)S(1)} %add_add_fusion.1), channel_id=1, source_target_pairs={{0,3},{1,2},{2,1},{3,0},{4,7},{5,6},{6,5},{7,4},{8,11},{9,10},{10,... | collective-permute-start | bytes 24584 | tf_op jit(solution)/shard_map/ppermute | solution.py:503
  (10 other events, 27.2 us)

commit v9 on v8

--- a/solution.py
+++ b/solution.py
@@ -69,9 +69,9 @@
         copy(c).wait()
         slot = lax.rem(c, slots)
         for n in range(step):
-            high, low = split(buffer_ref[slot, n].T)
-            out_ref[c * step + n, :, :TILE] = high
-            out_ref[c * step + n, :, TILE:] = low
+            high, low = split(buffer_ref[slot, n])
+            out_ref[c * step + n, :, :TILE] = high.T
+            out_ref[c * step + n, :, TILE:] = low.T
 
         @pl.when(c + slots < chunks)
         def _():
@@ -593,7 +593,7 @@
         "image", 1.0, 0, state3, None, (gram, lambda gram: factor(stage(3)(gram), width, count_all))
     )
     first_basis = basis(matrix, filtered[0])
-    sums = add_over(sums, stages_of("tm") + stages_of("space"))
+    sums = add_over(sums, stages_of("space") + stages_of("tm"))
     ritz_basis, ritz_matrix = close(sums, second, count_all)
     return ritz_basis, first_basis, ritz_matrix
 

time: 124 us -> 124 us (level)
    ppermute x7, starting transfers between devices: 12.4 us -> 10.5 us  [step(): far_slice = lax.ppermute(ends[1], 'tm', outer_pairs('tm'))]
  transfers between devices with their start and end apart: 40 -> 40, of which waited for: 18 -> 17; matrix products, arithmetic and copies ran while one was open for 0% -> 0% of each run, Pallas kernels for 28% -> 28%
where the time goes in v9:
time: 124 us
  starting transfers between devices  45.7 us (37%)
  Pallas kernels  39.8 us (32%)
  waiting for transfers between devices  35.7 us (29%)
  local copies, waits for them, and re-layouts  1.81 us (1%)
    pallas_call x25, Pallas kernels, call(): pl.pallas_call(kernel, out_shape=out_shape, in_specs=specs, out_specs=[WH...  33.1 us
    ppermute x12, waiting for transfers between devices, add_over(): lax.ppermute(value, axis, [(i, i ^ k) for i in range(count)])  24.1 us
    ppermute x14, starting transfers between devices, step(): halos[side] = lax.ppermute(sides[1 - side], 'space', pairs)  23.8 us
    ppermute x12, starting transfers between devices, add_over(): lax.ppermute(value, axis, [(i, i ^ k) for i in range(count)])  11 us
    ppermute x7, starting transfers between devices, step(): far_slice = lax.ppermute(ends[1], 'tm', outer_pairs('tm'))  10.5 us
    ppermute x14, waiting for transfers between devices, step(): halos[side] = lax.ppermute(sides[1 - side], 'space', pairs)  6.57 us
    ppermute x7, waiting for transfers between devices, step(): far_slice = lax.ppermute(ends[1], 'tm', outer_pairs('tm'))  5.04 us
    pallas_call x1, Pallas kernels, prep(): pl.pallas_call(prep_kernel, out_shape=VM((tiles.shape[0], TILE, 2 * TILE)...  4.73 us
  transfers between devices with their start and end apart: 40, of which 17 were waited for; matrix products, arithmetic and copies ran while one was open for 0% of the time, Pallas kernels for 28%

profile of v9, /device:TPU:0, one launch (start us, length us, event | category | flops | bytes accessed | tf_op | source)
XLA Modules:
  0.0 124.0 jit_solution(15433119838461005144)
XLA Ops:
  2.4 3.1 %collective-permute-start = (f32[2,32,1024]{2,1,0:T(8,128)S(1)}, f32[2,32,1024]{2,1,0:T(8,128)S(1)}, u32[]{:S(2)}, u32[]{:S(2)}) collective-permute-start(f32[2,32,1024]{2,1,0:T(8,128)S(1)} %get-tuple-element.72.refs_1_.refs_3_), channel_id=1, source_target_pairs={{0,1},{1,2},{2,3},{3,0},{4,5},{5,6},{6,7},{7,4},{8,9},{9,10},{10,1... | collective-permute-start | bytes 786440 | tf_op jit(solution)/shard_map/ppermute | solution.py:557
  5.5 2.6 %collective-permute-start.2 = (f32[1,32,2048]{2,1,0:T(8,128)S(1)}, f32[1,32,2048]{2,1,0:T(8,128)S(1)}, u32[]{:S(2)}, u32[]{:S(2)}) collective-permute-start(f32[1,32,2048]{2,1,0:T(8,128)S(1)} %get-tuple-element.75), channel_id=1, source_target_pairs={{0,28},{4,8},{8,4},{12,16},{16,12},{20,24},{24,20},{28,0},{1,29},{... | collective-permute-start | bytes 786440 | tf_op jit(solution)/shard_map/ppermute | solution.py:558
  8.0 2.2 %collective-permute-start.3 = (f32[2,32,1024]{2,1,0:T(8,128)S(1)}, f32[2,32,1024]{2,1,0:T(8,128)S(1)}, u32[]{:S(2)}, u32[]{:S(2)}) collective-permute-start(f32[2,32,1024]{2,1,0:T(8,128)S(1)} %get-tuple-element.71.refs_0_.refs_2_), channel_id=1, source_target_pairs={{1,0},{2,1},{3,2},{0,3},{5,4},{6,5},{7,6},{4,7},{9,8},{10,9},{11,1... | collective-permute-start | bytes 786440 | tf_op jit(solution)/shard_map/ppermute | solution.py:557
  11.0 1.9 %plan.1.plan_ref = s32[640]{0:T(1024)S(4)} custom-call(s32[2,80]{1,0:T(2,128)S(1)} %copy-done.1, s32[5]{0:T(128)S(1)} %stack.31.flags_ref.odd_ref), custom_call_target="tpu_custom_call" | custom-call | tf_op jit(solution)/shard_map/plan/pallas_call | solution.py:160
  12.9 4.7 %prep.1.tiles_ref = bf16[160,128,256]{2,1,0:T(8,128)(2,1)S(1)} custom-call(f32[160,128,128]{2,1,0:T(8,128)} %bitcast.6), custom_call_target="tpu_custom_call" | custom-call | bytes 10485760 | tf_op jit(solution)/shard_map/prep/pallas_call | solution.py:88
  17.6 2.1 %local_first.2 = (f32[2,32,1024]{2,1,0:T(8,128)S(1)}, f32[2,32,1024]{2,1,0:T(8,128)S(1)}) custom-call(s32[640]{0:T(1024)S(4)} %plan.1.plan_ref, bf16[160,128,256]{2,1,0:T(8,128)(2,1)S(1)} %prep.1.tiles_ref, f32[2,32,1024]{2,1,0:T(8,128)S(1)} %get-tuple-element.71.refs_0_.refs_2_, f32[2,32,1024]{2,1,0:T(8,128)S(1)} %get-tuple-element.72.refs_1_.refs_3_), custom_call_target="tpu_custom_call" | custom-call | flops 671088640 | bytes 1572864 | tf_op jit(solution)/shard_map/local_first/pallas_call | solution.py:42
  20.5 1.8 %collective-permute-start.4 = (f32[2,32,1024]{2,1,0:T(8,128)S(1)}, f32[2,32,1024]{2,1,0:T(8,128)S(1)}, u32[]{:S(2)}, u32[]{:S(2)}) collective-permute-start(f32[2,32,1024]{2,1,0:T(8,128)S(1)} %left_first.2.refs_0_.refs_2_), channel_id=1, source_target_pairs={{1,0},{2,1},{3,2},{0,3},{5,4},{6,5},{7,6},{4,7},{9,8},{10,9},{11,1... | collective-permute-start | bytes 786440 | tf_op jit(solution)/shard_map/ppermute | solution.py:557
  23.2 2.2 %collective-permute-start.7 = (f32[1,32,2048]{2,1,0:T(8,128)S(1)}, f32[1,32,2048]{2,1,0:T(8,128)S(1)}, u32[]{:S(2)}, u32[]{:S(2)}) collective-permute-start(f32[1,32,2048]{2,1,0:T(8,128)S(1)} %get-tuple-element.82), channel_id=1, source_target_pairs={{0,28},{4,8},{8,4},{12,16},{16,12},{20,24},{24,20},{28,0},{1,29},{... | collective-permute-start | bytes 786440 | tf_op jit(solution)/shard_map/ppermute | solution.py:558
  25.4 2.1 %local_step.3 = (f32[2,32,1024]{2,1,0:T(8,128)S(1)}, f32[2,32,1024]{2,1,0:T(8,128)S(1)}) custom-call(s32[640]{0:T(1024)S(4)} %plan.1.plan_ref, bf16[160,128,256]{2,1,0:T(8,128)(2,1)S(1)} %prep.1.tiles_ref, f32[2,32,1024]{2,1,0:T(8,128)S(1)} %left_first.2.refs_0_.refs_2_, f32[2,32,1024]{2,1,0:T(8,128)S(1)} %get-tuple-element.78.refs_1_.refs_3_, ...), custom_call_target="tpu_custom_call" | custom-call | flops 671088640 | bytes 1572864 | tf_op jit(solution)/shard_map/local_step/pallas_call | solution.py:42
  28.5 4.0 %collective-permute-done.7.far_ref = f32[1,32,2048]{2,1,0:T(8,128)S(1)} collective-permute-done((f32[1,32,2048]{2,1,0:T(8,128)S(1)}, f32[1,32,2048]{2,1,0:T(8,128)S(1)}, u32[]{:S(2)}, u32[]{:S(2)}) %collective-permute-start.7) | collective-permute-done | bytes 262176 | tf_op jit(solution)/shard_map/ppermute | solution.py:558
  35.7 1.6 %collective-permute-start.10 = (f32[1,32,2048]{2,1,0:T(8,128)S(1)}, f32[1,32,2048]{2,1,0:T(8,128)S(1)}, u32[]{:S(2)}, u32[]{:S(2)}) collective-permute-start(f32[1,32,2048]{2,1,0:T(8,128)S(1)} %get-tuple-element.87), channel_id=1, source_target_pairs={{0,28},{4,8},{8,4},{12,16},{16,12},{20,24},{24,20},{28,0},{1,29},{... | collective-permute-start | bytes 786440 | tf_op jit(solution)/shard_map/ppermute | solution.py:558
  37.3 1.9 %collective-permute-start.11 = (f32[2,32,1024]{2,1,0:T(8,128)S(1)}, f32[2,32,1024]{2,1,0:T(8,128)S(1)}, u32[]{:S(2)}, u32[]{:S(2)}) collective-permute-start(f32[2,32,1024]{2,1,0:T(8,128)S(1)} %get-tuple-element.84.refs_0_), channel_id=1, source_target_pairs={{1,0},{2,1},{3,2},{0,3},{5,4},{6,5},{7,6},{4,7},{9,8},{10,9},{11,1... | collective-permute-start | bytes 786440 | tf_op jit(solution)/shard_map/ppermute | solution.py:557
  39.2 2.1 %local_gram.1 = (f32[2,32,1024]{2,1,0:T(8,128)S(1)}, f32[2,32,1024]{2,1,0:T(8,128)S(1)}) custom-call(s32[640]{0:T(1024)S(4)} %plan.1.plan_ref, bf16[160,128,256]{2,1,0:T(8,128)(2,1)S(1)} %prep.1.tiles_ref, f32[2,32,1024]{2,1,0:T(8,128)S(1)} %get-tuple-element.84.refs_0_, f32[2,32,1024]{2,1,0:T(8,128)S(1)} %right_step.3.refs_0_.refs_1_, ...), custom_call_target="tpu_custom_call" | custom-call | flops 671088640 | bytes 1572864 | tf_op jit(solution)/shard_map/local_gram/pallas_call | solution.py:42
  41.3 3.0 %collective-permute-done.8.halo_ref = f32[2,32,1024]{2,1,0:T(8,128)S(1)} collective-permute-done((f32[2,32,1024]{2,1,0:T(8,128)S(1)}, f32[2,32,1024]{2,1,0:T(8,128)S(1)}, u32[]{:S(2)}, u32[]{:S(2)}) %collective-permute-start.8) | collective-permute-done | bytes 262176 | tf_op jit(solution)/shard_map/ppermute | solution.py:557
  45.7 2.2 %collective-permute-start.12 = (f32[2,32,1024]{2,1,0:T(8,128)S(1)}, f32[2,32,1024]{2,1,0:T(8,128)S(1)}, u32[]{:S(2)}, u32[]{:S(2)}) collective-permute-start(f32[2,32,1024]{2,1,0:T(8,128)S(1)} %left_gram.1.refs_0_.refs_2_.left_ref), channel_id=1, source_target_pairs={{1,0},{2,1},{3,2},{0,3},{5,4},{6,5},{7,6},{4,7},{9,8},{10,9},{11,1... | collective-permute-start | bytes 786440 | tf_op jit(solution)/shard_map/ppermute | solution.py:557
  52.6 2.1 %local_first.3 = (f32[2,32,1024]{2,1,0:T(8,128)S(1)}, f32[2,32,1024]{2,1,0:T(8,128)S(1)}) custom-call(s32[640]{0:T(1024)S(4)} %plan.1.plan_ref, bf16[160,128,256]{2,1,0:T(8,128)(2,1)S(1)} %prep.1.tiles_ref, f32[2,32,1024]{2,1,0:T(8,128)S(1)} %left_gram.1.refs_0_.refs_2_.left_ref, f32[2,32,1024]{2,1,0:T(8,128)S(1)} %get-tuple-element.90.refs_1_.refs_3_.right_ref), custom_call_target="tpu_custom_call" | custom-call | flops 671088640 | bytes 1572864 | tf_op jit(solution)/shard_map/local_first/pallas_call | solution.py:42
  56.4 3.1 %collective-permute-done.14 = f32[8,128]{1,0:T(8,128)S(1)} collective-permute-done((f32[8,128]{1,0:T(8,128)S(1)}, f32[8,128]{1,0:T(8,128)S(1)}, u32[]{:S(2)}, u32[]{:S(2)}) %collective-permute-start.14) | collective-permute-done | bytes 4128 | tf_op jit(solution)/shard_map/ppermute | solution.py:503
  62.3 2.2 %collective-permute-start.20 = (f32[1,32,2048]{2,1,0:T(8,128)S(1)}, f32[1,32,2048]{2,1,0:T(8,128)S(1)}, u32[]{:S(2)}, u32[]{:S(2)}) collective-permute-start(f32[1,32,2048]{2,1,0:T(8,128)S(1)} %get-tuple-element.107), channel_id=1, source_target_pairs={{0,28},{4,8},{8,4},{12,16},{16,12},{20,24},{24,20},{28,0},{1,29},{... | collective-permute-start | bytes 786440 | tf_op jit(solution)/shard_map/ppermute | solution.py:558
  64.5 2.0 %collective-permute-start.22 = (f32[2,32,1024]{2,1,0:T(8,128)S(1)}, f32[2,32,1024]{2,1,0:T(8,128)S(1)}, u32[]{:S(2)}, u32[]{:S(2)}) collective-permute-start(f32[2,32,1024]{2,1,0:T(8,128)S(1)} %get-tuple-element.101.refs_0_.refs_2_), channel_id=1, source_target_pairs={{1,0},{2,1},{3,2},{0,3},{5,4},{6,5},{7,6},{4,7},{9,8},{10,9},{11,1... | collective-permute-start | bytes 786440 | tf_op jit(solution)/shard_map/ppermute | solution.py:557
  66.5 2.1 %local_step.4 = (f32[2,32,1024]{2,1,0:T(8,128)S(1)}, f32[2,32,1024]{2,1,0:T(8,128)S(1)}) custom-call(s32[640]{0:T(1024)S(4)} %plan.1.plan_ref, bf16[160,128,256]{2,1,0:T(8,128)(2,1)S(1)} %prep.1.tiles_ref, f32[2,32,1024]{2,1,0:T(8,128)S(1)} %get-tuple-element.101.refs_0_.refs_2_, f32[2,32,1024]{2,1,0:T(8,128)S(1)} %right_first.3.refs_0_.refs_1_.refs_3_, ...), custom_call_target="tpu_custom_call" | custom-call | flops 671088640 | bytes 1572864 | tf_op jit(solution)/shard_map/local_step/pallas_call | solution.py:42
  69.8 2.5 %collective-permute-done.21 = f32[8,128]{1,0:T(8,128)S(1)} collective-permute-done((f32[8,128]{1,0:T(8,128)S(1)}, f32[8,128]{1,0:T(8,128)S(1)}, u32[]{:S(2)}, u32[]{:S(2)}) %collective-permute-start.21) | collective-permute-done | bytes 4128 | tf_op jit(solution)/shard_map/ppermute | solution.py:503
  73.1 4.7 %collective-permute-start.23 = (f32[2,32,1024]{2,1,0:T(8,128)S(1)}, f32[2,32,1024]{2,1,0:T(8,128)S(1)}, u32[]{:S(2)}, u32[]{:S(2)}) collective-permute-start(f32[2,32,1024]{2,1,0:T(8,128)S(1)} %left_step.4.refs_0_), channel_id=1, source_target_pairs={{1,0},{2,1},{3,2},{0,3},{5,4},{6,5},{7,6},{4,7},{9,8},{10,9},{11,1... | collective-permute-start | bytes 786440 | tf_op jit(solution)/shard_map/ppermute | solution.py:557
  78.8 2.1 %local_step.5 = (f32[2,32,1024]{2,1,0:T(8,128)S(1)}, f32[2,32,1024]{2,1,0:T(8,128)S(1)}) custom-call(s32[640]{0:T(1024)S(4)} %plan.1.plan_ref, bf16[160,128,256]{2,1,0:T(8,128)(2,1)S(1)} %prep.1.tiles_ref, f32[2,32,1024]{2,1,0:T(8,128)S(1)} %left_step.4.refs_0_, f32[2,32,1024]{2,1,0:T(8,128)S(1)} %get-tuple-element.112.refs_1_, ...), custom_call_target="tpu_custom_call" | custom-call | flops 671088640 | bytes 1572864 | tf_op jit(solution)/shard_map/local_step/pallas_call | solution.py:42
  81.4 5.9 %collective-permute-done.24 = f32[8,128]{1,0:T(8,128)S(1)} collective-permute-done((f32[8,128]{1,0:T(8,128)S(1)}, f32[8,128]{1,0:T(8,128)S(1)}, u32[]{:S(2)}, u32[]{:S(2)}) %collective-permute-start.24) | collective-permute-done | bytes 4128 | tf_op jit(solution)/shard_map/ppermute | solution.py:503
  88.1 2.5 %collective-permute-start.28 = (f32[2,32,1024]{2,1,0:T(8,128)S(1)}, f32[2,32,1024]{2,1,0:T(8,128)S(1)}, u32[]{:S(2)}, u32[]{:S(2)}) collective-permute-start(f32[2,32,1024]{2,1,0:T(8,128)S(1)} %right_step.5.refs_0_.refs_1_.refs_2_), channel_id=1, source_target_pairs={{0,1},{1,2},{2,3},{3,0},{4,5},{5,6},{6,7},{7,4},{8,9},{9,10},{10,1... | collective-permute-start | bytes 786440 | tf_op jit(solution)/shard_map/ppermute | solution.py:557
  91.8 2.0 %collective-permute-start.30 = (f32[2,32,1024]{2,1,0:T(8,128)S(1)}, f32[2,32,1024]{2,1,0:T(8,128)S(1)}, u32[]{:S(2)}, u32[]{:S(2)}) collective-permute-start(f32[2,32,1024]{2,1,0:T(8,128)S(1)} %get-tuple-element.123.refs_0_.refs_1_), channel_id=1, source_target_pairs={{1,0},{2,1},{3,2},{0,3},{5,4},{6,5},{7,6},{4,7},{9,8},{10,9},{11,1... | collective-permute-start | bytes 786440 | tf_op jit(solution)/shard_map/ppermute | solution.py:557
  93.8 2.1 %local_image.1 = (f32[2,32,1024]{2,1,0:T(8,128)S(1)}, f32[2,32,1024]{2,1,0:T(8,128)S(1)}) custom-call(s32[640]{0:T(1024)S(4)} %plan.1.plan_ref, bf16[160,128,256]{2,1,0:T(8,128)(2,1)S(1)} %prep.1.tiles_ref, f32[2,32,1024]{2,1,0:T(8,128)S(1)} %get-tuple-element.123.refs_0_.refs_1_, f32[2,32,1024]{2,1,0:T(8,128)S(1)} %right_step.5.refs_0_.refs_1_.refs_2_), custom_call_target="tpu_custom_call" | custom-call | flops 671088640 | bytes 1572864 | tf_op jit(solution)/shard_map/local_image/pallas_call | solution.py:42
  96.6 6.9 %collective-permute-done.29 = f32[8,128]{1,0:T(8,128)S(1)} collective-permute-done((f32[8,128]{1,0:T(8,128)S(1)}, f32[8,128]{1,0:T(8,128)S(1)}, u32[]{:S(2)}, u32[]{:S(2)}) %collective-permute-start.29) | collective-permute-done | bytes 4128 | tf_op jit(solution)/shard_map/ppermute | solution.py:503
  105.7 2.2 %right_image.1 = (f32[2,32,1024]{2,1,0:T(8,128)S(1)}, f32[2,32,2048]{2,1,0:T(8,128)S(1)}, f32[16,128]{1,0:T(8,128)S(1)}) custom-call(s32[640]{0:T(1024)S(4)} %plan.1.plan_ref, bf16[160,128,256]{2,1,0:T(8,128)(2,1)S(1)} %prep.1.tiles_ref, f32[2,32,1024]{2,1,0:T(8,128)S(1)} %get-tuple-element.130.part_ref, ...), custom_call_target="tpu_custom_call", output_to_operand_aliasing={{0}: (2, {})} | custom-call | flops 134217728 | bytes 1572864 | tf_op jit(solution)/shard_map/right_image/pallas_call | solution.py:42
  110.0 2.3 %collective-permute-start.33 = (f32[16,128]{1,0:T(8,128)S(1)}, f32[16,128]{1,0:T(8,128)S(1)}, u32[]{:S(2)}, u32[]{:S(2)}) collective-permute-start(f32[16,128]{1,0:T(8,128)S(1)} %get-tuple-element.134), channel_id=1, source_target_pairs={{0,1},{1,0},{2,3},{3,2},{4,5},{5,4},{6,7},{7,6},{8,9},{9,8},{10,11... | collective-permute-start | bytes 24584 | tf_op jit(solution)/shard_map/ppermute | solution.py:503
  115.3 2.0 %collective-permute-start.39 = (f32[16,128]{1,0:T(8,128)S(1)}, f32[16,128]{1,0:T(8,128)S(1)}, u32[]{:S(2)}, u32[]{:S(2)}) collective-permute-start(f32[16,128]{1,0:T(8,128)S(1)} %add.53), channel_id=1, source_target_pairs={{0,24},{4,28},{8,16},{12,20},{16,8},{20,12},{24,0},{28,4},{1,25},{... | collective-permute-start | bytes 24584 | tf_op jit(solution)/shard_map/ppermute | solution.py:503
  121.5 2.5 %close.1 = (f32[2,32,2048]{2,1,0:T(8,128)}, f32[32,32]{1,0:T(8,128)}) custom-call(f32[16,128]{1,0:T(8,128)S(1)} %add_add_fusion.sums_ref, f32[2,32,2048]{2,1,0:T(8,128)S(1)} %get-tuple-element.135.y_ref), custom_call_target="tpu_custom_call" | custom-call | flops 8388608 | bytes 1048576 | tf_op jit(solution)/shard_map/close/pallas_call | solution.py:42
  (88 shorter events, 36.2 us)
Async XLA Ops:
  2.4 17.3 %collective-permute-start = (f32[2,32,1024]{2,1,0:T(8,128)S(1)}, f32[2,32,1024]{2,1,0:T(8,128)S(1)}, u32[]{:S(2)}, u32[]{:S(2)}) collective-permute-start(f32[2,32,1024]{2,1,0:T(8,128)S(1)} %get-tuple-element.72.refs_1_.refs_3_), channel_id=1, source_target_pairs={{0,1},{1,2},{2,3},{3,0},{4,5},{5,6},{6,7},{7,4},{8,9},{9,10},{10,1... | collective-permute-start | bytes 786440 | tf_op jit(solution)/shard_map/ppermute | solution.py:557
  5.5 14.3 %collective-permute-start.1 = (f32[1,32,2048]{2,1,0:T(8,128)S(1)}, f32[1,32,2048]{2,1,0:T(8,128)S(1)}, u32[]{:S(2)}, u32[]{:S(2)}) collective-permute-start(f32[1,32,2048]{2,1,0:T(8,128)S(1)} %get-tuple-element.74), channel_id=1, source_target_pairs={{0,4},{4,0},{8,12},{12,8},{16,20},{20,16},{24,28},{28,24},{1,5},{5... | collective-permute-start | bytes 786440 | tf_op jit(solution)/shard_map/ppermute | solution.py:559
  5.5 14.3 %collective-permute-start.2 = (f32[1,32,2048]{2,1,0:T(8,128)S(1)}, f32[1,32,2048]{2,1,0:T(8,128)S(1)}, u32[]{:S(2)}, u32[]{:S(2)}) collective-permute-start(f32[1,32,2048]{2,1,0:T(8,128)S(1)} %get-tuple-element.75), channel_id=1, source_target_pairs={{0,28},{4,8},{8,4},{12,16},{16,12},{20,24},{24,20},{28,0},{1,29},{... | collective-permute-start | bytes 786440 | tf_op jit(solution)/shard_map/ppermute | solution.py:558
  8.0 14.3 %collective-permute-start.3 = (f32[2,32,1024]{2,1,0:T(8,128)S(1)}, f32[2,32,1024]{2,1,0:T(8,128)S(1)}, u32[]{:S(2)}, u32[]{:S(2)}) collective-permute-start(f32[2,32,1024]{2,1,0:T(8,128)S(1)} %get-tuple-element.71.refs_0_.refs_2_), channel_id=1, source_target_pairs={{1,0},{2,1},{3,2},{0,3},{5,4},{6,5},{7,6},{4,7},{9,8},{10,9},{11,1... | collective-permute-start | bytes 786440 | tf_op jit(solution)/shard_map/ppermute | solution.py:557
  20.5 8.0 %collective-permute-start.4 = (f32[2,32,1024]{2,1,0:T(8,128)S(1)}, f32[2,32,1024]{2,1,0:T(8,128)S(1)}, u32[]{:S(2)}, u32[]{:S(2)}) collective-permute-start(f32[2,32,1024]{2,1,0:T(8,128)S(1)} %left_first.2.refs_0_.refs_2_), channel_id=1, source_target_pairs={{1,0},{2,1},{3,2},{0,3},{5,4},{6,5},{7,6},{4,7},{9,8},{10,9},{11,1... | collective-permute-start | bytes 786440 | tf_op jit(solution)/shard_map/ppermute | solution.py:557
  23.1 5.4 %collective-permute-start.6 = (f32[1,32,2048]{2,1,0:T(8,128)S(1)}, f32[1,32,2048]{2,1,0:T(8,128)S(1)}, u32[]{:S(2)}, u32[]{:S(2)}) collective-permute-start(f32[1,32,2048]{2,1,0:T(8,128)S(1)} %get-tuple-element.81), channel_id=1, source_target_pairs={{0,4},{4,0},{8,12},{12,8},{16,20},{20,16},{24,28},{28,24},{1,5},{5... | collective-permute-start | bytes 786440 | tf_op jit(solution)/shard_map/ppermute | solution.py:559
  23.2 9.3 %collective-permute-start.7 = (f32[1,32,2048]{2,1,0:T(8,128)S(1)}, f32[1,32,2048]{2,1,0:T(8,128)S(1)}, u32[]{:S(2)}, u32[]{:S(2)}) collective-permute-start(f32[1,32,2048]{2,1,0:T(8,128)S(1)} %get-tuple-element.82), channel_id=1, source_target_pairs={{0,28},{4,8},{8,4},{12,16},{16,12},{20,24},{24,20},{28,0},{1,29},{... | collective-permute-start | bytes 786440 | tf_op jit(solution)/shard_map/ppermute | solution.py:558
  25.4 9.4 %collective-permute-start.5 = (f32[2,32,1024]{2,1,0:T(8,128)S(1)}, f32[2,32,1024]{2,1,0:T(8,128)S(1)}, u32[]{:S(2)}, u32[]{:S(2)}) collective-permute-start(f32[2,32,1024]{2,1,0:T(8,128)S(1)} %get-tuple-element.78.refs_1_.refs_3_), channel_id=1, source_target_pairs={{0,1},{1,2},{2,3},{3,0},{4,5},{5,6},{6,7},{7,4},{8,9},{9,10},{10,1... | collective-permute-start | bytes 786440 | tf_op jit(solution)/shard_map/ppermute | solution.py:557
  33.2 11.1 %collective-permute-start.8 = (f32[2,32,1024]{2,1,0:T(8,128)S(1)}, f32[2,32,1024]{2,1,0:T(8,128)S(1)}, u32[]{:S(2)}, u32[]{:S(2)}) collective-permute-start(f32[2,32,1024]{2,1,0:T(8,128)S(1)} %right_step.3.refs_0_.refs_1_), channel_id=1, source_target_pairs={{0,1},{1,2},{2,3},{3,0},{4,5},{5,6},{6,7},{7,4},{8,9},{9,10},{10,1... | collective-permute-start | bytes 786440 | tf_op jit(solution)/shard_map/ppermute | solution.py:557
  35.6 8.7 %collective-permute-start.9 = (f32[1,32,2048]{2,1,0:T(8,128)S(1)}, f32[1,32,2048]{2,1,0:T(8,128)S(1)}, u32[]{:S(2)}, u32[]{:S(2)}) collective-permute-start(f32[1,32,2048]{2,1,0:T(8,128)S(1)} %get-tuple-element.86), channel_id=1, source_target_pairs={{0,4},{4,0},{8,12},{12,8},{16,20},{20,16},{24,28},{28,24},{1,5},{5... | collective-permute-start | bytes 786440 | tf_op jit(solution)/shard_map/ppermute | solution.py:559
  35.7 9.3 %collective-permute-start.10 = (f32[1,32,2048]{2,1,0:T(8,128)S(1)}, f32[1,32,2048]{2,1,0:T(8,128)S(1)}, u32[]{:S(2)}, u32[]{:S(2)}) collective-permute-start(f32[1,32,2048]{2,1,0:T(8,128)S(1)} %get-tuple-element.87), channel_id=1, source_target_pairs={{0,28},{4,8},{8,4},{12,16},{16,12},{20,24},{24,20},{28,0},{1,29},{... | collective-permute-start | bytes 786440 | tf_op jit(solution)/shard_map/ppermute | solution.py:558
  37.3 11.8 %collective-permute-start.11 = (f32[2,32,1024]{2,1,0:T(8,128)S(1)}, f32[2,32,1024]{2,1,0:T(8,128)S(1)}, u32[]{:S(2)}, u32[]{:S(2)}) collective-permute-start(f32[2,32,1024]{2,1,0:T(8,128)S(1)} %get-tuple-element.84.refs_0_), channel_id=1, source_target_pairs={{1,0},{2,1},{3,2},{0,3},{5,4},{6,5},{7,6},{4,7},{9,8},{10,9},{11,1... | collective-permute-start | bytes 786440 | tf_op jit(solution)/shard_map/ppermute | solution.py:557
  45.7 13.8 %collective-permute-start.12 = (f32[2,32,1024]{2,1,0:T(8,128)S(1)}, f32[2,32,1024]{2,1,0:T(8,128)S(1)}, u32[]{:S(2)}, u32[]{:S(2)}) collective-permute-start(f32[2,32,1024]{2,1,0:T(8,128)S(1)} %left_gram.1.refs_0_.refs_2_.left_ref), channel_id=1, source_target_pairs={{1,0},{2,1},{3,2},{0,3},{5,4},{6,5},{7,6},{4,7},{9,8},{10,9},{11,1... | collective-permute-start | bytes 786440 | tf_op jit(solution)/shard_map/ppermute | solution.py:557
  50.4 9.2 %collective-permute-start.16 = (f32[1,32,2048]{2,1,0:T(8,128)S(1)}, f32[1,32,2048]{2,1,0:T(8,128)S(1)}, u32[]{:S(2)}, u32[]{:S(2)}) collective-permute-start(f32[1,32,2048]{2,1,0:T(8,128)S(1)} %get-tuple-element.98), channel_id=1, source_target_pairs={{0,4},{4,0},{8,12},{12,8},{16,20},{20,16},{24,28},{28,24},{1,5},{5... | collective-permute-start | bytes 786440 | tf_op jit(solution)/shard_map/ppermute | solution.py:559
  50.4 9.5 %collective-permute-start.17 = (f32[1,32,2048]{2,1,0:T(8,128)S(1)}, f32[1,32,2048]{2,1,0:T(8,128)S(1)}, u32[]{:S(2)}, u32[]{:S(2)}) collective-permute-start(f32[1,32,2048]{2,1,0:T(8,128)S(1)} %get-tuple-element.99), channel_id=1, source_target_pairs={{0,28},{4,8},{8,4},{12,16},{16,12},{20,24},{24,20},{28,0},{1,29},{... | collective-permute-start | bytes 786440 | tf_op jit(solution)/shard_map/ppermute | solution.py:558
  52.0 9.4 %collective-permute-start.15 = (f32[2,32,1024]{2,1,0:T(8,128)S(1)}, f32[2,32,1024]{2,1,0:T(8,128)S(1)}, u32[]{:S(2)}, u32[]{:S(2)}) collective-permute-start(f32[2,32,1024]{2,1,0:T(8,128)S(1)} %get-tuple-element.90.refs_1_.refs_3_.right_ref), channel_id=1, source_target_pairs={{0,1},{1,2},{2,3},{3,0},{4,5},{5,6},{6,7},{7,4},{8,9},{9,10},{10,1... | collective-permute-start | bytes 786440 | tf_op jit(solution)/shard_map/ppermute | solution.py:557
  60.8 11.5 %collective-permute-start.18 = (f32[2,32,1024]{2,1,0:T(8,128)S(1)}, f32[2,32,1024]{2,1,0:T(8,128)S(1)}, u32[]{:S(2)}, u32[]{:S(2)}) collective-permute-start(f32[2,32,1024]{2,1,0:T(8,128)S(1)} %right_first.3.refs_0_.refs_1_.refs_3_), channel_id=1, source_target_pairs={{0,1},{1,2},{2,3},{3,0},{4,5},{5,6},{6,7},{7,4},{8,9},{9,10},{10,1... | collective-permute-start | bytes 786440 | tf_op jit(solution)/shard_map/ppermute | solution.py:557
  62.2 10.1 %collective-permute-start.19 = (f32[1,32,2048]{2,1,0:T(8,128)S(1)}, f32[1,32,2048]{2,1,0:T(8,128)S(1)}, u32[]{:S(2)}, u32[]{:S(2)}) collective-permute-start(f32[1,32,2048]{2,1,0:T(8,128)S(1)} %get-tuple-element.106), channel_id=1, source_target_pairs={{0,4},{4,0},{8,12},{12,8},{16,20},{20,16},{24,28},{28,24},{1,5},{5... | collective-permute-start | bytes 786440 | tf_op jit(solution)/shard_map/ppermute | solution.py:559
  62.3 10.0 %collective-permute-start.20 = (f32[1,32,2048]{2,1,0:T(8,128)S(1)}, f32[1,32,2048]{2,1,0:T(8,128)S(1)}, u32[]{:S(2)}, u32[]{:S(2)}) collective-permute-start(f32[1,32,2048]{2,1,0:T(8,128)S(1)} %get-tuple-element.107), channel_id=1, source_target_pairs={{0,28},{4,8},{8,4},{12,16},{16,12},{20,24},{24,20},{28,0},{1,29},{... | collective-permute-start | bytes 786440 | tf_op jit(solution)/shard_map/ppermute | solution.py:558
  64.5 13.3 %collective-permute-start.22 = (f32[2,32,1024]{2,1,0:T(8,128)S(1)}, f32[2,32,1024]{2,1,0:T(8,128)S(1)}, u32[]{:S(2)}, u32[]{:S(2)}) collective-permute-start(f32[2,32,1024]{2,1,0:T(8,128)S(1)} %get-tuple-element.101.refs_0_.refs_2_), channel_id=1, source_target_pairs={{1,0},{2,1},{3,2},{0,3},{5,4},{6,5},{7,6},{4,7},{9,8},{10,9},{11,1... | collective-permute-start | bytes 786440 | tf_op jit(solution)/shard_map/ppermute | solution.py:557
  73.1 14.3 %collective-permute-start.23 = (f32[2,32,1024]{2,1,0:T(8,128)S(1)}, f32[2,32,1024]{2,1,0:T(8,128)S(1)}, u32[]{:S(2)}, u32[]{:S(2)}) collective-permute-start(f32[2,32,1024]{2,1,0:T(8,128)S(1)} %left_step.4.refs_0_), channel_id=1, source_target_pairs={{1,0},{2,1},{3,2},{0,3},{5,4},{6,5},{7,6},{4,7},{9,8},{10,9},{11,1... | collective-permute-start | bytes 786440 | tf_op jit(solution)/shard_map/ppermute | solution.py:557
  78.6 8.8 %collective-permute-start.26 = (f32[1,32,2048]{2,1,0:T(8,128)S(1)}, f32[1,32,2048]{2,1,0:T(8,128)S(1)}, u32[]{:S(2)}, u32[]{:S(2)}) collective-permute-start(f32[1,32,2048]{2,1,0:T(8,128)S(1)} %get-tuple-element.120), channel_id=1, source_target_pairs={{0,4},{4,0},{8,12},{12,8},{16,20},{20,16},{24,28},{28,24},{1,5},{5... | collective-permute-start | bytes 786440 | tf_op jit(solution)/shard_map/ppermute | solution.py:559
  78.6 8.7 %collective-permute-start.27 = (f32[1,32,2048]{2,1,0:T(8,128)S(1)}, f32[1,32,2048]{2,1,0:T(8,128)S(1)}, u32[]{:S(2)}, u32[]{:S(2)}) collective-permute-start(f32[1,32,2048]{2,1,0:T(8,128)S(1)} %get-tuple-element.121), channel_id=1, source_target_pairs={{0,28},{4,8},{8,4},{12,16},{16,12},{20,24},{24,20},{28,0},{1,29},{... | collective-permute-start | bytes 786440 | tf_op jit(solution)/shard_map/ppermute | solution.py:558
  78.7 12.0 %collective-permute-start.25 = (f32[2,32,1024]{2,1,0:T(8,128)S(1)}, f32[2,32,1024]{2,1,0:T(8,128)S(1)}, u32[]{:S(2)}, u32[]{:S(2)}) collective-permute-start(f32[2,32,1024]{2,1,0:T(8,128)S(1)} %get-tuple-element.112.refs_1_), channel_id=1, source_target_pairs={{0,1},{1,2},{2,3},{3,0},{4,5},{5,6},{6,7},{7,4},{8,9},{9,10},{10,1... | collective-permute-start | bytes 786440 | tf_op jit(solution)/shard_map/ppermute | solution.py:557
  80.9 6.4 %collective-permute-start.24 = (f32[8,128]{1,0:T(8,128)S(1)}, f32[8,128]{1,0:T(8,128)S(1)}, u32[]{:S(2)}, u32[]{:S(2)}) collective-permute-start(f32[8,128]{1,0:T(8,128)S(1)} %add.47), channel_id=1, source_target_pairs={{0,1},{1,0},{2,3},{3,2},{4,5},{5,4},{6,7},{7,6},{8,9},{9,8},{10,11... | collective-permute-start | bytes 12296 | tf_op jit(solution)/shard_map/ppermute | solution.py:503
  88.1 16.8 %collective-permute-start.28 = (f32[2,32,1024]{2,1,0:T(8,128)S(1)}, f32[2,32,1024]{2,1,0:T(8,128)S(1)}, u32[]{:S(2)}, u32[]{:S(2)}) collective-permute-start(f32[2,32,1024]{2,1,0:T(8,128)S(1)} %right_step.5.refs_0_.refs_1_.refs_2_), channel_id=1, source_target_pairs={{0,1},{1,2},{2,3},{3,0},{4,5},{5,6},{6,7},{7,4},{8,9},{9,10},{10,1... | collective-permute-start | bytes 786440 | tf_op jit(solution)/shard_map/ppermute | solution.py:557
  91.5 13.5 %collective-permute-start.31 = (f32[1,32,2048]{2,1,0:T(8,128)S(1)}, f32[1,32,2048]{2,1,0:T(8,128)S(1)}, u32[]{:S(2)}, u32[]{:S(2)}) collective-permute-start(f32[1,32,2048]{2,1,0:T(8,128)S(1)} %get-tuple-element.131), channel_id=1, source_target_pairs={{0,4},{4,0},{8,12},{12,8},{16,20},{20,16},{24,28},{28,24},{1,5},{5... | collective-permute-start | bytes 786440 | tf_op jit(solution)/shard_map/ppermute | solution.py:559
  91.5 13.4 %collective-permute-start.32 = (f32[1,32,2048]{2,1,0:T(8,128)S(1)}, f32[1,32,2048]{2,1,0:T(8,128)S(1)}, u32[]{:S(2)}, u32[]{:S(2)}) collective-permute-start(f32[1,32,2048]{2,1,0:T(8,128)S(1)} %get-tuple-element.132), channel_id=1, source_target_pairs={{0,28},{4,8},{8,4},{12,16},{16,12},{20,24},{24,20},{28,0},{1,29},{... | collective-permute-start | bytes 786440 | tf_op jit(solution)/shard_map/ppermute | solution.py:558
  91.8 13.9 %collective-permute-start.30 = (f32[2,32,1024]{2,1,0:T(8,128)S(1)}, f32[2,32,1024]{2,1,0:T(8,128)S(1)}, u32[]{:S(2)}, u32[]{:S(2)}) collective-permute-start(f32[2,32,1024]{2,1,0:T(8,128)S(1)} %get-tuple-element.123.refs_0_.refs_1_), channel_id=1, source_target_pairs={{1,0},{2,1},{3,2},{0,3},{5,4},{6,5},{7,6},{4,7},{9,8},{10,9},{11,1... | collective-permute-start | bytes 786440 | tf_op jit(solution)/shard_map/ppermute | solution.py:557
  95.9 7.6 %collective-permute-start.29 = (f32[8,128]{1,0:T(8,128)S(1)}, f32[8,128]{1,0:T(8,128)S(1)}, u32[]{:S(2)}, u32[]{:S(2)}) collective-permute-start(f32[8,128]{1,0:T(8,128)S(1)} %add.48), channel_id=1, source_target_pairs={{0,2},{1,3},{2,0},{3,1},{4,6},{5,7},{6,4},{7,5},{8,10},{9,11},{10,... | collective-permute-start | bytes 12296 | tf_op jit(solution)/shard_map/ppermute | solution.py:503
  107.9 5.5 %collective-permute-start.35 = (f32[16,128]{1,0:T(8,128)S(1)}, f32[16,128]{1,0:T(8,128)S(1)}, u32[]{:S(2)}, u32[]{:S(2)}) collective-permute-start(f32[16,128]{1,0:T(8,128)S(1)} %get-tuple-element.134), channel_id=1, source_target_pairs={{0,3},{1,2},{2,1},{3,0},{4,7},{5,6},{6,5},{7,4},{8,11},{9,10},{10,... | collective-permute-start | bytes 24584 | tf_op jit(solution)/shard_map/ppermute | solution.py:503
  115.3 4.6 %collective-permute-start.39 = (f32[16,128]{1,0:T(8,128)S(1)}, f32[16,128]{1,0:T(8,128)S(1)}, u32[]{:S(2)}, u32[]{:S(2)}) collective-permute-start(f32[16,128]{1,0:T(8,128)S(1)} %add.53), channel_id=1, source_target_pairs={{0,24},{4,28},{8,16},{12,20},{16,8},{20,12},{24,0},{28,4},{1,25},{... | collective-permute-start | bytes 24584 | tf_op jit(solution)/shard_map/ppermute | solution.py:503
  (10 other events, 27.4 us)
